TPU v7x, 32 devices: a whole 2x2x4 slice. The times are simulated.
32 devices in a mesh: dp: 4 (over y, core), fsdp: 8 (over z, x).
Axes of the slice: x: 2, y: 2, z: 4, core: 2. Of those that a mesh axis runs over, the one named last changes fastest.
Arguments:
- series: float32 [4, 512, 720], P('dp', 'fsdp'), may hold values from -23 to 23
- observed: int32 [4, 512, 720], P('dp', 'fsdp'), may hold values 0 or 1
- targets: float32 [4, 512, 360], P('dp', 'fsdp'), may hold values from -23 to 23
- target_mask: int32 [4, 512, 360], P('dp', 'fsdp'), may hold values 0 or 1
- counts: int32 [4], P('dp'), may hold values from 64 to 512, as said below
- matrices: float32 [1703936], P(('dp', 'fsdp')), may hold values from -0.9375 to 0.9375
- feed_weights: float32 [1048576], P(('dp', 'fsdp')), may hold values from -0.3125 to 0.3125
- vectors: float32 [265216], P(('dp', 'fsdp')), may hold values from -5 to 5
- matrices_first: float32 [1703936], P(('dp', 'fsdp')), may hold values from -9.536743e-06 to 9.536743e-06
- matrices_second: float32 [1703936], P(('dp', 'fsdp')), may hold values from 3.313751e-14 to 1.3255004e-13
- feed_first: float32 [1048576], P(('dp', 'fsdp')), may hold values from -9.536743e-06 to 9.536743e-06
- feed_second: float32 [1048576], P(('dp', 'fsdp')), may hold values from 3.313751e-14 to 1.3255004e-13
- vectors_first: float32 [265216], P(('dp', 'fsdp')), may hold values from -3.8146973e-05 to 3.8146973e-05
- vectors_second: float32 [265216], P(('dp', 'fsdp')), may hold values from 5.302002e-13 to 2.1208007e-12
Outputs:
- grad_norm: float32 [], replicated
- new_matrices: float32 [1703936], P(('dp', 'fsdp'))
- new_matrices_first: float32 [1703936], P(('dp', 'fsdp'))
- new_matrices_second: float32 [1703936], P(('dp', 'fsdp'))
- new_feed: float32 [1048576], P(('dp', 'fsdp'))
- new_feed_first: float32 [1048576], P(('dp', 'fsdp'))
- new_feed_second: float32 [1048576], P(('dp', 'fsdp'))
- new_vectors: float32 [265216], P(('dp', 'fsdp'))
- new_vectors_first: float32 [265216], P(('dp', 'fsdp'))
- new_vectors_second: float32 [265216], P(('dp', 'fsdp'))
Inputs may be any that keep to these rules, and one draw needn't show every extreme that they name: A series' variables occupy slots 0 to counts - 1, the other slots are padding; some series fills all 512 slots.
All inputs are finite; a program needn't handle non-finite values. No bound on the sum of `observed` or of `target_mask` on one device may be relied on, other than what follows from the above.
Results may differ from a plain program's by a relative error of at most 0.0003.
The roundings to bfloat16 on the way count: a program that leaves them out, or rounds other values in their place, can miss the bound.
Values may be sent and summed in bfloat16 or wider, within the bound.
A program may use at most 512 MiB of HBM per device.

v0:
```python
import jax
import jax.numpy as jnp
from jax import lax
from jax.sharding import PartitionSpec as P

D = 256
HEADS = 8
FF = 512
ROUT = 10
SEGLEN = 12
PRED = 12
SEG = 60
NSQ = 26
NVEC = 1036


highest_score = lax.Precision.HIGHEST
negative = -1e30
norm_eps = 1e-05
beta_one = 0.9
beta_two = 0.999
adam_eps = 1e-08
weight_decay = 0.01
learn_rate = 0.2
clip_norm = 0.01
step_count = 10.0


def combined_all(part, axis, combine):
    gathered = jax.tree.map(lambda a: lax.all_gather(a, axis), part)

    def take(source):
        return jax.tree.map(lambda a: lax.dynamic_index_in_dim(a, source, 0, False), gathered)

    return lax.fori_loop(
        1, lax.axis_size(axis), lambda source, state: combine(state, take(source)), take(0)
    )


def dense(inputs, matrix):
    return jnp.einsum("...d,de->...e", inputs, matrix, precision=highest_score)


def layer_norm(inputs, norm_gain, norm_bias):
    center = inputs - jnp.mean(inputs, -1, keepdims=True)
    spread = jnp.mean(center * center, -1, keepdims=True)
    return center * lax.rsqrt(spread + norm_eps) * norm_gain + norm_bias


def feed_forward(inputs, w_up, b_up, w_down, b_down):
    return dense(jax.nn.gelu(dense(inputs, w_up) + b_up, approximate=False), w_down) + b_down


def split_heads(inputs):
    return inputs.reshape(inputs.shape[:-1] + (HEADS, inputs.shape[-1] // HEADS))


def unpack(matrices, feed_weights, vectors):
    square = matrices.reshape(NSQ, D, D)
    feed_pack = feed_weights.reshape(8, D * FF)
    return (
        square,
        feed_pack[:4].reshape(4, D, FF),
        feed_pack[4:].reshape(4, FF, D),
        vectors.reshape(NVEC, D),
    )


def gathered_params(gathered):
    return unpack(
        gathered[0].astype(jnp.float32),
        gathered[1].astype(jnp.float32),
        gathered[2].astype(jnp.float32),
    )


def layer_rows(params, layer_index):
    first_row = SEGLEN + 1 + SEG + 23 * layer_index
    return (
        params[0][12 * layer_index : 12 * layer_index + 12],
        params[3][first_row : first_row + 23],
    )


def router_rows(params, layer_index):
    first_row = SEGLEN + SEG + 52 + PRED + layer_index * SEG * ROUT
    segments = SEG // (1 + layer_index)
    return params[3][first_row : first_row + segments * ROUT].reshape(segments, ROUT, D)


def normalize(series, observed):
    seen_mask = observed.astype(jnp.float32)
    counted = jnp.maximum(jnp.sum(seen_mask, -1, keepdims=True), 1.0)
    series_mean = jnp.sum(seen_mask * series, -1, keepdims=True) / counted
    center = (series - series_mean) * seen_mask
    series_scale = jnp.sqrt(jnp.sum(center * center, -1, keepdims=True) / counted + norm_eps)
    return (center / series_scale, series_mean, series_scale)


def embed(normed, params):
    vector_rows = params[3]
    pieces = normed.reshape(normed.shape[0], SEG, SEGLEN)
    tokens = jnp.einsum("vsl,ld->vsd", pieces, vector_rows[:SEGLEN], precision=highest_score)
    return tokens + vector_rows[SEGLEN] + vector_rows[SEGLEN + 1 : SEGLEN + 1 + SEG]


def time_part(tokens, params, layer_index):
    layer_mats, layer_vecs = layer_rows(params, layer_index)
    score_factor = (D // HEADS) ** (-0.5)
    query_rows = split_heads(dense(tokens, layer_mats[0]) + layer_vecs[0])
    key_matrix = split_heads(dense(tokens, layer_mats[1]))
    value_rows = split_heads(dense(tokens, layer_mats[2]) + layer_vecs[1])
    attention_scores = (
        jnp.einsum("vqhe,vkhe->vhqk", query_rows, key_matrix, precision=highest_score)
        * score_factor
    )
    attention_weights = jax.nn.softmax(attention_scores, -1)
    mixed_output_rows = jnp.einsum(
        "vhqk,vkhe->vqhe", attention_weights, value_rows, precision=highest_score
    ).reshape(tokens.shape)
    hidden = layer_norm(
        tokens + dense(mixed_output_rows, layer_mats[3]) + layer_vecs[2],
        layer_vecs[3],
        layer_vecs[4],
    )
    branch = feed_forward(
        hidden,
        params[1][2 * layer_index],
        layer_vecs[5:7].reshape(-1),
        params[2][2 * layer_index],
        layer_vecs[7],
    )
    return layer_norm(hidden + branch, layer_vecs[8], layer_vecs[9])


def router_query(params, layer_index):
    layer_mats, layer_vecs = layer_rows(params, layer_index)
    return dense(router_rows(params, layer_index), layer_mats[4]) + layer_vecs[10]


def sender_keys(dimension_sender, params, layer_index):
    layer_mats, layer_vecs = layer_rows(params, layer_index)
    return (
        split_heads(dense(dimension_sender, layer_mats[5])),
        split_heads(dense(dimension_sender, layer_mats[6]) + layer_vecs[11]),
    )


def sender_scores(router_queries, key_matrix):
    score_factor = (D // HEADS) ** (-0.5)
    return (
        jnp.einsum(
            "srhe,vshe->srhv", split_heads(router_queries), key_matrix, precision=highest_score
        )
        * score_factor
    )


def sender_weigh(attention_scores, value_rows, present, top_score):
    attention_weights = jnp.where(present, jnp.exp(attention_scores - top_score[..., None]), 0.0)
    total_weight = jnp.sum(attention_weights, -1)
    weighted = jnp.einsum("srhv,vshe->srhe", attention_weights, value_rows, precision=highest_score)
    return (total_weight, weighted.reshape(weighted.shape[:2] + (D,)))


def sender_part(dimension_sender, router_queries, params, layer_index, present, top_score):
    key_matrix, value_rows = sender_keys(dimension_sender, params, layer_index)
    return sender_weigh(sender_scores(router_queries, key_matrix), value_rows, present, top_score)


def combine_partial(earlier, later):
    top_score = jnp.maximum(earlier[0], later[0])
    earlier_factor = jnp.exp(earlier[0] - top_score)
    later_factor = jnp.exp(later[0] - top_score)
    head_width = D // HEADS
    total_weight = earlier[1] * earlier_factor + later[1] * later_factor
    weighted = earlier[2] * jnp.repeat(earlier_factor, head_width, -1) + later[2] * jnp.repeat(
        later_factor, head_width, -1
    )
    return (top_score, total_weight, weighted)


def sender_stats(dimension_sender, router_queries, params, layer_index, present):
    key_matrix, value_rows = sender_keys(dimension_sender, params, layer_index)
    attention_scores = sender_scores(router_queries, key_matrix)
    local_top = jnp.max(jnp.where(present, attention_scores, negative), -1)
    total_weight, weighted = sender_weigh(attention_scores, value_rows, present, local_top)
    merged = combined_all((local_top, total_weight, weighted), "fsdp", combine_partial)
    return merged


def router_output(total_weight, weighted, params, layer_index):
    layer_mats, layer_vecs = layer_rows(params, layer_index)
    mixed_output_rows = weighted / jnp.repeat(total_weight, D // HEADS, -1)
    return dense(mixed_output_rows, layer_mats[7]) + layer_vecs[12]


def receive_part(dimension_sender, buffer, params, layer_index):
    layer_mats, layer_vecs = layer_rows(params, layer_index)
    score_factor = (D // HEADS) ** (-0.5)
    query_rows = split_heads(dense(dimension_sender, layer_mats[8]) + layer_vecs[13])
    key_matrix = split_heads(dense(buffer, layer_mats[9]))
    value_rows = split_heads(dense(buffer, layer_mats[10]) + layer_vecs[14])
    attention_scores = (
        jnp.einsum("tmiq,muiq->tmiu", query_rows, key_matrix, precision=highest_score)
        * score_factor
    )
    attention_weights = jax.nn.softmax(attention_scores, -1)
    mixed_output_rows = jnp.einsum(
        "cfkj,fjky->cfky", attention_weights, value_rows, precision=highest_score
    ).reshape(dimension_sender.shape)
    hidden = layer_norm(
        dimension_sender + dense(mixed_output_rows, layer_mats[11]) + layer_vecs[15],
        layer_vecs[16],
        layer_vecs[17],
    )
    branch = feed_forward(
        hidden,
        params[1][2 * layer_index + 1],
        layer_vecs[18:20].reshape(-1),
        params[2][2 * layer_index + 1],
        layer_vecs[20],
    )
    return layer_norm(hidden + branch, layer_vecs[21], layer_vecs[22])


def merge_segments(tokens, params):
    vector_rows = params[3]
    first_row = SEGLEN + SEG + 47
    paired = tokens.reshape(tokens.shape[0], tokens.shape[1] // 2, 2 * D)
    normed = layer_norm(
        paired,
        vector_rows[first_row : first_row + 2].reshape(-1),
        vector_rows[first_row + 2 : first_row + 4].reshape(-1),
    )
    return (
        dense(normed, jnp.concatenate([params[0][24], params[0][25]], 0))
        + vector_rows[first_row + 4]
    )


def head_loss(tokens, params, series_mean, series_scale, targets, kept_mask):
    first_row = SEGLEN + SEG + 52
    predicted = jnp.einsum(
        "vsd,pd->vsp", tokens, params[3][first_row : first_row + PRED], precision=highest_score
    )
    misfit = predicted.reshape(targets.shape) * series_scale + series_mean - targets
    return jnp.sum(kept_mask * misfit * misfit)


def sum_buffer(d_total, d_weighted):
    return lax.psum((d_total, d_weighted), "fsdp")


def sender_back(
    dimension_sender, router_queries, params, layer_index, present, top_score, d_total, d_weighted
):

    def local_part(dim_in, queries_in, params_in):
        return sender_part(dim_in, queries_in, params_in, layer_index, present, top_score)

    outputs, pull_part = jax.vjp(local_part, dimension_sender, router_queries, params)
    return pull_part((d_total, d_weighted))


def adam_update(weight, first_moment, second_moment, gradient):
    first_new = beta_one * first_moment + (1.0 - beta_one) * gradient
    second_new = beta_two * second_moment + (1.0 - beta_two) * gradient * gradient
    corrected = (
        first_new
        / (1.0 - beta_one**step_count)
        / (jnp.sqrt(second_new / (1.0 - beta_two**step_count)) + adam_eps)
    )
    return (weight - learn_rate * (corrected + weight_decay * weight), first_new, second_new)


def on_device(
    series,
    observed,
    targets,
    target_mask,
    counts,
    matrices,
    feed_weights,
    vectors,
    matrices_first,
    matrices_second,
    feed_first,
    feed_second,
    vectors_first,
    vectors_second,
):
    local_vars = series.shape[1]
    present = (
        lax.axis_index("fsdp") * local_vars + jnp.arange(local_vars, dtype=jnp.int32) < counts[0]
    )
    kept_mask = target_mask[0].astype(jnp.float32) * present[:, None].astype(jnp.float32)
    target_total = jnp.maximum(lax.psum(jnp.sum(kept_mask), ("dp", "fsdp")), 1.0)
    shards = (
        matrices.astype(jnp.bfloat16),
        feed_weights.astype(jnp.bfloat16),
        vectors.astype(jnp.bfloat16),
    )
    params = gathered_params(
        (
            lax.all_gather(shards[0], ("dp", "fsdp"), axis=0, tiled=True),
            lax.all_gather(shards[1], ("dp", "fsdp"), axis=0, tiled=True),
            lax.all_gather(shards[2], ("dp", "fsdp"), axis=0, tiled=True),
        )
    )
    normed, series_mean, series_scale = normalize(series[0], observed[0])
    target_rows = targets[0]

    def make_queries(params_in):
        return (router_query(params_in, 0), router_query(params_in, 1))

    def front(params_in):
        return time_part(embed(normed, params_in), params_in, 0)

    def middle(dim_one, total_one, weighted_one, params_in):
        tokens = receive_part(
            dim_one, router_output(total_one, weighted_one, params_in, 0), params_in, 0
        )
        return time_part(merge_segments(tokens, params_in), params_in, 1)

    def tail(dim_two, total_two, weighted_two, params_in):
        final_tokens = receive_part(
            dim_two, router_output(total_two, weighted_two, params_in, 1), params_in, 1
        )
        return head_loss(final_tokens, params_in, series_mean, series_scale, target_rows, kept_mask)

    query_rows = make_queries(params)
    dim_one = front(params)
    stats_one = sender_stats(dim_one, query_rows[0], params, 0, present)
    dim_two = middle(dim_one, stats_one[1], stats_one[2], params)
    stats_two = sender_stats(dim_two, query_rows[1], params, 1, present)
    params = gathered_params(
        (
            lax.all_gather(shards[0], ("dp", "fsdp"), axis=0, tiled=True),
            lax.all_gather(shards[1], ("dp", "fsdp"), axis=0, tiled=True),
            lax.all_gather(shards[2], ("dp", "fsdp"), axis=0, tiled=True),
        )
    )
    query_rows, pull_queries = jax.vjp(make_queries, params)
    dim_one, pull_front = jax.vjp(front, params)
    dim_two, pull_middle = jax.vjp(middle, dim_one, stats_one[1], stats_one[2], params)
    loss_sum, pull_tail = jax.vjp(tail, dim_two, stats_two[1], stats_two[2], params)
    d_dim_two, d_total_two, d_weighted_two, weight_grads = pull_tail(
        jnp.ones_like(loss_sum) / target_total
    )
    d_total_two, d_weighted_two = sum_buffer(d_total_two, d_weighted_two)
    d_dim_sent, d_query_two, grads_sent = sender_back(
        dim_two, query_rows[1], params, 1, present, stats_two[0], d_total_two, d_weighted_two
    )
    weight_grads = jax.tree.map(jnp.add, weight_grads, grads_sent)
    d_dim_one, d_total_one, d_weighted_one, grads_middle = pull_middle(d_dim_two + d_dim_sent)
    weight_grads = jax.tree.map(jnp.add, weight_grads, grads_middle)
    d_total_one, d_weighted_one = sum_buffer(d_total_one, d_weighted_one)
    d_dim_first, d_query_one, grads_first = sender_back(
        dim_one, query_rows[0], params, 0, present, stats_one[0], d_total_one, d_weighted_one
    )
    weight_grads = jax.tree.map(jnp.add, weight_grads, grads_first)
    grads_front = pull_front(d_dim_one + d_dim_first)[0]
    grads_query = pull_queries((d_query_one, d_query_two))[0]
    weight_grads = jax.tree.map(jnp.add, weight_grads, grads_front)
    weight_grads = jax.tree.map(jnp.add, weight_grads, grads_query)
    grad_feed = jnp.concatenate(
        [weight_grads[1].reshape(4, D * FF), weight_grads[2].reshape(4, D * FF)], 0
    )
    flat_square = weight_grads[0].reshape(-1)
    flat_feed = grad_feed.reshape(-1)
    flat_vector = weight_grads[3].reshape(-1)
    shard_grads = (
        lax.psum_scatter(flat_square, ("dp", "fsdp"), scatter_dimension=0, tiled=True),
        lax.psum_scatter(flat_feed, ("dp", "fsdp"), scatter_dimension=0, tiled=True),
        lax.psum_scatter(flat_vector, ("dp", "fsdp"), scatter_dimension=0, tiled=True),
    )
    square_sum = (
        jnp.sum(shard_grads[0] * shard_grads[0])
        + jnp.sum(shard_grads[1] * shard_grads[1])
        + jnp.sum(shard_grads[2] * shard_grads[2])
    )
    grad_norm = jnp.sqrt(lax.psum(square_sum, ("dp", "fsdp")))
    factor = clip_norm / jnp.maximum(grad_norm, clip_norm)
    mat_new = adam_update(matrices, matrices_first, matrices_second, shard_grads[0] * factor)
    feed_new = adam_update(feed_weights, feed_first, feed_second, shard_grads[1] * factor)
    vec_new = adam_update(vectors, vectors_first, vectors_second, shard_grads[2] * factor)
    return (
        grad_norm,
        mat_new[0],
        mat_new[1],
        mat_new[2],
        feed_new[0],
        feed_new[1],
        feed_new[2],
        vec_new[0],
        vec_new[1],
        vec_new[2],
    )


def solution(mesh):
    in_specs = (
        P("dp", "fsdp", None),
        P("dp", "fsdp", None),
        P("dp", "fsdp", None),
        P("dp", "fsdp", None),
        P("dp"),
        P(("dp", "fsdp")),
        P(("dp", "fsdp")),
        P(("dp", "fsdp")),
        P(("dp", "fsdp")),
        P(("dp", "fsdp")),
        P(("dp", "fsdp")),
        P(("dp", "fsdp")),
        P(("dp", "fsdp")),
        P(("dp", "fsdp")),
    )
    out_specs = (
        P(),
        P(("dp", "fsdp")),
        P(("dp", "fsdp")),
        P(("dp", "fsdp")),
        P(("dp", "fsdp")),
        P(("dp", "fsdp")),
        P(("dp", "fsdp")),
        P(("dp", "fsdp")),
        P(("dp", "fsdp")),
        P(("dp", "fsdp")),
    )
    return jax.shard_map(
        on_device, mesh=mesh, in_specs=in_specs, out_specs=out_specs, check_vma=False
    )
```

profile of v0, /device:TPU:0, one launch (start us, length us, event | category | flops | bytes accessed | tf_op | source)
XLA Modules:
  0.0 2755.9 jit_solution(16393530201087597004)
XLA Ops:
  17.0 125.6 %all-reduce.119.cloned.1.call-done = bf16[265216]{0:T(1024)(128)(2,1)} async-done(((bf16[265216]{0:T(1024)(128)(2,1)}), bf16[265216]{0:T(1024)(128)(2,1)}) %all-reduce.119.cloned.1.call-update) | async-done | bytes 530448
  153.0 51.1 %all-gather.11.cloned.1.call-done = bf16[1048576]{0:T(1024)(128)(2,1)} async-done(((bf16[32768]{0:T(1024)(128)(2,1)}), bf16[1048576]{0:T(1024)(128)(2,1)}) %all-gather.11.cloned.1.call-update) | async-done | bytes 2097168 | tf_op jit(solution)/shard_map/all_gather | solution.py:340
  207.1 59.6 %all-gather.9.cloned.1.call-done = bf16[1703936]{0:T(1024)(128)(2,1)} async-done(((bf16[53248]{0:T(1024)(128)(2,1)}), bf16[1703936]{0:T(1024)(128)(2,1)}) %all-gather.9.cloned.1.call-update) | async-done | bytes 3407888 | tf_op jit(solution)/shard_map/all_gather | solution.py:339
  311.2 29.5 %multiply_reduce_fusion.1 = (f32[64,8,60]{2,1,0:T(8,128)S(1)}, f32[64,8,60,60]{2,3,1,0:T(8,128)}) fusion(f32[64,60,8,32]{1,3,2,0:T(8,128)S(1)} %bitcast.801, f32[64,60,8,32]{1,3,2,0:T(8,128)S(1)} %fusion.28), kind=kOutput, calls=%fused_computation.23 | convolution fusion | flops 711444480 | bytes 15360000 | tf_op jit(solution)/shard_map/jvp(vqhe,vkhe->vhqk)/dot_general | solution.py:114
  340.7 10.4 fusion.22
  351.2 30.5 %fusion.67 = f32[64,8,32,60]{3,2,1,0:T(8,128)S(1)} fusion(f32[64,60,8,32]{1,3,2,0:T(8,128)} %bitcast.798, f32[64,8,60]{2,1,0:T(8,128)S(1)} %fusion.22, f32[64,8,60]{2,1,0:T(8,128)S(1)} %get-tuple-element.611, f32[64,8,60,60]{2,3,1,0:T(8,128)} %get-tuple-element.612), kind=kOutput, calls=%fused_computation.194 | convolution fusion | flops 713318400 | bytes 15482880 | tf_op jit(solution)/shard_map/jvp(vhqk,vkhe->vqhe)/dot_general | solution.py:118
  392.4 20.8 fusion.6
  447.4 15.3 fusion.103
  504.2 59.5 %all-gather.1 = f32[480,10,8]{1,2,0:T(8,128)S(1)} all-gather(f32[60,10,8]{1,2,0:T(8,128)S(1)} %fusion.73), channel_id=3, replica_groups=mesh['dp'=4,'fsdp'=8] {'fsdp'}, dimensions={0}, use_global_device_ids=true | all-gather | bytes 172800 | tf_op jit(solution)/shard_map/all_gather | solution.py:30
  565.4 46.9 %all-gather = f32[480,10,8]{1,2,0:T(8,128)S(1)} all-gather(f32[60,10,8]{1,2,0:T(8,128)S(1)} %get-tuple-element.617), channel_id=2, replica_groups=mesh['dp'=4,'fsdp'=8] {'fsdp'}, dimensions={0}, use_global_device_ids=true | all-gather | bytes 172800 | tf_op jit(solution)/shard_map/all_gather | solution.py:30
  615.5 21.4 while.38
  652.8 10.3 bitcast_reduce_fusion.6
  666.9 13.8 fusion.275
  690.2 20.5 fusion.7
  780.2 16.5 multiply_reduce_fusion.3
  803.4 12.2 fusion.167
  863.3 41.1 %psum.42 = f32[]{:T(128)} all-reduce(f32[]{:T(128)} %fusion.296), channel_id=1, replica_groups=mesh['dp'=4,'fsdp'=8] {'dp','fsdp'}, use_global_device_ids=true, to_apply=%region_40.41 | all-reduce | flops 1 | bytes 8 | tf_op jit(solution)/shard_map/psum | solution.py:298
  974.5 34.6 %all-gather.3 = f32[240,10,8]{1,2,0:T(8,128)} all-gather(f32[30,10,8]{1,2,0:T(8,128)S(1)} %fusion.172), channel_id=5, replica_groups=mesh['dp'=4,'fsdp'=8] {'fsdp'}, dimensions={0}, use_global_device_ids=true | all-gather | bytes 86400 | tf_op jit(solution)/shard_map/all_gather | solution.py:30
  1011.0 34.8 %all-gather.2 = f32[240,10,8]{1,2,0:T(8,128)} all-gather(f32[30,10,8]{1,2,0:T(8,128)S(1)} %get-tuple-element.634), channel_id=4, replica_groups=mesh['dp'=4,'fsdp'=8] {'fsdp'}, dimensions={0}, use_global_device_ids=true | all-gather | bytes 86400 | tf_op jit(solution)/shard_map/all_gather | solution.py:30
  1050.9 60.0 %while.39 = (s32[]{:T(128)}, f32[30,10,8]{2,0,1:T(8,128)}, f32[30,10,8]{2,0,1:T(8,128)}, f32[30,10,256]{2,0,1:T(8,128)}, f32[8,30,10,8]{2,3,1,0:T(8,128)}, /*ind...) while((s32[]{:T(128)}, f32[30,10,8]{2,0,1:T(8,128)}, ...), condition=%wide.region_32.33_spmd, body=%wide.region_31.32_spmd.sunk | while | flops 244805 | bytes 3552143 | solution.py:35
  1261.0 40.5 %psum.44 = f32[30,8,10]{1,0,2:T(8,128)S(1)} all-reduce(f32[30,8,10]{1,0,2:T(8,128)} %bitcast.872), channel_id=1, replica_groups=mesh['dp'=4,'fsdp'=8] {'fsdp'}, use_global_device_ids=true, to_apply=%region_48.49 | all-reduce | flops 2400 | bytes 19200 | tf_op jit(solution)/shard_map/psum | solution.py:252
  1304.3 47.1 %all-reduce.115.cloned.1.call-done = f32[30,8,32,10]{2,3,1,0:T(8,128)} async-done(((f32[30,8,32,10]{2,3,1,0:T(8,128)}), f32[30,8,32,10]{2,3,1,0:T(8,128)}) %all-reduce.115.cloned.1.call-update) | async-done | bytes 307216 | tf_op jit(solution)/shard_map/psum | solution.py:252
  1351.4 9.9 bitcast_reduce_fusion.4
  1442.9 21.4 multiply_reduce_fusion.2
  1464.3 18.1 convolution_bitcast_fusion.1
  1482.4 19.9 fusion.383
  1502.3 18.4 fusion.384
  1520.7 9.6 copy.483
  1530.3 9.4 convolution_bitcast_fusion.26
  1544.3 9.7 copy.488
  1567.9 9.4 copy.492
  1593.3 9.5 fusion.205
  1639.2 17.3 fusion.208
  1656.6 10.0 fusion.381
  1697.0 15.4 fusion.380
  1712.4 9.7 fusion.42
  1722.1 16.1 convolution_bitcast_fusion.4
  1738.3 15.4 bitcast_reduce_fusion.3
  1753.8 14.9 convolution_bitcast_fusion.21
  1809.1 36.2 %psum.46 = f32[60,8,10]{0,1,2:T(8,128)S(1)} all-reduce(f32[60,8,10]{0,1,2:T(8,128)S(1)} %bitcast.885), channel_id=1, replica_groups=mesh['dp'=4,'fsdp'=8] {'fsdp'}, use_global_device_ids=true, to_apply=%region_63.64 | all-reduce | flops 4800 | bytes 38400 | tf_op jit(solution)/shard_map/psum | solution.py:252
  1869.1 128.8 %all-reduce.117.cloned.1.call-done = f32[60,8,32,10]{2,3,1,0:T(8,128)} async-done(((f32[60,8,32,10]{2,3,1,0:T(8,128)}), f32[60,8,32,10]{2,3,1,0:T(8,128)}) %all-reduce.117.cloned.1.call-update) | async-done | bytes 614416 | tf_op jit(solution)/shard_map/psum | solution.py:252
  1997.8 11.2 multiply_multiply_fusion.14
  2009.1 16.7 fusion.375
  2025.8 13.7 fusion.395
  2039.5 15.0 bitcast_reduce_fusion.2
  2054.6 14.8 convolution_bitcast_fusion.19
  2077.7 15.0 convolution_bitcast_fusion.18
  2092.7 12.1 multiply_reduce_fusion.5
  2112.1 17.3 fusion.211
  2129.5 9.9 fusion.379
  2171.6 9.6 fusion.214
  2186.8 10.3 copy.528
  2197.1 37.1 %multiply_reduce_fusion = (f32[64,8,60]{2,1,0:T(8,128)S(1)}, f32[64,8,60,60]{2,3,1,0:T(8,128)}) fusion(f32[64,8,60]{2,1,0:T(8,128)S(1)} %copy-done.116, f32[64,8,60]{2,1,0:T(8,128)S(1)} %copy-done.98, f32[64,8,60,60]{2,3,1,0:T(8,128)} %get-tuple-element.612, f32[64,8,32,60]{3,2,1,0:T(8,128)} %copy.528, f32[64,60,8,32]{1,3,2,0:T(8,128)} %bitcast.799), kind=kOutput, calls=%fused_computation.21 | convolution fusion | flops 716974080 | bytes 22978560 | tf_op jit(solution)/shard_map/transpose(jvp(vhqk,vkhe->vqhe))/dot_general | solution.py:118
  2234.3 37.0 %fusion.337 = f32[64,8,60,32]{2,3,1,0:T(8,128)} fusion(f32[64,60,8,32]{1,3,2,0:T(8,128)} %bitcast.800, f32[64,8,60,60]{2,3,1,0:T(8,128)} %get-tuple-element.660, f32[64,8,60]{2,1,0:T(8,128)S(1)} %neg.120, f32[64,8,60]{2,1,0:T(8,128)S(1)} %copy-done.167, f32[64,8,60]{2,1,0:T(8,128)S(1)} %copy-done.98, f32[64,8,60,60]{2,3,1,0:T(8,128)} %get-tuple-element.612), kind=kOutput, calls=%fused_computation.610 | convolution fusion | flops 718848000 | bytes 22978560 | tf_op jit(solution)/shard_map/transpose(jvp(vqhe,vkhe->vhqk))/dot_general | solution.py:114
  2271.3 24.9 bitcast_reduce_fusion
  2296.2 31.8 %bitcast_reduce_fusion.1 = (f32[8,32]{1,0:T(8,128)S(1)}, f32[64,8,32,60]{3,2,1,0:T(8,128)}) fusion(f32[64,8,32,60]{3,2,1,0:T(8,128)} %copy.528, f32[64,8,60]{2,1,0:T(8,128)S(1)} %copy-done.167, f32[64,8,60]{2,1,0:T(8,128)S(1)} %copy-done.98, f32[64,8,60,60]{2,3,1,0:T(8,128)S(1)} %bitcast.782), kind=kOutput, calls=%fused_computation.27 | convolution fusion | flops 714301184 | bytes 15483904 | tf_op jit(solution)/shard_map/transpose(jvp(vhqk,vkhe->vqhe))/dot_general | solution.py:118
  2335.5 12.2 fusion.400
  2355.2 12.2 fusion.398
  2380.7 10.5 convolution_bitcast_fusion.15
  2405.8 10.4 convolution_bitcast_fusion.16
  2416.2 12.3 fusion.399
  2428.5 11.1 fusion.340
  2468.0 227.5 %all-reduce.121.cloned.1.call-done = (f32[1703936]{0:T(1024)}, f32[1048576]{0:T(1024)}, f32[265216]{0:T(1024)}) async-done(((f32[1703936]{0:T(1024)}, f32[1048576]{0:T(1024)}, f32[265216]{0:T(1024)}), (f32[1703936]{0:T(1024)}, f32[1048576]{0:T(1024)}, f32[265216]{0:T(1024)})) %all-reduce.121.cloned.1.call-update) | async-done | bytes 12070928
  2702.0 39.5 %psum.47 = f32[]{:T(128)} all-reduce(f32[]{:T(128)S(6)} %add.1144), channel_id=1, replica_groups=mesh['dp'=4,'fsdp'=8] {'dp','fsdp'}, use_global_device_ids=true, to_apply=%region_123.124 | all-reduce | flops 1 | bytes 8 | tf_op jit(solution)/shard_map/psum | solution.py:383
  (1353 shorter events, 997.8 us)
Async XLA Ops:
  7.2 135.4 %all-reduce.119.cloned.1.call-start = ((), (), s32[]{:S(2)}) async-start(), calls=%async_computation.6 | async-start | bytes 1060864
  9.4 194.6 %all-gather.11.cloned.1.call-start = ((), (), s32[]{:S(2)}) async-start(), calls=%async_computation.1 | async-start | bytes 2162688 | tf_op jit(solution)/shard_map/all_gather | solution.py:340
  11.1 255.7 %all-gather.9.cloned.1.call-start = ((), (), s32[]{:S(2)}) async-start(), calls=%async_computation | async-start | bytes 3514368 | tf_op jit(solution)/shard_map/all_gather | solution.py:339
  12.7 601.2 %all-gather.13.cloned.1.call-start = ((), (), s32[]{:S(2)}) async-start(), calls=%async_computation.2 | async-start | bytes 5898240 | tf_op jit(solution)/shard_map/all_gather | solution.py:30
  14.6 138.5 %copy-start.89 = (f32[64,60,12]{0,2,1:T(8,128)}, f32[64,60,12]{0,2,1:T(8,128)S(1)}, u32[]{:S(2)}) copy-start(f32[64,60,12]{0,2,1:T(8,128)S(1)} %convert_element_type.49) | copy-start | bytes 552964
  15.9 190.9 %copy-start.91 = (f32[64,60,12]{0,2,1:T(8,128)}, f32[64,60,12]{0,2,1:T(8,128)S(1)}, u32[]{:S(2)}) copy-start(f32[64,60,12]{0,2,1:T(8,128)S(1)} %squeeze.91) | copy-start | bytes 552964
  16.5 429.0 %copy-start.295 = (pred[64]{0:T(512)(128)(4,1)}, pred[64]{0:T(512)(128)(4,1)S(1)}, u32[]{:S(2)}) copy-start(pred[64]{0:T(512)(128)(4,1)S(1)} %get-tuple-element.516) | copy-start | bytes 196
  16.8 190.1 %copy-start.336 = (f32[64]{0:T(128)}, f32[64]{0:T(128)S(1)}, u32[]{:S(2)}) copy-start(f32[64]{0:T(128)S(1)} %maximum_divide_fusion) | copy-start | bytes 772
  17.0 189.8 %copy-start.341 = (f32[64]{0:T(128)}, f32[64]{0:T(128)S(1)}, u32[]{:S(2)}) copy-start(f32[64]{0:T(128)S(1)} %add_sqrt_fusion) | copy-start | bytes 772
  145.8 126.1 %copy-start.103 = (bf16[60,10,256]{2,1,0:T(8,128)(2,1)}, bf16[60,10,256]{2,1,0:T(8,128)(2,1)S(1)}, u32[]{:S(2)}) copy-start(bf16[60,10,256]{2,1,0:T(8,128)(2,1)S(1)} %reshape.1387) | copy-start | bytes 921604
  147.8 265.4 %copy-start.328 = (f32[512]{0:T(512)}, f32[512]{0:T(512)S(1)}, u32[]{:S(2)}) copy-start(f32[512]{0:T(512)S(1)} %get-tuple-element.585) | copy-start | bytes 6148
  149.3 263.9 %copy-start.300 = (f32[256]{0:T(256)}, f32[256]{0:T(256)S(1)}, u32[]{:S(2)}) copy-start(f32[256]{0:T(256)S(1)} %get-tuple-element.602) | copy-start | bytes 3076
  149.3 263.9 %copy-start.323 = (f32[256]{0:T(256)}, f32[256]{0:T(256)S(1)}, u32[]{:S(2)}) copy-start(f32[256]{0:T(256)S(1)} %get-tuple-element.603) | copy-start | bytes 3076
  149.3 281.9 %copy-start.277 = (f32[256]{0:T(256)}, f32[256]{0:T(256)S(1)}, u32[]{:S(2)}) copy-start(f32[256]{0:T(256)S(1)} %get-tuple-element.600) | copy-start | bytes 3076
  149.3 281.9 %copy-start.288 = (f32[256]{0:T(256)}, f32[256]{0:T(256)S(1)}, u32[]{:S(2)}) copy-start(f32[256]{0:T(256)S(1)} %get-tuple-element.601) | copy-start | bytes 3076
  206.9 206.3 %copy-start.164 = (bf16[512,256,1]{1,0,2:T(8,128)(2,1)}, bf16[512,256,1]{1,0,2:T(8,128)(2,1)S(1)}, u32[]{:S(2)}) copy-start(bf16[512,256,1]{1,0,2:T(8,128)(2,1)S(1)} %reshape.1460) | copy-start | bytes 786436
  207.1 185.3 %copy-start.162 = (bf16[256,512,1]{1,0,2:T(8,128)(2,1)}, bf16[256,512,1]{1,0,2:T(8,128)(2,1)S(1)}, u32[]{:S(2)}) copy-start(bf16[256,512,1]{1,0,2:T(8,128)(2,1)S(1)} %reshape.1459) | copy-start | bytes 786436
  268.0 21.7 copy-start.136
  271.3 148.8 %copy-start.138 = (bf16[256,256,1]{1,0,2:T(8,128)(2,1)}, bf16[256,256,1]{1,0,2:T(8,128)(2,1)S(1)}, u32[]{:S(2)}) copy-start(bf16[256,256,1]{1,0,2:T(8,128)(2,1)S(1)} %reshape.1464) | copy-start | bytes 393220
  311.2 29.5 %copy-start.28 = (f32[64,60,8,32]{1,3,2,0:T(8,128)}, f32[64,60,8,32]{1,3,2,0:T(8,128)S(1)}, u32[]{:S(2)}) copy-start(f32[64,60,8,32]{1,3,2,0:T(8,128)S(1)} %fusion.28) | copy-start | bytes 11796484
  351.1 30.5 %copy-start.166 = (f32[64,8,60]{2,1,0:T(8,128)}, f32[64,8,60]{2,1,0:T(8,128)S(1)}, u32[]{:S(2)}) copy-start(f32[64,8,60]{2,1,0:T(8,128)S(1)} %fusion.22) | copy-start | bytes 368644
  390.9 22.3 copy-start.6
  390.9 22.3 copy-start.117
  392.3 20.8 copy-start.249
  392.3 20.9 copy-start.131
  418.6 262.1 %copy-start.93 = (f32[64,60]{0,1:T(8,128)}, f32[64,60]{0,1:T(8,128)S(1)}, u32[]{:S(2)}) copy-start(f32[64,60]{0,1:T(8,128)S(1)} %broadcast_multiply_fusion.2) | copy-start | bytes 46084
  420.0 260.6 %copy-start.99 = (f32[64,60]{0,1:T(8,128)}, f32[64,60]{0,1:T(8,128)S(1)}, u32[]{:S(2)}) copy-start(f32[64,60]{0,1:T(8,128)S(1)} %fusion.299) | copy-start | bytes 46084
  467.4 581.7 %all-gather.15.cloned.1.call-start = ((), (), s32[]{:S(2)}) async-start(), calls=%async_computation.3 | async-start | bytes 2949120 | tf_op jit(solution)/shard_map/all_gather | solution.py:30
  615.5 22.7 copy-start.384
  688.7 22.2 copy-start.9
  688.7 22.1 copy-start.124
  690.2 20.7 copy-start.133
  743.8 78.4 %copy-start.17 = (f32[64,30,256]{2,0,1:T(8,128)}, f32[64,30,256]{2,0,1:T(8,128)S(1)}, u32[]{:S(2)}) copy-start(f32[64,30,256]{2,0,1:T(8,128)S(1)} %fusion.191) | copy-start | bytes 5898244
  860.8 52.6 %copy-start.313 = (bf16[3072]{0:T(1024)(128)(2,1)S(1)}, bf16[3072]{0:T(1024)(128)(2,1)}, u32[]{:S(2)}) copy-start(bf16[3072]{0:T(1024)(128)(2,1)} %get-tuple-element.586) | copy-start | bytes 18436
  862.5 488.9 %all-reduce.115.cloned.1.call-start = ((), (), s32[]{:S(2)}) async-start(), calls=%async_computation.4 | async-start | bytes 3932160 | tf_op jit(solution)/shard_map/psum | solution.py:252
  904.4 43.9 %copy-start.20 = (f32[60,10,256]{0,2,1:T(8,128)S(1)}, f32[60,10,256]{0,2,1:T(8,128)}, u32[]{:S(2)}) copy-start(f32[60,10,256]{0,2,1:T(8,128)} %copy-done.19) | copy-start | bytes 1843204
  971.9 75.7 %copy-start.113 = (f32[64,60,8]{0,2,1:T(8,128)S(1)}, f32[64,60,8]{0,2,1:T(8,128)}, u32[]{:S(2)}) copy-start(f32[64,60,8]{0,2,1:T(8,128)} %copy-done.112) | copy-start | bytes 368644
  971.9 76.4 %copy-start.194 = (f32[64,8,30]{2,1,0:T(8,128)S(1)}, f32[64,8,30]{2,1,0:T(8,128)}, u32[]{:S(2)}) copy-start(f32[64,8,30]{2,1,0:T(8,128)} %copy-done.193) | copy-start | bytes 184324
  1115.1 118.8 %copy-start.102 = (f32[30,10,256]{2,0,1:T(8,128)}, f32[30,10,256]{2,0,1:T(8,128)S(1)}, u32[]{:S(2)}) copy-start(f32[30,10,256]{2,0,1:T(8,128)S(1)} %convolution_add_fusion.14) | copy-start | bytes 921604
  1250.5 51.2 %copy-start.127 = (f32[30,10,256]{2,0,1:T(8,128)S(1)}, f32[30,10,256]{2,0,1:T(8,128)}, u32[]{:S(2)}) copy-start(f32[30,10,256]{2,0,1:T(8,128)} %copy-done.126) | copy-start | bytes 921604
  1250.6 747.3 %all-reduce.117.cloned.1.call-start = ((), (), s32[]{:S(2)}) async-start(), calls=%async_computation.5 | async-start | bytes 7864320 | tf_op jit(solution)/shard_map/psum | solution.py:252
  1304.3 57.0 %copy-start.283 = (f32[256]{0:T(256)S(1)}, f32[256]{0:T(256)}, u32[]{:S(2)}) copy-start(f32[256]{0:T(256)} %get-tuple-element.572) | copy-start | bytes 3076
  1304.3 57.0 %copy-start.294 = (f32[256]{0:T(256)S(1)}, f32[256]{0:T(256)}, u32[]{:S(2)}) copy-start(f32[256]{0:T(256)} %get-tuple-element.573) | copy-start | bytes 3076
  1442.9 21.4 copy-start.195
  1442.9 39.5 %slice-start.4 = ((s8[8388608]{0:T(1024)(128)(4,1)}), s8[4194304]{0:T(1024)(128)(4,1)S(1)}, s32[]{:S(2)}) async-start(s8[8388608]{0:T(1024)(128)(4,1)} %bitcast.784), calls=%async_computation.12 | async-start | bytes 8388608
  1697.0 25.1 slice-start.8
  1851.0 844.5 %all-reduce.121.cloned.1.call-start = ((), (), s32[]{:S(2)}) async-start(), calls=%async_computation.7 | async-start | bytes 24141824
  1861.5 136.3 %copy-start.205 = (f32[60,8,10]{2,1,0:T(8,128)S(1)}, f32[60,8,10]{2,1,0:T(8,128)}, u32[]{:S(2)}) copy-start(f32[60,8,10]{2,1,0:T(8,128)} %copy.520) | copy-start | bytes 57604
  1861.5 136.3 %copy-start.207 = (f32[60,8,10]{2,1,0:T(8,128)S(1)}, f32[60,8,10]{2,1,0:T(8,128)}, u32[]{:S(2)}) copy-start(f32[60,8,10]{2,1,0:T(8,128)} %copy.519) | copy-start | bytes 57604
  1861.5 136.3 %copy-start.299 = (pred[64]{0:T(512)(128)(4,1)S(1)}, pred[64]{0:T(512)(128)(4,1)}, u32[]{:S(2)}) copy-start(pred[64]{0:T(512)(128)(4,1)} %copy-done.295) | copy-start | bytes 196
  2197.1 37.2 %copy-start.167 = (f32[64,8,60]{2,1,0:T(8,128)S(1)}, f32[64,8,60]{2,1,0:T(8,128)}, u32[]{:S(2)}) copy-start(f32[64,8,60]{2,1,0:T(8,128)} %copy-done.166) | copy-start | bytes 368644
  2197.1 74.2 %slice-start = ((s8[16777216]{0:T(1024)(128)(4,1)}), s8[4194304]{0:T(1024)(128)(4,1)S(1)}, s32[]{:S(2)}) async-start(s8[16777216]{0:T(1024)(128)(4,1)} %bitcast.781), calls=%async_computation.8 | async-start | bytes 8388608
  2197.1 74.2 %slice-start.1 = ((s8[16777216]{0:T(1024)(128)(4,1)}), s8[4194304]{0:T(1024)(128)(4,1)S(1)}, s32[]{:S(2)}) async-start(s8[16777216]{0:T(1024)(128)(4,1)} %bitcast.781), calls=%async_computation.9 | async-start | bytes 8388608
  2197.1 74.2 %slice-start.2 = ((s8[16777216]{0:T(1024)(128)(4,1)}), s8[4194304]{0:T(1024)(128)(4,1)S(1)}, s32[]{:S(2)}) async-start(s8[16777216]{0:T(1024)(128)(4,1)} %bitcast.781), calls=%async_computation.10 | async-start | bytes 8388608
  2234.3 37.1 %slice-start.3 = ((s8[16777216]{0:T(1024)(128)(4,1)}), s8[4194304]{0:T(1024)(128)(4,1)S(1)}, s32[]{:S(2)}) async-start(s8[16777216]{0:T(1024)(128)(4,1)} %bitcast.781), calls=%async_computation.11 | async-start | bytes 8388608
  2467.9 274.4 %copy-start.208 = (f32[53248]{0:T(1024)S(1)}, f32[53248]{0:T(1024)}, u32[]{:S(2)}) copy-start(f32[53248]{0:T(1024)} %param.23) | copy-start | bytes 638980
  2467.9 274.5 %copy-start.264 = (f32[53248]{0:T(1024)S(1)}, f32[53248]{0:T(1024)}, u32[]{:S(2)}) copy-start(f32[53248]{0:T(1024)} %param.26) | copy-start | bytes 638980
  2467.9 274.5 %copy-start.265 = (f32[53248]{0:T(1024)S(1)}, f32[53248]{0:T(1024)}, u32[]{:S(2)}) copy-start(f32[53248]{0:T(1024)} %param.27) | copy-start | bytes 638980
  2467.9 276.3 %copy-start.234 = (f32[32768]{0:T(1024)S(1)}, f32[32768]{0:T(1024)}, u32[]{:S(2)}) copy-start(f32[32768]{0:T(1024)} %param.24) | copy-start | bytes 393220
  2467.9 276.3 %copy-start.275 = (f32[32768]{0:T(1024)S(1)}, f32[32768]{0:T(1024)}, u32[]{:S(2)}) copy-start(f32[32768]{0:T(1024)} %param.28) | copy-start | bytes 393220
  2467.9 276.3 %copy-start.276 = (f32[32768]{0:T(1024)S(1)}, f32[32768]{0:T(1024)}, u32[]{:S(2)}) copy-start(f32[32768]{0:T(1024)} %param.29) | copy-start | bytes 393220
  2467.9 278.0 %copy-start.274 = (f32[8288]{0:T(1024)S(1)}, f32[8288]{0:T(1024)}, u32[]{:S(2)}) copy-start(f32[8288]{0:T(1024)} %param.25) | copy-start | bytes 99460
  2467.9 278.0 %copy-start.302 = (f32[8288]{0:T(1024)S(1)}, f32[8288]{0:T(1024)}, u32[]{:S(2)}) copy-start(f32[8288]{0:T(1024)} %param.30) | copy-start | bytes 99460
  2467.9 278.0 %copy-start.303 = (f32[8288]{0:T(1024)S(1)}, f32[8288]{0:T(1024)}, u32[]{:S(2)}) copy-start(f32[8288]{0:T(1024)} %param.31) | copy-start | bytes 99460
  (364 other events, 2644.7 us)
Sparse Core Ops, SparseCore 0:
  13.3 129.2 all-reduce.118
  146.6 57.4 all-gather.10
  208.0 58.6 all-gather.8
  467.5 134.9 all-gather.12
  862.6 54.7 all-gather.14
  1250.7 100.6 all-reduce.114
  1851.1 146.6 all-reduce.116
  2468.1 227.3 all-reduce.120
where the time goes:
time: 2770 us; the launch traced here: 2760 us
  matrix products  1140 us (41%)
  waiting for transfers between devices  640 us (23%)
  local copies, waits for them, and re-layouts  416 us (15%)
  blocking collectives  333 us (12%)
  other arithmetic  200 us (7%)
    dot_general x99, matrix products, dense(): return jnp.einsum('...d,de->...e', inputs, matrix, precision=highest_score)  589 us
    unnamed x10, waiting for transfers between devices  353 us
    psum x2, waiting for transfers between devices, sum_buffer(): return lax.psum((d_total, d_weighted), 'fsdp')  176 us
    all_gather x4, blocking collectives, combined_all(): gathered = jax.tree.map(lambda a: lax.all_gather(a, axis), part)  176 us
    dot_general x6, matrix products, time_part(): jnp.einsum('vhqk,vkhe->vqhe', attention_weights, value_rows, precision=hi...  151 us
    dot_general x6, matrix products, time_part(): jnp.einsum('vqhe,vkhe->vhqk', query_rows, key_matrix, precision=highest_s...  146 us
    psum x2, blocking collectives, sum_buffer(): return lax.psum((d_total, d_weighted), 'fsdp')  76.7 us
    reshape x15, local copies, waits for them, and re-layouts, split_heads(): inputs.reshape(inputs.shape[:-1] + (HEADS, inputs.shape[-1] // HEADS))  74.6 us
  transfers between devices with their start and end apart: 8, of which 6 were waited for; matrix products, arithmetic and copies ran while one was open for 6% of the time, Pallas kernels for 0%

commit v1 on v0

v1 whole, which is shorter than its diff:
```python
import functools
import jax
import jax.numpy as jnp
from jax import lax
from jax.experimental import pallas as pl
from jax.experimental.pallas import tpu as pltpu
from jax.sharding import PartitionSpec as P

D = 256
HEADS = 8
FF = 512
ROUT = 10
RPAD = 16
SEGLEN = 12
PRED = 12
PPAD = 16
SEG = 60
NSQ = 26
NVEC = 1036
HALF = 128
VB = 8

BF = jnp.bfloat16
F32 = jnp.float32
SCALE = (D // HEADS) ** (-0.5)
negative = -1e30
norm_eps = 1e-05
beta_one = 0.9
beta_two = 0.999
adam_eps = 1e-08
weight_decay = 0.01
learn_rate = 0.2
clip_norm = 0.01
step_count = 10.0
VMEM_LIMIT = 60 << 20


def split2(x):
    hi = x.astype(BF)
    return hi, (x - hi.astype(F32)).astype(BF)


def dots(a, b, ca, cb):
    return lax.dot_general(a, b, (((ca,), (cb,)), ((), ())), preferred_element_type=F32)


def mmw(x2, w):
    return dots(x2[0], w, 1, 0) + dots(x2[1], w, 1, 0)


def mmwt(x2, w):
    return dots(x2[0], w, 1, 1) + dots(x2[1], w, 1, 1)


def rows2(a2):
    return jnp.concatenate([a2[0], a2[1]], 0)


def nn3(a2, b2):
    m = a2[0].shape[0]
    both = dots(rows2(a2), b2[0], 1, 0)
    return both[:m] + both[m:] + dots(a2[0], b2[1], 1, 0)


def nt3(a2, b2):
    m = a2[0].shape[0]
    both = dots(rows2(a2), b2[0], 1, 1)
    return both[:m] + both[m:] + dots(a2[0], b2[1], 1, 1)


def tn3(a2, b2):
    n = b2[0].shape[1]
    both = dots(a2[0], jnp.concatenate([b2[0], b2[1]], 1), 0, 0)
    return both[:, :n] + both[:, n:] + dots(a2[1], b2[0], 0, 0)


def norm_fwd(z, gain, bias):
    center = z - jnp.mean(z, -1, keepdims=True)
    inv = lax.rsqrt(jnp.mean(center * center, -1, keepdims=True) + norm_eps)
    unit = center * inv
    return unit * gain + bias, unit, inv


def norm_bwd(dy, unit, inv, gain):
    t = dy * gain
    return inv * (t - jnp.mean(t, -1, keepdims=True) - unit * jnp.mean(t * unit, -1, keepdims=True))


def colsum(x):
    return jnp.sum(x.reshape(x.shape[0] // 8, 8, x.shape[1]), 0)


def gelu_cdf(u):
    return 0.5 + 0.5 * lax.erf(u * 0.7071067811865476)


def gelu_slope(u, cdf):
    return cdf + u * (jnp.exp(-0.5 * u * u) * 0.3989422804014327)


def halves(x):
    return x[:, :HALF], x[:, HALF:]


def lane_head(rows):
    return lax.broadcasted_iota(jnp.int32, (rows, HALF), 1) // 32


def spread_heads(x, zero):
    head = lane_head(x.shape[0])
    return jnp.concatenate([jnp.where(head == h, x, zero) for h in range(4)], 0)


def gather_heads(x, group):
    head = lane_head(group)
    out = x[3 * group :]
    for h in range(3):
        out = jnp.where(head == h, x[h * group : (h + 1) * group], out)
    return out


def ones_heads(group, count):
    row = lax.broadcasted_iota(jnp.int32, (4 * group, HALF), 0)
    lane = lax.broadcasted_iota(jnp.int32, (4 * group, HALF), 1)
    return jnp.where((row // group == lane // 32) & (row % group < count), 1.0, 0.0).astype(BF)


def group_max(s, group, count):
    lane = lax.broadcasted_iota(jnp.int32, (s.shape[0], HALF), 1)
    outs = []
    for t in range(s.shape[1] // HALF):
        part = s[:, t * HALF : (t + 1) * HALF]
        top = None
        for g in range(HALF // group):
            here = (lane // group == g)
            best = jnp.max(jnp.where((lane // group == g) & (lane % group < count), part, negative), -1, keepdims=True)
            top = jnp.broadcast_to(best, part.shape) if top is None else jnp.where(here, best, top)
        outs.append(jnp.where(lane % group < count, part - top, negative))
    return jnp.concatenate(outs, 1)


def time_attend(c, v, group, count, q_s, k_s, v_s, o_s, p_s, l_s):
    at = pl.ds(v, group, stride=VB)
    q2 = split2(q_s[c, at, :])
    k2 = split2(k_s[c, at, :])
    w2 = split2(v_s[c, at, :])
    zero = jnp.zeros((), BF)
    k_hi, k_lo = spread_heads(k2[0], zero), spread_heads(k2[1], zero)
    w_hi, w_lo = spread_heads(w2[0], zero), spread_heads(w2[1], zero)
    s = dots(jnp.concatenate(q2, 1), jnp.concatenate([k_hi, k_hi], 1), 1, 1) + dots(q2[0], k_lo, 1, 1)
    p = jnp.exp(group_max(s, group, count))
    p2 = split2(p)
    both = dots(rows2(p2), jnp.concatenate([w_hi, ones_heads(group, count)], 1), 1, 0)
    both = both[:group] + both[group:]
    total = both[:, HALF:]
    o_s[c, at, :] = (both[:, :HALF] + dots(p2[0], w_lo, 1, 0)) / total
    if p_s is not None:
        p_s[c, v] = p
        l_s[c, v] = total


def time_attend_back(c, v, group, count, q_s, k_s, v_s, o_s, p_s, l_s, do_s):
    at = pl.ds(v, group, stride=VB)
    q2 = split2(q_s[c, at, :])
    k2 = split2(k_s[c, at, :])
    w2 = split2(v_s[c, at, :])
    zero = jnp.zeros((), BF)
    k_hi, k_lo = spread_heads(k2[0], zero), spread_heads(k2[1], zero)
    w_hi, w_lo = spread_heads(w2[0], zero), spread_heads(w2[1], zero)
    d = do_s[c, at, :] / l_s[c, v]
    d2 = split2(d)
    e2 = split2(d * o_s[c, at, :])
    p = p_s[c, v]
    x2 = (jnp.concatenate([d2[0], e2[0]], 1), jnp.concatenate([d2[1], e2[1]], 1))
    both = dots(rows2(x2), jnp.concatenate([w_hi, -ones_heads(group, count)], 1), 1, 1)
    dp = both[:group] + both[group:] + dots(d2[0], w_lo, 1, 1)
    p2 = split2(p)
    s2 = split2(p * dp)
    both = dots(rows2(s2), k_hi, 1, 0)
    q_s[c, at, :] = both[:group] + both[group:] + dots(s2[0], k_lo, 1, 0)
    k_s[c, at, :] = gather_heads(tn3(s2, q2), group)
    v_s[c, at, :] = gather_heads(tn3(p2, d2), group)


def store_halves(ref, x):
    rows = x.shape[0]
    ref[0, :rows, :] = x[:, :HALF]
    ref[1, :rows, :] = x[:, HALF:]


def load_halves(ref, rows):
    return jnp.concatenate([ref[0, :rows, :], ref[1, :rows, :]], 1)


def zero_tail(ref, rows):
    tail = ref.shape[1] - rows
    ref[:, rows:, :] = jnp.zeros((2, tail, HALF), F32)


def time_forward(x, w, vec, count, group, q_s, k_s, v_s, o_s, p_s=None, l_s=None):
    rows = count * VB
    x2 = split2(x)
    store_halves(q_s, (mmw(x2, w["q"]) + vec[0:1]) * SCALE)
    store_halves(k_s, mmw(x2, w["k"]))
    store_halves(v_s, mmw(x2, w["v"]) + vec[1:2])
    for ref in (q_s, k_s, v_s):
        zero_tail(ref, rows)

    def one(v, carry):
        for c in range(2):
            time_attend(c, v, group, count, q_s, k_s, v_s, o_s, p_s, l_s)
        return carry

    lax.fori_loop(0, VB, one, 0)
    mixed = load_halves(o_s, rows)
    h, unit1, inv1 = norm_fwd(x + mmw(split2(mixed), w["o"]) + vec[2:3], vec[3:4], vec[4:5])
    bias_up = jnp.concatenate([vec[5:6], vec[6:7]], 1)
    u = mmw(split2(h), w["up"]) + bias_up
    cdf = gelu_cdf(u)
    z2 = h + mmw(split2(u * cdf), w["down"]) + vec[7:8]
    y, unit2, inv2 = norm_fwd(z2, vec[8:9], vec[9:10])
    return y, (x2, mixed, h, unit1, inv1, u, cdf, unit2, inv2)


def embed_block(pieces, emb, place):
    return mmw(split2(pieces), emb) + place


TIME_W = ("q", "k", "v", "o", "up", "down")


def time_fwd_kernel(first, count, group, *refs):
    if first:
        x_ref, emb_ref, place_ref = refs[:3]
        refs = refs[3:]
    else:
        x_ref = refs[0]
        refs = refs[1:]
    w = {name: refs[i][...] for i, name in enumerate(TIME_W)}
    vec_ref, y_ref, q_s, k_s, v_s, o_s = refs[6:]
    rows = count * VB
    if first:
        place = jnp.broadcast_to(place_ref[...], (count, VB, D)).reshape(rows, D)
        x = embed_block(x_ref[...].reshape(rows, 16), emb_ref[...], place)
    else:
        x = x_ref[...].reshape(rows, D)
    y, _ = time_forward(x, w, vec_ref[...], count, group, q_s, k_s, v_s, o_s)
    y_ref[...] = y.reshape(count, VB, D)


def whole(shape):
    return pl.BlockSpec(shape, lambda i: (0,) * len(shape))


def params_spec():
    return pltpu.CompilerParams(vmem_limit_bytes=VMEM_LIMIT)


def time_weight_specs():
    return [whole((D, D))] * 4 + [whole((D, FF)), whole((FF, D)), whole((24, D))]


def time_fwd(first, x, extra, weights, count):
    group = 64 if count > 32 else 32
    nv = x.shape[1]
    width = x.shape[2]
    specs = [pl.BlockSpec((count, VB, width), lambda i: (0, i, 0))]
    if first:
        specs += [whole((16, D)), whole((count, 1, D))]
    pad = group * VB
    return pl.pallas_call(
        functools.partial(time_fwd_kernel, first, count, group),
        grid=(nv // VB,),
        in_specs=specs + time_weight_specs(),
        out_specs=pl.BlockSpec((count, VB, D), lambda i: (0, i, 0)),
        out_shape=jax.ShapeDtypeStruct((count, nv, D), F32),
        scratch_shapes=[pltpu.VMEM((2, pad, HALF), F32)] * 4,
        compiler_params=params_spec(),
        name="time_fwd",
    )(x, *extra, *weights)


def time_bwd_kernel(first, count, group, *refs):
    if first:
        x_ref, emb_ref, place_ref = refs[:3]
        refs = refs[3:]
    else:
        x_ref = refs[0]
        refs = refs[1:]
    dy_ref = refs[0]
    w = {name: refs[1 + i][...] for i, name in enumerate(TIME_W)}
    vec_ref = refs[7]
    outs = refs[8:]
    n_out = 9 if first else 8
    g = dict(zip(TIME_W + ("rows",), outs[:7]))
    tail = outs[7:n_out]
    q_s, k_s, v_s, o_s, do_s, p_s, l_s = outs[n_out:]
    rows = count * VB
    step = pl.program_id(0)

    @pl.when(step == 0)
    def _():
        for ref in list(g.values()) + (list(tail) if first else []):
            ref[...] = jnp.zeros(ref.shape, F32)

    vec = vec_ref[...]
    if first:
        place = jnp.broadcast_to(place_ref[...], (count, VB, D)).reshape(rows, D)
        pieces = x_ref[...].reshape(rows, 16)
        x = embed_block(pieces, emb_ref[...], place)
    else:
        x = x_ref[...].reshape(rows, D)
    _, (x2, mixed, h, unit1, inv1, u, cdf, unit2, inv2) = time_forward(
        x, w, vec, count, group, q_s, k_s, v_s, o_s, p_s, l_s
    )
    dy = dy_ref[...].reshape(rows, D)
    g["rows"][8] += colsum(dy * unit2)
    g["rows"][9] += colsum(dy)
    dz2 = norm_bwd(dy, unit2, inv2, vec[8:9])
    g["rows"][7] += colsum(dz2)
    dz22 = split2(dz2)
    g["down"][...] += tn3(split2(u * cdf), dz22)
    du = mmwt(dz22, w["down"]) * gelu_slope(u, cdf)
    g["rows"][5] += colsum(du[:, :D])
    g["rows"][6] += colsum(du[:, D:])
    du2 = split2(du)
    g["up"][...] += tn3(split2(h), du2)
    dh = dz2 + mmwt(du2, w["up"])
    g["rows"][3] += colsum(dh * unit1)
    g["rows"][4] += colsum(dh)
    dz1 = norm_bwd(dh, unit1, inv1, vec[3:4])
    g["rows"][2] += colsum(dz1)
    dz12 = split2(dz1)
    g["o"][...] += tn3(split2(mixed), dz12)
    store_halves(do_s, mmwt(dz12, w["o"]))
    zero_tail(do_s, rows)

    def one(v, carry):
        for c in range(2):
            time_attend_back(c, v, group, count, q_s, k_s, v_s, o_s, p_s, l_s, do_s)
        return carry

    lax.fori_loop(0, VB, one, 0)
    dq = load_halves(q_s, rows) * SCALE
    g["rows"][0] += colsum(dq)
    dq2 = split2(dq)
    g["q"][...] += tn3(x2, dq2)
    dx = dz1 + mmwt(dq2, w["q"])
    dk2 = split2(load_halves(k_s, rows))
    g["k"][...] += tn3(x2, dk2)
    dx = dx + mmwt(dk2, w["k"])
    dv = load_halves(v_s, rows)
    g["rows"][1] += colsum(dv)
    dv2 = split2(dv)
    g["v"][...] += tn3(x2, dv2)
    dx = dx + mmwt(dv2, w["v"])
    if first:
        tail[0][...] += tn3(split2(pieces), split2(dx))
        tail[1][...] += dx
    else:
        tail[0][...] = dx.reshape(count, VB, D)


def time_bwd(first, x, extra, dy, weights, count):
    group = 64 if count > 32 else 32
    nv = x.shape[1]
    width = x.shape[2]
    pad = group * VB
    block = pl.BlockSpec((count, VB, D), lambda i: (0, i, 0))
    specs = [pl.BlockSpec((count, VB, width), lambda i: (0, i, 0))]
    if first:
        specs += [whole((16, D)), whole((count, 1, D))]
    grad_shapes = [(D, D)] * 4 + [(D, FF), (FF, D), (10, 8, D)]
    if first:
        grad_shapes += [(16, D), (count * VB, D)]
    out_specs = [whole(s) for s in grad_shapes]
    out_shape = [jax.ShapeDtypeStruct(s, F32) for s in grad_shapes]
    if not first:
        out_specs.append(block)
        out_shape.append(jax.ShapeDtypeStruct((count, nv, D), F32))
    return pl.pallas_call(
        functools.partial(time_bwd_kernel, first, count, group),
        grid=(nv // VB,),
        in_specs=specs + [block] + time_weight_specs(),
        out_specs=out_specs,
        out_shape=out_shape,
        scratch_shapes=[pltpu.VMEM((2, pad, HALF), F32)] * 5
        + [pltpu.VMEM((2, VB, group, 4 * group), F32), pltpu.VMEM((2, VB, group, HALF), F32)],
        compiler_params=params_spec(),
        name="time_bwd",
    )(x, *extra, dy, *weights)

SB_ROWS = 64


def head_rows():
    sub = lax.broadcasted_iota(jnp.int32, (8, D), 0)
    lane = lax.broadcasted_iota(jnp.int32, (8, D), 1)
    return jnp.where(sub == lane // 32, 1.0, 0.0).astype(F32)


def spread_rows(x):
    wide = jnp.broadcast_to(x[:, None, :], (RPAD, HEADS, D)) * head_rows()[None]
    return wide.reshape(RPAD * HEADS, D)


def gather_rows(x):
    return jnp.sum(x.reshape(RPAD, HEADS, D) * head_rows()[None], 1)


def valid_lane(rows):
    return lax.broadcasted_iota(jnp.int32, (rows, HALF), 1) < ROUT * HEADS


def router_reduce(x, op):
    for shift in (8, 16, 32, 64):
        x = op(x, pltpu.roll(x, shift, 1))
    return x


def merge_rows(y, pairs, vec):
    wide = y.reshape(pairs, 2, SB_ROWS, D)
    wide = jnp.concatenate([wide[:, 0].reshape(pairs * SB_ROWS, D), wide[:, 1].reshape(pairs * SB_ROWS, D)], 1)
    gain = jnp.concatenate([vec[0:1], vec[1:2]], 1)
    bias = jnp.concatenate([vec[2:3], vec[3:4]], 1)
    return norm_fwd(wide, gain, bias) + (gain,)


RECV_W = ("so", "rk", "rv", "rq", "ro", "up", "down")


def recv_forward(send, o_rows, w, vec, q_s, mix_s, p_s, kb_s, vb_s):
    sb = send.shape[0] // SB_ROWS
    send2 = split2(send)
    o2 = split2(o_rows)
    buf = mmw(o2, w["so"]) + vec[12:13]
    buf2 = split2(buf)
    kb_s[...] = mmw(buf2, w["rk"])
    vb_s[...] = mmw(buf2, w["rv"]) + vec[14:15]
    q_s[...] = (mmw(send2, w["rq"]) + vec[13:14]) * SCALE

    def one(s, carry):
        at = pl.ds(pl.multiple_of(s * SB_ROWS, SB_ROWS), SB_ROWS)
        ar = pl.ds(pl.multiple_of(s * RPAD, RPAD), RPAD)
        k2 = split2(spread_rows(kb_s[ar, :]))
        v2 = split2(spread_rows(vb_s[ar, :]))
        sc = jnp.where(valid_lane(SB_ROWS), nt3(split2(q_s[at, :]), k2), negative)
        p = jnp.exp(sc - router_reduce(sc, jnp.maximum))
        p = p / router_reduce(p, jnp.add)
        p_s[at, :] = p
        mix_s[at, :] = nn3(split2(p), v2)
        return carry

    lax.fori_loop(0, sb, one, 0)
    mixed = mix_s[...]
    g, unit3, inv3 = norm_fwd(send + mmw(split2(mixed), w["ro"]) + vec[15:16], vec[16:17], vec[17:18])
    u = mmw(split2(g), w["up"]) + jnp.concatenate([vec[18:19], vec[19:20]], 1)
    cdf = gelu_cdf(u)
    y, unit4, inv4 = norm_fwd(g + mmw(split2(u * cdf), w["down"]) + vec[20:21], vec[21:22], vec[22:23])
    return y, (send2, o2, buf2, mixed, g, unit3, inv3, u, cdf, unit4, inv4)


RECV_G = RECV_W + ("rows",)


def recv_backward(dy, kept, w, vec, g, q_s, do_s, p_s, kb_s, vb_s):
    send2, o2, buf2, mixed, gg, unit3, inv3, u, cdf, unit4, inv4 = kept
    sb = dy.shape[0] // SB_ROWS
    rows = g["rows"]
    rows[9] += colsum(dy * unit4)
    rows[10] += colsum(dy)
    dz4 = norm_bwd(dy, unit4, inv4, vec[21:22])
    rows[8] += colsum(dz4)
    dz42 = split2(dz4)
    g["down"][...] += tn3(split2(u * cdf), dz42)
    du = mmwt(dz42, w["down"]) * gelu_slope(u, cdf)
    rows[6] += colsum(du[:, :D])
    rows[7] += colsum(du[:, D:])
    du2 = split2(du)
    g["up"][...] += tn3(split2(gg), du2)
    dg = dz4 + mmwt(du2, w["up"])
    rows[4] += colsum(dg * unit3)
    rows[5] += colsum(dg)
    dz3 = norm_bwd(dg, unit3, inv3, vec[16:17])
    rows[3] += colsum(dz3)
    dz32 = split2(dz3)
    g["ro"][...] += tn3(split2(mixed), dz32)
    do_s[...] = mmwt(dz32, w["ro"])

    def one(s, carry):
        at = pl.ds(pl.multiple_of(s * SB_ROWS, SB_ROWS), SB_ROWS)
        ar = pl.ds(pl.multiple_of(s * RPAD, RPAD), RPAD)
        k2 = split2(spread_rows(kb_s[ar, :]))
        v2 = split2(spread_rows(vb_s[ar, :]))
        q2 = split2(q_s[at, :])
        d2 = split2(do_s[at, :])
        p = p_s[at, :]
        dp = nt3(d2, v2)
        ds = p * (dp - router_reduce(p * dp, jnp.add))
        s2 = split2(ds)
        kb_s[ar, :] = gather_rows(tn3(s2, q2))
        vb_s[ar, :] = gather_rows(tn3(split2(p), d2))
        q_s[at, :] = nn3(s2, k2)
        return carry

    lax.fori_loop(0, sb, one, 0)
    dq = q_s[...] * SCALE
    rows[1] += colsum(dq)
    dq2 = split2(dq)
    g["rq"][...] += tn3(send2, dq2)
    dsend = dz3 + mmwt(dq2, w["rq"])
    dk2 = split2(kb_s[...])
    dv = vb_s[...]
    dv2 = split2(dv)
    rows[2] += colsum(dv)
    g["rk"][...] += tn3(buf2, dk2)
    g["rv"][...] += tn3(buf2, dv2)
    dbuf = mmwt(dk2, w["rk"]) + mmwt(dv2, w["rv"])
    rows[0] += colsum(dbuf)
    dbuf2 = split2(dbuf)
    g["so"][...] += tn3(o2, dbuf2)
    return dsend, mmwt(dbuf2, w["so"])


def recv_scratch(sb):
    return [
        pltpu.VMEM((sb * SB_ROWS, D), F32),
        pltpu.VMEM((sb * SB_ROWS, D), F32),
        pltpu.VMEM((sb * SB_ROWS, HALF), F32),
        pltpu.VMEM((sb * RPAD, D), F32),
        pltpu.VMEM((sb * RPAD, D), F32),
    ]


def recv_weight_specs():
    return [whole((D, D))] * 5 + [whole((D, FF)), whole((FF, D)), whole((24, D))]


def seg_block(sb, rows=SB_ROWS, width=D):
    return pl.BlockSpec((sb, rows, width), lambda i: (i, 0, 0))


def recv_fwd_kernel(sb, send_ref, o_ref, *refs):
    w = {n: refs[i][...] for i, n in enumerate(RECV_W)}
    vec_ref, mvec_ref, mw_ref, out_ref = refs[7:11]
    q_s, mix_s, p_s, kb_s, vb_s = refs[11:]
    y, _ = recv_forward(
        send_ref[...].reshape(sb * SB_ROWS, D), o_ref[...].reshape(sb * RPAD, D), w, vec_ref[...], q_s, mix_s, p_s, kb_s, vb_s
    )
    mvec = mvec_ref[...]
    wide, _, _, _ = merge_rows(y, sb // 2, mvec)
    out_ref[...] = (mmw(split2(wide), mw_ref[...]) + mvec[4:5]).reshape(sb // 2, SB_ROWS, D)


def recv_fwd(send, o, weights, mvec, mw, sb):
    n = send.shape[0]
    return pl.pallas_call(
        functools.partial(recv_fwd_kernel, sb),
        grid=(n // sb,),
        in_specs=[seg_block(sb), seg_block(sb, RPAD)] + recv_weight_specs() + [whole((8, D)), whole((2 * D, D))],
        out_specs=seg_block(sb // 2),
        out_shape=jax.ShapeDtypeStruct((n // 2, SB_ROWS, D), F32),
        scratch_shapes=recv_scratch(sb),
        compiler_params=params_spec(),
        name="recv_fwd",
    )(send, o, *weights, mvec, mw)


def recv_bwd_kernel(sb, send_ref, o_ref, dx_ref, *refs):
    w = {n: refs[i][...] for i, n in enumerate(RECV_W)}
    vec_ref, mvec_ref, mw_ref, dsend_ref, do_ref = refs[7:12]
    g = dict(zip(RECV_G, refs[12:20]))
    dmw_ref, dmv_ref = refs[20:22]
    q_s, mix_s, p_s, kb_s, vb_s = refs[22:]

    @pl.when(pl.program_id(0) == 0)
    def _():
        for ref in list(g.values()) + [dmw_ref, dmv_ref]:
            ref[...] = jnp.zeros(ref.shape, F32)

    vec = vec_ref[...]
    y, kept = recv_forward(
        send_ref[...].reshape(sb * SB_ROWS, D), o_ref[...].reshape(sb * RPAD, D), w, vec, q_s, mix_s, p_s, kb_s, vb_s
    )
    pairs = sb // 2
    wide, unit, inv, gain = merge_rows(y, pairs, mvec_ref[...])
    dx = dx_ref[...].reshape(pairs * SB_ROWS, D)
    dmv_ref[4] += colsum(dx)
    dx2 = split2(dx)
    dmw_ref[...] += tn3(split2(wide), dx2)
    dn = mmwt(dx2, mw_ref[...])
    part = colsum(dn * unit)
    dmv_ref[0] += part[:, :D]
    dmv_ref[1] += part[:, D:]
    part = colsum(dn)
    dmv_ref[2] += part[:, :D]
    dmv_ref[3] += part[:, D:]
    dwide = norm_bwd(dn, unit, inv, gain)
    left = dwide[:, :D].reshape(pairs, 1, SB_ROWS, D)
    right = dwide[:, D:].reshape(pairs, 1, SB_ROWS, D)
    dy = jnp.concatenate([left, right], 1).reshape(sb * SB_ROWS, D)
    dsend, do = recv_backward(dy, kept, w, vec, g, q_s, mix_s, p_s, kb_s, vb_s)
    dsend_ref[...] = dsend.reshape(sb, SB_ROWS, D)
    do_ref[...] = do.reshape(sb, RPAD, D)


RECV_GRADS = [(D, D)] * 5 + [(D, FF), (FF, D), (11, 8, D)]


def recv_bwd(send, o, dx, weights, mvec, mw, sb):
    n = send.shape[0]
    shapes = RECV_GRADS + [(2 * D, D), (5, 8, D)]
    return pl.pallas_call(
        functools.partial(recv_bwd_kernel, sb),
        grid=(n // sb,),
        in_specs=[seg_block(sb), seg_block(sb, RPAD), seg_block(sb // 2)]
        + recv_weight_specs()
        + [whole((8, D)), whole((2 * D, D))],
        out_specs=[seg_block(sb), seg_block(sb, RPAD)] + [whole(s) for s in shapes],
        out_shape=[jax.ShapeDtypeStruct((n, SB_ROWS, D), F32), jax.ShapeDtypeStruct((n, RPAD, D), F32)]
        + [jax.ShapeDtypeStruct(s, F32) for s in shapes],
        scratch_shapes=recv_scratch(sb),
        compiler_params=params_spec(),
        name="recv_bwd",
    )(send, o, dx, *weights, mvec, mw)


def tail_kernel(sb, send_ref, o_ref, tgt_ref, kept_ref, scale_ref, mean_ref, *refs):
    w = {n: refs[i][...] for i, n in enumerate(RECV_W)}
    vec_ref, head_ref, dsend_ref, do_ref = refs[7:11]
    g = dict(zip(RECV_G, refs[11:19]))
    dhead_ref = refs[19]
    q_s, mix_s, p_s, kb_s, vb_s = refs[20:]

    @pl.when(pl.program_id(0) == 0)
    def _():
        for ref in list(g.values()) + [dhead_ref]:
            ref[...] = jnp.zeros(ref.shape, F32)

    vec = vec_ref[...]
    rows = sb * SB_ROWS
    y, kept = recv_forward(
        send_ref[...].reshape(rows, D), o_ref[...].reshape(sb * RPAD, D), w, vec, q_s, mix_s, p_s, kb_s, vb_s
    )
    head = head_ref[...]
    y2 = split2(y)
    scale = jnp.broadcast_to(scale_ref[...][None], (sb, SB_ROWS, PPAD)).reshape(rows, PPAD)
    mean = jnp.broadcast_to(mean_ref[...][None], (sb, SB_ROWS, PPAD)).reshape(rows, PPAD)
    misfit = mmwt(y2, head) * scale + mean - tgt_ref[...].reshape(rows, PPAD)
    dpred = kept_ref[...].reshape(rows, PPAD) * misfit * scale
    dpred2 = split2(dpred)
    dhead_ref[...] += tn3(dpred2, y2)
    dy = mmw(dpred2, head)
    dsend, do = recv_backward(dy, kept, w, vec, g, q_s, mix_s, p_s, kb_s, vb_s)
    dsend_ref[...] = dsend.reshape(sb, SB_ROWS, D)
    do_ref[...] = do.reshape(sb, RPAD, D)


def tail(send, o, tgt, kept, scale, mean, weights, head, sb):
    n = send.shape[0]
    shapes = RECV_GRADS + [(PPAD, D)]
    return pl.pallas_call(
        functools.partial(tail_kernel, sb),
        grid=(n // sb,),
        in_specs=[seg_block(sb), seg_block(sb, RPAD), seg_block(sb, SB_ROWS, PPAD), seg_block(sb, SB_ROWS, PPAD)]
        + [whole((SB_ROWS, PPAD))] * 2
        + recv_weight_specs()
        + [whole((PPAD, D))],
        out_specs=[seg_block(sb), seg_block(sb, RPAD)] + [whole(s) for s in shapes],
        out_shape=[jax.ShapeDtypeStruct((n, SB_ROWS, D), F32), jax.ShapeDtypeStruct((n, RPAD, D), F32)]
        + [jax.ShapeDtypeStruct(s, F32) for s in shapes],
        scratch_shapes=recv_scratch(sb),
        compiler_params=params_spec(),
        name="tail",
    )(send, o, tgt, kept, scale, mean, *weights, head)


SEND_W = ("sq", "sk", "sv")


def send_project(dim2, r_rows, w, vec, k_s, v_s, q_s):
    k_s[...] = mmw(dim2, w["sk"])
    v_s[...] = mmw(dim2, w["sv"]) + vec[11:12]
    r2 = split2(r_rows)
    q_s[...] = (mmw(r2, w["sq"]) + vec[10:11]) * SCALE
    return r2


def send_fwd_kernel(sb, dim_ref, r_ref, here_ref, *refs):
    w = {n: refs[i][...] for i, n in enumerate(SEND_W)}
    vec_ref, o_ref, lse_ref, k_s, v_s, q_s = refs[3:]
    dim2 = split2(dim_ref[...].reshape(sb * SB_ROWS, D))
    send_project(dim2, r_ref[...].reshape(sb * RPAD, D), w, vec_ref[...], k_s, v_s, q_s)
    here = here_ref[...] > 0.5

    def one(s, carry):
        at = pl.ds(pl.multiple_of(s * SB_ROWS, SB_ROWS), SB_ROWS)
        ar = pl.ds(pl.multiple_of(s * RPAD, RPAD), RPAD)
        q2 = split2(spread_rows(q_s[ar, :]))
        sc = jnp.where(here, nt3(split2(k_s[at, :]), q2), negative)
        top = jnp.max(sc, 0, keepdims=True)
        p = jnp.where(here, jnp.exp(sc - top), 0.0)
        total = jnp.sum(p, 0, keepdims=True)
        safe = jnp.where(total > 0.0, total, 1.0)
        o_ref[s] = gather_rows(tn3(split2(p / safe), split2(v_s[at, :])))
        lse_ref[s] = jnp.where(total > 0.0, top + jnp.log(safe), negative)
        return carry

    lax.fori_loop(0, sb, one, 0)


def send_weight_specs():
    return [whole((D, D))] * 3 + [whole((24, D))]


def send_scratch(sb):
    return [
        pltpu.VMEM((sb * SB_ROWS, D), F32),
        pltpu.VMEM((sb * SB_ROWS, D), F32),
        pltpu.VMEM((sb * RPAD, D), F32),
    ]


def send_fwd(dim, routers, here, weights, sb):
    n = dim.shape[0]
    return pl.pallas_call(
        functools.partial(send_fwd_kernel, sb),
        grid=(n // sb,),
        in_specs=[seg_block(sb), seg_block(sb, RPAD), whole((SB_ROWS, HALF))] + send_weight_specs(),
        out_specs=[seg_block(sb, RPAD), seg_block(sb, 1, HALF)],
        out_shape=[jax.ShapeDtypeStruct((n, RPAD, D), F32), jax.ShapeDtypeStruct((n, 1, HALF), F32)],
        scratch_shapes=send_scratch(sb),
        compiler_params=params_spec(),
        name="send_fwd",
    )(dim, routers, here, *weights)


def send_bwd_kernel(sb, dim_ref, dpart_ref, r_ref, o_ref, lse_ref, do_ref, here_ref, *refs):
    w = {n: refs[i][...] for i, n in enumerate(SEND_W)}
    vec_ref, ddim_ref, dr_ref = refs[3:6]
    dsq_ref, dsk_ref, dsv_ref, rows = refs[6:10]
    k_s, v_s, q_s = refs[10:]

    @pl.when(pl.program_id(0) == 0)
    def _():
        for ref in (dsq_ref, dsk_ref, dsv_ref, rows):
            ref[...] = jnp.zeros(ref.shape, F32)

    dim2 = split2(dim_ref[...].reshape(sb * SB_ROWS, D))
    r2 = send_project(dim2, r_ref[...].reshape(sb * RPAD, D), w, vec_ref[...], k_s, v_s, q_s)
    here = (here_ref[...] > 0.5) & valid_lane(SB_ROWS)

    def one(s, carry):
        at = pl.ds(pl.multiple_of(s * SB_ROWS, SB_ROWS), SB_ROWS)
        ar = pl.ds(pl.multiple_of(s * RPAD, RPAD), RPAD)
        q2 = split2(spread_rows(q_s[ar, :]))
        k2 = split2(k_s[at, :])
        p = jnp.where(here, jnp.exp(nt3(k2, q2) - lse_ref[s]), 0.0)
        dwide = spread_rows(do_ref[s])
        d2 = split2(dwide)
        owide = jnp.broadcast_to(o_ref[s][:, None, :], (RPAD, HEADS, D)).reshape(RPAD * HEADS, D)
        e2 = split2(dwide * owide)
        one_row = jnp.ones((8, D), BF)
        mean = (dots(one_row, e2[0], 1, 1) + dots(one_row, e2[1], 1, 1))[0:1]
        dp = nt3(split2(v_s[at, :]), d2)
        s2 = split2(p * (dp - mean))
        q_s[ar, :] = gather_rows(tn3(s2, k2))
        k_s[at, :] = nn3(s2, q2)
        v_s[at, :] = nn3(split2(p), d2)
        return carry

    lax.fori_loop(0, sb, one, 0)
    dk2 = split2(k_s[...])
    dv = v_s[...]
    dv2 = split2(dv)
    rows[1] += colsum(dv)
    dsk_ref[...] += tn3(dim2, dk2)
    dsv_ref[...] += tn3(dim2, dv2)
    out = dpart_ref[...].reshape(sb * SB_ROWS, D) + mmwt(dk2, w["sk"]) + mmwt(dv2, w["sv"])
    ddim_ref[...] = out.reshape(sb, SB_ROWS, D)
    dq = q_s[...] * SCALE
    rows[0] += colsum(dq)
    dq2 = split2(dq)
    dsq_ref[...] += tn3(r2, dq2)
    dr_ref[...] = mmwt(dq2, w["sq"]).reshape(sb, RPAD, D)


def send_bwd(dim, dpart, routers, o, lse, do, here, weights, sb):
    n = dim.shape[0]
    shapes = [(D, D)] * 3 + [(2, 8, D)]
    return pl.pallas_call(
        functools.partial(send_bwd_kernel, sb),
        grid=(n // sb,),
        in_specs=[seg_block(sb), seg_block(sb), seg_block(sb, RPAD), seg_block(sb, RPAD), seg_block(sb, 1, HALF), seg_block(sb, RPAD), whole((SB_ROWS, HALF))]
        + send_weight_specs(),
        out_specs=[seg_block(sb), seg_block(sb, RPAD)] + [whole(s) for s in shapes],
        out_shape=[jax.ShapeDtypeStruct((n, SB_ROWS, D), F32), jax.ShapeDtypeStruct((n, RPAD, D), F32)]
        + [jax.ShapeDtypeStruct(s, F32) for s in shapes],
        scratch_shapes=send_scratch(sb),
        compiler_params=params_spec(),
        name="send_bwd",
    )(dim, dpart, routers, o, lse, do, here, *weights)


def merge_stats(o, lse, axis):
    every_o = lax.all_gather(o, axis)
    every_l = lax.all_gather(lse, axis)
    top = jnp.max(every_l, 0)
    total = top + jnp.log(jnp.sum(jnp.exp(every_l - top), 0))
    share = jnp.exp(every_l - total)
    n = o.shape[0]
    share = jnp.repeat(share.reshape(share.shape[0], n, RPAD, HEADS), D // HEADS, -1)
    return jnp.sum(every_o * share, 0), total


def series_stats(series, observed):
    seen = observed.astype(F32)
    counted = jnp.maximum(jnp.sum(seen, -1, keepdims=True), 1.0)
    mean = jnp.sum(seen * series, -1, keepdims=True) / counted
    center = (series - mean) * seen
    scale = jnp.sqrt(jnp.sum(center * center, -1, keepdims=True) / counted + norm_eps)
    return center / scale, mean, scale


def adam_update(weight, first_moment, second_moment, gradient):
    first_new = beta_one * first_moment + (1.0 - beta_one) * gradient
    second_new = beta_two * second_moment + (1.0 - beta_two) * gradient * gradient
    corrected = (
        first_new
        / (1.0 - beta_one**step_count)
        / (jnp.sqrt(second_new / (1.0 - beta_two**step_count)) + adam_eps)
    )
    return (weight - learn_rate * (corrected + weight_decay * weight), first_new, second_new)


def segment_major(x, width):
    nv = x.shape[0]
    x = x.reshape(nv, -1, 12).transpose(1, 0, 2)
    return jnp.pad(x, ((0, 0), (0, 0), (0, width - 12)))


def pad_rows(x, rows):
    return jnp.pad(x, ((0, rows - x.shape[0]), (0, 0)))


def gradient_parts(series, observed, targets, target_mask, present, square, up, down, vectors):
    nv = series.shape[0]
    normed, mean, scale = series_stats(series, observed)
    pieces = segment_major(normed, 16)
    factor = 2.0 / (1 << 20)
    kept = segment_major(target_mask.astype(F32) * present[:, None] * factor, PPAD)
    tgt = segment_major(targets, PPAD)
    scale16 = jnp.broadcast_to(scale, (nv, PPAD))
    mean16 = jnp.broadcast_to(mean, (nv, PPAD))
    here = jnp.broadcast_to(present[:, None], (nv, HALF))

    emb = pad_rows(vectors[:12], 16).astype(BF)
    place = (vectors[12:13] + vectors[13:73])[:, None, :]
    layer_start = SEGLEN + 1 + SEG
    vecs = [pad_rows(vectors[layer_start + 23 * l : layer_start + 23 * l + 23], 24) for l in range(2)]
    merge_at = layer_start + 46
    mvec = pad_rows(vectors[merge_at : merge_at + 5], 8)
    mw = square[24:26].reshape(2 * D, D)
    head = pad_rows(vectors[merge_at + 5 : merge_at + 17], PPAD).astype(BF)
    router_at = merge_at + 17
    routers = []
    for l, n in ((0, SEG), (1, SEG // 2)):
        r = vectors[router_at + l * SEG * ROUT : router_at + l * SEG * ROUT + n * ROUT].reshape(n, ROUT, D)
        routers.append(jnp.pad(r, ((0, 0), (0, RPAD - ROUT), (0, 0))))
    time_w = [
        (*[square[12 * l + i] for i in (0, 1, 2, 3)], up[2 * l], down[2 * l], vecs[l]) for l in range(2)
    ]
    send_w = [(*[square[12 * l + i] for i in (4, 5, 6)], vecs[l]) for l in range(2)]
    recv_w = [
        (*[square[12 * l + i] for i in (7, 9, 10, 8, 11)], up[2 * l + 1], down[2 * l + 1], vecs[l]) for l in range(2)
    ]

    sb0, sb1 = 4, 6
    dim0 = time_fwd(True, pieces, (emb, place), time_w[0], SEG)
    o0, lse0 = send_fwd(dim0, routers[0], here, send_w[0], sb0)
    o0, lse0 = merge_stats(o0, lse0, "fsdp")
    x1 = recv_fwd(dim0, o0, recv_w[0], mvec, mw, sb0)
    dim1 = time_fwd(False, x1, (), time_w[1], SEG // 2)
    o1, lse1 = send_fwd(dim1, routers[1], here, send_w[1], sb1)
    o1, lse1 = merge_stats(o1, lse1, "fsdp")
    out = tail(dim1, o1, tgt, kept, scale16, mean16, recv_w[1], head, sb1)
    ddim1, do1, grecv1, dhead = out[0], out[1], out[2:10], out[10]
    do1 = lax.psum(do1, "fsdp")
    out = send_bwd(dim1, ddim1, routers[1], o1, lse1, do1, here, send_w[1], sb1)
    ddim1, dr1, gsend1 = out[0], out[1], out[2:]
    out = time_bwd(False, x1, (), ddim1, time_w[1], SEG // 2)
    gtime1, dx1 = out[:7], out[7]
    out = recv_bwd(dim0, o0, dx1, recv_w[0], mvec, mw, sb0)
    ddim0, do0, grecv0, dmw, dmv = out[0], out[1], out[2:10], out[10], out[11]
    do0 = lax.psum(do0, "fsdp")
    out = send_bwd(dim0, ddim0, routers[0], o0, lse0, do0, here, send_w[0], sb0)
    ddim0, dr0, gsend0 = out[0], out[1], out[2:]
    out = time_bwd(True, pieces, (emb, place), ddim0, time_w[0], SEG)
    gtime0, demb, dplace = out[:7], out[7], out[8]

    mats, ups, downs, rows = [], [], [], []
    for gt, gs, gr in ((gtime0, gsend0, grecv0), (gtime1, gsend1, grecv1)):
        mats += [gt[0], gt[1], gt[2], gt[3], gs[0], gs[1], gs[2], gr[0], gr[3], gr[1], gr[2], gr[4]]
        ups += [gt[4], gr[5]]
        downs += [gt[5], gr[6]]
        rt, rs, rr = gt[6].sum(1), gs[3].sum(1), gr[7].sum(1)
        rows += [rt, rs, rr]
    mats += [dmw]
    dplace = dplace.reshape(SEG, VB, D).sum(1)
    vec = jnp.concatenate(
        [demb[:12], dplace.sum(0, keepdims=True), dplace]
        + rows
        + [dmv.sum(1), dhead[:12]]
        + [dr[:, :ROUT].reshape(-1, D) for dr in (dr0, dr1)],
        0,
    )
    return jnp.concatenate(mats, 0), jnp.concatenate(ups, 0), jnp.concatenate(downs, 0), vec


def on_device(series, observed, targets, target_mask, counts, matrices, feed_weights, vectors, matrices_first, matrices_second, feed_first, feed_second, vectors_first, vectors_second):
    everywhere = ("dp", "fsdp")
    local_vars = series.shape[1]
    slot = lax.axis_index("fsdp") * local_vars + jnp.arange(local_vars, dtype=jnp.int32)
    present = (slot < counts[0]).astype(F32)
    square = lax.all_gather(matrices.astype(BF), everywhere, axis=0, tiled=True).reshape(NSQ, D, D)
    feed = lax.all_gather(feed_weights.astype(BF), everywhere, axis=0, tiled=True)
    up = feed[: 4 * D * FF].reshape(4, D, FF)
    down = feed[4 * D * FF :].reshape(4, FF, D)
    vecs = lax.all_gather(vectors.astype(BF), everywhere, axis=0, tiled=True).astype(F32).reshape(NVEC, D)
    g_mat, g_up, g_down, g_vec = gradient_parts(
        series[0], observed[0], targets[0], target_mask[0], present, square, up, down, vecs
    )
    flat = (g_mat.reshape(-1), jnp.concatenate([g_up.reshape(-1), g_down.reshape(-1)]), g_vec.reshape(-1))
    shards = [lax.psum_scatter(f, everywhere, scatter_dimension=0, tiled=True) for f in flat]
    kept = jnp.sum(target_mask[0].astype(F32) * present[:, None])
    squares = sum(jnp.sum(s * s) for s in shards)
    sums = lax.psum(jnp.stack([squares, kept]), everywhere)
    upscale = (1 << 20) / jnp.maximum(sums[1], 1.0)
    grad_norm = jnp.sqrt(sums[0]) * upscale
    factor = upscale * (clip_norm / jnp.maximum(grad_norm, clip_norm))
    new = (
        adam_update(matrices, matrices_first, matrices_second, shards[0] * factor)
        + adam_update(feed_weights, feed_first, feed_second, shards[1] * factor)
        + adam_update(vectors, vectors_first, vectors_second, shards[2] * factor)
    )
    return (grad_norm,) + new


def solution(mesh):
    both = P(("dp", "fsdp"))
    data = P("dp", "fsdp", None)
    return jax.shard_map(
        on_device,
        mesh=mesh,
        in_specs=(data,) * 4 + (P("dp"),) + (both,) * 9,
        out_specs=(P(),) + (both,) * 9,
        check_vma=False,
    )
```

time: 2770 us -> 1880 us (0.68)
  matrix products: 1140 us -> 0 us
  Pallas kernels: 0 us -> 916 us
  local copies, waits for them, and re-layouts: 416 us -> 130 us
  blocking collectives: 333 us -> 103 us
  other arithmetic: 200 us -> 44.3 us
    dot_general x140 -> x0, matrix products: 1140 us -> none  [the longest x99 589 us: dense(): return jnp.einsum('...d,de->...e', inputs, matrix, precision=highest_score)]
    pallas_call x0 -> x11, Pallas kernels: none -> 916 us  [the longest x2 289 us: time_bwd(): pl.pallas_call(functools.partial(time_bwd_kernel, first, count, group), g...]
    psum x4 -> x1, blocking collectives: 157 us -> 39.5 us  [on_device(): sums = lax.psum(jnp.stack([squares, kept]), everywhere)]
    all_gather x4 -> x2, blocking collectives: 176 us -> 63.7 us  [merge_stats(): every_l = lax.all_gather(lse, axis)]
    reshape x47 -> x8, local copies, waits for them, and re-layouts: 116 us -> 28.1 us  [the longest x2 25.7 us: merge_stats(): jnp.repeat(share.reshape(share.shape[0], n, RPAD, HEADS), D // HEADS, -1)]
    reduce_sum x49 -> x20, other arithmetic: 108 us -> 24.9 us  [the longest x2 13.6 us: merge_stats(): return (jnp.sum(every_o * share, 0), total)]
    transpose x15 -> x0, local copies, waits for them, and re-layouts: 71.2 us -> none  [the longest x3 29.2 us: time_part(): jnp.einsum('vhqk,vkhe->vqhe', attention_weights, value_rows, precision=hi...]
    all_gather x4, waiting for transfers between devices: 111 us -> 171 us  [the longest x1 59.3 us: on_device(): lax.all_gather(matrices.astype(BF), everywhere, axis=0, tiled=True)]
  transfers between devices with their start and end apart: 8 -> 8, of which waited for: 6 -> 8; matrix products, arithmetic and copies ran while one was open for 6% -> 5% of each run, Pallas kernels for 0% -> 0%
where the time goes in v1:
time: 1880 us
  Pallas kernels  916 us (49%)
  waiting for transfers between devices  661 us (35%)
  local copies, waits for them, and re-layouts  130 us (7%)
  blocking collectives  103 us (5%)
  other arithmetic  44.3 us (2%)
  between operations  20.5 us (1%)
    unnamed x10, waiting for transfers between devices  347 us
    pallas_call x2, Pallas kernels, time_bwd(): pl.pallas_call(functools.partial(time_bwd_kernel, first, count, group), g...  289 us
    pallas_call x1, Pallas kernels, recv_bwd(): pl.pallas_call(functools.partial(recv_bwd_kernel, sb), grid=(n // sb,), i...  179 us
    pallas_call x2, Pallas kernels, time_fwd(): pl.pallas_call(functools.partial(time_fwd_kernel, first, count, group), g...  134 us
    pallas_call x1, Pallas kernels, recv_fwd(): pl.pallas_call(functools.partial(recv_fwd_kernel, sb), grid=(n // sb,), i...  90.8 us
    pallas_call x1, Pallas kernels, tail(): pl.pallas_call(functools.partial(tail_kernel, sb), grid=(n // sb,), in_sp...  84.1 us
    pallas_call x2, Pallas kernels, send_bwd(): pl.pallas_call(functools.partial(send_bwd_kernel, sb), grid=(n // sb,), i...  80.8 us
    psum x1, waiting for transfers between devices, gradient_parts(): do0 = lax.psum(do0, 'fsdp')  73.6 us
  transfers between devices with their start and end apart: 8, of which 8 were waited for; matrix products, arithmetic and copies ran while one was open for 5% of the time, Pallas kernels for 0%

profile of v1, /device:TPU:0, one launch (start us, length us, event | category | flops | bytes accessed | tf_op | source)
XLA Modules:
  0.0 1875.7 jit_solution(18423605324330931002)
XLA Ops:
  7.3 0.9 convert_element_type.62
  8.6 0.9 copy-done.1
  9.6 1.5 convert_element_type.65
  11.2 1.6 convert_element_type.64
  12.8 0.9 convert_element_type.59
  14.7 1.1 copy.70
  15.8 2.0 copy.71
  18.9 2.0 divide_bitcast_fusion
  21.0 1.5 pad.39.refs_0_
  22.4 120.1 %all-reduce.24.cloned.1.call-done = bf16[265216]{0:T(1024)(128)(2,1)} async-done(((bf16[265216]{0:T(1024)(128)(2,1)}), bf16[265216]{0:T(1024)(128)(2,1)}) %all-reduce.24.cloned.1.call-update) | async-done | bytes 530448
  147.5 1.0 slice.701
  148.7 1.0 pad.42.r_ref
  149.7 54.4 %all-gather.11.cloned.1.call-done = bf16[1048576]{0:T(1024)(128)(2,1)} async-done(((bf16[32768]{0:T(1024)(128)(2,1)}), bf16[1048576]{0:T(1024)(128)(2,1)}) %all-gather.11.cloned.1.call-update) | async-done | bytes 2097168 | tf_op jit(solution)/shard_map/all_gather | solution.py:926
  204.1 1.6 fusion.13
  207.4 59.3 %all-gather.9.cloned.1.call-done = bf16[1703936]{0:T(1024)(128)(2,1)} async-done(((bf16[53248]{0:T(1024)(128)(2,1)}), bf16[1703936]{0:T(1024)(128)(2,1)}) %all-gather.9.cloned.1.call-update) | async-done | bytes 3407888 | tf_op jit(solution)/shard_map/all_gather | solution.py:925
  266.7 1.2 fusion.12
  270.7 2.7 fusion.11
  275.6 77.4 %time_fwd.2.dim_ref.send_ref = f32[60,64,256]{2,1,0:T(8,128)} custom-call(f32[60,64,16]{2,1,0:T(8,128)} %pad.39.refs_0_, bf16[16,256]{1,0:T(8,128)(2,1)} %pad.40.refs_1_, f32[60,1,256]{2,1,0:T(1,128)} %broadcast_in_dim.14.refs_2_, bf16[256,256]{1,0:T(8,128)(2,1)} %slice.610.refs_3_.refs_4_, bf16[256,256]{1,0:T(8,128)(2,1)} %slice.612.refs_4_.refs_5_, ...), custom_call_target="tpu_custom_call" | custom-call | tf_op jit(solution)/shard_map/time_fwd/pallas_call | solution.py:271
  353.7 38.5 %send_fwd.2 = (f32[60,16,256]{2,1,0:T(8,128)}, f32[60,1,128]{2,1,0:T(1,128)}) custom-call(f32[60,64,256]{2,1,0:T(8,128)} %time_fwd.2.dim_ref.send_ref, f32[60,16,256]{2,1,0:T(8,128)} %pad.42.r_ref, f32[64,128]{1,0:T(8,128)} %broadcast_in_dim.15.here_ref, bf16[256,256]{1,0:T(8,128)(2,1)} %slice.625.refs_0_, bf16[256,256]{1,0:T(8,128)(2,1)} %slice.627.refs_1_, ...), custom_call_target="tpu_custom_call" | custom-call | tf_op jit(solution)/shard_map/send_fwd/pallas_call | solution.py:726
  394.5 0.9 slice.641.refs_5_
  396.1 0.9 slice.657.refs_5_.refs_6_
  397.8 32.4 %all-gather.1 = f32[480,1,128]{2,1,0:T(1,128)S(1)} all-gather(f32[60,1,128]{2,1,0:T(1,128)} %get-tuple-element.67), channel_id=3, replica_groups=mesh['dp'=4,'fsdp'=8] {'fsdp'}, dimensions={0}, use_global_device_ids=true | all-gather | bytes 276480 | tf_op jit(solution)/shard_map/all_gather | solution.py:807
  431.3 6.8 broadcast_in_dim.16
  438.2 13.7 copy.76
  461.2 50.7 %all-gather.13.cloned.1.call-done = f32[480,16,256]{2,1,0:T(8,128)} async-done(((f32[60,16,256]{2,1,0:T(8,128)}), f32[480,16,256]{2,1,0:T(8,128)}) %all-gather.13.cloned.1.call-update) | async-done | bytes 7864336 | tf_op jit(solution)/shard_map/all_gather | solution.py:806
  511.8 8.5 multiply_reduce_fusion.o_ref
  520.3 90.8 %recv_fwd.1.refs_0_ = f32[30,64,256]{2,1,0:T(8,128)} custom-call(f32[60,64,256]{2,1,0:T(8,128)} %time_fwd.2.dim_ref.send_ref, f32[60,16,256]{2,1,0:T(8,128)} %multiply_reduce_fusion.o_ref, bf16[256,256]{1,0:T(8,128)(2,1)} %slice.631.refs_0_, bf16[256,256]{1,0:T(8,128)(2,1)} %slice.633.refs_1_, bf16[256,256]{1,0:T(8,128)(2,1)} %slice.635.refs_2_, ...), custom_call_target="tpu_custom_call" | custom-call | tf_op jit(solution)/shard_map/recv_fwd/pallas_call | solution.py:557
  611.1 56.3 %time_fwd.3.dim_ref.send_ref = f32[30,64,256]{2,1,0:T(8,128)} custom-call(f32[30,64,256]{2,1,0:T(8,128)} %recv_fwd.1.refs_0_, bf16[256,256]{1,0:T(8,128)(2,1)} %slice.649.refs_1_.refs_2_, bf16[256,256]{1,0:T(8,128)(2,1)} %slice.651.refs_2_.refs_3_, bf16[256,256]{1,0:T(8,128)(2,1)} %slice.653.refs_3_.refs_4_, bf16[256,256]{1,0:T(8,128)(2,1)} %slice.655.refs_4_.refs_5_, ...), custom_call_target="tpu_custom_call" | custom-call | tf_op jit(solution)/shard_map/time_fwd/pallas_call | solution.py:271
  667.4 19.7 %send_fwd.3 = (f32[30,16,256]{2,1,0:T(8,128)}, f32[30,1,128]{2,1,0:T(1,128)}) custom-call(f32[30,64,256]{2,1,0:T(8,128)} %time_fwd.3.dim_ref.send_ref, f32[30,16,256]{2,1,0:T(8,128)} %pad.45.r_ref, f32[64,128]{1,0:T(8,128)} %broadcast_in_dim.15.here_ref, bf16[256,256]{1,0:T(8,128)(2,1)} %slice.664.refs_0_, bf16[256,256]{1,0:T(8,128)(2,1)} %slice.666.refs_1_, ...), custom_call_target="tpu_custom_call" | custom-call | tf_op jit(solution)/shard_map/send_fwd/pallas_call | solution.py:726
  687.9 1.1 pad.47.kept_ref
  689.6 1.0 pad.46.tgt_ref
  691.2 0.9 slice.680.refs_5_
  696.4 31.3 %all-gather.3 = f32[240,1,128]{2,1,0:T(1,128)S(1)} all-gather(f32[30,1,128]{2,1,0:T(1,128)S(1)} %copy-done.61), channel_id=5, replica_groups=mesh['dp'=4,'fsdp'=8] {'fsdp'}, dimensions={0}, use_global_device_ids=true | all-gather | bytes 138240 | tf_op jit(solution)/shard_map/all_gather | solution.py:807
  728.4 1.0 copy.80
  729.4 8.8 broadcast_in_dim.17
  738.2 12.0 reshape.598
  750.2 6.4 all-gather.15.cloned.1.call-done
  756.6 5.1 multiply_reduce_fusion.1.o_ref
  763.0 84.1 %tail.1 = (f32[30,64,256]{2,1,0:T(8,128)}, f32[30,16,256]{2,1,0:T(8,128)}, f32[256,256]{1,0:T(8,128)}, f32[256,256]{1,0:T(8,128)}, f32[256,256]{1,0:T(8,128)}, /...) custom-call(f32[30,64,256]{2,1,0:T(8,128)} %time_fwd.3.dim_ref.send_, ...), custom_call_target="tpu_custom_call" | custom-call | tf_op jit(solution)/shard_map/tail/pallas_call | solution.py:662
  848.3 69.8 %all-reduce.20.cloned.1.call-done.do_ref = f32[30,16,256]{2,1,0:T(8,128)} async-done(((f32[30,16,256]{2,1,0:T(8,128)}), f32[30,16,256]{2,1,0:T(8,128)}) %all-reduce.20.cloned.1.call-update) | async-done | bytes 491536 | tf_op jit(solution)/shard_map/psum | solution.py:888
  918.0 27.2 %send_bwd.2 = (f32[30,64,256]{2,1,0:T(8,128)}, f32[30,16,256]{2,1,0:T(8,128)}, f32[256,256]{1,0:T(8,128)}, f32[256,256]{1,0:T(8,128)}, f32[256,256]{1,0:T(8,128)}, /*index=5*/f32[2,8,256]{2,1,0:T(8,128)}) custom-call(f32[30,64,256]{2,1,0:T(8,128)} %time_fwd.3.dim_ref.send_ref, f32[30,64,256]{2,1,0:T(8,128)} %get-tuple-element.70.dpart_ref, ...), custom_call_target="tpu_custom_call" | custom-call | tf_op jit(solution)/shard_map/send_bwd/pallas_call | solution.py:791
  945.3 120.3 %time_bwd.2 = (f32[256,256]{1,0:T(8,128)}, f32[256,256]{1,0:T(8,128)}, f32[256,256]{1,0:T(8,128)}, f32[256,256]{1,0:T(8,128)}, f32[256,512]{1,0:T(8,128)}, /*ind...) custom-call(f32[30,64,256]{2,1,0:T(8,128)} %recv_fwd.1.refs_0_, ...), custom_call_target="tpu_custom_call" | custom-call | tf_op jit(solution)/shard_map/time_bwd/pallas_call | solution.py:381
  1065.7 178.8 %recv_bwd.1 = (f32[60,64,256]{2,1,0:T(8,128)}, f32[60,16,256]{2,1,0:T(8,128)}, f32[256,256]{1,0:T(8,128)}, f32[256,256]{1,0:T(8,128)}, f32[256,256]{1,0:T(8,128)...) custom-call(f32[60,64,256]{2,1,0:T(8,128)} %time_fwd.2.dim_ref.send_, ...), custom_call_target="tpu_custom_call" | custom-call | tf_op jit(solution)/shard_map/recv_bwd/pallas_call | solution.py:613
  1245.4 0.9 reduce_sum.193
  1247.2 73.6 %all-reduce.22.cloned.1.call-done.do_ref = f32[60,16,256]{2,1,0:T(8,128)} async-done(((f32[60,16,256]{2,1,0:T(8,128)}), f32[60,16,256]{2,1,0:T(8,128)}) %all-reduce.22.cloned.1.call-update) | async-done | bytes 983056 | tf_op jit(solution)/shard_map/psum | solution.py:895
  1320.8 53.6 %send_bwd.3 = (f32[60,64,256]{2,1,0:T(8,128)}, f32[60,16,256]{2,1,0:T(8,128)}, f32[256,256]{1,0:T(8,128)}, f32[256,256]{1,0:T(8,128)}, f32[256,256]{1,0:T(8,128)}, /*index=5*/f32[2,8,256]{2,1,0:T(8,128)}) custom-call(f32[60,64,256]{2,1,0:T(8,128)} %time_fwd.2.dim_ref.send_ref, f32[60,64,256]{2,1,0:T(8,128)} %get-tuple-element.74.dpart_ref, ...), custom_call_target="tpu_custom_call" | custom-call | tf_op jit(solution)/shard_map/send_bwd/pallas_call | solution.py:791
  1374.4 169.1 %time_bwd.3 = (f32[256,256]{1,0:T(8,128)}, f32[256,256]{1,0:T(8,128)}, f32[256,256]{1,0:T(8,128)}, f32[256,256]{1,0:T(8,128)}, f32[256,512]{1,0:T(8,128)}, /*ind...) custom-call(f32[60,64,16]{2,1,0:T(8,128)} %pad.39.refs_0_, ...), custom_call_target="tpu_custom_call" | custom-call | tf_op jit(solution)/shard_map/time_bwd/pallas_call | solution.py:381
  1543.6 1.2 bitcast_reduce_fusion
  1544.7 1.1 reduce_sum.189
  1545.8 0.9 reduce_sum.191
  1546.9 1.9 concatenate.19
  1548.8 1.0 reshape.605
  1549.9 1.6 maximum_bitcast_fusion
  1552.5 2.4 copy.91
  1573.3 9.3 copy.89
  1582.5 3.8 pad_maximum_fusion
  1587.2 226.4 %all-reduce.26.cloned.1.call-done = (f32[1703936]{0:T(1024)}, f32[1048576]{0:T(1024)}, f32[265216]{0:T(1024)}) async-done(((f32[1703936]{0:T(1024)}, f32[1048576]{0:T(1024)}, f32[265216]{0:T(1024)}), (f32[1703936]{0:T(1024)}, f32[1048576]{0:T(1024)}, f32[265216]{0:T(1024)})) %all-reduce.26.cloned.1.call-update) | async-done | bytes 12070928
  1813.6 1.6 multiply_reduce_fusion.2
  1815.2 1.5 multiply_reduce_fusion.3
  1818.0 1.5 multiply_reduce_fusion.4
  1820.8 39.5 %psum.23 = f32[2]{0:T(128)S(1)} all-reduce(f32[2]{0:T(128)S(1)} %pad_maximum_fusion.1), channel_id=1, replica_groups=mesh['dp'=4,'fsdp'=8] {'dp','fsdp'}, use_global_device_ids=true, to_apply=%region_27.28 | all-reduce | flops 2 | bytes 16 | tf_op jit(solution)/shard_map/psum | solution.py:937
  1862.4 1.5 multiply_subtract_fusion.2
  1863.9 1.7 multiply_subtract_fusion.1
  1865.6 1.9 multiply_subtract_fusion
  (265 shorter events, 60.9 us)
Async XLA Ops:
  7.2 11.3 copy-start
  7.2 11.4 copy-start.3
  7.2 135.4 %all-reduce.24.cloned.1.call-start = ((), (), s32[]{:S(2)}) async-start(), calls=%async_computation.6 | async-start | bytes 1060864
  9.5 194.6 %all-gather.11.cloned.1.call-start = ((), (), s32[]{:S(2)}) async-start(), calls=%async_computation.1 | async-start | bytes 2162688 | tf_op jit(solution)/shard_map/all_gather | solution.py:926
  11.1 255.6 %all-gather.9.cloned.1.call-start = ((), (), s32[]{:S(2)}) async-start(), calls=%async_computation | async-start | bytes 3514368 | tf_op jit(solution)/shard_map/all_gather | solution.py:925
  12.8 499.1 %all-gather.13.cloned.1.call-start = ((), (), s32[]{:S(2)}) async-start(), calls=%async_computation.4 | async-start | bytes 8847360 | tf_op jit(solution)/shard_map/all_gather | solution.py:806
  274.9 117.4 %copy-start.2 = (bf16[265216]{0:T(1024)(128)(2,1)S(1)}, bf16[265216]{0:T(1024)(128)(2,1)}, u32[]{:S(2)}) copy-start(bf16[265216]{0:T(1024)(128)(2,1)} %all-reduce.24.cloned.1.call-done) | copy-start | bytes 1591300
  392.2 364.3 %all-gather.15.cloned.1.call-start = ((), (), s32[]{:S(2)}) async-start(), calls=%async_computation.5 | async-start | bytes 4423680 | tf_op jit(solution)/shard_map/all_gather | solution.py:806
  438.2 13.8 copy-start.14
  438.2 14.5 copy-start.13
  438.2 15.2 copy-start.12
  438.2 15.9 copy-start.11
  438.2 16.6 copy-start.10
  438.2 17.3 slice-start
  438.2 18.0 copy-start.9
  438.2 18.7 copy-start.8
  438.2 19.5 %copy-start.7 = (bf16[65536]{0:T(1024)(128)(2,1)S(1)}, bf16[65536]{0:T(1024)(128)(2,1)}, u32[]{:S(2)}) copy-start(bf16[65536]{0:T(1024)(128)(2,1)} %get-tuple-element.143) | copy-start | bytes 393220
  438.2 20.1 %copy-start.6 = (bf16[65536]{0:T(1024)(128)(2,1)S(1)}, bf16[65536]{0:T(1024)(128)(2,1)}, u32[]{:S(2)}) copy-start(bf16[65536]{0:T(1024)(128)(2,1)} %get-tuple-element.142) | copy-start | bytes 393220
  520.3 166.9 %copy-start.23 = (s32[1,64,360]{2,1,0:T(8,128)S(1)}, s32[1,64,360]{2,1,0:T(8,128)}, u32[]{:S(2)}) copy-start(s32[1,64,360]{2,1,0:T(8,128)} %param.17) | copy-start | bytes 276484
  611.1 77.9 %copy-start.53 = (f32[1,64,360]{2,1,0:T(8,128)S(1)}, f32[1,64,360]{2,1,0:T(8,128)}, u32[]{:S(2)}) copy-start(f32[1,64,360]{2,1,0:T(8,128)} %param.16) | copy-start | bytes 276484
  687.1 9.3 copy-start.61
  687.1 230.9 %all-reduce.20.cloned.1.call-start = ((), (), s32[]{:S(2)}) async-start(), calls=%async_computation.2 | async-start | bytes 983040 | tf_op jit(solution)/shard_map/psum | solution.py:888
  847.2 473.6 %all-reduce.22.cloned.1.call-start = ((), (), s32[]{:S(2)}) async-start(), calls=%async_computation.3 | async-start | bytes 1966080 | tf_op jit(solution)/shard_map/psum | solution.py:895
  945.3 300.1 %copy-start.54 = (f32[11,8,256]{2,1,0:T(8,128)S(1)}, f32[11,8,256]{2,1,0:T(8,128)}, u32[]{:S(2)}) copy-start(f32[11,8,256]{2,1,0:T(8,128)} %get-tuple-element.117) | copy-start | bytes 270340
  945.3 301.8 %copy-start.22 = (f32[30,16,256]{2,1,0:T(8,128)S(1)}, f32[30,16,256]{2,1,0:T(8,128)}, u32[]{:S(2)}) copy-start(f32[30,16,256]{2,1,0:T(8,128)} %get-tuple-element.121) | copy-start | bytes 1474564
  945.3 301.9 %copy-start.59 = (f32[2,8,256]{2,1,0:T(8,128)S(1)}, f32[2,8,256]{2,1,0:T(8,128)}, u32[]{:S(2)}) copy-start(f32[2,8,256]{2,1,0:T(8,128)} %get-tuple-element.116) | copy-start | bytes 49156
  1065.6 181.4 %copy-start.55 = (f32[10,8,256]{2,1,0:T(8,128)S(1)}, f32[10,8,256]{2,1,0:T(8,128)}, u32[]{:S(2)}) copy-start(f32[10,8,256]{2,1,0:T(8,128)} %get-tuple-element.115) | copy-start | bytes 245764
  1244.5 569.1 %all-reduce.26.cloned.1.call-start = ((), (), s32[]{:S(2)}) async-start(), calls=%async_computation.7 | async-start | bytes 24141824
  1374.4 172.4 %copy-start.4 = (f32[60,16,256]{2,1,0:T(8,128)S(1)}, f32[60,16,256]{2,1,0:T(8,128)}, u32[]{:S(2)}) copy-start(f32[60,16,256]{2,1,0:T(8,128)} %get-tuple-element.120) | copy-start | bytes 2949124
  1374.4 172.5 %copy-start.60 = (f32[2,8,256]{2,1,0:T(8,128)S(1)}, f32[2,8,256]{2,1,0:T(8,128)}, u32[]{:S(2)}) copy-start(f32[2,8,256]{2,1,0:T(8,128)} %get-tuple-element.113) | copy-start | bytes 49156
  1374.4 172.5 %copy-start.58 = (f32[16,256]{1,0:T(8,128)S(1)}, f32[16,256]{1,0:T(8,128)}, u32[]{:S(2)}) copy-start(f32[16,256]{1,0:T(8,128)} %get-tuple-element.119) | copy-start | bytes 49156
  1374.4 175.5 %copy-start.18 = (f32[256,512]{1,0:T(8,128)S(1)}, f32[256,512]{1,0:T(8,128)}, u32[]{:S(2)}) copy-start(f32[256,512]{1,0:T(8,128)} %get-tuple-element.105) | copy-start | bytes 1572868
  1546.8 5.4 copy-start.17
  1551.6 5.5 copy-start.44
  1551.6 6.2 copy-start.43
  1551.6 7.0 copy-start.42
  1552.2 7.2 copy-start.41
  1552.2 7.9 copy-start.40
  1552.2 8.6 copy-start.39
  1552.2 9.3 copy-start.38
  1552.3 10.0 copy-start.37
  1552.3 10.7 copy-start.36
  1552.3 11.4 copy-start.35
  1552.3 12.2 copy-start.34
  1552.4 12.7 copy-start.33
  1552.4 13.5 copy-start.32
  1552.5 14.2 copy-start.31
  1552.5 14.9 copy-start.30
  1552.5 15.6 copy-start.29
  1552.5 16.3 copy-start.28
  1552.5 17.0 copy-start.27
  1552.5 17.8 copy-start.26
  1554.9 16.1 copy-start.25
  1554.9 16.8 copy-start.24
  1554.9 17.5 copy-start.15
  1586.4 276.0 %copy-start.50 = (f32[8288]{0:T(1024)S(1)}, f32[8288]{0:T(1024)}, u32[]{:S(2)}) copy-start(f32[8288]{0:T(1024)} %param.21) | copy-start | bytes 99460
  1586.4 276.0 %copy-start.56 = (f32[8288]{0:T(1024)S(1)}, f32[8288]{0:T(1024)}, u32[]{:S(2)}) copy-start(f32[8288]{0:T(1024)} %param.26) | copy-start | bytes 99460
  1586.4 276.0 %copy-start.57 = (f32[8288]{0:T(1024)S(1)}, f32[8288]{0:T(1024)}, u32[]{:S(2)}) copy-start(f32[8288]{0:T(1024)} %param.27) | copy-start | bytes 99460
  1586.4 277.5 %copy-start.16 = (f32[32768]{0:T(1024)S(1)}, f32[32768]{0:T(1024)}, u32[]{:S(2)}) copy-start(f32[32768]{0:T(1024)} %param.20) | copy-start | bytes 393220
  1586.4 277.5 %copy-start.51 = (f32[32768]{0:T(1024)S(1)}, f32[32768]{0:T(1024)}, u32[]{:S(2)}) copy-start(f32[32768]{0:T(1024)} %param.24) | copy-start | bytes 393220
  1586.4 277.5 %copy-start.52 = (f32[32768]{0:T(1024)S(1)}, f32[32768]{0:T(1024)}, u32[]{:S(2)}) copy-start(f32[32768]{0:T(1024)} %param.25) | copy-start | bytes 393220
  1586.4 279.2 %copy-start.5 = (f32[53248]{0:T(1024)S(1)}, f32[53248]{0:T(1024)}, u32[]{:S(2)}) copy-start(f32[53248]{0:T(1024)} %param.19) | copy-start | bytes 638980
  1586.4 279.2 %copy-start.48 = (f32[53248]{0:T(1024)S(1)}, f32[53248]{0:T(1024)}, u32[]{:S(2)}) copy-start(f32[53248]{0:T(1024)} %param.22) | copy-start | bytes 638980
  1586.4 279.2 %copy-start.49 = (f32[53248]{0:T(1024)S(1)}, f32[53248]{0:T(1024)}, u32[]{:S(2)}) copy-start(f32[53248]{0:T(1024)} %param.23) | copy-start | bytes 638980
  (7 other events, 20.1 us)
Sparse Core Ops, SparseCore 0:
  13.3 129.2 all-reduce.23
  146.6 57.4 all-gather.10
  208.0 58.6 all-gather.8
  392.3 119.4 all-gather.12
  687.3 69.2 all-gather.14
  847.3 70.6 all-reduce.19
  1244.6 76.1 all-reduce.21
  1586.6 226.9 all-reduce.25

commit v2 on v1

--- a/solution.py
+++ b/solution.py
@@ -408,6 +408,28 @@
     return jnp.sum(x.reshape(RPAD, HEADS, D) * head_rows()[None], 1)
 
 
+PACK = 24
+
+
+def pack_rows(x, last=None):
+    last = jnp.zeros((1, HALF), F32) if last is None else last
+    return jnp.concatenate([x[:ROUT, :HALF], x[:ROUT, HALF:], last, jnp.zeros((PACK - 2 * ROUT - 1, HALF), F32)], 0)
+
+
+def unpack_rows(x):
+    x = jnp.concatenate([x[:ROUT], x[ROUT : 2 * ROUT]], 1)
+    return jnp.concatenate([x, jnp.zeros((RPAD - ROUT, D), F32)], 0)
+
+
+def unpack_block(ref, sb):
+    return jnp.concatenate([unpack_rows(ref[s]) for s in range(sb)], 0)
+
+
+def pack_block(ref, x, sb):
+    for s in range(sb):
+        ref[s] = pack_rows(x[s * RPAD : (s + 1) * RPAD])
+
+
 def valid_lane(rows):
     return lax.broadcasted_iota(jnp.int32, (rows, HALF), 1) < ROUT * HEADS
 
@@ -540,12 +562,16 @@
     return pl.BlockSpec((sb, rows, width), lambda i: (i, 0, 0))
 
 
+def pack_spec(sb):
+    return seg_block(sb, PACK, HALF)
+
+
 def recv_fwd_kernel(sb, send_ref, o_ref, *refs):
     w = {n: refs[i][...] for i, n in enumerate(RECV_W)}
     vec_ref, mvec_ref, mw_ref, out_ref = refs[7:11]
     q_s, mix_s, p_s, kb_s, vb_s = refs[11:]
     y, _ = recv_forward(
-        send_ref[...].reshape(sb * SB_ROWS, D), o_ref[...].reshape(sb * RPAD, D), w, vec_ref[...], q_s, mix_s, p_s, kb_s, vb_s
+        send_ref[...].reshape(sb * SB_ROWS, D), unpack_block(o_ref, sb), w, vec_ref[...], q_s, mix_s, p_s, kb_s, vb_s
     )
     mvec = mvec_ref[...]
     wide, _, _, _ = merge_rows(y, sb // 2, mvec)
@@ -557,7 +583,7 @@
     return pl.pallas_call(
         functools.partial(recv_fwd_kernel, sb),
         grid=(n // sb,),
-        in_specs=[seg_block(sb), seg_block(sb, RPAD)] + recv_weight_specs() + [whole((8, D)), whole((2 * D, D))],
+        in_specs=[seg_block(sb), pack_spec(sb)] + recv_weight_specs() + [whole((8, D)), whole((2 * D, D))],
         out_specs=seg_block(sb // 2),
         out_shape=jax.ShapeDtypeStruct((n // 2, SB_ROWS, D), F32),
         scratch_shapes=recv_scratch(sb),
@@ -580,7 +606,7 @@
 
     vec = vec_ref[...]
     y, kept = recv_forward(
-        send_ref[...].reshape(sb * SB_ROWS, D), o_ref[...].reshape(sb * RPAD, D), w, vec, q_s, mix_s, p_s, kb_s, vb_s
+        send_ref[...].reshape(sb * SB_ROWS, D), unpack_block(o_ref, sb), w, vec, q_s, mix_s, p_s, kb_s, vb_s
     )
     pairs = sb // 2
     wide, unit, inv, gain = merge_rows(y, pairs, mvec_ref[...])
@@ -601,7 +627,7 @@
     dy = jnp.concatenate([left, right], 1).reshape(sb * SB_ROWS, D)
     dsend, do = recv_backward(dy, kept, w, vec, g, q_s, mix_s, p_s, kb_s, vb_s)
     dsend_ref[...] = dsend.reshape(sb, SB_ROWS, D)
-    do_ref[...] = do.reshape(sb, RPAD, D)
+    pack_block(do_ref, do, sb)
 
 
 RECV_GRADS = [(D, D)] * 5 + [(D, FF), (FF, D), (11, 8, D)]
@@ -613,11 +639,11 @@
     return pl.pallas_call(
         functools.partial(recv_bwd_kernel, sb),
         grid=(n // sb,),
-        in_specs=[seg_block(sb), seg_block(sb, RPAD), seg_block(sb // 2)]
+        in_specs=[seg_block(sb), pack_spec(sb), seg_block(sb // 2)]
         + recv_weight_specs()
         + [whole((8, D)), whole((2 * D, D))],
-        out_specs=[seg_block(sb), seg_block(sb, RPAD)] + [whole(s) for s in shapes],
-        out_shape=[jax.ShapeDtypeStruct((n, SB_ROWS, D), F32), jax.ShapeDtypeStruct((n, RPAD, D), F32)]
+        out_specs=[seg_block(sb), pack_spec(sb)] + [whole(s) for s in shapes],
+        out_shape=[jax.ShapeDtypeStruct((n, SB_ROWS, D), F32), jax.ShapeDtypeStruct(o.shape, F32)]
         + [jax.ShapeDtypeStruct(s, F32) for s in shapes],
         scratch_shapes=recv_scratch(sb),
         compiler_params=params_spec(),
@@ -640,7 +666,7 @@
     vec = vec_ref[...]
     rows = sb * SB_ROWS
     y, kept = recv_forward(
-        send_ref[...].reshape(rows, D), o_ref[...].reshape(sb * RPAD, D), w, vec, q_s, mix_s, p_s, kb_s, vb_s
+        send_ref[...].reshape(rows, D), unpack_block(o_ref, sb), w, vec, q_s, mix_s, p_s, kb_s, vb_s
     )
     head = head_ref[...]
     y2 = split2(y)
@@ -653,7 +679,7 @@
     dy = mmw(dpred2, head)
     dsend, do = recv_backward(dy, kept, w, vec, g, q_s, mix_s, p_s, kb_s, vb_s)
     dsend_ref[...] = dsend.reshape(sb, SB_ROWS, D)
-    do_ref[...] = do.reshape(sb, RPAD, D)
+    pack_block(do_ref, do, sb)
 
 
 def tail(send, o, tgt, kept, scale, mean, weights, head, sb):
@@ -662,12 +688,12 @@
     return pl.pallas_call(
         functools.partial(tail_kernel, sb),
         grid=(n // sb,),
-        in_specs=[seg_block(sb), seg_block(sb, RPAD), seg_block(sb, SB_ROWS, PPAD), seg_block(sb, SB_ROWS, PPAD)]
+        in_specs=[seg_block(sb), pack_spec(sb), seg_block(sb, SB_ROWS, PPAD), seg_block(sb, SB_ROWS, PPAD)]
         + [whole((SB_ROWS, PPAD))] * 2
         + recv_weight_specs()
         + [whole((PPAD, D))],
-        out_specs=[seg_block(sb), seg_block(sb, RPAD)] + [whole(s) for s in shapes],
-        out_shape=[jax.ShapeDtypeStruct((n, SB_ROWS, D), F32), jax.ShapeDtypeStruct((n, RPAD, D), F32)]
+        out_specs=[seg_block(sb), pack_spec(sb)] + [whole(s) for s in shapes],
+        out_shape=[jax.ShapeDtypeStruct((n, SB_ROWS, D), F32), jax.ShapeDtypeStruct(o.shape, F32)]
         + [jax.ShapeDtypeStruct(s, F32) for s in shapes],
         scratch_shapes=recv_scratch(sb),
         compiler_params=params_spec(),
@@ -688,7 +714,7 @@
 
 def send_fwd_kernel(sb, dim_ref, r_ref, here_ref, *refs):
     w = {n: refs[i][...] for i, n in enumerate(SEND_W)}
-    vec_ref, o_ref, lse_ref, k_s, v_s, q_s = refs[3:]
+    vec_ref, o_ref, k_s, v_s, q_s = refs[3:]
     dim2 = split2(dim_ref[...].reshape(sb * SB_ROWS, D))
     send_project(dim2, r_ref[...].reshape(sb * RPAD, D), w, vec_ref[...], k_s, v_s, q_s)
     here = here_ref[...] > 0.5
@@ -702,8 +728,8 @@
         p = jnp.where(here, jnp.exp(sc - top), 0.0)
         total = jnp.sum(p, 0, keepdims=True)
         safe = jnp.where(total > 0.0, total, 1.0)
-        o_ref[s] = gather_rows(tn3(split2(p / safe), split2(v_s[at, :])))
-        lse_ref[s] = jnp.where(total > 0.0, top + jnp.log(safe), negative)
+        lse = jnp.where(total > 0.0, top + jnp.log(safe), negative)
+        o_ref[s] = pack_rows(gather_rows(tn3(split2(p / safe), split2(v_s[at, :]))), lse)
         return carry
 
     lax.fori_loop(0, sb, one, 0)
@@ -721,21 +747,21 @@
     ]
 
 
-def send_fwd(dim, routers, here, weights, sb):
+def send_fwd(dim, routers, here, weights, sb, npad):
     n = dim.shape[0]
     return pl.pallas_call(
         functools.partial(send_fwd_kernel, sb),
         grid=(n // sb,),
         in_specs=[seg_block(sb), seg_block(sb, RPAD), whole((SB_ROWS, HALF))] + send_weight_specs(),
-        out_specs=[seg_block(sb, RPAD), seg_block(sb, 1, HALF)],
-        out_shape=[jax.ShapeDtypeStruct((n, RPAD, D), F32), jax.ShapeDtypeStruct((n, 1, HALF), F32)],
+        out_specs=pack_spec(sb),
+        out_shape=jax.ShapeDtypeStruct((npad, PACK, HALF), F32),
         scratch_shapes=send_scratch(sb),
         compiler_params=params_spec(),
         name="send_fwd",
     )(dim, routers, here, *weights)
 
 
-def send_bwd_kernel(sb, dim_ref, dpart_ref, r_ref, o_ref, lse_ref, do_ref, here_ref, *refs):
+def send_bwd_kernel(sb, dim_ref, dpart_ref, r_ref, o_ref, do_ref, here_ref, *refs):
     w = {n: refs[i][...] for i, n in enumerate(SEND_W)}
     vec_ref, ddim_ref, dr_ref = refs[3:6]
     dsq_ref, dsk_ref, dsv_ref, rows = refs[6:10]
@@ -755,10 +781,10 @@
         ar = pl.ds(pl.multiple_of(s * RPAD, RPAD), RPAD)
         q2 = split2(spread_rows(q_s[ar, :]))
         k2 = split2(k_s[at, :])
-        p = jnp.where(here, jnp.exp(nt3(k2, q2) - lse_ref[s]), 0.0)
-        dwide = spread_rows(do_ref[s])
+        p = jnp.where(here, jnp.exp(nt3(k2, q2) - o_ref[s][2 * ROUT : 2 * ROUT + 1]), 0.0)
+        dwide = spread_rows(unpack_rows(do_ref[s]))
         d2 = split2(dwide)
-        owide = jnp.broadcast_to(o_ref[s][:, None, :], (RPAD, HEADS, D)).reshape(RPAD * HEADS, D)
+        owide = jnp.broadcast_to(unpack_rows(o_ref[s])[:, None, :], (RPAD, HEADS, D)).reshape(RPAD * HEADS, D)
         e2 = split2(dwide * owide)
         one_row = jnp.ones((8, D), BF)
         mean = (dots(one_row, e2[0], 1, 1) + dots(one_row, e2[1], 1, 1))[0:1]
@@ -785,13 +811,13 @@
     dr_ref[...] = mmwt(dq2, w["sq"]).reshape(sb, RPAD, D)
 
 
-def send_bwd(dim, dpart, routers, o, lse, do, here, weights, sb):
+def send_bwd(dim, dpart, routers, o, do, here, weights, sb):
     n = dim.shape[0]
     shapes = [(D, D)] * 3 + [(2, 8, D)]
     return pl.pallas_call(
         functools.partial(send_bwd_kernel, sb),
         grid=(n // sb,),
-        in_specs=[seg_block(sb), seg_block(sb), seg_block(sb, RPAD), seg_block(sb, RPAD), seg_block(sb, 1, HALF), seg_block(sb, RPAD), whole((SB_ROWS, HALF))]
+        in_specs=[seg_block(sb), seg_block(sb), seg_block(sb, RPAD), pack_spec(sb), pack_spec(sb), whole((SB_ROWS, HALF))]
         + send_weight_specs(),
         out_specs=[seg_block(sb), seg_block(sb, RPAD)] + [whole(s) for s in shapes],
         out_shape=[jax.ShapeDtypeStruct((n, SB_ROWS, D), F32), jax.ShapeDtypeStruct((n, RPAD, D), F32)]
@@ -799,18 +825,363 @@
         scratch_shapes=send_scratch(sb),
         compiler_params=params_spec(),
         name="send_bwd",
-    )(dim, dpart, routers, o, lse, do, here, *weights)
-
-
-def merge_stats(o, lse, axis):
-    every_o = lax.all_gather(o, axis)
-    every_l = lax.all_gather(lse, axis)
-    top = jnp.max(every_l, 0)
-    total = top + jnp.log(jnp.sum(jnp.exp(every_l - top), 0))
-    share = jnp.exp(every_l - total)
-    n = o.shape[0]
-    share = jnp.repeat(share.reshape(share.shape[0], n, RPAD, HEADS), D // HEADS, -1)
-    return jnp.sum(every_o * share, 0), total
+    )(dim, dpart, routers, o, do, here, *weights)
+
+MESH = pl.DeviceIdType.MESH
+ANY = pl.BlockSpec(memory_space=pl.ANY)
+INVMEM = pl.BlockSpec(memory_space=pltpu.VMEM)
+
+
+def grid_sizes():
+    nf = lax.axis_size("fsdp")
+    nx = 1
+    while 2 * nx * nx < nf:
+        nx *= 2
+    return lax.axis_size("dp") // 2, nf // nx, nx
+
+
+class Place:
+    def __init__(self):
+        self.ny, self.nz, self.nx = grid_sizes()
+        dp, fs = lax.axis_index("dp"), lax.axis_index("fsdp")
+        self.core, self.y = lax.rem(dp, 2), lax.div(dp, 2)
+        self.x, self.z = lax.rem(fs, self.nx), lax.div(fs, self.nx)
+
+    def at(self, y=None, core=None, z=None, x=None):
+        y = self.y if y is None else y
+        core = self.core if core is None else core
+        z = self.z if z is None else z
+        x = self.x if x is None else x
+        return (y * 2 + core, z * self.nx + x)
+
+    def other(self):
+        return 1 - self.core
+
+    def next_x(self, k):
+        return lax.rem(self.x + k, self.nx)
+
+    def next_y(self, k):
+        return lax.rem(self.y + k, self.ny)
+
+    def next_z(self, k):
+        return lax.rem(self.z + k, self.nz)
+
+    def neighbours(self):
+        out = [self.at(core=self.other())]
+        out += [self.at(x=self.next_x(k)) for k in range(1, self.nx)]
+        out += [self.at(y=self.next_y(k)) for k in range(1, self.ny)]
+        out += [self.at(z=self.next_z(k)) for k in range(1, self.nz)]
+        return out
+
+
+def greet(devices):
+    barrier = pltpu.get_barrier_semaphore()
+    for device in devices:
+        pl.semaphore_signal(barrier, inc=1, device_id=device, device_id_type=MESH)
+    pl.semaphore_wait(barrier, len(devices))
+
+
+def remote(src, dst, send, recv, device):
+    return pltpu.make_async_remote_copy(
+        src_ref=src, dst_ref=dst, send_sem=send, recv_sem=recv, device_id=device, device_id_type=MESH
+    )
+
+
+def gather_kernel(n, *refs):
+    shards, outs = refs[:n], refs[n : 2 * n]
+    send, recv, local = refs[2 * n :]
+    me = Place()
+    y, c, z, x = me.y, me.core, me.z, me.x
+    m = me.nx
+    greet(me.neighbours())
+    copies, slot = [], [0]
+
+    def push(src, dst, device):
+        copy = remote(src, dst, send.at[slot[0]], recv.at[slot[0]], device)
+        slot[0] += 1
+        copy.start()
+        return copy
+
+    own = [pltpu.make_async_copy(shards[j], outs[j].at[y, c, z, x], local.at[j]) for j in range(n)]
+    for copy in own:
+        copy.start()
+    first = [
+        push(shards[j], outs[j].at[y, c, z, x], me.at(z=me.next_z(k))) for j in range(n) for k in range(1, me.nz)
+    ]
+    for copy in own:
+        copy.wait()
+    for copy in first:
+        copy.wait()
+    base = slot[0]
+
+    def rest(by_core):
+        slot[0] = base
+        shared, started = [], []
+        sibling = me.at(core=1 - by_core)
+        second = []
+        for j in range(n):
+            piece = outs[j].at[y, by_core, :, x]
+            for k in range(1, m):
+                peer = me.at(x=me.next_x(k)) if by_core == 0 else me.at(y=me.next_y(k))
+                second.append(push(piece, piece, peer))
+            shared.append(push(piece, piece, sibling))
+        for copy in second:
+            copy.wait()
+        third = []
+        for j in range(n):
+            wide = outs[j].at[y, by_core] if by_core == 0 else outs[j].at[:, by_core, :, x]
+            for k in range(1, m):
+                peer = me.at(y=me.next_y(k)) if by_core == 0 else me.at(x=me.next_x(k))
+                third.append(push(wide, wide, peer))
+            for k in range(1, m):
+                piece = outs[j].at[y, by_core, :, me.next_x(k)] if by_core == 0 else outs[j].at[me.next_y(k), by_core, :, x]
+                shared.append(push(piece, piece, sibling))
+        for copy in third:
+            copy.wait()
+        for j in range(n):
+            for k in range(1, m):
+                wide = outs[j].at[me.next_y(k), by_core] if by_core == 0 else outs[j].at[:, by_core, :, me.next_x(k)]
+                shared.append(push(wide, wide, sibling))
+        for copy in shared:
+            copy.wait()
+
+    for by_core in (0, 1):
+        pl.when(c == by_core)(functools.partial(rest, by_core))
+
+
+def gather_all(shards):
+    ny, nz, nx = grid_sizes()
+    n = len(shards)
+    count = n * ((nz - 1) + (nx - 1) + 1 + (nx - 1) * 3)
+    return pl.pallas_call(
+        functools.partial(gather_kernel, n),
+        in_specs=[ANY] * n,
+        out_specs=[ANY] * n,
+        out_shape=[jax.ShapeDtypeStruct((ny, 2, nz, nx) + s.shape, s.dtype) for s in shards],
+        scratch_shapes=[pltpu.SemaphoreType.DMA((count,)), pltpu.SemaphoreType.DMA((count,)), pltpu.SemaphoreType.DMA((n,))],
+        compiler_params=pltpu.CompilerParams(collective_id=0, has_side_effects=True, vmem_limit_bytes=16 << 20),
+        name="gather_all",
+    )(*shards)
+
+
+def add_into(acc, at, terms, rows):
+    total = acc[at]
+    for ref, index in terms:
+        total = total + ref[index]
+    acc[at] = total
+
+
+def scatter_kernel(n, *refs):
+    grads, tile_ref = refs[:n], refs[n]
+    outs, stat_ref = refs[n + 1 : 2 * n + 1], refs[2 * n + 1]
+    acc, r1, r2, r3, r4 = (refs[2 * n + 2 + i * n : 2 * n + 2 + (i + 1) * n] for i in range(5))
+    tc, tx, ty, tz, send, recv, local = refs[7 * n + 2 :]
+    me = Place()
+    y, c, z, x = me.y, me.core, me.z, me.x
+    ny, nz, nx, m = me.ny, me.nz, me.nx, me.nx
+    greet(me.neighbours())
+    slot = [0]
+
+    def push(src, dst, device):
+        copy = remote(src, dst, send.at[slot[0]], recv.at[slot[0]], device)
+        slot[0] += 1
+        copy.start()
+        return copy
+
+    stage, own = [], []
+    for j in range(n):
+        stage.append([push(grads[j].at[:, me.other(), :, k], r1[j].at[:, k], me.at(core=me.other())) for k in range(nx)])
+        mine = [
+            pltpu.make_async_copy(grads[j].at[:, c, :, k], acc[j].at[:, k], local.at[j * nx + k]) for k in range(nx)
+        ]
+        for copy in mine:
+            copy.start()
+        own.append(mine)
+    base = slot[0]
+
+    def rest(by_core):
+        slot[0] = base
+        two, three, four = [], [], []
+        for j in range(n):
+            for copy in own[j] + stage[j]:
+                copy.wait()
+
+            def add1(i, carry):
+                at = (lax.div(i, nx * nz), lax.rem(lax.div(i, nz), nx), lax.rem(i, nz))
+                add_into(acc[j], at, [(r1[j], at)], None)
+                return carry
+
+            lax.fori_loop(0, ny * nx * nz, add1, 0)
+            if by_core == 0:
+                two.append([push(acc[j].at[:, me.next_x(k)], r2[j].at[k - 1], me.at(x=me.next_x(k))) for k in range(1, m)])
+            else:
+                two.append([push(acc[j].at[me.next_y(k)], r2[j].at[k - 1], me.at(y=me.next_y(k))) for k in range(1, m)])
+        for j in range(n):
+            for copy in two[j]:
+                copy.wait()
+
+            def add2(i, carry):
+                a, b = lax.div(i, nz), lax.rem(i, nz)
+                at = (a, x, b) if by_core == 0 else (y, a, b)
+                add_into(acc[j], at, [(r2[j], (k, a, b)) for k in range(m - 1)], None)
+                return carry
+
+            lax.fori_loop(0, m * nz, add2, 0)
+            if by_core == 0:
+                three.append([push(acc[j].at[me.next_y(k), x], r3[j].at[k - 1], me.at(y=me.next_y(k))) for k in range(1, m)])
+            else:
+                three.append([push(acc[j].at[y, me.next_x(k)], r3[j].at[k - 1], me.at(x=me.next_x(k))) for k in range(1, m)])
+        for j in range(n):
+            for copy in three[j]:
+                copy.wait()
+
+            def add3(i, carry):
+                add_into(acc[j], (y, x, i), [(r3[j], (k, i)) for k in range(m - 1)], None)
+                return carry
+
+            lax.fori_loop(0, nz, add3, 0)
+            four.append(
+                [push(acc[j].at[y, x, me.next_z(k)], r4[j].at[k - 1], me.at(z=me.next_z(k))) for k in range(1, nz)]
+            )
+        squares = jnp.zeros((8, HALF), F32)
+        for j in range(n):
+            for copy in four[j]:
+                copy.wait()
+            total = acc[j][y, x, z]
+            for k in range(nz - 1):
+                total = total + r4[j][k]
+            outs[j][...] = total
+            sq = colsum_any(total * total)
+            squares = squares + sq[:, :HALF] + sq[:, HALF:]
+        tc[c] = jnp.concatenate([squares, tile_ref[...]], 0)
+
+    for by_core in (0, 1):
+        pl.when(c == by_core)(functools.partial(rest, by_core))
+
+    slot[0] = base + n * ((m - 1) * 2 + nz - 1)
+    push(tc.at[c], tc.at[c], me.at(core=me.other())).wait()
+    tx[x] = tc[0] + tc[1]
+    for copy in [push(tx.at[x], tx.at[x], me.at(x=me.next_x(k))) for k in range(1, nx)]:
+        copy.wait()
+    ty[y] = functools.reduce(jnp.add, [tx[k] for k in range(nx)])
+    for copy in [push(ty.at[y], ty.at[y], me.at(y=me.next_y(k))) for k in range(1, ny)]:
+        copy.wait()
+    tz[z] = functools.reduce(jnp.add, [ty[k] for k in range(ny)])
+    for copy in [push(tz.at[z], tz.at[z], me.at(z=me.next_z(k))) for k in range(1, nz)]:
+        copy.wait()
+    stat_ref[...] = functools.reduce(jnp.add, [tz[k] for k in range(nz)])
+
+
+def colsum_any(x):
+    rows = x.shape[0]
+    even = rows // 8 * 8
+    out = colsum(x[:even]) if even else jnp.zeros((8, x.shape[1]), F32)
+    if rows > even:
+        out = out + jnp.pad(x[even:], ((0, 8 - rows + even), (0, 0)))
+    return out
+
+
+def scatter_sum(grads, tile):
+    ny, nz, nx = grid_sizes()
+    n = len(grads)
+    shapes = [g.shape[-2:] for g in grads]
+    count = n * nx + n * ((nx - 1) * 2 + nz - 1) + 1 + (nx - 1) + (ny - 1) + (nz - 1)
+
+    def buffers(*lead):
+        return [pltpu.VMEM(lead + s, F32) for s in shapes]
+
+    return pl.pallas_call(
+        functools.partial(scatter_kernel, n),
+        in_specs=[ANY] * n + [INVMEM],
+        out_specs=[INVMEM] * (n + 1),
+        out_shape=[jax.ShapeDtypeStruct(s, F32) for s in shapes] + [jax.ShapeDtypeStruct((16, HALF), F32)],
+        scratch_shapes=buffers(ny, nx, nz)
+        + buffers(ny, nx, nz)
+        + buffers(nx - 1, nx, nz)
+        + buffers(nx - 1, nz)
+        + buffers(nz - 1)
+        + [pltpu.VMEM((k, 16, HALF), F32) for k in (2, nx, ny, nz)]
+        + [pltpu.SemaphoreType.DMA((count,)), pltpu.SemaphoreType.DMA((count,)), pltpu.SemaphoreType.DMA((n * nx,))],
+        compiler_params=pltpu.CompilerParams(collective_id=1, has_side_effects=True, vmem_limit_bytes=VMEM_LIMIT),
+        name="scatter_sum",
+    )(*grads, tile)
+
+
+def group_kernel(stats, per, in_ref, out_ref, got, result, send, recv, local):
+    nf = lax.axis_size("fsdp")
+    dp, f = lax.axis_index("dp"), lax.axis_index("fsdp")
+    peers = [lax.rem(f + k, nf) for k in range(1, nf)]
+    greet([(dp, p) for p in peers])
+
+    def part(ref, who):
+        return ref.at[pl.ds(pl.multiple_of(who * per, per), per)]
+
+    own = pltpu.make_async_copy(part(in_ref, f), got.at[f], local)
+    own.start()
+    copies = [
+        remote(part(in_ref, p), got.at[f], send.at[k], recv.at[k], (dp, p)) for k, p in enumerate(peers)
+    ]
+    for copy in copies:
+        copy.start()
+    own.wait()
+    for copy in copies:
+        copy.wait()
+    if stats:
+        row = lax.broadcasted_iota(jnp.int32, (PACK, HALF), 0)
+        lane = lax.broadcasted_iota(jnp.int32, (PACK, HALF), 1)
+        router = jnp.where(row < ROUT, row, row - ROUT)
+        pick = (lane // 8 == router) & (row < 2 * ROUT)
+        src = lax.broadcasted_iota(jnp.int32, (HALF, D), 0)
+        dst = lax.broadcasted_iota(jnp.int32, (HALF, D), 1)
+        widen = jnp.where(src % 8 == dst // 32, 1.0, 0.0).astype(BF)
+
+        def one(s, carry):
+            lse = [got[d, s, 2 * ROUT : 2 * ROUT + 1, :] for d in range(nf)]
+            top = functools.reduce(jnp.maximum, lse)
+            total = top + jnp.log(functools.reduce(jnp.add, [jnp.exp(l - top) for l in lse]))
+            out = jnp.where(row == 2 * ROUT, total, 0.0)
+            share = jnp.concatenate([jnp.where(pick, jnp.exp(l - total), 0.0) for l in lse], 0)
+            wide = mmw(split2(share), widen)
+            for d in range(nf):
+                w = wide[d * PACK : (d + 1) * PACK]
+                w = jnp.where(row < ROUT, w[:, :HALF], w[:, HALF:])
+                out = out + jnp.where(row < 2 * ROUT, w * got[d, s], 0.0)
+            result[s] = out
+            return carry
+
+        lax.fori_loop(0, per, one, 0)
+    else:
+        result[...] = functools.reduce(jnp.add, [got[d] for d in range(nf)])
+    own = pltpu.make_async_copy(result, part(out_ref, f), local)
+    own.start()
+    copies = [
+        remote(result, part(out_ref, f), send.at[nf - 1 + k], recv.at[nf - 1 + k], (dp, p)) for k, p in enumerate(peers)
+    ]
+    for copy in copies:
+        copy.start()
+    own.wait()
+    for copy in copies:
+        copy.wait()
+
+
+def group_combine(packed, stats, cid):
+    nf = lax.axis_size("fsdp")
+    per = packed.shape[0] // nf
+    return pl.pallas_call(
+        functools.partial(group_kernel, stats, per),
+        in_specs=[INVMEM],
+        out_specs=INVMEM,
+        out_shape=jax.ShapeDtypeStruct(packed.shape, F32),
+        scratch_shapes=[
+            pltpu.VMEM((nf, per, PACK, HALF), F32),
+            pltpu.VMEM((per, PACK, HALF), F32),
+            pltpu.SemaphoreType.DMA((2 * nf - 2,)),
+            pltpu.SemaphoreType.DMA((2 * nf - 2,)),
+            pltpu.SemaphoreType.DMA,
+        ],
+        compiler_params=pltpu.CompilerParams(collective_id=cid, has_side_effects=True, vmem_limit_bytes=32 << 20),
+        name="group_stats" if stats else "group_sum",
+    )(packed)
 
 
 def series_stats(series, observed):
@@ -843,7 +1214,7 @@
     return jnp.pad(x, ((0, rows - x.shape[0]), (0, 0)))
 
 
-def gradient_parts(series, observed, targets, target_mask, present, square, up, down, vectors):
+def gradient_parts(series, observed, targets, target_mask, present, square, up, down, vectors, combine, nf):
     nv = series.shape[0]
     normed, mean, scale = series_stats(series, observed)
     pieces = segment_major(normed, 16)
@@ -877,23 +1248,23 @@
 
     sb0, sb1 = 4, 6
     dim0 = time_fwd(True, pieces, (emb, place), time_w[0], SEG)
-    o0, lse0 = send_fwd(dim0, routers[0], here, send_w[0], sb0)
-    o0, lse0 = merge_stats(o0, lse0, "fsdp")
+    o0 = send_fwd(dim0, routers[0], here, send_w[0], sb0, -(-SEG // nf) * nf)
+    o0 = combine(o0, True, 2)
     x1 = recv_fwd(dim0, o0, recv_w[0], mvec, mw, sb0)
     dim1 = time_fwd(False, x1, (), time_w[1], SEG // 2)
-    o1, lse1 = send_fwd(dim1, routers[1], here, send_w[1], sb1)
-    o1, lse1 = merge_stats(o1, lse1, "fsdp")
+    o1 = send_fwd(dim1, routers[1], here, send_w[1], sb1, -(-SEG // 2 // nf) * nf)
+    o1 = combine(o1, True, 3)
     out = tail(dim1, o1, tgt, kept, scale16, mean16, recv_w[1], head, sb1)
     ddim1, do1, grecv1, dhead = out[0], out[1], out[2:10], out[10]
-    do1 = lax.psum(do1, "fsdp")
-    out = send_bwd(dim1, ddim1, routers[1], o1, lse1, do1, here, send_w[1], sb1)
+    do1 = combine(do1, False, 4)
+    out = send_bwd(dim1, ddim1, routers[1], o1, do1, here, send_w[1], sb1)
     ddim1, dr1, gsend1 = out[0], out[1], out[2:]
     out = time_bwd(False, x1, (), ddim1, time_w[1], SEG // 2)
     gtime1, dx1 = out[:7], out[7]
     out = recv_bwd(dim0, o0, dx1, recv_w[0], mvec, mw, sb0)
     ddim0, do0, grecv0, dmw, dmv = out[0], out[1], out[2:10], out[10], out[11]
-    do0 = lax.psum(do0, "fsdp")
-    out = send_bwd(dim0, ddim0, routers[0], o0, lse0, do0, here, send_w[0], sb0)
+    do0 = combine(do0, False, 5)
+    out = send_bwd(dim0, ddim0, routers[0], o0, do0, here, send_w[0], sb0)
     ddim0, dr0, gsend0 = out[0], out[1], out[2:]
     out = time_bwd(True, pieces, (emb, place), ddim0, time_w[0], SEG)
     gtime0, demb, dplace = out[:7], out[7], out[8]
@@ -918,25 +1289,43 @@
 
 
 def on_device(series, observed, targets, target_mask, counts, matrices, feed_weights, vectors, matrices_first, matrices_second, feed_first, feed_second, vectors_first, vectors_second):
-    everywhere = ("dp", "fsdp")
     local_vars = series.shape[1]
+    nf = lax.axis_size("fsdp")
+    devices = nf * lax.axis_size("dp")
     slot = lax.axis_index("fsdp") * local_vars + jnp.arange(local_vars, dtype=jnp.int32)
     present = (slot < counts[0]).astype(F32)
-    square = lax.all_gather(matrices.astype(BF), everywhere, axis=0, tiled=True).reshape(NSQ, D, D)
-    feed = lax.all_gather(feed_weights.astype(BF), everywhere, axis=0, tiled=True)
-    up = feed[: 4 * D * FF].reshape(4, D, FF)
-    down = feed[4 * D * FF :].reshape(4, FF, D)
-    vecs = lax.all_gather(vectors.astype(BF), everywhere, axis=0, tiled=True).astype(F32).reshape(NVEC, D)
+    own_rows = NVEC * D // devices
+    vec_rows = -(-own_rows // D)
+
+    def as_rows(x):
+        return x.reshape(-1, D)
+
+    def pad_flat(x):
+        return jnp.pad(x, [(0, 0)] * (x.ndim - 1) + [(0, vec_rows * D - own_rows)])
+
+    square, feed, vecs = gather_all(
+        [as_rows(matrices.astype(BF)), as_rows(feed_weights.astype(BF)), as_rows(pad_flat(vectors.astype(BF)))]
+    )
+    square = square.reshape(NSQ, D, D)
+    feed = feed.reshape(-1, D)
+    up = feed[: 4 * FF].reshape(4, D, FF)
+    down = feed[4 * FF :].reshape(4, FF, D)
+    vecs = vecs.reshape(devices, -1)[:, :own_rows].reshape(NVEC, D).astype(F32)
     g_mat, g_up, g_down, g_vec = gradient_parts(
-        series[0], observed[0], targets[0], target_mask[0], present, square, up, down, vecs
+        series[0], observed[0], targets[0], target_mask[0], present, square, up, down, vecs, group_combine, nf
     )
-    flat = (g_mat.reshape(-1), jnp.concatenate([g_up.reshape(-1), g_down.reshape(-1)]), g_vec.reshape(-1))
-    shards = [lax.psum_scatter(f, everywhere, scatter_dimension=0, tiled=True) for f in flat]
-    kept = jnp.sum(target_mask[0].astype(F32) * present[:, None])
-    squares = sum(jnp.sum(s * s) for s in shards)
-    sums = lax.psum(jnp.stack([squares, kept]), everywhere)
-    upscale = (1 << 20) / jnp.maximum(sums[1], 1.0)
-    grad_norm = jnp.sqrt(sums[0]) * upscale
+    g_feed = jnp.concatenate([g_up.reshape(-1, D), g_down], 0)
+    g_vec = pad_flat(g_vec.reshape(devices, own_rows))
+    ny, nz, nx = grid_sizes()
+    lead = (ny, 2, nz, nx)
+    kept = target_mask[0].astype(F32) * present[:, None]
+    tile = jnp.pad(jnp.sum(kept).reshape(1, 1), ((0, 7), (0, HALF - 1)))
+    s_mat, s_feed, s_vec, sums = scatter_sum(
+        [g_mat.reshape(lead + (-1, D)), g_feed.reshape(lead + (-1, D)), g_vec.reshape(lead + (-1, D))], tile
+    )
+    shards = (s_mat.reshape(-1), s_feed.reshape(-1), s_vec.reshape(-1)[:own_rows])
+    upscale = (1 << 20) / jnp.maximum(jnp.sum(sums[8:]), 1.0)
+    grad_norm = jnp.sqrt(jnp.sum(sums[:8])) * upscale
     factor = upscale * (clip_norm / jnp.maximum(grad_norm, clip_norm))
     new = (
         adam_update(matrices, matrices_first, matrices_second, shards[0] * factor)

time: 1880 us -> 1350 us (0.72)
  waiting for transfers between devices: 661 us -> 0 us
  Pallas kernels: 916 us -> 1200 us
  blocking collectives: 103 us -> 0 us
  local copies, waits for them, and re-layouts: 130 us -> 94.5 us
    unnamed x10 -> x0, waiting for transfers between devices: 347 us -> none
    pallas_call x0 -> x6, Pallas kernels: none -> 287 us  [the longest x4 122 us: group_combine(): pl.pallas_call(functools.partial(group_kernel, stats, per), in_specs=[INV...]
    all_gather x4 -> x0, waiting for transfers between devices: 171 us -> none  [the longest x1 59.3 us: on_device(): lax.all_gather(matrices.astype(BF), everywhere, axis=0, tiled=True)]
    psum x2 -> x0, waiting for transfers between devices: 143 us -> none  [the longest x1 73.6 us: gradient_parts(): do0 = lax.psum(do0, 'fsdp')]
    all_gather x2 -> x0, blocking collectives: 63.7 us -> none  [merge_stats(): every_l = lax.all_gather(lse, axis)]
    psum x1 -> x0, blocking collectives: 39.5 us -> none  [on_device(): sums = lax.psum(jnp.stack([squares, kept]), everywhere)]
    slice x37 -> x2, local copies, waits for them, and re-layouts: 29.6 us -> 0.99 us  [the longest x1 0.83 us: on_device(): vecs = vecs.reshape(devices, -1)[:, :own_rows].reshape(NVEC, D).astype(F32)]
    reshape x4 -> x8, local copies, waits for them, and re-layouts: 27.8 us -> 6.51 us  [the longest x1 1.74 us: on_device(): g_feed = jnp.concatenate([g_up.reshape(-1, D), g_down], 0)]
  transfers between devices with their start and end apart: 8 -> 0, of which waited for: 8 -> 0; matrix products, arithmetic and copies ran while one was open for 5% -> 0% of each run, Pallas kernels for 0% -> 0%
where the time goes in v2:
time: 1350 us; the launch traced here: 1340 us
  Pallas kernels  1200 us (89%)
  local copies, waits for them, and re-layouts  94.5 us (7%)
  other arithmetic  33.2 us (2%)
    pallas_call x2, Pallas kernels, time_bwd(): pl.pallas_call(functools.partial(time_bwd_kernel, first, count, group), g...  290 us
    pallas_call x1, Pallas kernels, recv_bwd(): pl.pallas_call(functools.partial(recv_bwd_kernel, sb), grid=(n // sb,), i...  179 us
    pallas_call x2, Pallas kernels, time_fwd(): pl.pallas_call(functools.partial(time_fwd_kernel, first, count, group), g...  134 us
    pallas_call x4, Pallas kernels, group_combine(): pl.pallas_call(functools.partial(group_kernel, stats, per), in_specs=[INV...  122 us
    pallas_call x1, Pallas kernels, scatter_sum(): pl.pallas_call(functools.partial(scatter_kernel, n), in_specs=[ANY] * n +...  108 us
    pallas_call x1, Pallas kernels, recv_fwd(): pl.pallas_call(functools.partial(recv_fwd_kernel, sb), grid=(n // sb,), i...  90.8 us
    pallas_call x1, Pallas kernels, tail(): pl.pallas_call(functools.partial(tail_kernel, sb), grid=(n // sb,), in_sp...  85.1 us
    pallas_call x2, Pallas kernels, send_bwd(): pl.pallas_call(functools.partial(send_bwd_kernel, sb), grid=(n // sb,), i...  80.6 us

profile of v2, /device:TPU:0, one launch (start us, length us, event | category | flops | bytes accessed | tf_op | source)
XLA Modules:
  0.0 1335.7 jit_solution(584009030324241963)
XLA Ops:
  1.3 1.6 fusion.6
  2.9 1.0 convert_reduce_fusion
  3.9 1.2 fusion.1
  5.1 1.2 fusion.4
  6.4 1.3 pad.62.refs_3_
  14.1 1.0 copy.42
  16.3 1.1 copy.36
  17.8 1.0 pad.58.tgt_ref
  19.4 1.0 pad.59.kept_ref
  21.1 2.0 copy.40
  23.1 2.0 divide_bitcast_fusion
  25.2 1.5 pad.50.refs_0_
  27.5 57.4 %gather_all.1 = (bf16[2,2,4,2,208,256]{5,4,3,2,1,0:T(8,128)(2,1)S(1)}, bf16[2,2,4,2,128,256]{5,4,3,2,1,0:T(8,128)(2,1)S(1)}, bf16[2,2,4,2,33,256]{5,4,3,2,1,0:T(8,128)(2,1)S(1)}) custom-call(bf16[208,256]{1,0:T(8,128)(2,1)S(1)} %reshape.142.refs_0_, bf16[128,256]{1,0:T(8,128)(2,1)S(1)} %copy-done.10, bf16[33,256]{1,0:T(8,128)(2,1)S(1)} %reshape.144.refs_2_), custom_call_target="tpu_custom_call" | custom-call | tf_op jit(solution)/shard_map/gather_all/pallas_call | solution.py:956
  84.9 1.3 copy-done.4
  87.2 2.6 convert_element_type.76
  95.8 1.7 slice.243
  97.5 1.8 reshape.151
  99.3 1.9 pad.57.r_ref
  101.1 1.8 slice.223
  103.0 2.1 reshape.149
  105.1 2.4 pad.54.r_ref
  107.5 1.1 convert_element_type.77
  110.8 1.4 slice_bitcast_fusion.8
  114.8 77.5 %time_fwd.2.dim_ref.send_ref = f32[60,64,256]{2,1,0:T(8,128)} custom-call(f32[60,64,16]{2,1,0:T(8,128)} %pad.50.refs_0_, bf16[16,256]{1,0:T(8,128)(2,1)} %fusion.9.refs_1_, f32[60,1,256]{2,1,0:T(1,128)} %copy.47.refs_2_, bf16[256,256]{1,0:T(8,128)(2,1)} %get-tuple-element.162.refs_3_.refs_4_, bf16[256,256]{1,0:T(8,128)(2,1)} %get-tuple-element.161.refs_4_.refs_5_, ...), custom_call_target="tpu_custom_call" | custom-call | tf_op jit(solution)/shard_map/time_fwd/pallas_call | solution.py:271
  192.2 38.0 %send_fwd.2.in_ref = f32[64,24,128]{2,1,0:T(8,128)} custom-call(f32[60,64,256]{2,1,0:T(8,128)} %time_fwd.2.dim_ref.send_ref, f32[60,16,256]{2,1,0:T(8,128)} %pad.54.r_ref, f32[64,128]{1,0:T(8,128)} %broadcast_in_dim.11.here_ref, bf16[256,256]{1,0:T(8,128)(2,1)} %get-tuple-element.158.refs_0_, bf16[256,256]{1,0:T(8,128)(2,1)} %get-tuple-element.157.refs_1_, ...), custom_call_target="tpu_custom_call" | custom-call | tf_op jit(solution)/shard_map/send_fwd/pallas_call | solution.py:752
  230.2 1.1 copy-done.3
  231.4 35.5 %group_stats.2.o_ref = f32[64,24,128]{2,1,0:T(8,128)S(1)} custom-call(f32[64,24,128]{2,1,0:T(8,128)S(1)} %copy-done.3), custom_call_target="tpu_custom_call" | custom-call | tf_op jit(solution)/shard_map/group_stats/pallas_call | solution.py:1170
  267.7 90.8 %recv_fwd.1.refs_0_ = f32[30,64,256]{2,1,0:T(8,128)} custom-call(f32[60,64,256]{2,1,0:T(8,128)} %time_fwd.2.dim_ref.send_ref, f32[64,24,128]{2,1,0:T(8,128)} %copy-done, bf16[256,256]{1,0:T(8,128)(2,1)} %get-tuple-element.155.refs_0_, bf16[256,256]{1,0:T(8,128)(2,1)} %get-tuple-element.154.refs_1_, bf16[256,256]{1,0:T(8,128)(2,1)} %get-tuple-element.153.refs_2_, ...), custom_call_target="tpu_custom_call" | custom-call | tf_op jit(solution)/shard_map/recv_fwd/pallas_call | solution.py:583
  358.5 56.2 %time_fwd.3.dim_ref.send_ref = f32[30,64,256]{2,1,0:T(8,128)} custom-call(f32[30,64,256]{2,1,0:T(8,128)} %recv_fwd.1.refs_0_, bf16[256,256]{1,0:T(8,128)(2,1)} %get-tuple-element.150.refs_1_.refs_2_, bf16[256,256]{1,0:T(8,128)(2,1)} %get-tuple-element.149.refs_2_.refs_3_, bf16[256,256]{1,0:T(8,128)(2,1)} %get-tuple-element.148.refs_3_.refs_4_, ...), custom_call_target="tpu_custom_call" | custom-call | tf_op jit(solution)/shard_map/time_fwd/pallas_call | solution.py:271
  414.7 19.5 %send_fwd.3.in_ref = f32[32,24,128]{2,1,0:T(8,128)} custom-call(f32[30,64,256]{2,1,0:T(8,128)} %time_fwd.3.dim_ref.send_ref, f32[30,16,256]{2,1,0:T(8,128)} %pad.57.r_ref, f32[64,128]{1,0:T(8,128)} %broadcast_in_dim.11.here_ref, bf16[256,256]{1,0:T(8,128)(2,1)} %get-tuple-element.146.refs_0_, bf16[256,256]{1,0:T(8,128)(2,1)} %get-tuple-element.145.refs_1_, ...), custom_call_target="tpu_custom_call" | custom-call | tf_op jit(solution)/shard_map/send_fwd/pallas_call | solution.py:752
  434.2 1.0 copy-done.6
  435.2 24.5 %group_stats.3.o_ref = f32[32,24,128]{2,1,0:T(8,128)S(1)} custom-call(f32[32,24,128]{2,1,0:T(8,128)S(1)} %copy-done.6), custom_call_target="tpu_custom_call" | custom-call | tf_op jit(solution)/shard_map/group_stats/pallas_call | solution.py:1170
  460.5 85.1 %tail.1 = (f32[30,64,256]{2,1,0:T(8,128)}, f32[32,24,128]{2,1,0:T(8,128)}, f32[256,256]{1,0:T(8,128)}, f32[256,256]{1,0:T(8,128)}, f32[256,256]{1,0:T(8,128)}, /...) custom-call(f32[30,64,256]{2,1,0:T(8,128)} %time_fwd.3.dim_ref.send_, ...), custom_call_target="tpu_custom_call" | custom-call | tf_op jit(solution)/shard_map/tail/pallas_call | solution.py:688
  546.5 1.0 copy-done.9
  547.5 24.8 %group_sum.2.do_ref = f32[32,24,128]{2,1,0:T(8,128)S(1)} custom-call(f32[32,24,128]{2,1,0:T(8,128)S(1)} %copy-done.9), custom_call_target="tpu_custom_call" | custom-call | tf_op jit(solution)/shard_map/group_sum/pallas_call | solution.py:1170
  573.0 27.1 %send_bwd.2 = (f32[30,64,256]{2,1,0:T(8,128)}, f32[30,16,256]{2,1,0:T(8,128)}, f32[256,256]{1,0:T(8,128)}, f32[256,256]{1,0:T(8,128)}, f32[256,256]{1,0:T(8,128)}, /*index=5*/f32[2,8,256]{2,1,0:T(8,128)}) custom-call(f32[30,64,256]{2,1,0:T(8,128)} %time_fwd.3.dim_ref.send_ref, f32[30,64,256]{2,1,0:T(8,128)} %get-tuple-element.72.dpart_ref, ...), custom_call_target="tpu_custom_call" | custom-call | tf_op jit(solution)/shard_map/send_bwd/pallas_call | solution.py:817
  600.1 120.3 %time_bwd.2 = (f32[256,256]{1,0:T(8,128)}, f32[256,256]{1,0:T(8,128)}, f32[256,256]{1,0:T(8,128)}, f32[256,256]{1,0:T(8,128)}, f32[256,512]{1,0:T(8,128)}, /*ind...) custom-call(f32[30,64,256]{2,1,0:T(8,128)} %recv_fwd.1.refs_0_, ...), custom_call_target="tpu_custom_call" | custom-call | tf_op jit(solution)/shard_map/time_bwd/pallas_call | solution.py:381
  720.4 1.3 reduce_sum.144
  721.7 1.5 reduce_sum.143
  723.2 1.1 reshape.157
  724.3 178.8 %recv_bwd.1 = (f32[60,64,256]{2,1,0:T(8,128)}, f32[64,24,128]{2,1,0:T(8,128)}, f32[256,256]{1,0:T(8,128)}, f32[256,256]{1,0:T(8,128)}, f32[256,256]{1,0:T(8,128)...) custom-call(f32[60,64,256]{2,1,0:T(8,128)} %time_fwd.2.dim_ref.send_, ...), custom_call_target="tpu_custom_call" | custom-call | tf_op jit(solution)/shard_map/recv_bwd/pallas_call | solution.py:639
  903.1 1.4 reduce_sum.146
  904.5 1.5 reduce_sum.142
  906.0 1.1 copy-done.8
  907.2 37.1 %group_sum.3.do_ref = f32[64,24,128]{2,1,0:T(8,128)S(1)} custom-call(f32[64,24,128]{2,1,0:T(8,128)S(1)} %copy-done.8), custom_call_target="tpu_custom_call" | custom-call | tf_op jit(solution)/shard_map/group_sum/pallas_call | solution.py:1170
  945.2 53.5 %send_bwd.3 = (f32[60,64,256]{2,1,0:T(8,128)}, f32[60,16,256]{2,1,0:T(8,128)}, f32[256,256]{1,0:T(8,128)}, f32[256,256]{1,0:T(8,128)}, f32[256,256]{1,0:T(8,128)}, /*index=5*/f32[2,8,256]{2,1,0:T(8,128)}) custom-call(f32[60,64,256]{2,1,0:T(8,128)} %time_fwd.2.dim_ref.send_ref, f32[60,64,256]{2,1,0:T(8,128)} %get-tuple-element.76.dpart_ref, ...), custom_call_target="tpu_custom_call" | custom-call | tf_op jit(solution)/shard_map/send_bwd/pallas_call | solution.py:817
  998.7 169.3 %time_bwd.3 = (f32[256,256]{1,0:T(8,128)}, f32[256,256]{1,0:T(8,128)}, f32[256,256]{1,0:T(8,128)}, f32[256,256]{1,0:T(8,128)}, f32[256,512]{1,0:T(8,128)}, /*ind...) custom-call(f32[60,64,16]{2,1,0:T(8,128)} %pad.50.refs_0_, ...), custom_call_target="tpu_custom_call" | custom-call | tf_op jit(solution)/shard_map/time_bwd/pallas_call | solution.py:381
  1168.0 1.7 reduce_sum.138
  1169.7 1.2 bitcast_reduce_fusion
  1170.9 1.5 reduce_sum.140
  1173.0 2.5 pad_maximum_fusion
  1175.5 1.7 reshape.153
  1178.2 8.9 concatenate.15
  1187.1 1.7 reshape.158
  1188.8 1.3 pad.61
  1190.1 1.3 reshape.159.refs_2_
  1191.5 1.5 constant_dynamic-update-slice_fusion.29
  1193.0 2.3 constant_dynamic-update-slice_fusion.28
  1195.3 1.7 constant_dynamic-update-slice_fusion.24
  1197.0 1.7 constant_dynamic-update-slice_fusion.23
  1198.6 1.7 constant_dynamic-update-slice_fusion.22
  1215.5 1.1 constant_dynamic-update-slice_fusion
  1218.3 108.0 %scatter_sum.1 = (f32[208,256]{1,0:T(8,128)}, f32[128,256]{1,0:T(8,128)}, f32[33,256]{1,0:T(8,128)}, f32[16,128]{1,0:T(8,128)}) custom-call(f32[2,2,4,2,208,256]{5,4,3,2,1,0:T(8,128)} %bitcast.43.refs_0_, f32[2,2,4,2,128,256]{5,4,3,2,1,0:T(8,128)} %bitcast.44.refs_1_, f32[2,2,4,2,33,256]{5,4,3,2,1,0:T(8,128)} %reshape.159.refs_2_, f32[8,128]{1,0:T(8,128)} %pad.62.refs_3_), custom_call_target="tpu_custom_call" | custom-call | tf_op jit(solution)/shard_map/scatter_sum/pallas_call | solution.py:1093
  1326.4 1.3 slice_reduce_fusion
  (175 shorter events, 49.7 us)
Async XLA Ops:
  26.7 0.8 copy-start.10
  27.5 81.1 %copy-start.50 = (pred[16]{0:T(512)(128)(4,1)S(1)}, pred[16]{0:T(512)(128)(4,1)}, u32[]{:S(2)}) copy-start(pred[16]{0:T(512)(128)(4,1)} %constant.21.clone.1) | copy-start | bytes 52
  84.9 1.3 copy-start.4
  105.1 7.2 copy-start.5
  230.2 1.1 copy-start.3
  266.9 0.9 copy-start
  434.2 1.0 copy-start.6
  459.7 0.8 copy-start.1
  546.5 1.0 copy-start.9
  572.3 0.8 copy-start.7
  906.0 1.1 copy-start.8
  944.3 0.9 copy-start.2
  998.7 173.7 %copy-start.49 = (f32[2,8,256]{2,1,0:T(8,128)S(1)}, f32[2,8,256]{2,1,0:T(8,128)}, u32[]{:S(2)}) copy-start(f32[2,8,256]{2,1,0:T(8,128)} %get-tuple-element.115) | copy-start | bytes 49156
  998.7 174.3 %copy-start.18 = (f32[256,512]{1,0:T(8,128)S(1)}, f32[256,512]{1,0:T(8,128)}, u32[]{:S(2)}) copy-start(f32[256,512]{1,0:T(8,128)} %get-tuple-element.107) | copy-start | bytes 1572868
  998.7 174.3 %copy-start.19 = (f32[256,512]{1,0:T(8,128)S(1)}, f32[256,512]{1,0:T(8,128)}, u32[]{:S(2)}) copy-start(f32[256,512]{1,0:T(8,128)} %get-tuple-element.106) | copy-start | bytes 1572868
  998.7 174.3 %copy-start.20 = (f32[256,512]{1,0:T(8,128)S(1)}, f32[256,512]{1,0:T(8,128)}, u32[]{:S(2)}) copy-start(f32[256,512]{1,0:T(8,128)} %get-tuple-element.105) | copy-start | bytes 1572868
  998.7 178.6 %copy-start.11 = (f32[60,16,256]{2,1,0:T(8,128)S(1)}, f32[60,16,256]{2,1,0:T(8,128)}, u32[]{:S(2)}) copy-start(f32[60,16,256]{2,1,0:T(8,128)} %get-tuple-element.122) | copy-start | bytes 2949124
  1190.1 17.5 %copy-start.31 = (f32[256,256]{1,0:T(8,128)S(1)}, f32[256,256]{1,0:T(8,128)}, u32[]{:S(2)}) copy-start(f32[256,256]{1,0:T(8,128)} %get-tuple-element.92) | copy-start | bytes 786436
  1191.3 9.0 copy-start.41
  1191.3 9.7 copy-start.40
  1191.4 10.4 copy-start.39
  1191.4 11.2 copy-start.38
  1191.4 11.9 copy-start.37
  1191.4 12.6 copy-start.36
  1191.4 13.3 copy-start.35
  1191.4 14.0 %copy-start.34 = (f32[256,256]{1,0:T(8,128)S(1)}, f32[256,256]{1,0:T(8,128)}, u32[]{:S(2)}) copy-start(f32[256,256]{1,0:T(8,128)} %get-tuple-element.89) | copy-start | bytes 786436
  1191.4 14.7 %copy-start.33 = (f32[256,256]{1,0:T(8,128)S(1)}, f32[256,256]{1,0:T(8,128)}, u32[]{:S(2)}) copy-start(f32[256,256]{1,0:T(8,128)} %get-tuple-element.90) | copy-start | bytes 786436
  1191.4 15.4 %copy-start.32 = (f32[256,256]{1,0:T(8,128)S(1)}, f32[256,256]{1,0:T(8,128)}, u32[]{:S(2)}) copy-start(f32[256,256]{1,0:T(8,128)} %get-tuple-element.91) | copy-start | bytes 786436
  1191.4 16.9 %copy-start.30 = (f32[256,256]{1,0:T(8,128)S(1)}, f32[256,256]{1,0:T(8,128)}, u32[]{:S(2)}) copy-start(f32[256,256]{1,0:T(8,128)} %get-tuple-element.93) | copy-start | bytes 786436
  1191.4 17.6 %copy-start.29 = (f32[256,256]{1,0:T(8,128)S(1)}, f32[256,256]{1,0:T(8,128)}, u32[]{:S(2)}) copy-start(f32[256,256]{1,0:T(8,128)} %get-tuple-element.94) | copy-start | bytes 786436
  1191.4 18.3 %copy-start.28 = (f32[256,256]{1,0:T(8,128)S(1)}, f32[256,256]{1,0:T(8,128)}, u32[]{:S(2)}) copy-start(f32[256,256]{1,0:T(8,128)} %get-tuple-element.95) | copy-start | bytes 786436
  1191.4 19.0 %copy-start.27 = (f32[256,256]{1,0:T(8,128)S(1)}, f32[256,256]{1,0:T(8,128)}, u32[]{:S(2)}) copy-start(f32[256,256]{1,0:T(8,128)} %get-tuple-element.96) | copy-start | bytes 786436
  1191.5 19.7 %copy-start.26 = (f32[256,256]{1,0:T(8,128)S(1)}, f32[256,256]{1,0:T(8,128)}, u32[]{:S(2)}) copy-start(f32[256,256]{1,0:T(8,128)} %get-tuple-element.97) | copy-start | bytes 786436
  1191.5 20.4 %copy-start.25 = (f32[256,256]{1,0:T(8,128)S(1)}, f32[256,256]{1,0:T(8,128)}, u32[]{:S(2)}) copy-start(f32[256,256]{1,0:T(8,128)} %get-tuple-element.98) | copy-start | bytes 786436
  1193.0 19.6 %copy-start.24 = (f32[256,256]{1,0:T(8,128)S(1)}, f32[256,256]{1,0:T(8,128)}, u32[]{:S(2)}) copy-start(f32[256,256]{1,0:T(8,128)} %get-tuple-element.99) | copy-start | bytes 786436
  1193.0 20.4 %copy-start.23 = (f32[256,256]{1,0:T(8,128)S(1)}, f32[256,256]{1,0:T(8,128)}, u32[]{:S(2)}) copy-start(f32[256,256]{1,0:T(8,128)} %get-tuple-element.100) | copy-start | bytes 786436
  1193.0 21.1 %copy-start.22 = (f32[256,256]{1,0:T(8,128)S(1)}, f32[256,256]{1,0:T(8,128)}, u32[]{:S(2)}) copy-start(f32[256,256]{1,0:T(8,128)} %get-tuple-element.101) | copy-start | bytes 786436
  1193.0 21.8 %copy-start.21 = (f32[256,256]{1,0:T(8,128)S(1)}, f32[256,256]{1,0:T(8,128)}, u32[]{:S(2)}) copy-start(f32[256,256]{1,0:T(8,128)} %get-tuple-element.102) | copy-start | bytes 786436
  1193.0 22.5 %copy-start.16 = (f32[512,256]{1,0:T(8,128)S(1)}, f32[512,256]{1,0:T(8,128)}, u32[]{:S(2)}) copy-start(f32[512,256]{1,0:T(8,128)} %get-tuple-element.109) | copy-start | bytes 1572868
  1193.0 22.5 %copy-start.17 = (f32[512,256]{1,0:T(8,128)S(1)}, f32[512,256]{1,0:T(8,128)}, u32[]{:S(2)}) copy-start(f32[512,256]{1,0:T(8,128)} %get-tuple-element.103) | copy-start | bytes 1572868
  1198.6 18.0 %copy-start.15 = (f32[512,256]{1,0:T(8,128)S(1)}, f32[512,256]{1,0:T(8,128)}, u32[]{:S(2)}) copy-start(f32[512,256]{1,0:T(8,128)} %get-tuple-element.110) | copy-start | bytes 1572868
  1201.1 16.4 %copy-start.14 = (f32[512,256]{1,0:T(8,128)S(1)}, f32[512,256]{1,0:T(8,128)}, u32[]{:S(2)}) copy-start(f32[512,256]{1,0:T(8,128)} %get-tuple-element.111) | copy-start | bytes 1572868
  1218.3 113.7 %copy-start.44 = (f32[8288]{0:T(1024)S(1)}, f32[8288]{0:T(1024)}, u32[]{:S(2)}) copy-start(f32[8288]{0:T(1024)} %param.21) | copy-start | bytes 99460
  1218.3 113.7 %copy-start.47 = (f32[8288]{0:T(1024)S(1)}, f32[8288]{0:T(1024)}, u32[]{:S(2)}) copy-start(f32[8288]{0:T(1024)} %param.26) | copy-start | bytes 99460
  1218.3 113.7 %copy-start.48 = (f32[8288]{0:T(1024)S(1)}, f32[8288]{0:T(1024)}, u32[]{:S(2)}) copy-start(f32[8288]{0:T(1024)} %param.27) | copy-start | bytes 99460
  1218.3 114.3 %copy-start.13 = (f32[32768]{0:T(1024)S(1)}, f32[32768]{0:T(1024)}, u32[]{:S(2)}) copy-start(f32[32768]{0:T(1024)} %param.20) | copy-start | bytes 393220
  1218.3 114.3 %copy-start.45 = (f32[32768]{0:T(1024)S(1)}, f32[32768]{0:T(1024)}, u32[]{:S(2)}) copy-start(f32[32768]{0:T(1024)} %param.24) | copy-start | bytes 393220
  1218.3 114.3 %copy-start.46 = (f32[32768]{0:T(1024)S(1)}, f32[32768]{0:T(1024)}, u32[]{:S(2)}) copy-start(f32[32768]{0:T(1024)} %param.25) | copy-start | bytes 393220
  1218.3 115.1 %copy-start.12 = (f32[53248]{0:T(1024)S(1)}, f32[53248]{0:T(1024)}, u32[]{:S(2)}) copy-start(f32[53248]{0:T(1024)} %param.19) | copy-start | bytes 638980
  1218.3 115.1 %copy-start.42 = (f32[53248]{0:T(1024)S(1)}, f32[53248]{0:T(1024)}, u32[]{:S(2)}) copy-start(f32[53248]{0:T(1024)} %param.22) | copy-start | bytes 638980
  1218.3 115.1 %copy-start.43 = (f32[53248]{0:T(1024)S(1)}, f32[53248]{0:T(1024)}, u32[]{:S(2)}) copy-start(f32[53248]{0:T(1024)} %param.23) | copy-start | bytes 638980

commit v3 on v2

--- a/solution.py
+++ b/solution.py
@@ -19,6 +19,8 @@
 NVEC = 1036
 HALF = 128
 VB = 8
+UNROLL = 4
+UNROLL_BACK = 4
 
 BF = jnp.bfloat16
 F32 = jnp.float32
@@ -139,47 +141,66 @@
     return jnp.concatenate(outs, 1)
 
 
-def time_attend(c, v, group, count, q_s, k_s, v_s, o_s, p_s, l_s):
-    at = pl.ds(v, group, stride=VB)
-    q2 = split2(q_s[c, at, :])
-    k2 = split2(k_s[c, at, :])
-    w2 = split2(v_s[c, at, :])
+def time_parts(units, group, ref):
+    return [split2(ref[c, pl.ds(v, group, stride=VB), :]) for c, v in units]
+
+
+def spread2(x2):
     zero = jnp.zeros((), BF)
-    k_hi, k_lo = spread_heads(k2[0], zero), spread_heads(k2[1], zero)
-    w_hi, w_lo = spread_heads(w2[0], zero), spread_heads(w2[1], zero)
-    s = dots(jnp.concatenate(q2, 1), jnp.concatenate([k_hi, k_hi], 1), 1, 1) + dots(q2[0], k_lo, 1, 1)
-    p = jnp.exp(group_max(s, group, count))
-    p2 = split2(p)
-    both = dots(rows2(p2), jnp.concatenate([w_hi, ones_heads(group, count)], 1), 1, 0)
-    both = both[:group] + both[group:]
-    total = both[:, HALF:]
-    o_s[c, at, :] = (both[:, :HALF] + dots(p2[0], w_lo, 1, 0)) / total
-    if p_s is not None:
-        p_s[c, v] = p
-        l_s[c, v] = total
-
-
-def time_attend_back(c, v, group, count, q_s, k_s, v_s, o_s, p_s, l_s, do_s):
-    at = pl.ds(v, group, stride=VB)
-    q2 = split2(q_s[c, at, :])
-    k2 = split2(k_s[c, at, :])
-    w2 = split2(v_s[c, at, :])
-    zero = jnp.zeros((), BF)
-    k_hi, k_lo = spread_heads(k2[0], zero), spread_heads(k2[1], zero)
-    w_hi, w_lo = spread_heads(w2[0], zero), spread_heads(w2[1], zero)
-    d = do_s[c, at, :] / l_s[c, v]
-    d2 = split2(d)
-    e2 = split2(d * o_s[c, at, :])
-    p = p_s[c, v]
-    x2 = (jnp.concatenate([d2[0], e2[0]], 1), jnp.concatenate([d2[1], e2[1]], 1))
-    both = dots(rows2(x2), jnp.concatenate([w_hi, -ones_heads(group, count)], 1), 1, 1)
-    dp = both[:group] + both[group:] + dots(d2[0], w_lo, 1, 1)
-    p2 = split2(p)
-    s2 = split2(p * dp)
-    both = dots(rows2(s2), k_hi, 1, 0)
-    q_s[c, at, :] = both[:group] + both[group:] + dots(s2[0], k_lo, 1, 0)
-    k_s[c, at, :] = gather_heads(tn3(s2, q2), group)
-    v_s[c, at, :] = gather_heads(tn3(p2, d2), group)
+    return spread_heads(x2[0], zero), spread_heads(x2[1], zero)
+
+
+def time_attend(units, group, count, q_s, k_s, v_s, o_s, p_s, l_s):
+    q = time_parts(units, group, q_s)
+    k = [spread2(x2) for x2 in time_parts(units, group, k_s)]
+    scores = [
+        dots(jnp.concatenate(q2, 1), jnp.concatenate([k2[0], k2[0]], 1), 1, 1) + dots(q2[0], k2[1], 1, 1)
+        for q2, k2 in zip(q, k)
+    ]
+    probs = [jnp.exp(group_max(s, group, count)) for s in scores]
+    probs2 = [split2(p) for p in probs]
+    w = [spread2(x2) for x2 in time_parts(units, group, v_s)]
+    ones = ones_heads(group, count)
+    both = [dots(rows2(p2), jnp.concatenate([w2[0], ones], 1), 1, 0) for p2, w2 in zip(probs2, w)]
+    both = [b[:group] + b[group:] for b in both]
+    mixed = [(b[:, :HALF] + dots(p2[0], w2[1], 1, 0)) / b[:, HALF:] for b, p2, w2 in zip(both, probs2, w)]
+    for (c, v), o, p, b in zip(units, mixed, probs, both):
+        o_s[c, pl.ds(v, group, stride=VB), :] = o
+        if p_s is not None:
+            p_s[c, v] = p
+            l_s[c, v] = b[:, HALF:]
+
+
+def time_attend_back(units, group, count, q_s, k_s, v_s, o_s, p_s, l_s, do_s):
+    d = [do_s[c, pl.ds(v, group, stride=VB), :] / l_s[c, v] for c, v in units]
+    e2 = [split2(x * o_s[c, pl.ds(v, group, stride=VB), :]) for x, (c, v) in zip(d, units)]
+    d2 = [split2(x) for x in d]
+    w = [spread2(x2) for x2 in time_parts(units, group, v_s)]
+    ones = -ones_heads(group, count)
+    both = [
+        dots(
+            jnp.concatenate([jnp.concatenate([a[0], b[0]], 1), jnp.concatenate([a[1], b[1]], 1)], 0),
+            jnp.concatenate([w2[0], ones], 1),
+            1,
+            1,
+        )
+        for a, b, w2 in zip(d2, e2, w)
+    ]
+    dp = [b[:group] + b[group:] + dots(a[0], w2[1], 1, 1) for b, a, w2 in zip(both, d2, w)]
+    probs = [p_s[c, v] for c, v in units]
+    s2 = [split2(p * x) for p, x in zip(probs, dp)]
+    p2 = [split2(p) for p in probs]
+    k = [spread2(x2) for x2 in time_parts(units, group, k_s)]
+    both = [dots(rows2(a), k2[0], 1, 0) for a, k2 in zip(s2, k)]
+    dq = [b[:group] + b[group:] + dots(a[0], k2[1], 1, 0) for b, a, k2 in zip(both, s2, k)]
+    q = time_parts(units, group, q_s)
+    dk = [gather_heads(tn3(a, q2), group) for a, q2 in zip(s2, q)]
+    dv = [gather_heads(tn3(a, x), group) for a, x in zip(p2, d2)]
+    for (c, v), x, y, z in zip(units, dq, dk, dv):
+        at = pl.ds(v, group, stride=VB)
+        q_s[c, at, :] = x
+        k_s[c, at, :] = y
+        v_s[c, at, :] = z
 
 
 def store_halves(ref, x):
@@ -206,12 +227,12 @@
     for ref in (q_s, k_s, v_s):
         zero_tail(ref, rows)
 
-    def one(v, carry):
-        for c in range(2):
-            time_attend(c, v, group, count, q_s, k_s, v_s, o_s, p_s, l_s)
+    def some(i, carry):
+        units = [(c, i * UNROLL + k) for k in range(UNROLL) for c in range(2)]
+        time_attend(units, group, count, q_s, k_s, v_s, o_s, p_s, l_s)
         return carry
 
-    lax.fori_loop(0, VB, one, 0)
+    lax.fori_loop(0, VB // UNROLL, some, 0)
     mixed = load_halves(o_s, rows)
     h, unit1, inv1 = norm_fwd(x + mmw(split2(mixed), w["o"]) + vec[2:3], vec[3:4], vec[4:5])
     bias_up = jnp.concatenate([vec[5:6], vec[6:7]], 1)
@@ -335,12 +356,12 @@
     store_halves(do_s, mmwt(dz12, w["o"]))
     zero_tail(do_s, rows)
 
-    def one(v, carry):
-        for c in range(2):
-            time_attend_back(c, v, group, count, q_s, k_s, v_s, o_s, p_s, l_s, do_s)
+    def some(i, carry):
+        units = [(c, i * UNROLL_BACK + k) for k in range(UNROLL_BACK) for c in range(2)]
+        time_attend_back(units, group, count, q_s, k_s, v_s, o_s, p_s, l_s, do_s)
         return carry
 
-    lax.fori_loop(0, VB, one, 0)
+    lax.fori_loop(0, VB // UNROLL_BACK, some, 0)
     dq = load_halves(q_s, rows) * SCALE
     g["rows"][0] += colsum(dq)
     dq2 = split2(dq)
@@ -451,42 +472,36 @@
 RECV_W = ("so", "rk", "rv", "rq", "ro", "up", "down")
 
 
-def recv_forward(send, o_rows, w, vec, q_s, mix_s, p_s, kb_s, vb_s):
+def recv_forward(send, o_rows, w, vec):
     sb = send.shape[0] // SB_ROWS
     send2 = split2(send)
     o2 = split2(o_rows)
     buf = mmw(o2, w["so"]) + vec[12:13]
     buf2 = split2(buf)
-    kb_s[...] = mmw(buf2, w["rk"])
-    vb_s[...] = mmw(buf2, w["rv"]) + vec[14:15]
-    q_s[...] = (mmw(send2, w["rq"]) + vec[13:14]) * SCALE
-
-    def one(s, carry):
-        at = pl.ds(pl.multiple_of(s * SB_ROWS, SB_ROWS), SB_ROWS)
-        ar = pl.ds(pl.multiple_of(s * RPAD, RPAD), RPAD)
-        k2 = split2(spread_rows(kb_s[ar, :]))
-        v2 = split2(spread_rows(vb_s[ar, :]))
-        sc = jnp.where(valid_lane(SB_ROWS), nt3(split2(q_s[at, :]), k2), negative)
-        p = jnp.exp(sc - router_reduce(sc, jnp.maximum))
-        p = p / router_reduce(p, jnp.add)
-        p_s[at, :] = p
-        mix_s[at, :] = nn3(split2(p), v2)
-        return carry
-
-    lax.fori_loop(0, sb, one, 0)
-    mixed = mix_s[...]
+    kb = mmw(buf2, w["rk"])
+    vb = mmw(buf2, w["rv"]) + vec[14:15]
+    q = (mmw(send2, w["rq"]) + vec[13:14]) * SCALE
+
+    segs = range(sb)
+    k = [split2(spread_rows(kb[s * RPAD : (s + 1) * RPAD])) for s in segs]
+    v = [split2(spread_rows(vb[s * RPAD : (s + 1) * RPAD])) for s in segs]
+    ok = valid_lane(SB_ROWS)
+    scores = [jnp.where(ok, nt3(split2(q[s * SB_ROWS : (s + 1) * SB_ROWS]), k[s]), negative) for s in segs]
+    probs = [jnp.exp(sc - router_reduce(sc, jnp.maximum)) for sc in scores]
+    probs = [p / router_reduce(p, jnp.add) for p in probs]
+    mixed = jnp.concatenate([nn3(split2(p), v2) for p, v2 in zip(probs, v)], 0)
     g, unit3, inv3 = norm_fwd(send + mmw(split2(mixed), w["ro"]) + vec[15:16], vec[16:17], vec[17:18])
     u = mmw(split2(g), w["up"]) + jnp.concatenate([vec[18:19], vec[19:20]], 1)
     cdf = gelu_cdf(u)
     y, unit4, inv4 = norm_fwd(g + mmw(split2(u * cdf), w["down"]) + vec[20:21], vec[21:22], vec[22:23])
-    return y, (send2, o2, buf2, mixed, g, unit3, inv3, u, cdf, unit4, inv4)
+    return y, (send2, o2, buf2, mixed, g, unit3, inv3, u, cdf, unit4, inv4, q, k, v, probs)
 
 
 RECV_G = RECV_W + ("rows",)
 
 
-def recv_backward(dy, kept, w, vec, g, q_s, do_s, p_s, kb_s, vb_s):
-    send2, o2, buf2, mixed, gg, unit3, inv3, u, cdf, unit4, inv4 = kept
+def recv_backward(dy, kept, w, vec, g):
+    send2, o2, buf2, mixed, gg, unit3, inv3, u, cdf, unit4, inv4, q, k, v, probs = kept
     sb = dy.shape[0] // SB_ROWS
     rows = g["rows"]
     rows[9] += colsum(dy * unit4)
@@ -507,32 +522,20 @@
     rows[3] += colsum(dz3)
     dz32 = split2(dz3)
     g["ro"][...] += tn3(split2(mixed), dz32)
-    do_s[...] = mmwt(dz32, w["ro"])
-
-    def one(s, carry):
-        at = pl.ds(pl.multiple_of(s * SB_ROWS, SB_ROWS), SB_ROWS)
-        ar = pl.ds(pl.multiple_of(s * RPAD, RPAD), RPAD)
-        k2 = split2(spread_rows(kb_s[ar, :]))
-        v2 = split2(spread_rows(vb_s[ar, :]))
-        q2 = split2(q_s[at, :])
-        d2 = split2(do_s[at, :])
-        p = p_s[at, :]
-        dp = nt3(d2, v2)
-        ds = p * (dp - router_reduce(p * dp, jnp.add))
-        s2 = split2(ds)
-        kb_s[ar, :] = gather_rows(tn3(s2, q2))
-        vb_s[ar, :] = gather_rows(tn3(split2(p), d2))
-        q_s[at, :] = nn3(s2, k2)
-        return carry
-
-    lax.fori_loop(0, sb, one, 0)
-    dq = q_s[...] * SCALE
+    do = mmwt(dz32, w["ro"])
+    segs = range(sb)
+    d = [split2(do[s * SB_ROWS : (s + 1) * SB_ROWS]) for s in segs]
+    dp = [nt3(d2, v2) for d2, v2 in zip(d, v)]
+    ds = [split2(p * (x - router_reduce(p * x, jnp.add))) for p, x in zip(probs, dp)]
+    dq = jnp.concatenate([nn3(s2, k2) for s2, k2 in zip(ds, k)], 0) * SCALE
+    q = [split2(q[s * SB_ROWS : (s + 1) * SB_ROWS]) for s in segs]
+    dk = jnp.concatenate([gather_rows(tn3(s2, q2)) for s2, q2 in zip(ds, q)], 0)
+    dv = jnp.concatenate([gather_rows(tn3(split2(p), d2)) for p, d2 in zip(probs, d)], 0)
     rows[1] += colsum(dq)
     dq2 = split2(dq)
     g["rq"][...] += tn3(send2, dq2)
     dsend = dz3 + mmwt(dq2, w["rq"])
-    dk2 = split2(kb_s[...])
-    dv = vb_s[...]
+    dk2 = split2(dk)
     dv2 = split2(dv)
     rows[2] += colsum(dv)
     g["rk"][...] += tn3(buf2, dk2)
@@ -544,16 +547,6 @@
     return dsend, mmwt(dbuf2, w["so"])
 
 
-def recv_scratch(sb):
-    return [
-        pltpu.VMEM((sb * SB_ROWS, D), F32),
-        pltpu.VMEM((sb * SB_ROWS, D), F32),
-        pltpu.VMEM((sb * SB_ROWS, HALF), F32),
-        pltpu.VMEM((sb * RPAD, D), F32),
-        pltpu.VMEM((sb * RPAD, D), F32),
-    ]
-
-
 def recv_weight_specs():
     return [whole((D, D))] * 5 + [whole((D, FF)), whole((FF, D)), whole((24, D))]
 
@@ -569,9 +562,8 @@
 def recv_fwd_kernel(sb, send_ref, o_ref, *refs):
     w = {n: refs[i][...] for i, n in enumerate(RECV_W)}
     vec_ref, mvec_ref, mw_ref, out_ref = refs[7:11]
-    q_s, mix_s, p_s, kb_s, vb_s = refs[11:]
     y, _ = recv_forward(
-        send_ref[...].reshape(sb * SB_ROWS, D), unpack_block(o_ref, sb), w, vec_ref[...], q_s, mix_s, p_s, kb_s, vb_s
+        send_ref[...].reshape(sb * SB_ROWS, D), unpack_block(o_ref, sb), w, vec_ref[...]
     )
     mvec = mvec_ref[...]
     wide, _, _, _ = merge_rows(y, sb // 2, mvec)
@@ -586,7 +578,6 @@
         in_specs=[seg_block(sb), pack_spec(sb)] + recv_weight_specs() + [whole((8, D)), whole((2 * D, D))],
         out_specs=seg_block(sb // 2),
         out_shape=jax.ShapeDtypeStruct((n // 2, SB_ROWS, D), F32),
-        scratch_shapes=recv_scratch(sb),
         compiler_params=params_spec(),
         name="recv_fwd",
     )(send, o, *weights, mvec, mw)
@@ -597,7 +588,6 @@
     vec_ref, mvec_ref, mw_ref, dsend_ref, do_ref = refs[7:12]
     g = dict(zip(RECV_G, refs[12:20]))
     dmw_ref, dmv_ref = refs[20:22]
-    q_s, mix_s, p_s, kb_s, vb_s = refs[22:]
 
     @pl.when(pl.program_id(0) == 0)
     def _():
@@ -606,7 +596,7 @@
 
     vec = vec_ref[...]
     y, kept = recv_forward(
-        send_ref[...].reshape(sb * SB_ROWS, D), unpack_block(o_ref, sb), w, vec, q_s, mix_s, p_s, kb_s, vb_s
+        send_ref[...].reshape(sb * SB_ROWS, D), unpack_block(o_ref, sb), w, vec
     )
     pairs = sb // 2
     wide, unit, inv, gain = merge_rows(y, pairs, mvec_ref[...])
@@ -625,7 +615,7 @@
     left = dwide[:, :D].reshape(pairs, 1, SB_ROWS, D)
     right = dwide[:, D:].reshape(pairs, 1, SB_ROWS, D)
     dy = jnp.concatenate([left, right], 1).reshape(sb * SB_ROWS, D)
-    dsend, do = recv_backward(dy, kept, w, vec, g, q_s, mix_s, p_s, kb_s, vb_s)
+    dsend, do = recv_backward(dy, kept, w, vec, g)
     dsend_ref[...] = dsend.reshape(sb, SB_ROWS, D)
     pack_block(do_ref, do, sb)
 
@@ -645,7 +635,6 @@
         out_specs=[seg_block(sb), pack_spec(sb)] + [whole(s) for s in shapes],
         out_shape=[jax.ShapeDtypeStruct((n, SB_ROWS, D), F32), jax.ShapeDtypeStruct(o.shape, F32)]
         + [jax.ShapeDtypeStruct(s, F32) for s in shapes],
-        scratch_shapes=recv_scratch(sb),
         compiler_params=params_spec(),
         name="recv_bwd",
     )(send, o, dx, *weights, mvec, mw)
@@ -656,7 +645,6 @@
     vec_ref, head_ref, dsend_ref, do_ref = refs[7:11]
     g = dict(zip(RECV_G, refs[11:19]))
     dhead_ref = refs[19]
-    q_s, mix_s, p_s, kb_s, vb_s = refs[20:]
 
     @pl.when(pl.program_id(0) == 0)
     def _():
@@ -666,7 +654,7 @@
     vec = vec_ref[...]
     rows = sb * SB_ROWS
     y, kept = recv_forward(
-        send_ref[...].reshape(rows, D), unpack_block(o_ref, sb), w, vec, q_s, mix_s, p_s, kb_s, vb_s
+        send_ref[...].reshape(rows, D), unpack_block(o_ref, sb), w, vec
     )
     head = head_ref[...]
     y2 = split2(y)
@@ -677,7 +665,7 @@
     dpred2 = split2(dpred)
     dhead_ref[...] += tn3(dpred2, y2)
     dy = mmw(dpred2, head)
-    dsend, do = recv_backward(dy, kept, w, vec, g, q_s, mix_s, p_s, kb_s, vb_s)
+    dsend, do = recv_backward(dy, kept, w, vec, g)
     dsend_ref[...] = dsend.reshape(sb, SB_ROWS, D)
     pack_block(do_ref, do, sb)
 
@@ -695,7 +683,6 @@
         out_specs=[seg_block(sb), pack_spec(sb)] + [whole(s) for s in shapes],
         out_shape=[jax.ShapeDtypeStruct((n, SB_ROWS, D), F32), jax.ShapeDtypeStruct(o.shape, F32)]
         + [jax.ShapeDtypeStruct(s, F32) for s in shapes],
-        scratch_shapes=recv_scratch(sb),
         compiler_params=params_spec(),
         name="tail",
     )(send, o, tgt, kept, scale, mean, *weights, head)
@@ -704,47 +691,37 @@
 SEND_W = ("sq", "sk", "sv")
 
 
-def send_project(dim2, r_rows, w, vec, k_s, v_s, q_s):
-    k_s[...] = mmw(dim2, w["sk"])
-    v_s[...] = mmw(dim2, w["sv"]) + vec[11:12]
+def send_project(dim2, r_rows, w, vec):
     r2 = split2(r_rows)
-    q_s[...] = (mmw(r2, w["sq"]) + vec[10:11]) * SCALE
-    return r2
+    sb = r_rows.shape[0] // RPAD
+    k = mmw(dim2, w["sk"])
+    v = mmw(dim2, w["sv"]) + vec[11:12]
+    q = (mmw(r2, w["sq"]) + vec[10:11]) * SCALE
+    k = [split2(k[s * SB_ROWS : (s + 1) * SB_ROWS]) for s in range(sb)]
+    v = [split2(v[s * SB_ROWS : (s + 1) * SB_ROWS]) for s in range(sb)]
+    q = [split2(spread_rows(q[s * RPAD : (s + 1) * RPAD])) for s in range(sb)]
+    return r2, k, v, q
 
 
 def send_fwd_kernel(sb, dim_ref, r_ref, here_ref, *refs):
     w = {n: refs[i][...] for i, n in enumerate(SEND_W)}
-    vec_ref, o_ref, k_s, v_s, q_s = refs[3:]
+    vec_ref, o_ref = refs[3:]
     dim2 = split2(dim_ref[...].reshape(sb * SB_ROWS, D))
-    send_project(dim2, r_ref[...].reshape(sb * RPAD, D), w, vec_ref[...], k_s, v_s, q_s)
+    _, k, v, q = send_project(dim2, r_ref[...].reshape(sb * RPAD, D), w, vec_ref[...])
     here = here_ref[...] > 0.5
-
-    def one(s, carry):
-        at = pl.ds(pl.multiple_of(s * SB_ROWS, SB_ROWS), SB_ROWS)
-        ar = pl.ds(pl.multiple_of(s * RPAD, RPAD), RPAD)
-        q2 = split2(spread_rows(q_s[ar, :]))
-        sc = jnp.where(here, nt3(split2(k_s[at, :]), q2), negative)
-        top = jnp.max(sc, 0, keepdims=True)
-        p = jnp.where(here, jnp.exp(sc - top), 0.0)
-        total = jnp.sum(p, 0, keepdims=True)
-        safe = jnp.where(total > 0.0, total, 1.0)
-        lse = jnp.where(total > 0.0, top + jnp.log(safe), negative)
-        o_ref[s] = pack_rows(gather_rows(tn3(split2(p / safe), split2(v_s[at, :]))), lse)
-        return carry
-
-    lax.fori_loop(0, sb, one, 0)
+    scores = [jnp.where(here, nt3(k2, q2), negative) for k2, q2 in zip(k, q)]
+    tops = [jnp.max(sc, 0, keepdims=True) for sc in scores]
+    probs = [jnp.where(here, jnp.exp(sc - top), 0.0) for sc, top in zip(scores, tops)]
+    totals = [jnp.sum(p, 0, keepdims=True) for p in probs]
+    safe = [jnp.where(t > 0.0, t, 1.0) for t in totals]
+    mixed = [gather_rows(tn3(split2(p / t), v2)) for p, t, v2 in zip(probs, safe, v)]
+    for s in range(sb):
+        lse = jnp.where(totals[s] > 0.0, tops[s] + jnp.log(safe[s]), negative)
+        o_ref[s] = pack_rows(mixed[s], lse)
 
 
 def send_weight_specs():
     return [whole((D, D))] * 3 + [whole((24, D))]
-
-
-def send_scratch(sb):
-    return [
-        pltpu.VMEM((sb * SB_ROWS, D), F32),
-        pltpu.VMEM((sb * SB_ROWS, D), F32),
-        pltpu.VMEM((sb * RPAD, D), F32),
-    ]
 
 
 def send_fwd(dim, routers, here, weights, sb, npad):
@@ -755,7 +732,6 @@
         in_specs=[seg_block(sb), seg_block(sb, RPAD), whole((SB_ROWS, HALF))] + send_weight_specs(),
         out_specs=pack_spec(sb),
         out_shape=jax.ShapeDtypeStruct((npad, PACK, HALF), F32),
-        scratch_shapes=send_scratch(sb),
         compiler_params=params_spec(),
         name="send_fwd",
     )(dim, routers, here, *weights)
@@ -765,7 +741,6 @@
     w = {n: refs[i][...] for i, n in enumerate(SEND_W)}
     vec_ref, ddim_ref, dr_ref = refs[3:6]
     dsq_ref, dsk_ref, dsv_ref, rows = refs[6:10]
-    k_s, v_s, q_s = refs[10:]
 
     @pl.when(pl.program_id(0) == 0)
     def _():
@@ -773,38 +748,31 @@
             ref[...] = jnp.zeros(ref.shape, F32)
 
     dim2 = split2(dim_ref[...].reshape(sb * SB_ROWS, D))
-    r2 = send_project(dim2, r_ref[...].reshape(sb * RPAD, D), w, vec_ref[...], k_s, v_s, q_s)
+    r2, k, v, q = send_project(dim2, r_ref[...].reshape(sb * RPAD, D), w, vec_ref[...])
     here = (here_ref[...] > 0.5) & valid_lane(SB_ROWS)
-
-    def one(s, carry):
-        at = pl.ds(pl.multiple_of(s * SB_ROWS, SB_ROWS), SB_ROWS)
-        ar = pl.ds(pl.multiple_of(s * RPAD, RPAD), RPAD)
-        q2 = split2(spread_rows(q_s[ar, :]))
-        k2 = split2(k_s[at, :])
-        p = jnp.where(here, jnp.exp(nt3(k2, q2) - o_ref[s][2 * ROUT : 2 * ROUT + 1]), 0.0)
-        dwide = spread_rows(unpack_rows(do_ref[s]))
-        d2 = split2(dwide)
-        owide = jnp.broadcast_to(unpack_rows(o_ref[s])[:, None, :], (RPAD, HEADS, D)).reshape(RPAD * HEADS, D)
-        e2 = split2(dwide * owide)
-        one_row = jnp.ones((8, D), BF)
-        mean = (dots(one_row, e2[0], 1, 1) + dots(one_row, e2[1], 1, 1))[0:1]
-        dp = nt3(split2(v_s[at, :]), d2)
-        s2 = split2(p * (dp - mean))
-        q_s[ar, :] = gather_rows(tn3(s2, k2))
-        k_s[at, :] = nn3(s2, q2)
-        v_s[at, :] = nn3(split2(p), d2)
-        return carry
-
-    lax.fori_loop(0, sb, one, 0)
-    dk2 = split2(k_s[...])
-    dv = v_s[...]
+    segs = range(sb)
+    scores = [nt3(k2, q2) for k2, q2 in zip(k, q)]
+    probs = [jnp.where(here, jnp.exp(scores[s] - o_ref[s][2 * ROUT : 2 * ROUT + 1]), 0.0) for s in segs]
+    dwide = [spread_rows(unpack_rows(do_ref[s])) for s in segs]
+    owide = [
+        jnp.broadcast_to(unpack_rows(o_ref[s])[:, None, :], (RPAD, HEADS, D)).reshape(RPAD * HEADS, D) for s in segs
+    ]
+    e = [split2(a * b) for a, b in zip(dwide, owide)]
+    d = [split2(a) for a in dwide]
+    one_row = jnp.ones((8, D), BF)
+    means = [(dots(one_row, e2[0], 1, 1) + dots(one_row, e2[1], 1, 1))[0:1] for e2 in e]
+    dp = [nt3(v2, d2) for v2, d2 in zip(v, d)]
+    ds = [split2(p * (x - mean)) for p, x, mean in zip(probs, dp, means)]
+    dk = jnp.concatenate([nn3(s2, q2) for s2, q2 in zip(ds, q)], 0)
+    dv = jnp.concatenate([nn3(split2(p), d2) for p, d2 in zip(probs, d)], 0)
+    dq = jnp.concatenate([gather_rows(tn3(s2, k2)) for s2, k2 in zip(ds, k)], 0) * SCALE
+    dk2 = split2(dk)
     dv2 = split2(dv)
     rows[1] += colsum(dv)
     dsk_ref[...] += tn3(dim2, dk2)
     dsv_ref[...] += tn3(dim2, dv2)
     out = dpart_ref[...].reshape(sb * SB_ROWS, D) + mmwt(dk2, w["sk"]) + mmwt(dv2, w["sv"])
     ddim_ref[...] = out.reshape(sb, SB_ROWS, D)
-    dq = q_s[...] * SCALE
     rows[0] += colsum(dq)
     dq2 = split2(dq)
     dsq_ref[...] += tn3(r2, dq2)
@@ -822,7 +790,6 @@
         out_specs=[seg_block(sb), seg_block(sb, RPAD)] + [whole(s) for s in shapes],
         out_shape=[jax.ShapeDtypeStruct((n, SB_ROWS, D), F32), jax.ShapeDtypeStruct((n, RPAD, D), F32)]
         + [jax.ShapeDtypeStruct(s, F32) for s in shapes],
-        scratch_shapes=send_scratch(sb),
         compiler_params=params_spec(),
         name="send_bwd",
     )(dim, dpart, routers, o, do, here, *weights)

time: 1350 us -> 939 us (0.70)
  Pallas kernels: 1200 us -> 801 us
    pallas_call x2, Pallas kernels: 290 us -> 167 us  [time_bwd(): pl.pallas_call(functools.partial(time_bwd_kernel, first, count, group), g...]
    pallas_call x2, Pallas kernels: 134 us -> 65.9 us  [time_fwd(): pl.pallas_call(functools.partial(time_fwd_kernel, first, count, group), g...]
    pallas_call x1, Pallas kernels: 179 us -> 112 us  [recv_bwd(): pl.pallas_call(functools.partial(recv_bwd_kernel, sb), grid=(n // sb,), i...]
    pallas_call x1, Pallas kernels: 90.8 us -> 49.8 us  [recv_fwd(): pl.pallas_call(functools.partial(recv_fwd_kernel, sb), grid=(n // sb,), i...]
    pallas_call x1, Pallas kernels: 85.1 us -> 45.3 us  [tail(): pl.pallas_call(functools.partial(tail_kernel, sb), grid=(n // sb,), in_sp...]
    pallas_call x2, Pallas kernels: 57.5 us -> 25.5 us  [send_fwd(): pl.pallas_call(functools.partial(send_fwd_kernel, sb), grid=(n // sb,), i...]
    pallas_call x2, Pallas kernels: 80.6 us -> 48.6 us  [send_bwd(): pl.pallas_call(functools.partial(send_bwd_kernel, sb), grid=(n // sb,), i...]
where the time goes in v3:
time: 939 us; the launch traced here: 933 us
  Pallas kernels  801 us (85%)
  local copies, waits for them, and re-layouts  94.7 us (10%)
  other arithmetic  33.2 us (4%)
    pallas_call x2, Pallas kernels, time_bwd(): pl.pallas_call(functools.partial(time_bwd_kernel, first, count, group), g...  167 us
    pallas_call x4, Pallas kernels, group_combine(): pl.pallas_call(functools.partial(group_kernel, stats, per), in_specs=[INV...  122 us
    pallas_call x1, Pallas kernels, recv_bwd(): pl.pallas_call(functools.partial(recv_bwd_kernel, sb), grid=(n // sb,), i...  112 us
    pallas_call x1, Pallas kernels, scatter_sum(): pl.pallas_call(functools.partial(scatter_kernel, n), in_specs=[ANY] * n +...  108 us
    pallas_call x2, Pallas kernels, time_fwd(): pl.pallas_call(functools.partial(time_fwd_kernel, first, count, group), g...  65.9 us
    pallas_call x1, Pallas kernels, gather_all(): pl.pallas_call(functools.partial(gather_kernel, n), in_specs=[ANY] * n, o...  57.4 us
    pallas_call x1, Pallas kernels, recv_fwd(): pl.pallas_call(functools.partial(recv_fwd_kernel, sb), grid=(n // sb,), i...  49.8 us
    pallas_call x2, Pallas kernels, send_bwd(): pl.pallas_call(functools.partial(send_bwd_kernel, sb), grid=(n // sb,), i...  48.6 us

profile of v3, /device:TPU:0, one launch (start us, length us, event | category | flops | bytes accessed | tf_op | source)
XLA Modules:
  0.0 933.4 jit_solution(10906804105462580493)
XLA Ops:
  1.3 1.6 fusion.6
  2.9 1.0 convert_reduce_fusion
  3.9 1.2 fusion.1
  5.1 1.2 fusion.4
  6.4 1.3 pad.62.refs_3_
  14.1 1.0 copy.42
  16.3 1.1 copy.36
  17.8 1.0 pad.58.tgt_ref
  19.4 1.0 pad.59.kept_ref
  21.1 2.0 copy.40
  23.1 2.0 divide_bitcast_fusion
  25.2 1.5 pad.50.refs_0_
  27.5 57.4 %gather_all.1 = (bf16[2,2,4,2,208,256]{5,4,3,2,1,0:T(8,128)(2,1)S(1)}, bf16[2,2,4,2,128,256]{5,4,3,2,1,0:T(8,128)(2,1)S(1)}, bf16[2,2,4,2,33,256]{5,4,3,2,1,0:T(8,128)(2,1)S(1)}) custom-call(bf16[208,256]{1,0:T(8,128)(2,1)S(1)} %reshape.142.refs_0_, bf16[128,256]{1,0:T(8,128)(2,1)S(1)} %copy-done.10, bf16[33,256]{1,0:T(8,128)(2,1)S(1)} %reshape.144.refs_2_), custom_call_target="tpu_custom_call" | custom-call | tf_op jit(solution)/shard_map/gather_all/pallas_call | solution.py:923
  84.9 1.3 copy-done.4
  87.2 2.6 convert_element_type.76
  95.9 1.7 slice.243
  97.5 1.8 reshape.151
  99.3 1.9 pad.57.r_ref
  101.2 1.8 slice.223
  103.0 2.1 reshape.149
  105.1 2.4 pad.54.r_ref
  107.5 1.1 convert_element_type.77
  110.8 1.4 slice_bitcast_fusion.8
  114.8 39.9 %time_fwd.2.dim_ref.send_ref = f32[60,64,256]{2,1,0:T(8,128)} custom-call(f32[60,64,16]{2,1,0:T(8,128)} %pad.50.refs_0_, bf16[16,256]{1,0:T(8,128)(2,1)} %fusion.9.refs_1_, f32[60,1,256]{2,1,0:T(1,128)} %copy.47.refs_2_, bf16[256,256]{1,0:T(8,128)(2,1)} %get-tuple-element.162.refs_3_.refs_4_, bf16[256,256]{1,0:T(8,128)(2,1)} %get-tuple-element.161.refs_4_.refs_5_, ...), custom_call_target="tpu_custom_call" | custom-call | tf_op jit(solution)/shard_map/time_fwd/pallas_call | solution.py:292
  154.7 17.4 %send_fwd.2.in_ref = f32[64,24,128]{2,1,0:T(8,128)} custom-call(f32[60,64,256]{2,1,0:T(8,128)} %time_fwd.2.dim_ref.send_ref, f32[60,16,256]{2,1,0:T(8,128)} %pad.54.r_ref, f32[64,128]{1,0:T(8,128)} %broadcast_in_dim.11.here_ref, bf16[256,256]{1,0:T(8,128)(2,1)} %get-tuple-element.158.refs_0_, bf16[256,256]{1,0:T(8,128)(2,1)} %get-tuple-element.157.refs_1_, ...), custom_call_target="tpu_custom_call" | custom-call | tf_op jit(solution)/shard_map/send_fwd/pallas_call | solution.py:729
  172.1 1.1 copy-done.3
  173.2 35.5 %group_stats.2.o_ref = f32[64,24,128]{2,1,0:T(8,128)S(1)} custom-call(f32[64,24,128]{2,1,0:T(8,128)S(1)} %copy-done.3), custom_call_target="tpu_custom_call" | custom-call | tf_op jit(solution)/shard_map/group_stats/pallas_call | solution.py:1137
  209.6 49.8 %recv_fwd.1.refs_0_ = f32[30,64,256]{2,1,0:T(8,128)} custom-call(f32[60,64,256]{2,1,0:T(8,128)} %time_fwd.2.dim_ref.send_ref, f32[64,24,128]{2,1,0:T(8,128)} %copy-done, bf16[256,256]{1,0:T(8,128)(2,1)} %get-tuple-element.155.refs_0_, bf16[256,256]{1,0:T(8,128)(2,1)} %get-tuple-element.154.refs_1_, bf16[256,256]{1,0:T(8,128)(2,1)} %get-tuple-element.153.refs_2_, ...), custom_call_target="tpu_custom_call" | custom-call | tf_op jit(solution)/shard_map/recv_fwd/pallas_call | solution.py:575
  259.4 26.0 %time_fwd.3.dim_ref.send_ref = f32[30,64,256]{2,1,0:T(8,128)} custom-call(f32[30,64,256]{2,1,0:T(8,128)} %recv_fwd.1.refs_0_, bf16[256,256]{1,0:T(8,128)(2,1)} %get-tuple-element.150.refs_1_.refs_2_, bf16[256,256]{1,0:T(8,128)(2,1)} %get-tuple-element.149.refs_2_.refs_3_, bf16[256,256]{1,0:T(8,128)(2,1)} %get-tuple-element.148.refs_3_.refs_4_, ...), custom_call_target="tpu_custom_call" | custom-call | tf_op jit(solution)/shard_map/time_fwd/pallas_call | solution.py:292
  285.4 8.1 send_fwd.3.in_ref
  293.6 1.0 copy-done.6
  294.6 24.5 %group_stats.3.o_ref = f32[32,24,128]{2,1,0:T(8,128)S(1)} custom-call(f32[32,24,128]{2,1,0:T(8,128)S(1)} %copy-done.6), custom_call_target="tpu_custom_call" | custom-call | tf_op jit(solution)/shard_map/group_stats/pallas_call | solution.py:1137
  319.8 45.3 %tail.1 = (f32[30,64,256]{2,1,0:T(8,128)}, f32[32,24,128]{2,1,0:T(8,128)}, f32[256,256]{1,0:T(8,128)}, f32[256,256]{1,0:T(8,128)}, f32[256,256]{1,0:T(8,128)}, /...) custom-call(f32[30,64,256]{2,1,0:T(8,128)} %time_fwd.3.dim_ref.send_, ...), custom_call_target="tpu_custom_call" | custom-call | tf_op jit(solution)/shard_map/tail/pallas_call | solution.py:676
  366.1 1.0 copy-done.9
  367.1 24.8 %group_sum.2.do_ref = f32[32,24,128]{2,1,0:T(8,128)S(1)} custom-call(f32[32,24,128]{2,1,0:T(8,128)S(1)} %copy-done.9), custom_call_target="tpu_custom_call" | custom-call | tf_op jit(solution)/shard_map/group_sum/pallas_call | solution.py:1137
  392.6 16.2 %send_bwd.2 = (f32[30,64,256]{2,1,0:T(8,128)}, f32[30,16,256]{2,1,0:T(8,128)}, f32[256,256]{1,0:T(8,128)}, f32[256,256]{1,0:T(8,128)}, f32[256,256]{1,0:T(8,128)}, /*index=5*/f32[2,8,256]{2,1,0:T(8,128)}) custom-call(f32[30,64,256]{2,1,0:T(8,128)} %time_fwd.3.dim_ref.send_ref, f32[30,64,256]{2,1,0:T(8,128)} %get-tuple-element.72.dpart_ref, ...), custom_call_target="tpu_custom_call" | custom-call | tf_op jit(solution)/shard_map/send_bwd/pallas_call | solution.py:785
  408.8 63.4 %time_bwd.2 = (f32[256,256]{1,0:T(8,128)}, f32[256,256]{1,0:T(8,128)}, f32[256,256]{1,0:T(8,128)}, f32[256,256]{1,0:T(8,128)}, f32[256,512]{1,0:T(8,128)}, /*ind...) custom-call(f32[30,64,256]{2,1,0:T(8,128)} %recv_fwd.1.refs_0_, ...), custom_call_target="tpu_custom_call" | custom-call | tf_op jit(solution)/shard_map/time_bwd/pallas_call | solution.py:402
  472.2 1.3 reduce_sum.144
  473.5 1.5 reduce_sum.143
  475.0 1.1 reshape.157
  476.1 111.5 %recv_bwd.1 = (f32[60,64,256]{2,1,0:T(8,128)}, f32[64,24,128]{2,1,0:T(8,128)}, f32[256,256]{1,0:T(8,128)}, f32[256,256]{1,0:T(8,128)}, f32[256,256]{1,0:T(8,128)...) custom-call(f32[60,64,256]{2,1,0:T(8,128)} %time_fwd.2.dim_ref.send_, ...), custom_call_target="tpu_custom_call" | custom-call | tf_op jit(solution)/shard_map/recv_bwd/pallas_call | solution.py:629
  587.6 1.4 reduce_sum.146
  589.0 1.5 reduce_sum.142
  590.5 1.1 copy-done.8
  591.7 37.1 %group_sum.3.do_ref = f32[64,24,128]{2,1,0:T(8,128)S(1)} custom-call(f32[64,24,128]{2,1,0:T(8,128)S(1)} %copy-done.8), custom_call_target="tpu_custom_call" | custom-call | tf_op jit(solution)/shard_map/group_sum/pallas_call | solution.py:1137
  629.6 32.4 %send_bwd.3 = (f32[60,64,256]{2,1,0:T(8,128)}, f32[60,16,256]{2,1,0:T(8,128)}, f32[256,256]{1,0:T(8,128)}, f32[256,256]{1,0:T(8,128)}, f32[256,256]{1,0:T(8,128)}, /*index=5*/f32[2,8,256]{2,1,0:T(8,128)}) custom-call(f32[60,64,256]{2,1,0:T(8,128)} %time_fwd.2.dim_ref.send_ref, f32[60,64,256]{2,1,0:T(8,128)} %get-tuple-element.76.dpart_ref, ...), custom_call_target="tpu_custom_call" | custom-call | tf_op jit(solution)/shard_map/send_bwd/pallas_call | solution.py:785
  662.1 103.5 %time_bwd.3 = (f32[256,256]{1,0:T(8,128)}, f32[256,256]{1,0:T(8,128)}, f32[256,256]{1,0:T(8,128)}, f32[256,256]{1,0:T(8,128)}, f32[256,512]{1,0:T(8,128)}, /*ind...) custom-call(f32[60,64,16]{2,1,0:T(8,128)} %pad.50.refs_0_, ...), custom_call_target="tpu_custom_call" | custom-call | tf_op jit(solution)/shard_map/time_bwd/pallas_call | solution.py:402
  765.6 1.7 reduce_sum.138
  767.2 1.2 bitcast_reduce_fusion
  768.4 1.5 reduce_sum.140
  770.5 2.5 pad_maximum_fusion
  773.1 1.7 reshape.153
  775.8 9.1 concatenate.15
  784.9 1.7 reshape.158
  786.5 1.3 pad.61
  787.8 1.3 reshape.159.refs_2_
  789.2 1.5 constant_dynamic-update-slice_fusion.29
  790.8 2.3 constant_dynamic-update-slice_fusion.28
  793.0 1.7 constant_dynamic-update-slice_fusion.24
  794.7 1.7 constant_dynamic-update-slice_fusion.23
  796.4 1.7 constant_dynamic-update-slice_fusion.22
  813.3 1.1 constant_dynamic-update-slice_fusion
  816.1 108.0 %scatter_sum.1 = (f32[208,256]{1,0:T(8,128)}, f32[128,256]{1,0:T(8,128)}, f32[33,256]{1,0:T(8,128)}, f32[16,128]{1,0:T(8,128)}) custom-call(f32[2,2,4,2,208,256]{5,4,3,2,1,0:T(8,128)} %bitcast.43.refs_0_, f32[2,2,4,2,128,256]{5,4,3,2,1,0:T(8,128)} %bitcast.44.refs_1_, f32[2,2,4,2,33,256]{5,4,3,2,1,0:T(8,128)} %reshape.159.refs_2_, f32[8,128]{1,0:T(8,128)} %pad.62.refs_3_), custom_call_target="tpu_custom_call" | custom-call | tf_op jit(solution)/shard_map/scatter_sum/pallas_call | solution.py:1060
  924.1 1.3 slice_reduce_fusion
  (175 shorter events, 49.7 us)
Async XLA Ops:
  26.7 0.8 copy-start.10
  27.5 81.1 %copy-start.50 = (pred[16]{0:T(512)(128)(4,1)S(1)}, pred[16]{0:T(512)(128)(4,1)}, u32[]{:S(2)}) copy-start(pred[16]{0:T(512)(128)(4,1)} %constant.21.clone.1) | copy-start | bytes 52
  84.9 1.3 copy-start.4
  105.1 7.2 copy-start.5
  172.1 1.1 copy-start.3
  208.7 0.9 copy-start
  293.6 1.0 copy-start.6
  319.1 0.8 copy-start.1
  366.1 1.0 copy-start.9
  391.9 0.8 copy-start.7
  590.5 1.1 copy-start.8
  628.8 0.9 copy-start.2
  662.0 107.9 %copy-start.49 = (f32[2,8,256]{2,1,0:T(8,128)S(1)}, f32[2,8,256]{2,1,0:T(8,128)}, u32[]{:S(2)}) copy-start(f32[2,8,256]{2,1,0:T(8,128)} %get-tuple-element.115) | copy-start | bytes 49156
  662.1 108.5 %copy-start.18 = (f32[256,512]{1,0:T(8,128)S(1)}, f32[256,512]{1,0:T(8,128)}, u32[]{:S(2)}) copy-start(f32[256,512]{1,0:T(8,128)} %get-tuple-element.107) | copy-start | bytes 1572868
  662.1 108.5 %copy-start.19 = (f32[256,512]{1,0:T(8,128)S(1)}, f32[256,512]{1,0:T(8,128)}, u32[]{:S(2)}) copy-start(f32[256,512]{1,0:T(8,128)} %get-tuple-element.106) | copy-start | bytes 1572868
  662.1 108.5 %copy-start.20 = (f32[256,512]{1,0:T(8,128)S(1)}, f32[256,512]{1,0:T(8,128)}, u32[]{:S(2)}) copy-start(f32[256,512]{1,0:T(8,128)} %get-tuple-element.105) | copy-start | bytes 1572868
  662.1 112.7 %copy-start.11 = (f32[60,16,256]{2,1,0:T(8,128)S(1)}, f32[60,16,256]{2,1,0:T(8,128)}, u32[]{:S(2)}) copy-start(f32[60,16,256]{2,1,0:T(8,128)} %get-tuple-element.122) | copy-start | bytes 2949124
  787.8 17.5 %copy-start.31 = (f32[256,256]{1,0:T(8,128)S(1)}, f32[256,256]{1,0:T(8,128)}, u32[]{:S(2)}) copy-start(f32[256,256]{1,0:T(8,128)} %get-tuple-element.92) | copy-start | bytes 786436
  789.1 9.0 copy-start.41
  789.1 9.7 %copy-start.40 = (f32[256,256]{1,0:T(8,128)S(1)}, f32[256,256]{1,0:T(8,128)}, u32[]{:S(2)}) copy-start(f32[256,256]{1,0:T(8,128)} %get-tuple-element.83) | copy-start | bytes 786436
  789.1 10.4 %copy-start.39 = (f32[256,256]{1,0:T(8,128)S(1)}, f32[256,256]{1,0:T(8,128)}, u32[]{:S(2)}) copy-start(f32[256,256]{1,0:T(8,128)} %get-tuple-element.84) | copy-start | bytes 786436
  789.1 11.2 %copy-start.38 = (f32[256,256]{1,0:T(8,128)S(1)}, f32[256,256]{1,0:T(8,128)}, u32[]{:S(2)}) copy-start(f32[256,256]{1,0:T(8,128)} %get-tuple-element.85) | copy-start | bytes 786436
  789.1 11.9 %copy-start.37 = (f32[256,256]{1,0:T(8,128)S(1)}, f32[256,256]{1,0:T(8,128)}, u32[]{:S(2)}) copy-start(f32[256,256]{1,0:T(8,128)} %get-tuple-element.86) | copy-start | bytes 786436
  789.1 12.6 %copy-start.36 = (f32[256,256]{1,0:T(8,128)S(1)}, f32[256,256]{1,0:T(8,128)}, u32[]{:S(2)}) copy-start(f32[256,256]{1,0:T(8,128)} %get-tuple-element.87) | copy-start | bytes 786436
  789.1 13.3 %copy-start.35 = (f32[256,256]{1,0:T(8,128)S(1)}, f32[256,256]{1,0:T(8,128)}, u32[]{:S(2)}) copy-start(f32[256,256]{1,0:T(8,128)} %get-tuple-element.88) | copy-start | bytes 786436
  789.1 14.0 %copy-start.34 = (f32[256,256]{1,0:T(8,128)S(1)}, f32[256,256]{1,0:T(8,128)}, u32[]{:S(2)}) copy-start(f32[256,256]{1,0:T(8,128)} %get-tuple-element.89) | copy-start | bytes 786436
  789.1 14.7 %copy-start.33 = (f32[256,256]{1,0:T(8,128)S(1)}, f32[256,256]{1,0:T(8,128)}, u32[]{:S(2)}) copy-start(f32[256,256]{1,0:T(8,128)} %get-tuple-element.90) | copy-start | bytes 786436
  789.2 15.4 %copy-start.32 = (f32[256,256]{1,0:T(8,128)S(1)}, f32[256,256]{1,0:T(8,128)}, u32[]{:S(2)}) copy-start(f32[256,256]{1,0:T(8,128)} %get-tuple-element.91) | copy-start | bytes 786436
  789.2 16.9 %copy-start.30 = (f32[256,256]{1,0:T(8,128)S(1)}, f32[256,256]{1,0:T(8,128)}, u32[]{:S(2)}) copy-start(f32[256,256]{1,0:T(8,128)} %get-tuple-element.93) | copy-start | bytes 786436
  789.2 17.6 %copy-start.29 = (f32[256,256]{1,0:T(8,128)S(1)}, f32[256,256]{1,0:T(8,128)}, u32[]{:S(2)}) copy-start(f32[256,256]{1,0:T(8,128)} %get-tuple-element.94) | copy-start | bytes 786436
  789.2 18.3 %copy-start.28 = (f32[256,256]{1,0:T(8,128)S(1)}, f32[256,256]{1,0:T(8,128)}, u32[]{:S(2)}) copy-start(f32[256,256]{1,0:T(8,128)} %get-tuple-element.95) | copy-start | bytes 786436
  789.2 19.0 %copy-start.27 = (f32[256,256]{1,0:T(8,128)S(1)}, f32[256,256]{1,0:T(8,128)}, u32[]{:S(2)}) copy-start(f32[256,256]{1,0:T(8,128)} %get-tuple-element.96) | copy-start | bytes 786436
  789.2 19.7 %copy-start.26 = (f32[256,256]{1,0:T(8,128)S(1)}, f32[256,256]{1,0:T(8,128)}, u32[]{:S(2)}) copy-start(f32[256,256]{1,0:T(8,128)} %get-tuple-element.97) | copy-start | bytes 786436
  789.2 20.4 %copy-start.25 = (f32[256,256]{1,0:T(8,128)S(1)}, f32[256,256]{1,0:T(8,128)}, u32[]{:S(2)}) copy-start(f32[256,256]{1,0:T(8,128)} %get-tuple-element.98) | copy-start | bytes 786436
  790.7 19.6 %copy-start.24 = (f32[256,256]{1,0:T(8,128)S(1)}, f32[256,256]{1,0:T(8,128)}, u32[]{:S(2)}) copy-start(f32[256,256]{1,0:T(8,128)} %get-tuple-element.99) | copy-start | bytes 786436
  790.7 20.4 %copy-start.23 = (f32[256,256]{1,0:T(8,128)S(1)}, f32[256,256]{1,0:T(8,128)}, u32[]{:S(2)}) copy-start(f32[256,256]{1,0:T(8,128)} %get-tuple-element.100) | copy-start | bytes 786436
  790.7 21.1 %copy-start.22 = (f32[256,256]{1,0:T(8,128)S(1)}, f32[256,256]{1,0:T(8,128)}, u32[]{:S(2)}) copy-start(f32[256,256]{1,0:T(8,128)} %get-tuple-element.101) | copy-start | bytes 786436
  790.7 21.8 %copy-start.21 = (f32[256,256]{1,0:T(8,128)S(1)}, f32[256,256]{1,0:T(8,128)}, u32[]{:S(2)}) copy-start(f32[256,256]{1,0:T(8,128)} %get-tuple-element.102) | copy-start | bytes 786436
  790.7 22.5 %copy-start.16 = (f32[512,256]{1,0:T(8,128)S(1)}, f32[512,256]{1,0:T(8,128)}, u32[]{:S(2)}) copy-start(f32[512,256]{1,0:T(8,128)} %get-tuple-element.109) | copy-start | bytes 1572868
  790.8 22.5 %copy-start.17 = (f32[512,256]{1,0:T(8,128)S(1)}, f32[512,256]{1,0:T(8,128)}, u32[]{:S(2)}) copy-start(f32[512,256]{1,0:T(8,128)} %get-tuple-element.103) | copy-start | bytes 1572868
  796.4 18.0 %copy-start.15 = (f32[512,256]{1,0:T(8,128)S(1)}, f32[512,256]{1,0:T(8,128)}, u32[]{:S(2)}) copy-start(f32[512,256]{1,0:T(8,128)} %get-tuple-element.110) | copy-start | bytes 1572868
  798.8 16.4 %copy-start.14 = (f32[512,256]{1,0:T(8,128)S(1)}, f32[512,256]{1,0:T(8,128)}, u32[]{:S(2)}) copy-start(f32[512,256]{1,0:T(8,128)} %get-tuple-element.111) | copy-start | bytes 1572868
  816.0 113.6 %copy-start.44 = (f32[8288]{0:T(1024)S(1)}, f32[8288]{0:T(1024)}, u32[]{:S(2)}) copy-start(f32[8288]{0:T(1024)} %param.21) | copy-start | bytes 99460
  816.0 113.6 %copy-start.47 = (f32[8288]{0:T(1024)S(1)}, f32[8288]{0:T(1024)}, u32[]{:S(2)}) copy-start(f32[8288]{0:T(1024)} %param.26) | copy-start | bytes 99460
  816.0 113.6 %copy-start.48 = (f32[8288]{0:T(1024)S(1)}, f32[8288]{0:T(1024)}, u32[]{:S(2)}) copy-start(f32[8288]{0:T(1024)} %param.27) | copy-start | bytes 99460
  816.0 114.3 %copy-start.13 = (f32[32768]{0:T(1024)S(1)}, f32[32768]{0:T(1024)}, u32[]{:S(2)}) copy-start(f32[32768]{0:T(1024)} %param.20) | copy-start | bytes 393220
  816.0 114.3 %copy-start.45 = (f32[32768]{0:T(1024)S(1)}, f32[32768]{0:T(1024)}, u32[]{:S(2)}) copy-start(f32[32768]{0:T(1024)} %param.24) | copy-start | bytes 393220
  816.1 114.3 %copy-start.46 = (f32[32768]{0:T(1024)S(1)}, f32[32768]{0:T(1024)}, u32[]{:S(2)}) copy-start(f32[32768]{0:T(1024)} %param.25) | copy-start | bytes 393220
  816.1 115.1 %copy-start.12 = (f32[53248]{0:T(1024)S(1)}, f32[53248]{0:T(1024)}, u32[]{:S(2)}) copy-start(f32[53248]{0:T(1024)} %param.19) | copy-start | bytes 638980
  816.1 115.1 %copy-start.42 = (f32[53248]{0:T(1024)S(1)}, f32[53248]{0:T(1024)}, u32[]{:S(2)}) copy-start(f32[53248]{0:T(1024)} %param.22) | copy-start | bytes 638980
  816.1 115.1 %copy-start.43 = (f32[53248]{0:T(1024)S(1)}, f32[53248]{0:T(1024)}, u32[]{:S(2)}) copy-start(f32[53248]{0:T(1024)} %param.23) | copy-start | bytes 638980

commit v4 on v3

--- a/solution.py
+++ b/solution.py
@@ -19,8 +19,8 @@
 NVEC = 1036
 HALF = 128
 VB = 8
-UNROLL = 4
-UNROLL_BACK = 4
+UNROLL = 8
+UNROLL_BACK = 8
 
 BF = jnp.bfloat16
 F32 = jnp.float32
@@ -163,16 +163,16 @@
     ones = ones_heads(group, count)
     both = [dots(rows2(p2), jnp.concatenate([w2[0], ones], 1), 1, 0) for p2, w2 in zip(probs2, w)]
     both = [b[:group] + b[group:] for b in both]
-    mixed = [(b[:, :HALF] + dots(p2[0], w2[1], 1, 0)) / b[:, HALF:] for b, p2, w2 in zip(both, probs2, w)]
-    for (c, v), o, p, b in zip(units, mixed, probs, both):
+    inv = [1.0 / b[:, HALF:] for b in both]
+    mixed = [(b[:, :HALF] + dots(p2[0], w2[1], 1, 0)) * i for b, p2, w2, i in zip(both, probs2, w, inv)]
+    for (c, v), o, p, i in zip(units, mixed, probs, inv):
         o_s[c, pl.ds(v, group, stride=VB), :] = o
-        if p_s is not None:
-            p_s[c, v] = p
-            l_s[c, v] = b[:, HALF:]
-
-
-def time_attend_back(units, group, count, q_s, k_s, v_s, o_s, p_s, l_s, do_s):
-    d = [do_s[c, pl.ds(v, group, stride=VB), :] / l_s[c, v] for c, v in units]
+        p_s[c, v] = p
+        l_s[c, v] = i
+
+
+def time_attend_back(units, group, count, q_s, k_s, v_s, o_s, p_s, l_s, do_s, dq_s, dk_s, dv_s):
+    d = [do_s[c, pl.ds(v, group, stride=VB), :] * l_s[c, v] for c, v in units]
     e2 = [split2(x * o_s[c, pl.ds(v, group, stride=VB), :]) for x, (c, v) in zip(d, units)]
     d2 = [split2(x) for x in d]
     w = [spread2(x2) for x2 in time_parts(units, group, v_s)]
@@ -198,9 +198,9 @@
     dv = [gather_heads(tn3(a, x), group) for a, x in zip(p2, d2)]
     for (c, v), x, y, z in zip(units, dq, dk, dv):
         at = pl.ds(v, group, stride=VB)
-        q_s[c, at, :] = x
-        k_s[c, at, :] = y
-        v_s[c, at, :] = z
+        dq_s[c, at, :] = x
+        dk_s[c, at, :] = y
+        dv_s[c, at, :] = z
 
 
 def store_halves(ref, x):
@@ -218,7 +218,8 @@
     ref[:, rows:, :] = jnp.zeros((2, tail, HALF), F32)
 
 
-def time_forward(x, w, vec, count, group, q_s, k_s, v_s, o_s, p_s=None, l_s=None):
+def time_forward(x, w, vec, count, group, kept):
+    q_s, k_s, v_s, o_s, p_s, l_s, z1_s, u_s, z2_s = kept
     rows = count * VB
     x2 = split2(x)
     store_halves(q_s, (mmw(x2, w["q"]) + vec[0:1]) * SCALE)
@@ -233,14 +234,14 @@
         return carry
 
     lax.fori_loop(0, VB // UNROLL, some, 0)
-    mixed = load_halves(o_s, rows)
-    h, unit1, inv1 = norm_fwd(x + mmw(split2(mixed), w["o"]) + vec[2:3], vec[3:4], vec[4:5])
-    bias_up = jnp.concatenate([vec[5:6], vec[6:7]], 1)
-    u = mmw(split2(h), w["up"]) + bias_up
-    cdf = gelu_cdf(u)
-    z2 = h + mmw(split2(u * cdf), w["down"]) + vec[7:8]
-    y, unit2, inv2 = norm_fwd(z2, vec[8:9], vec[9:10])
-    return y, (x2, mixed, h, unit1, inv1, u, cdf, unit2, inv2)
+    z1 = x + mmw(split2(load_halves(o_s, rows)), w["o"]) + vec[2:3]
+    z1_s[...] = z1
+    h, _, _ = norm_fwd(z1, vec[3:4], vec[4:5])
+    u = mmw(split2(h), w["up"]) + jnp.concatenate([vec[5:6], vec[6:7]], 1)
+    u_s[...] = u
+    z2 = h + mmw(split2(u * gelu_cdf(u)), w["down"]) + vec[7:8]
+    z2_s[...] = z2
+    return norm_fwd(z2, vec[8:9], vec[9:10])[0]
 
 
 def embed_block(pieces, emb, place):
@@ -258,14 +259,14 @@
         x_ref = refs[0]
         refs = refs[1:]
     w = {name: refs[i][...] for i, name in enumerate(TIME_W)}
-    vec_ref, y_ref, q_s, k_s, v_s, o_s = refs[6:]
+    vec_ref, y_ref = refs[6:8]
     rows = count * VB
     if first:
         place = jnp.broadcast_to(place_ref[...], (count, VB, D)).reshape(rows, D)
         x = embed_block(x_ref[...].reshape(rows, 16), emb_ref[...], place)
     else:
         x = x_ref[...].reshape(rows, D)
-    y, _ = time_forward(x, w, vec_ref[...], count, group, q_s, k_s, v_s, o_s)
+    y = time_forward(x, w, vec_ref[...], count, group, refs[8:])
     y_ref[...] = y.reshape(count, VB, D)
 
 
@@ -279,6 +280,13 @@
 
 def time_weight_specs():
     return [whole((D, D))] * 4 + [whole((D, FF)), whole((FF, D)), whole((24, D))]
+
+
+def time_kept(count, group, nb):
+    pad, rows = group * VB, count * VB
+    shapes = [(2, pad, HALF)] * 4 + [(2, VB, group, 4 * group), (2, VB, group, HALF), (rows, D), (rows, FF), (rows, D)]
+    specs = [pl.BlockSpec((None,) + s, lambda i, n=len(s): (i,) + (0,) * n) for s in shapes]
+    return specs, [jax.ShapeDtypeStruct((nb,) + s, F32) for s in shapes]
 
 
 def time_fwd(first, x, extra, weights, count):
@@ -288,17 +296,17 @@
     specs = [pl.BlockSpec((count, VB, width), lambda i: (0, i, 0))]
     if first:
         specs += [whole((16, D)), whole((count, 1, D))]
-    pad = group * VB
-    return pl.pallas_call(
+    kept_specs, kept_shapes = time_kept(count, group, nv // VB)
+    out = pl.pallas_call(
         functools.partial(time_fwd_kernel, first, count, group),
         grid=(nv // VB,),
         in_specs=specs + time_weight_specs(),
-        out_specs=pl.BlockSpec((count, VB, D), lambda i: (0, i, 0)),
-        out_shape=jax.ShapeDtypeStruct((count, nv, D), F32),
-        scratch_shapes=[pltpu.VMEM((2, pad, HALF), F32)] * 4,
+        out_specs=[pl.BlockSpec((count, VB, D), lambda i: (0, i, 0))] + kept_specs,
+        out_shape=[jax.ShapeDtypeStruct((count, nv, D), F32)] + kept_shapes,
         compiler_params=params_spec(),
         name="time_fwd",
     )(x, *extra, *weights)
+    return out[0], out[1:]
 
 
 def time_bwd_kernel(first, count, group, *refs):
@@ -309,13 +317,14 @@
         x_ref = refs[0]
         refs = refs[1:]
     dy_ref = refs[0]
-    w = {name: refs[1 + i][...] for i, name in enumerate(TIME_W)}
-    vec_ref = refs[7]
-    outs = refs[8:]
+    q_s, k_s, v_s, o_s, p_s, l_s, z1_s, u_s, z2_s = refs[1:10]
+    w = {name: refs[10 + i][...] for i, name in enumerate(TIME_W)}
+    vec_ref = refs[16]
+    outs = refs[17:]
     n_out = 9 if first else 8
     g = dict(zip(TIME_W + ("rows",), outs[:7]))
     tail = outs[7:n_out]
-    q_s, k_s, v_s, o_s, do_s, p_s, l_s = outs[n_out:]
+    do_s, dq_s, dk_s, dv_s = outs[n_out:]
     rows = count * VB
     step = pl.program_id(0)
 
@@ -331,9 +340,12 @@
         x = embed_block(pieces, emb_ref[...], place)
     else:
         x = x_ref[...].reshape(rows, D)
-    _, (x2, mixed, h, unit1, inv1, u, cdf, unit2, inv2) = time_forward(
-        x, w, vec, count, group, q_s, k_s, v_s, o_s, p_s, l_s
-    )
+    x2 = split2(x)
+    mixed = load_halves(o_s, rows)
+    h, unit1, inv1 = norm_fwd(z1_s[...], vec[3:4], vec[4:5])
+    u = u_s[...]
+    cdf = gelu_cdf(u)
+    _, unit2, inv2 = norm_fwd(z2_s[...], vec[8:9], vec[9:10])
     dy = dy_ref[...].reshape(rows, D)
     g["rows"][8] += colsum(dy * unit2)
     g["rows"][9] += colsum(dy)
@@ -358,19 +370,19 @@
 
     def some(i, carry):
         units = [(c, i * UNROLL_BACK + k) for k in range(UNROLL_BACK) for c in range(2)]
-        time_attend_back(units, group, count, q_s, k_s, v_s, o_s, p_s, l_s, do_s)
+        time_attend_back(units, group, count, q_s, k_s, v_s, o_s, p_s, l_s, do_s, dq_s, dk_s, dv_s)
         return carry
 
     lax.fori_loop(0, VB // UNROLL_BACK, some, 0)
-    dq = load_halves(q_s, rows) * SCALE
+    dq = load_halves(dq_s, rows) * SCALE
     g["rows"][0] += colsum(dq)
     dq2 = split2(dq)
     g["q"][...] += tn3(x2, dq2)
     dx = dz1 + mmwt(dq2, w["q"])
-    dk2 = split2(load_halves(k_s, rows))
+    dk2 = split2(load_halves(dk_s, rows))
     g["k"][...] += tn3(x2, dk2)
     dx = dx + mmwt(dk2, w["k"])
-    dv = load_halves(v_s, rows)
+    dv = load_halves(dv_s, rows)
     g["rows"][1] += colsum(dv)
     dv2 = split2(dv)
     g["v"][...] += tn3(x2, dv2)
@@ -382,7 +394,7 @@
         tail[0][...] = dx.reshape(count, VB, D)
 
 
-def time_bwd(first, x, extra, dy, weights, count):
+def time_bwd(first, x, extra, dy, kept, weights, count):
     group = 64 if count > 32 else 32
     nv = x.shape[1]
     width = x.shape[2]
@@ -402,14 +414,13 @@
     return pl.pallas_call(
         functools.partial(time_bwd_kernel, first, count, group),
         grid=(nv // VB,),
-        in_specs=specs + [block] + time_weight_specs(),
+        in_specs=specs + [block] + time_kept(count, group, nv // VB)[0] + time_weight_specs(),
         out_specs=out_specs,
         out_shape=out_shape,
-        scratch_shapes=[pltpu.VMEM((2, pad, HALF), F32)] * 5
-        + [pltpu.VMEM((2, VB, group, 4 * group), F32), pltpu.VMEM((2, VB, group, HALF), F32)],
+        scratch_shapes=[pltpu.VMEM((2, pad, HALF), F32)] * 4,
         compiler_params=params_spec(),
         name="time_bwd",
-    )(x, *extra, dy, *weights)
+    )(x, *extra, dy, *kept, *weights)
 
 SB_ROWS = 64
 
@@ -472,29 +483,53 @@
 RECV_W = ("so", "rk", "rv", "rq", "ro", "up", "down")
 
 
+def recv_buffer(o2, w, vec):
+    buf2 = split2(mmw(o2, w["so"]) + vec[12:13])
+    kb = mmw(buf2, w["rk"])
+    vb = mmw(buf2, w["rv"]) + vec[14:15]
+    segs = range(kb.shape[0] // RPAD)
+    k = [split2(spread_rows(kb[s * RPAD : (s + 1) * RPAD])) for s in segs]
+    v = [split2(spread_rows(vb[s * RPAD : (s + 1) * RPAD])) for s in segs]
+    return buf2, k, v
+
+
 def recv_forward(send, o_rows, w, vec):
     sb = send.shape[0] // SB_ROWS
     send2 = split2(send)
     o2 = split2(o_rows)
-    buf = mmw(o2, w["so"]) + vec[12:13]
-    buf2 = split2(buf)
-    kb = mmw(buf2, w["rk"])
-    vb = mmw(buf2, w["rv"]) + vec[14:15]
+    buf2, k, v = recv_buffer(o2, w, vec)
     q = (mmw(send2, w["rq"]) + vec[13:14]) * SCALE
-
     segs = range(sb)
-    k = [split2(spread_rows(kb[s * RPAD : (s + 1) * RPAD])) for s in segs]
-    v = [split2(spread_rows(vb[s * RPAD : (s + 1) * RPAD])) for s in segs]
     ok = valid_lane(SB_ROWS)
     scores = [jnp.where(ok, nt3(split2(q[s * SB_ROWS : (s + 1) * SB_ROWS]), k[s]), negative) for s in segs]
     probs = [jnp.exp(sc - router_reduce(sc, jnp.maximum)) for sc in scores]
     probs = [p / router_reduce(p, jnp.add) for p in probs]
     mixed = jnp.concatenate([nn3(split2(p), v2) for p, v2 in zip(probs, v)], 0)
-    g, unit3, inv3 = norm_fwd(send + mmw(split2(mixed), w["ro"]) + vec[15:16], vec[16:17], vec[17:18])
+    z3 = send + mmw(split2(mixed), w["ro"]) + vec[15:16]
+    g, unit3, inv3 = norm_fwd(z3, vec[16:17], vec[17:18])
     u = mmw(split2(g), w["up"]) + jnp.concatenate([vec[18:19], vec[19:20]], 1)
     cdf = gelu_cdf(u)
-    y, unit4, inv4 = norm_fwd(g + mmw(split2(u * cdf), w["down"]) + vec[20:21], vec[21:22], vec[22:23])
-    return y, (send2, o2, buf2, mixed, g, unit3, inv3, u, cdf, unit4, inv4, q, k, v, probs)
+    z4 = g + mmw(split2(u * cdf), w["down"]) + vec[20:21]
+    y, unit4, inv4 = norm_fwd(z4, vec[21:22], vec[22:23])
+    kept = (send2, o2, buf2, mixed, g, unit3, inv3, u, cdf, unit4, inv4, q, k, v, probs)
+    return y, kept, (q, mixed, jnp.concatenate(probs, 0), z3, u, z4)
+
+
+def recv_restore(send, o_rows, w, vec, saved):
+    q, mixed, p, z3, u, z4 = saved
+    o2 = split2(o_rows)
+    buf2, k, v = recv_buffer(o2, w, vec)
+    g, unit3, inv3 = norm_fwd(z3, vec[16:17], vec[17:18])
+    y, unit4, inv4 = norm_fwd(z4, vec[21:22], vec[22:23])
+    probs = [p[s * SB_ROWS : (s + 1) * SB_ROWS] for s in range(send.shape[0] // SB_ROWS)]
+    return y, (split2(send), o2, buf2, mixed, g, unit3, inv3, u, gelu_cdf(u), unit4, inv4, q, k, v, probs)
+
+
+KEPT_WIDTHS = (D, D, HALF, D, FF, D)
+
+
+def kept_specs(sb):
+    return [pl.BlockSpec((sb * SB_ROWS, k), lambda i: (i, 0)) for k in KEPT_WIDTHS]
 
 
 RECV_G = RECV_W + ("rows",)
@@ -562,9 +597,9 @@
 def recv_fwd_kernel(sb, send_ref, o_ref, *refs):
     w = {n: refs[i][...] for i, n in enumerate(RECV_W)}
     vec_ref, mvec_ref, mw_ref, out_ref = refs[7:11]
-    y, _ = recv_forward(
-        send_ref[...].reshape(sb * SB_ROWS, D), unpack_block(o_ref, sb), w, vec_ref[...]
-    )
+    y, _, saved = recv_forward(send_ref[...].reshape(sb * SB_ROWS, D), unpack_block(o_ref, sb), w, vec_ref[...])
+    for ref, x in zip(refs[11:], saved):
+        ref[...] = x
     mvec = mvec_ref[...]
     wide, _, _, _ = merge_rows(y, sb // 2, mvec)
     out_ref[...] = (mmw(split2(wide), mw_ref[...]) + mvec[4:5]).reshape(sb // 2, SB_ROWS, D)
@@ -576,14 +611,17 @@
         functools.partial(recv_fwd_kernel, sb),
         grid=(n // sb,),
         in_specs=[seg_block(sb), pack_spec(sb)] + recv_weight_specs() + [whole((8, D)), whole((2 * D, D))],
-        out_specs=seg_block(sb // 2),
-        out_shape=jax.ShapeDtypeStruct((n // 2, SB_ROWS, D), F32),
+        out_specs=[seg_block(sb // 2)] + kept_specs(sb),
+        out_shape=[jax.ShapeDtypeStruct((n // 2, SB_ROWS, D), F32)]
+        + [jax.ShapeDtypeStruct((n * SB_ROWS, k), F32) for k in KEPT_WIDTHS],
         compiler_params=params_spec(),
         name="recv_fwd",
     )(send, o, *weights, mvec, mw)
 
 
 def recv_bwd_kernel(sb, send_ref, o_ref, dx_ref, *refs):
+    saved = [ref[...] for ref in refs[:6]]
+    refs = refs[6:]
     w = {n: refs[i][...] for i, n in enumerate(RECV_W)}
     vec_ref, mvec_ref, mw_ref, dsend_ref, do_ref = refs[7:12]
     g = dict(zip(RECV_G, refs[12:20]))
@@ -595,9 +633,7 @@
             ref[...] = jnp.zeros(ref.shape, F32)
 
     vec = vec_ref[...]
-    y, kept = recv_forward(
-        send_ref[...].reshape(sb * SB_ROWS, D), unpack_block(o_ref, sb), w, vec
-    )
+    y, kept = recv_restore(send_ref[...].reshape(sb * SB_ROWS, D), unpack_block(o_ref, sb), w, vec, saved)
     pairs = sb // 2
     wide, unit, inv, gain = merge_rows(y, pairs, mvec_ref[...])
     dx = dx_ref[...].reshape(pairs * SB_ROWS, D)
@@ -623,13 +659,14 @@
 RECV_GRADS = [(D, D)] * 5 + [(D, FF), (FF, D), (11, 8, D)]
 
 
-def recv_bwd(send, o, dx, weights, mvec, mw, sb):
+def recv_bwd(send, o, dx, kept, weights, mvec, mw, sb):
     n = send.shape[0]
     shapes = RECV_GRADS + [(2 * D, D), (5, 8, D)]
     return pl.pallas_call(
         functools.partial(recv_bwd_kernel, sb),
         grid=(n // sb,),
         in_specs=[seg_block(sb), pack_spec(sb), seg_block(sb // 2)]
+        + kept_specs(sb)
         + recv_weight_specs()
         + [whole((8, D)), whole((2 * D, D))],
         out_specs=[seg_block(sb), pack_spec(sb)] + [whole(s) for s in shapes],
@@ -637,7 +674,7 @@
         + [jax.ShapeDtypeStruct(s, F32) for s in shapes],
         compiler_params=params_spec(),
         name="recv_bwd",
-    )(send, o, dx, *weights, mvec, mw)
+    )(send, o, dx, *kept, *weights, mvec, mw)
 
 
 def tail_kernel(sb, send_ref, o_ref, tgt_ref, kept_ref, scale_ref, mean_ref, *refs):
@@ -653,7 +690,7 @@
 
     vec = vec_ref[...]
     rows = sb * SB_ROWS
-    y, kept = recv_forward(
+    y, kept, _ = recv_forward(
         send_ref[...].reshape(rows, D), unpack_block(o_ref, sb), w, vec
     )
     head = head_ref[...]
@@ -1213,27 +1250,28 @@
         (*[square[12 * l + i] for i in (7, 9, 10, 8, 11)], up[2 * l + 1], down[2 * l + 1], vecs[l]) for l in range(2)
     ]
 
-    sb0, sb1 = 4, 6
-    dim0 = time_fwd(True, pieces, (emb, place), time_w[0], SEG)
-    o0 = send_fwd(dim0, routers[0], here, send_w[0], sb0, -(-SEG // nf) * nf)
+    sb0, sb1, sf0, sf1, st = 12, 10, 20, 10, 10
+    rf, rb = 20, 20
+    dim0, kept0 = time_fwd(True, pieces, (emb, place), time_w[0], SEG)
+    o0 = send_fwd(dim0, routers[0], here, send_w[0], sf0, -(-SEG // nf) * nf)
     o0 = combine(o0, True, 2)
-    x1 = recv_fwd(dim0, o0, recv_w[0], mvec, mw, sb0)
-    dim1 = time_fwd(False, x1, (), time_w[1], SEG // 2)
-    o1 = send_fwd(dim1, routers[1], here, send_w[1], sb1, -(-SEG // 2 // nf) * nf)
+    x1, *saved = recv_fwd(dim0, o0, recv_w[0], mvec, mw, rf)
+    dim1, kept1 = time_fwd(False, x1, (), time_w[1], SEG // 2)
+    o1 = send_fwd(dim1, routers[1], here, send_w[1], sf1, -(-SEG // 2 // nf) * nf)
     o1 = combine(o1, True, 3)
-    out = tail(dim1, o1, tgt, kept, scale16, mean16, recv_w[1], head, sb1)
+    out = tail(dim1, o1, tgt, kept, scale16, mean16, recv_w[1], head, st)
     ddim1, do1, grecv1, dhead = out[0], out[1], out[2:10], out[10]
     do1 = combine(do1, False, 4)
     out = send_bwd(dim1, ddim1, routers[1], o1, do1, here, send_w[1], sb1)
     ddim1, dr1, gsend1 = out[0], out[1], out[2:]
-    out = time_bwd(False, x1, (), ddim1, time_w[1], SEG // 2)
+    out = time_bwd(False, x1, (), ddim1, kept1, time_w[1], SEG // 2)
     gtime1, dx1 = out[:7], out[7]
-    out = recv_bwd(dim0, o0, dx1, recv_w[0], mvec, mw, sb0)
+    out = recv_bwd(dim0, o0, dx1, saved, recv_w[0], mvec, mw, rb)
     ddim0, do0, grecv0, dmw, dmv = out[0], out[1], out[2:10], out[10], out[11]
     do0 = combine(do0, False, 5)
     out = send_bwd(dim0, ddim0, routers[0], o0, do0, here, send_w[0], sb0)
     ddim0, dr0, gsend0 = out[0], out[1], out[2:]
-    out = time_bwd(True, pieces, (emb, place), ddim0, time_w[0], SEG)
+    out = time_bwd(True, pieces, (emb, place), ddim0, kept0, time_w[0], SEG)
     gtime0, demb, dplace = out[:7], out[7], out[8]
 
     mats, ups, downs, rows = [], [], [], []

time: 939 us -> 764 us (0.81)
  Pallas kernels: 801 us -> 628 us
    pallas_call x2, Pallas kernels: 167 us -> 106 us  [time_bwd(): pl.pallas_call(functools.partial(time_bwd_kernel, first, count, group), g...]
    pallas_call x1, Pallas kernels: 112 us -> 53.8 us  [recv_bwd(): pl.pallas_call(functools.partial(recv_bwd_kernel, sb), grid=(n // sb,), i...]
    pallas_call x1, Pallas kernels: 49.8 us -> 26.5 us  [recv_fwd(): pl.pallas_call(functools.partial(recv_fwd_kernel, sb), grid=(n // sb,), i...]
    unnamed x134 -> x140, local copies, waits for them, and re-layouts: 37 us -> 37.3 us
where the time goes in v4:
time: 764 us; the launch traced here: 759 us
  Pallas kernels  628 us (82%)
  local copies, waits for them, and re-layouts  93.7 us (12%)
  other arithmetic  31.7 us (4%)
    pallas_call x4, Pallas kernels, group_combine(): pl.pallas_call(functools.partial(group_kernel, stats, per), in_specs=[INV...  122 us
    pallas_call x1, Pallas kernels, scatter_sum(): pl.pallas_call(functools.partial(scatter_kernel, n), in_specs=[ANY] * n +...  108 us
    pallas_call x2, Pallas kernels, time_bwd(): pl.pallas_call(functools.partial(time_bwd_kernel, first, count, group), g...  106 us
    pallas_call x2, Pallas kernels, time_fwd(): pl.pallas_call(functools.partial(time_fwd_kernel, first, count, group), g...  58.8 us
    pallas_call x1, Pallas kernels, gather_all(): pl.pallas_call(functools.partial(gather_kernel, n), in_specs=[ANY] * n, o...  57.4 us
    pallas_call x1, Pallas kernels, recv_bwd(): pl.pallas_call(functools.partial(recv_bwd_kernel, sb), grid=(n // sb,), i...  53.8 us
    pallas_call x2, Pallas kernels, send_bwd(): pl.pallas_call(functools.partial(send_bwd_kernel, sb), grid=(n // sb,), i...  40.3 us
    pallas_call x1, Pallas kernels, tail(): pl.pallas_call(functools.partial(tail_kernel, sb), grid=(n // sb,), in_sp...  37.4 us

profile of v4, /device:TPU:0, one launch (start us, length us, event | category | flops | bytes accessed | tf_op | source)
XLA Modules:
  0.0 758.5 jit_solution(17541957029637983386)
XLA Ops:
  1.3 1.6 fusion.6
  2.9 1.0 convert_reduce_fusion
  3.9 1.2 fusion.1
  5.1 1.2 fusion.4
  6.4 1.3 pad.62.refs_3_
  14.1 1.0 copy.42
  16.3 1.1 copy.36
  17.8 1.1 pad.58.tgt_ref
  19.5 1.1 pad.59.kept_ref
  21.2 2.0 copy.40
  23.1 2.0 divide_bitcast_fusion
  25.2 1.4 pad.50.refs_0_
  27.4 57.4 %gather_all.1 = (bf16[2,2,4,2,208,256]{5,4,3,2,1,0:T(8,128)(2,1)S(1)}, bf16[2,2,4,2,128,256]{5,4,3,2,1,0:T(8,128)(2,1)S(1)}, bf16[2,2,4,2,33,256]{5,4,3,2,1,0:T(8,128)(2,1)S(1)}) custom-call(bf16[208,256]{1,0:T(8,128)(2,1)S(1)} %reshape.142.refs_0_, bf16[128,256]{1,0:T(8,128)(2,1)S(1)} %copy-done.10, bf16[33,256]{1,0:T(8,128)(2,1)S(1)} %reshape.144.refs_2_), custom_call_target="tpu_custom_call" | custom-call | tf_op jit(solution)/shard_map/gather_all/pallas_call | solution.py:960
  84.8 1.3 copy-done.4
  87.1 2.6 convert_element_type.76
  95.8 1.6 slice.243
  97.4 1.8 reshape.151
  99.2 1.9 pad.57.r_ref
  101.1 1.8 slice.223
  102.9 2.1 reshape.149
  105.0 2.4 pad.54.r_ref
  107.4 1.1 convert_element_type.77
  110.8 1.4 slice_bitcast_fusion.8
  112.4 1.0 slice_bitcast_fusion
  113.8 1.0 slice_bitcast_fusion.1
  114.8 35.7 %time_fwd.2 = (f32[60,64,256]{2,1,0:T(8,128)}, f32[8,2,512,128]{3,2,1,0:T(8,128)}, f32[8,2,512,128]{3,2,1,0:T(8,128)}, f32[8,2,512,128]{3,2,1,0:T(8,128)}, f32[8...) custom-call(f32[60,64,16]{2,1,0:T(8,128)} %pad.50.refs_0_, ...), custom_call_target="tpu_custom_call" | custom-call | tf_op jit(solution)/shard_map/time_fwd/pallas_call | solution.py:300
  150.5 11.4 %send_fwd.2.in_ref = f32[64,24,128]{2,1,0:T(8,128)} custom-call(f32[60,64,256]{2,1,0:T(8,128)} %get-tuple-element.99.dim_ref.send_ref, f32[60,16,256]{2,1,0:T(8,128)} %pad.54.r_ref, f32[64,128]{1,0:T(8,128)} %broadcast_in_dim.11.here_ref, bf16[256,256]{1,0:T(8,128)(2,1)} %get-tuple-element.212.refs_0_, bf16[256,256]{1,0:T(8,128)(2,1)} %get-tuple-element.211.refs_1_, ...), custom_call_target="tpu_custom_call" | custom-call | tf_op jit(solution)/shard_map/send_fwd/pallas_call | solution.py:766
  161.9 1.1 copy-done.3
  163.0 35.5 %group_stats.2.o_ref = f32[64,24,128]{2,1,0:T(8,128)S(1)} custom-call(f32[64,24,128]{2,1,0:T(8,128)S(1)} %copy-done.3), custom_call_target="tpu_custom_call" | custom-call | tf_op jit(solution)/shard_map/group_stats/pallas_call | solution.py:1174
  199.4 26.5 %recv_fwd.1 = (f32[30,64,256]{2,1,0:T(8,128)}, f32[3840,256]{1,0:T(8,128)}, f32[3840,256]{1,0:T(8,128)}, f32[3840,128]{1,0:T(8,128)}, f32[3840,256]{1,0:T(8,128)...) custom-call(f32[60,64,256]{2,1,0:T(8,128)} %get-tuple-element.99.dim_ref.send_ref, f32[64,24,128]{2,1,0:T(8,128)} %copy-done, ...), custom_call_target="tpu_custom_call" | custom-call | tf_op jit(solution)/shard_map/recv_fwd/pallas_call | solution.py:610
  225.9 23.2 %time_fwd.3 = (f32[30,64,256]{2,1,0:T(8,128)}, f32[8,2,256,128]{3,2,1,0:T(8,128)}, f32[8,2,256,128]{3,2,1,0:T(8,128)}, f32[8,2,256,128]{3,2,1,0:T(8,128)}, f32[8...) custom-call(f32[30,64,256]{2,1,0:T(8,128)} %get-tuple-element.100.re, ...), custom_call_target="tpu_custom_call" | custom-call | tf_op jit(solution)/shard_map/time_fwd/pallas_call | solution.py:300
  249.1 7.3 send_fwd.3.in_ref
  256.3 1.0 copy-done.6
  257.3 24.5 %group_stats.3.o_ref = f32[32,24,128]{2,1,0:T(8,128)S(1)} custom-call(f32[32,24,128]{2,1,0:T(8,128)S(1)} %copy-done.6), custom_call_target="tpu_custom_call" | custom-call | tf_op jit(solution)/shard_map/group_stats/pallas_call | solution.py:1174
  282.6 37.4 %tail.1 = (f32[30,64,256]{2,1,0:T(8,128)}, f32[32,24,128]{2,1,0:T(8,128)}, f32[256,256]{1,0:T(8,128)}, f32[256,256]{1,0:T(8,128)}, f32[256,256]{1,0:T(8,128)}, /...) custom-call(f32[30,64,256]{2,1,0:T(8,128)} %get-tuple-element.101.di, ...), custom_call_target="tpu_custom_call" | custom-call | tf_op jit(solution)/shard_map/tail/pallas_call | solution.py:713
  320.9 1.0 copy-done.9
  321.9 24.8 %group_sum.2.do_ref = f32[32,24,128]{2,1,0:T(8,128)S(1)} custom-call(f32[32,24,128]{2,1,0:T(8,128)S(1)} %copy-done.9), custom_call_target="tpu_custom_call" | custom-call | tf_op jit(solution)/shard_map/group_sum/pallas_call | solution.py:1174
  347.5 15.0 %send_bwd.2 = (f32[30,64,256]{2,1,0:T(8,128)}, f32[30,16,256]{2,1,0:T(8,128)}, f32[256,256]{1,0:T(8,128)}, f32[256,256]{1,0:T(8,128)}, f32[256,256]{1,0:T(8,128)}, /*index=5*/f32[2,8,256]{2,1,0:T(8,128)}) custom-call(f32[30,64,256]{2,1,0:T(8,128)} %get-tuple-element.101.dim_ref.send_ref, f32[30,64,256]{2,1,0:T(8,128)} %get-tuple-element.102.dpart_ref, ...), custom_call_target="tpu_custom_call" | custom-call | tf_op jit(solution)/shard_map/send_bwd/pallas_call | solution.py:822
  362.4 38.0 %time_bwd.2 = (f32[256,256]{1,0:T(8,128)}, f32[256,256]{1,0:T(8,128)}, f32[256,256]{1,0:T(8,128)}, f32[256,256]{1,0:T(8,128)}, f32[256,512]{1,0:T(8,128)}, /*ind...) custom-call(f32[30,64,256]{2,1,0:T(8,128)} %get-tuple-element.100.refs_0_, ...), custom_call_target="tpu_custom_call" | custom-call | tf_op jit(solution)/shard_map/time_bwd/pallas_call | solution.py:414
  400.4 53.8 %recv_bwd.1 = (f32[60,64,256]{2,1,0:T(8,128)}, f32[64,24,128]{2,1,0:T(8,128)}, f32[256,256]{1,0:T(8,128)}, f32[256,256]{1,0:T(8,128)}, f32[256,256]{1,0:T(8,128)...) custom-call(f32[60,64,256]{2,1,0:T(8,128)} %get-tuple-element.99.dim, ...), custom_call_target="tpu_custom_call" | custom-call | tf_op jit(solution)/shard_map/recv_bwd/pallas_call | solution.py:665
  454.8 1.4 reduce_sum.146
  456.2 1.5 reduce_sum.142
  458.4 1.1 copy-done.8
  459.5 37.1 %group_sum.3.do_ref = f32[64,24,128]{2,1,0:T(8,128)S(1)} custom-call(f32[64,24,128]{2,1,0:T(8,128)S(1)} %copy-done.8), custom_call_target="tpu_custom_call" | custom-call | tf_op jit(solution)/shard_map/group_sum/pallas_call | solution.py:1174
  497.5 25.4 %send_bwd.3 = (f32[60,64,256]{2,1,0:T(8,128)}, f32[60,16,256]{2,1,0:T(8,128)}, f32[256,256]{1,0:T(8,128)}, f32[256,256]{1,0:T(8,128)}, f32[256,256]{1,0:T(8,128)}, /*index=5*/f32[2,8,256]{2,1,0:T(8,128)}) custom-call(f32[60,64,256]{2,1,0:T(8,128)} %get-tuple-element.99.dim_ref.send_ref, f32[60,64,256]{2,1,0:T(8,128)} %get-tuple-element.121.dpart_ref, ...), custom_call_target="tpu_custom_call" | custom-call | tf_op jit(solution)/shard_map/send_bwd/pallas_call | solution.py:822
  523.0 67.8 %time_bwd.3 = (f32[256,256]{1,0:T(8,128)}, f32[256,256]{1,0:T(8,128)}, f32[256,256]{1,0:T(8,128)}, f32[256,256]{1,0:T(8,128)}, f32[256,512]{1,0:T(8,128)}, /*ind...) custom-call(f32[60,64,16]{2,1,0:T(8,128)} %pad.50.refs_0_, ...), custom_call_target="tpu_custom_call" | custom-call | tf_op jit(solution)/shard_map/time_bwd/pallas_call | solution.py:414
  590.8 1.8 reduce_sum.138
  592.5 1.2 bitcast_reduce_fusion
  593.7 1.5 reduce_sum.140
  595.8 2.6 pad_maximum_fusion
  598.4 1.7 reshape.153
  601.0 8.9 %concatenate.15 = f32[1036,256]{1,0:T(8,128)S(1)} concatenate(f32[12,256]{1,0:T(8,128)} %bitcast.138, f32[1,256]{1,0:T(1,128)} %bitcast.139, f32[60,256]{1,0:T(8,128)S(1)} %bitcast_reduce_fusion, f32[10,256]{1,0:T(8,128)} %reduce_sum.140, f32[2,256]{1,0:T(2,128)} %reduce_sum.141, f32[11,256]{1,0:T(8,128)} %reduce_sum.142, f32[10,256]{1,0:T(8,128)} %reduce_sum.143, ...), dimensions={0} | concatenate | bytes 2121728 | tf_op jit(solution)/shard_map/concatenate | solution.py:1286
  609.9 1.6 reshape.158
  611.5 1.3 pad.61
  612.9 1.2 reshape.159.refs_2_
  614.2 1.5 constant_dynamic-update-slice_fusion.29
  615.8 2.2 constant_dynamic-update-slice_fusion.28
  618.0 1.7 constant_dynamic-update-slice_fusion.24
  619.7 1.7 constant_dynamic-update-slice_fusion.23
  621.4 1.7 constant_dynamic-update-slice_fusion.22
  638.4 1.1 constant_dynamic-update-slice_fusion
  641.3 108.0 %scatter_sum.1 = (f32[208,256]{1,0:T(8,128)}, f32[128,256]{1,0:T(8,128)}, f32[33,256]{1,0:T(8,128)}, f32[16,128]{1,0:T(8,128)}) custom-call(f32[2,2,4,2,208,256]{5,4,3,2,1,0:T(8,128)} %bitcast.43.refs_0_, f32[2,2,4,2,128,256]{5,4,3,2,1,0:T(8,128)} %bitcast.44.refs_1_, f32[2,2,4,2,33,256]{5,4,3,2,1,0:T(8,128)} %reshape.159.refs_2_, f32[8,128]{1,0:T(8,128)} %pad.62.refs_3_), custom_call_target="tpu_custom_call" | custom-call | tf_op jit(solution)/shard_map/scatter_sum/pallas_call | solution.py:1097
  749.2 1.3 slice_reduce_fusion
  753.0 1.0 multiply_bitcast_fusion.1
  (181 shorter events, 48.2 us)
Async XLA Ops:
  26.6 0.8 copy-start.10
  27.4 81.1 %copy-start.53 = (pred[16]{0:T(512)(128)(4,1)S(1)}, pred[16]{0:T(512)(128)(4,1)}, u32[]{:S(2)}) copy-start(pred[16]{0:T(512)(128)(4,1)} %constant.21.clone.1) | copy-start | bytes 52
  84.8 1.3 copy-start.4
  105.0 7.2 copy-start.5
  161.9 1.1 copy-start.3
  198.5 0.9 copy-start
  256.3 1.0 copy-start.6
  281.8 0.7 copy-start.1
  320.9 1.0 copy-start.9
  346.7 0.8 copy-start.7
  400.4 53.8 %copy-start.51 = (f32[2,8,256]{2,1,0:T(8,128)S(1)}, f32[2,8,256]{2,1,0:T(8,128)}, u32[]{:S(2)}) copy-start(f32[2,8,256]{2,1,0:T(8,128)} %get-tuple-element.172) | copy-start | bytes 49156
  400.4 57.3 %copy-start.48 = (f32[10,8,256]{2,1,0:T(8,128)S(1)}, f32[10,8,256]{2,1,0:T(8,128)}, u32[]{:S(2)}) copy-start(f32[10,8,256]{2,1,0:T(8,128)} %get-tuple-element.171) | copy-start | bytes 245764
  400.4 57.9 %copy-start.21 = (f32[30,16,256]{2,1,0:T(8,128)S(1)}, f32[30,16,256]{2,1,0:T(8,128)}, u32[]{:S(2)}) copy-start(f32[30,16,256]{2,1,0:T(8,128)} %get-tuple-element.177) | copy-start | bytes 1474564
  458.4 1.1 copy-start.8
  496.6 0.9 copy-start.2
  522.9 72.3 %copy-start.52 = (f32[2,8,256]{2,1,0:T(8,128)S(1)}, f32[2,8,256]{2,1,0:T(8,128)}, u32[]{:S(2)}) copy-start(f32[2,8,256]{2,1,0:T(8,128)} %get-tuple-element.169) | copy-start | bytes 49156
  522.9 72.9 %copy-start.18 = (f32[256,512]{1,0:T(8,128)S(1)}, f32[256,512]{1,0:T(8,128)}, u32[]{:S(2)}) copy-start(f32[256,512]{1,0:T(8,128)} %get-tuple-element.161) | copy-start | bytes 1572868
  522.9 72.9 %copy-start.19 = (f32[256,512]{1,0:T(8,128)S(1)}, f32[256,512]{1,0:T(8,128)}, u32[]{:S(2)}) copy-start(f32[256,512]{1,0:T(8,128)} %get-tuple-element.160) | copy-start | bytes 1572868
  522.9 72.8 %copy-start.20 = (f32[256,512]{1,0:T(8,128)S(1)}, f32[256,512]{1,0:T(8,128)}, u32[]{:S(2)}) copy-start(f32[256,512]{1,0:T(8,128)} %get-tuple-element.159) | copy-start | bytes 1572868
  590.8 9.3 %copy-start.11 = (f32[60,16,256]{2,1,0:T(8,128)S(1)}, f32[60,16,256]{2,1,0:T(8,128)}, u32[]{:S(2)}) copy-start(f32[60,16,256]{2,1,0:T(8,128)} %get-tuple-element.176) | copy-start | bytes 2949124
  612.8 17.6 %copy-start.32 = (f32[256,256]{1,0:T(8,128)S(1)}, f32[256,256]{1,0:T(8,128)}, u32[]{:S(2)}) copy-start(f32[256,256]{1,0:T(8,128)} %get-tuple-element.146) | copy-start | bytes 786436
  614.1 9.0 %copy-start.42 = (f32[256,256]{1,0:T(8,128)S(1)}, f32[256,256]{1,0:T(8,128)}, u32[]{:S(2)}) copy-start(f32[256,256]{1,0:T(8,128)} %get-tuple-element.136) | copy-start | bytes 786436
  614.1 9.8 %copy-start.41 = (f32[256,256]{1,0:T(8,128)S(1)}, f32[256,256]{1,0:T(8,128)}, u32[]{:S(2)}) copy-start(f32[256,256]{1,0:T(8,128)} %get-tuple-element.137) | copy-start | bytes 786436
  614.1 10.5 %copy-start.40 = (f32[256,256]{1,0:T(8,128)S(1)}, f32[256,256]{1,0:T(8,128)}, u32[]{:S(2)}) copy-start(f32[256,256]{1,0:T(8,128)} %get-tuple-element.138) | copy-start | bytes 786436
  614.1 11.2 %copy-start.39 = (f32[256,256]{1,0:T(8,128)S(1)}, f32[256,256]{1,0:T(8,128)}, u32[]{:S(2)}) copy-start(f32[256,256]{1,0:T(8,128)} %get-tuple-element.139) | copy-start | bytes 786436
  614.1 12.0 %copy-start.38 = (f32[256,256]{1,0:T(8,128)S(1)}, f32[256,256]{1,0:T(8,128)}, u32[]{:S(2)}) copy-start(f32[256,256]{1,0:T(8,128)} %get-tuple-element.140) | copy-start | bytes 786436
  614.1 12.7 %copy-start.37 = (f32[256,256]{1,0:T(8,128)S(1)}, f32[256,256]{1,0:T(8,128)}, u32[]{:S(2)}) copy-start(f32[256,256]{1,0:T(8,128)} %get-tuple-element.141) | copy-start | bytes 786436
  614.1 13.4 %copy-start.36 = (f32[256,256]{1,0:T(8,128)S(1)}, f32[256,256]{1,0:T(8,128)}, u32[]{:S(2)}) copy-start(f32[256,256]{1,0:T(8,128)} %get-tuple-element.142) | copy-start | bytes 786436
  614.1 14.1 %copy-start.35 = (f32[256,256]{1,0:T(8,128)S(1)}, f32[256,256]{1,0:T(8,128)}, u32[]{:S(2)}) copy-start(f32[256,256]{1,0:T(8,128)} %get-tuple-element.143) | copy-start | bytes 786436
  614.1 14.8 %copy-start.34 = (f32[256,256]{1,0:T(8,128)S(1)}, f32[256,256]{1,0:T(8,128)}, u32[]{:S(2)}) copy-start(f32[256,256]{1,0:T(8,128)} %get-tuple-element.144) | copy-start | bytes 786436
  614.1 15.6 %copy-start.33 = (f32[256,256]{1,0:T(8,128)S(1)}, f32[256,256]{1,0:T(8,128)}, u32[]{:S(2)}) copy-start(f32[256,256]{1,0:T(8,128)} %get-tuple-element.145) | copy-start | bytes 786436
  614.2 17.0 %copy-start.31 = (f32[256,256]{1,0:T(8,128)S(1)}, f32[256,256]{1,0:T(8,128)}, u32[]{:S(2)}) copy-start(f32[256,256]{1,0:T(8,128)} %get-tuple-element.147) | copy-start | bytes 786436
  614.2 17.7 %copy-start.30 = (f32[256,256]{1,0:T(8,128)S(1)}, f32[256,256]{1,0:T(8,128)}, u32[]{:S(2)}) copy-start(f32[256,256]{1,0:T(8,128)} %get-tuple-element.148) | copy-start | bytes 786436
  614.2 18.4 %copy-start.29 = (f32[256,256]{1,0:T(8,128)S(1)}, f32[256,256]{1,0:T(8,128)}, u32[]{:S(2)}) copy-start(f32[256,256]{1,0:T(8,128)} %get-tuple-element.149) | copy-start | bytes 786436
  614.2 19.1 %copy-start.28 = (f32[256,256]{1,0:T(8,128)S(1)}, f32[256,256]{1,0:T(8,128)}, u32[]{:S(2)}) copy-start(f32[256,256]{1,0:T(8,128)} %get-tuple-element.150) | copy-start | bytes 786436
  614.2 19.9 %copy-start.27 = (f32[256,256]{1,0:T(8,128)S(1)}, f32[256,256]{1,0:T(8,128)}, u32[]{:S(2)}) copy-start(f32[256,256]{1,0:T(8,128)} %get-tuple-element.151) | copy-start | bytes 786436
  614.2 20.6 %copy-start.26 = (f32[256,256]{1,0:T(8,128)S(1)}, f32[256,256]{1,0:T(8,128)}, u32[]{:S(2)}) copy-start(f32[256,256]{1,0:T(8,128)} %get-tuple-element.152) | copy-start | bytes 786436
  615.7 19.8 %copy-start.25 = (f32[256,256]{1,0:T(8,128)S(1)}, f32[256,256]{1,0:T(8,128)}, u32[]{:S(2)}) copy-start(f32[256,256]{1,0:T(8,128)} %get-tuple-element.153) | copy-start | bytes 786436
  615.7 20.5 %copy-start.24 = (f32[256,256]{1,0:T(8,128)S(1)}, f32[256,256]{1,0:T(8,128)}, u32[]{:S(2)}) copy-start(f32[256,256]{1,0:T(8,128)} %get-tuple-element.154) | copy-start | bytes 786436
  615.7 21.2 %copy-start.23 = (f32[256,256]{1,0:T(8,128)S(1)}, f32[256,256]{1,0:T(8,128)}, u32[]{:S(2)}) copy-start(f32[256,256]{1,0:T(8,128)} %get-tuple-element.155) | copy-start | bytes 786436
  615.7 22.0 %copy-start.22 = (f32[256,256]{1,0:T(8,128)S(1)}, f32[256,256]{1,0:T(8,128)}, u32[]{:S(2)}) copy-start(f32[256,256]{1,0:T(8,128)} %get-tuple-element.156) | copy-start | bytes 786436
  615.8 22.7 %copy-start.16 = (f32[512,256]{1,0:T(8,128)S(1)}, f32[512,256]{1,0:T(8,128)}, u32[]{:S(2)}) copy-start(f32[512,256]{1,0:T(8,128)} %get-tuple-element.163) | copy-start | bytes 1572868
  615.8 22.7 %copy-start.17 = (f32[512,256]{1,0:T(8,128)S(1)}, f32[512,256]{1,0:T(8,128)}, u32[]{:S(2)}) copy-start(f32[512,256]{1,0:T(8,128)} %get-tuple-element.157) | copy-start | bytes 1572868
  621.4 18.1 %copy-start.15 = (f32[512,256]{1,0:T(8,128)S(1)}, f32[512,256]{1,0:T(8,128)}, u32[]{:S(2)}) copy-start(f32[512,256]{1,0:T(8,128)} %get-tuple-element.164) | copy-start | bytes 1572868
  623.9 16.5 %copy-start.14 = (f32[512,256]{1,0:T(8,128)S(1)}, f32[512,256]{1,0:T(8,128)}, u32[]{:S(2)}) copy-start(f32[512,256]{1,0:T(8,128)} %get-tuple-element.165) | copy-start | bytes 1572868
  641.2 113.6 %copy-start.45 = (f32[8288]{0:T(1024)S(1)}, f32[8288]{0:T(1024)}, u32[]{:S(2)}) copy-start(f32[8288]{0:T(1024)} %param.21) | copy-start | bytes 99460
  641.2 113.6 %copy-start.49 = (f32[8288]{0:T(1024)S(1)}, f32[8288]{0:T(1024)}, u32[]{:S(2)}) copy-start(f32[8288]{0:T(1024)} %param.26) | copy-start | bytes 99460
  641.2 113.6 %copy-start.50 = (f32[8288]{0:T(1024)S(1)}, f32[8288]{0:T(1024)}, u32[]{:S(2)}) copy-start(f32[8288]{0:T(1024)} %param.27) | copy-start | bytes 99460
  641.2 114.3 %copy-start.13 = (f32[32768]{0:T(1024)S(1)}, f32[32768]{0:T(1024)}, u32[]{:S(2)}) copy-start(f32[32768]{0:T(1024)} %param.20) | copy-start | bytes 393220
  641.2 114.3 %copy-start.46 = (f32[32768]{0:T(1024)S(1)}, f32[32768]{0:T(1024)}, u32[]{:S(2)}) copy-start(f32[32768]{0:T(1024)} %param.24) | copy-start | bytes 393220
  641.2 114.3 %copy-start.47 = (f32[32768]{0:T(1024)S(1)}, f32[32768]{0:T(1024)}, u32[]{:S(2)}) copy-start(f32[32768]{0:T(1024)} %param.25) | copy-start | bytes 393220
  641.2 115.1 %copy-start.12 = (f32[53248]{0:T(1024)S(1)}, f32[53248]{0:T(1024)}, u32[]{:S(2)}) copy-start(f32[53248]{0:T(1024)} %param.19) | copy-start | bytes 638980
  641.2 115.0 %copy-start.43 = (f32[53248]{0:T(1024)S(1)}, f32[53248]{0:T(1024)}, u32[]{:S(2)}) copy-start(f32[53248]{0:T(1024)} %param.22) | copy-start | bytes 638980
  641.3 115.0 %copy-start.44 = (f32[53248]{0:T(1024)S(1)}, f32[53248]{0:T(1024)}, u32[]{:S(2)}) copy-start(f32[53248]{0:T(1024)} %param.23) | copy-start | bytes 638980

commit v5 on v4

--- a/solution.py
+++ b/solution.py
@@ -35,6 +35,10 @@
 clip_norm = 0.01
 step_count = 10.0
 VMEM_LIMIT = 60 << 20
+
+
+ANY = pl.BlockSpec(memory_space=pl.ANY)
+INVMEM = pl.BlockSpec(memory_space=pltpu.VMEM)
 
 
 def split2(x):
@@ -278,8 +282,50 @@
     return pltpu.CompilerParams(vmem_limit_bytes=VMEM_LIMIT)
 
 
-def time_weight_specs():
-    return [whole((D, D))] * 4 + [whole((D, FF)), whole((FF, D)), whole((24, D))]
+def pick(shape, index):
+    return pl.BlockSpec((None,) + shape, lambda i: (index,) + (0,) * len(shape))
+
+
+def weight_specs(squares, feed, layer):
+    specs = [pick((D, D), k) for k in squares]
+    if feed is not None:
+        specs += [pick((D, FF), feed), pick((FF, D), 4 + feed)]
+    return specs + [pick((24, D), layer)]
+
+
+def weight_args(model, squares, feed):
+    square, up, down, vecs = model
+    return [square] * len(squares) + ([up, down] if feed is not None else []) + [vecs]
+
+
+def flush(step, last, accs, mat_at, up_acc, down_acc, feed_at, up_rows, g_mat, g_feed, sems):
+    @pl.when(step == last)
+    def _():
+        copies = []
+
+        def add(src, dst):
+            copies.append(pltpu.make_async_copy(src, dst, sems.at[len(copies)]))
+
+        for acc, at in zip(accs, mat_at):
+            add(acc, g_mat.at[pl.ds(at, acc.shape[0])] if len(acc.shape) == 3 else g_mat.at[at])
+        if up_acc is not None:
+            for k in range(D // up_rows):
+                for half in range(2):
+                    base = 2 * D * feed_at + (2 * k + half) * up_rows
+                    add(up_acc.at[pl.ds(k * up_rows, up_rows), pl.ds(half * D, D)], g_feed.at[pl.ds(base, up_rows)])
+            add(down_acc, g_feed.at[pl.ds(4 * FF + feed_at * FF, FF)])
+        for copy in copies:
+            copy.start()
+        for copy in copies:
+            copy.wait()
+
+
+def pack_shapes():
+    return [jax.ShapeDtypeStruct((NSQ, D, D), F32), jax.ShapeDtypeStruct((8 * FF, D), F32)]
+
+
+def flush_count(mats, up_rows):
+    return mats + (2 * D // up_rows + 1 if up_rows else 0)
 
 
 def time_kept(count, group, nb):
@@ -289,7 +335,8 @@
     return specs, [jax.ShapeDtypeStruct((nb,) + s, F32) for s in shapes]
 
 
-def time_fwd(first, x, extra, weights, count):
+def time_fwd(first, x, extra, model, layer, count):
+    squares = [12 * layer + k for k in range(4)]
     group = 64 if count > 32 else 32
     nv = x.shape[1]
     width = x.shape[2]
@@ -300,16 +347,16 @@
     out = pl.pallas_call(
         functools.partial(time_fwd_kernel, first, count, group),
         grid=(nv // VB,),
-        in_specs=specs + time_weight_specs(),
+        in_specs=specs + weight_specs(squares, 2 * layer, layer),
         out_specs=[pl.BlockSpec((count, VB, D), lambda i: (0, i, 0))] + kept_specs,
         out_shape=[jax.ShapeDtypeStruct((count, nv, D), F32)] + kept_shapes,
         compiler_params=params_spec(),
         name="time_fwd",
-    )(x, *extra, *weights)
+    )(x, *extra, *weight_args(model, squares, 2 * layer))
     return out[0], out[1:]
 
 
-def time_bwd_kernel(first, count, group, *refs):
+def time_bwd_kernel(first, count, group, layer, up_rows, *refs):
     if first:
         x_ref, emb_ref, place_ref = refs[:3]
         refs = refs[3:]
@@ -320,11 +367,14 @@
     q_s, k_s, v_s, o_s, p_s, l_s, z1_s, u_s, z2_s = refs[1:10]
     w = {name: refs[10 + i][...] for i, name in enumerate(TIME_W)}
     vec_ref = refs[16]
-    outs = refs[17:]
-    n_out = 9 if first else 8
-    g = dict(zip(TIME_W + ("rows",), outs[:7]))
-    tail = outs[7:n_out]
-    do_s, dq_s, dk_s, dv_s = outs[n_out:]
+    g_mat, g_feed = refs[19:21]
+    outs = refs[21:]
+    n_out = 3 if first else 2
+    tail = outs[1:n_out]
+    accs = outs[n_out : n_out + 6]
+    sems = outs[n_out + 6]
+    g = dict(zip(TIME_W + ("rows",), tuple(accs) + (outs[0],)))
+    do_s, dq_s, dk_s, dv_s = outs[n_out + 7 :]
     rows = count * VB
     step = pl.program_id(0)
 
@@ -392,35 +442,42 @@
         tail[1][...] += dx
     else:
         tail[0][...] = dx.reshape(count, VB, D)
-
-
-def time_bwd(first, x, extra, dy, kept, weights, count):
+    flush(
+        step, pl.num_programs(0) - 1, accs[:4], [12 * layer + k for k in range(4)], accs[4], accs[5], 2 * layer, up_rows,
+        g_mat, g_feed, sems,
+    )
+
+
+def time_bwd(first, x, extra, dy, kept, model, layer, count, packs, up_rows):
     group = 64 if count > 32 else 32
     nv = x.shape[1]
     width = x.shape[2]
     pad = group * VB
+    squares = [12 * layer + k for k in range(4)]
     block = pl.BlockSpec((count, VB, D), lambda i: (0, i, 0))
     specs = [pl.BlockSpec((count, VB, width), lambda i: (0, i, 0))]
     if first:
         specs += [whole((16, D)), whole((count, 1, D))]
-    grad_shapes = [(D, D)] * 4 + [(D, FF), (FF, D), (10, 8, D)]
-    if first:
-        grad_shapes += [(16, D), (count * VB, D)]
-    out_specs = [whole(s) for s in grad_shapes]
-    out_shape = [jax.ShapeDtypeStruct(s, F32) for s in grad_shapes]
+    specs += [block] + time_kept(count, group, nv // VB)[0] + weight_specs(squares, 2 * layer, layer)
+    grad_shapes = [(10, 8, D)] + ([(16, D), (count * VB, D)] if first else [])
+    out_specs = [ANY] * 2 + [whole(s) for s in grad_shapes]
+    out_shape = pack_shapes() + [jax.ShapeDtypeStruct(s, F32) for s in grad_shapes]
     if not first:
         out_specs.append(block)
         out_shape.append(jax.ShapeDtypeStruct((count, nv, D), F32))
     return pl.pallas_call(
-        functools.partial(time_bwd_kernel, first, count, group),
+        functools.partial(time_bwd_kernel, first, count, group, layer, up_rows),
         grid=(nv // VB,),
-        in_specs=specs + [block] + time_kept(count, group, nv // VB)[0] + time_weight_specs(),
+        in_specs=specs + [ANY] * 2,
         out_specs=out_specs,
         out_shape=out_shape,
-        scratch_shapes=[pltpu.VMEM((2, pad, HALF), F32)] * 4,
+        input_output_aliases={len(specs): 0, len(specs) + 1: 1},
+        scratch_shapes=[pltpu.VMEM((D, D), F32)] * 4
+        + [pltpu.VMEM((D, FF), F32), pltpu.VMEM((FF, D), F32), pltpu.SemaphoreType.DMA((flush_count(4, up_rows),))]
+        + [pltpu.VMEM((2, pad, HALF), F32)] * 4,
         compiler_params=params_spec(),
         name="time_bwd",
-    )(x, *extra, dy, *kept, *weights)
+    )(x, *extra, dy, *kept, *weight_args(model, squares, 2 * layer), *packs)
 
 SB_ROWS = 64
 
@@ -582,12 +639,15 @@
     return dsend, mmwt(dbuf2, w["so"])
 
 
-def recv_weight_specs():
-    return [whole((D, D))] * 5 + [whole((D, FF)), whole((FF, D)), whole((24, D))]
+def recv_squares(layer):
+    return [12 * layer + k for k in (7, 9, 10, 8, 11)]
 
 
 def seg_block(sb, rows=SB_ROWS, width=D):
     return pl.BlockSpec((sb, rows, width), lambda i: (i, 0, 0))
+
+
+MERGE = pl.BlockSpec((2, D, D), lambda i: (12, 0, 0))
 
 
 def pack_spec(sb):
@@ -602,30 +662,32 @@
         ref[...] = x
     mvec = mvec_ref[...]
     wide, _, _, _ = merge_rows(y, sb // 2, mvec)
-    out_ref[...] = (mmw(split2(wide), mw_ref[...]) + mvec[4:5]).reshape(sb // 2, SB_ROWS, D)
-
-
-def recv_fwd(send, o, weights, mvec, mw, sb):
+    out_ref[...] = (mmw(split2(wide), mw_ref[...].reshape(2 * D, D)) + mvec[4:5]).reshape(sb // 2, SB_ROWS, D)
+
+
+def recv_fwd(send, o, model, mvec, sb):
+    squares = recv_squares(0)
     n = send.shape[0]
     return pl.pallas_call(
         functools.partial(recv_fwd_kernel, sb),
         grid=(n // sb,),
-        in_specs=[seg_block(sb), pack_spec(sb)] + recv_weight_specs() + [whole((8, D)), whole((2 * D, D))],
+        in_specs=[seg_block(sb), pack_spec(sb)] + weight_specs(squares, 1, 0) + [whole((8, D)), MERGE],
         out_specs=[seg_block(sb // 2)] + kept_specs(sb),
         out_shape=[jax.ShapeDtypeStruct((n // 2, SB_ROWS, D), F32)]
         + [jax.ShapeDtypeStruct((n * SB_ROWS, k), F32) for k in KEPT_WIDTHS],
         compiler_params=params_spec(),
         name="recv_fwd",
-    )(send, o, *weights, mvec, mw)
-
-
-def recv_bwd_kernel(sb, send_ref, o_ref, dx_ref, *refs):
+    )(send, o, *weight_args(model, squares, 1), mvec, model[0])
+
+
+def recv_bwd_kernel(sb, up_rows, send_ref, o_ref, dx_ref, *refs):
     saved = [ref[...] for ref in refs[:6]]
     refs = refs[6:]
     w = {n: refs[i][...] for i, n in enumerate(RECV_W)}
-    vec_ref, mvec_ref, mw_ref, dsend_ref, do_ref = refs[7:12]
-    g = dict(zip(RECV_G, refs[12:20]))
-    dmw_ref, dmv_ref = refs[20:22]
+    vec_ref, mvec_ref, mw_ref = refs[7:10]
+    g_mat, g_feed, dsend_ref, do_ref, rows_ref, dmv_ref = refs[12:18]
+    accs, dmw_ref, sems = refs[18:25], refs[25], refs[26]
+    g = dict(zip(RECV_G, tuple(accs) + (rows_ref,)))
 
     @pl.when(pl.program_id(0) == 0)
     def _():
@@ -639,8 +701,8 @@
     dx = dx_ref[...].reshape(pairs * SB_ROWS, D)
     dmv_ref[4] += colsum(dx)
     dx2 = split2(dx)
-    dmw_ref[...] += tn3(split2(wide), dx2)
-    dn = mmwt(dx2, mw_ref[...])
+    dmw_ref[...] += tn3(split2(wide), dx2).reshape(2, D, D)
+    dn = mmwt(dx2, mw_ref[...].reshape(2 * D, D))
     part = colsum(dn * unit)
     dmv_ref[0] += part[:, :D]
     dmv_ref[1] += part[:, D:]
@@ -654,34 +716,45 @@
     dsend, do = recv_backward(dy, kept, w, vec, g)
     dsend_ref[...] = dsend.reshape(sb, SB_ROWS, D)
     pack_block(do_ref, do, sb)
-
-
-RECV_GRADS = [(D, D)] * 5 + [(D, FF), (FF, D), (11, 8, D)]
-
-
-def recv_bwd(send, o, dx, kept, weights, mvec, mw, sb):
+    recv_flush(accs, [(dmw_ref, 24)], 0, up_rows, g_mat, g_feed, sems)
+
+
+RECV_ACC = [pltpu.VMEM((D, D), F32)] * 5 + [pltpu.VMEM((D, FF), F32), pltpu.VMEM((FF, D), F32)]
+
+
+def recv_flush(accs, more, layer, up_rows, g_mat, g_feed, sems):
+    flush(
+        pl.program_id(0), pl.num_programs(0) - 1, list(accs[:5]) + [m for m, _ in more],
+        recv_squares(layer) + [at for _, at in more], accs[5], accs[6], 2 * layer + 1, up_rows, g_mat, g_feed, sems,
+    )
+
+
+def recv_bwd(send, o, dx, kept, model, mvec, sb, packs, up_rows):
     n = send.shape[0]
-    shapes = RECV_GRADS + [(2 * D, D), (5, 8, D)]
+    squares = recv_squares(0)
+    shapes = [(11, 8, D), (5, 8, D)]
+    specs = [seg_block(sb), pack_spec(sb), seg_block(sb // 2)] + kept_specs(sb)
+    specs += weight_specs(squares, 1, 0) + [whole((8, D)), MERGE]
     return pl.pallas_call(
-        functools.partial(recv_bwd_kernel, sb),
+        functools.partial(recv_bwd_kernel, sb, up_rows),
         grid=(n // sb,),
-        in_specs=[seg_block(sb), pack_spec(sb), seg_block(sb // 2)]
-        + kept_specs(sb)
-        + recv_weight_specs()
-        + [whole((8, D)), whole((2 * D, D))],
-        out_specs=[seg_block(sb), pack_spec(sb)] + [whole(s) for s in shapes],
-        out_shape=[jax.ShapeDtypeStruct((n, SB_ROWS, D), F32), jax.ShapeDtypeStruct(o.shape, F32)]
+        in_specs=specs + [ANY] * 2,
+        out_specs=[ANY] * 2 + [seg_block(sb), pack_spec(sb)] + [whole(s) for s in shapes],
+        out_shape=pack_shapes()
+        + [jax.ShapeDtypeStruct((n, SB_ROWS, D), F32), jax.ShapeDtypeStruct(o.shape, F32)]
         + [jax.ShapeDtypeStruct(s, F32) for s in shapes],
+        input_output_aliases={len(specs): 0, len(specs) + 1: 1},
+        scratch_shapes=RECV_ACC + [pltpu.VMEM((2, D, D), F32), pltpu.SemaphoreType.DMA((flush_count(6, up_rows),))],
         compiler_params=params_spec(),
         name="recv_bwd",
-    )(send, o, dx, *kept, *weights, mvec, mw)
-
-
-def tail_kernel(sb, send_ref, o_ref, tgt_ref, kept_ref, scale_ref, mean_ref, *refs):
+    )(send, o, dx, *kept, *weight_args(model, squares, 1), mvec, model[0], *packs)
+
+
+def tail_kernel(sb, up_rows, send_ref, o_ref, tgt_ref, kept_ref, scale_ref, mean_ref, *refs):
     w = {n: refs[i][...] for i, n in enumerate(RECV_W)}
-    vec_ref, head_ref, dsend_ref, do_ref = refs[7:11]
-    g = dict(zip(RECV_G, refs[11:19]))
-    dhead_ref = refs[19]
+    vec_ref, head_ref, g_mat, g_feed, dsend_ref, do_ref, rows_ref, dhead_ref = refs[7:15]
+    accs, sems = refs[15:22], refs[22]
+    g = dict(zip(RECV_G, tuple(accs) + (rows_ref,)))
 
     @pl.when(pl.program_id(0) == 0)
     def _():
@@ -705,24 +778,28 @@
     dsend, do = recv_backward(dy, kept, w, vec, g)
     dsend_ref[...] = dsend.reshape(sb, SB_ROWS, D)
     pack_block(do_ref, do, sb)
-
-
-def tail(send, o, tgt, kept, scale, mean, weights, head, sb):
+    recv_flush(accs, [], 1, up_rows, g_mat, g_feed, sems)
+
+
+def tail(send, o, tgt, kept, scale, mean, model, head, sb, up_rows):
     n = send.shape[0]
-    shapes = RECV_GRADS + [(PPAD, D)]
+    squares = recv_squares(1)
+    shapes = [(11, 8, D), (PPAD, D)]
     return pl.pallas_call(
-        functools.partial(tail_kernel, sb),
+        functools.partial(tail_kernel, sb, up_rows),
         grid=(n // sb,),
         in_specs=[seg_block(sb), pack_spec(sb), seg_block(sb, SB_ROWS, PPAD), seg_block(sb, SB_ROWS, PPAD)]
         + [whole((SB_ROWS, PPAD))] * 2
-        + recv_weight_specs()
+        + weight_specs(squares, 3, 1)
         + [whole((PPAD, D))],
-        out_specs=[seg_block(sb), pack_spec(sb)] + [whole(s) for s in shapes],
-        out_shape=[jax.ShapeDtypeStruct((n, SB_ROWS, D), F32), jax.ShapeDtypeStruct(o.shape, F32)]
+        out_specs=[ANY] * 2 + [seg_block(sb), pack_spec(sb)] + [whole(s) for s in shapes],
+        out_shape=pack_shapes()
+        + [jax.ShapeDtypeStruct((n, SB_ROWS, D), F32), jax.ShapeDtypeStruct(o.shape, F32)]
         + [jax.ShapeDtypeStruct(s, F32) for s in shapes],
+        scratch_shapes=RECV_ACC + [pltpu.SemaphoreType.DMA((flush_count(5, up_rows),))],
         compiler_params=params_spec(),
         name="tail",
-    )(send, o, tgt, kept, scale, mean, *weights, head)
+    )(send, o, tgt, kept, scale, mean, *weight_args(model, squares, 3), head)
 
 
 SEND_W = ("sq", "sk", "sv")
@@ -757,27 +834,30 @@
         o_ref[s] = pack_rows(mixed[s], lse)
 
 
-def send_weight_specs():
-    return [whole((D, D))] * 3 + [whole((24, D))]
-
-
-def send_fwd(dim, routers, here, weights, sb, npad):
+def send_squares(layer):
+    return [12 * layer + k for k in (4, 5, 6)]
+
+
+def send_fwd(dim, routers, here, model, layer, sb, npad):
+    squares = send_squares(layer)
     n = dim.shape[0]
     return pl.pallas_call(
         functools.partial(send_fwd_kernel, sb),
         grid=(n // sb,),
-        in_specs=[seg_block(sb), seg_block(sb, RPAD), whole((SB_ROWS, HALF))] + send_weight_specs(),
+        in_specs=[seg_block(sb), seg_block(sb, RPAD), whole((SB_ROWS, HALF))]
+        + weight_specs(squares, None, layer),
         out_specs=pack_spec(sb),
         out_shape=jax.ShapeDtypeStruct((npad, PACK, HALF), F32),
         compiler_params=params_spec(),
         name="send_fwd",
-    )(dim, routers, here, *weights)
-
-
-def send_bwd_kernel(sb, dim_ref, dpart_ref, r_ref, o_ref, do_ref, here_ref, *refs):
+    )(dim, routers, here, *weight_args(model, squares, None))
+
+
+def send_bwd_kernel(sb, layer, dim_ref, dpart_ref, r_ref, o_ref, do_ref, here_ref, *refs):
     w = {n: refs[i][...] for i, n in enumerate(SEND_W)}
-    vec_ref, ddim_ref, dr_ref = refs[3:6]
-    dsq_ref, dsk_ref, dsv_ref, rows = refs[6:10]
+    vec_ref = refs[3]
+    g_mat, ddim_ref, dr_ref, rows = refs[5:9]
+    dsq_ref, dsk_ref, dsv_ref, sems = refs[9:13]
 
     @pl.when(pl.program_id(0) == 0)
     def _():
@@ -814,26 +894,32 @@
     dq2 = split2(dq)
     dsq_ref[...] += tn3(r2, dq2)
     dr_ref[...] = mmwt(dq2, w["sq"]).reshape(sb, RPAD, D)
-
-
-def send_bwd(dim, dpart, routers, o, do, here, weights, sb):
+    flush(
+        pl.program_id(0), pl.num_programs(0) - 1, [dsq_ref, dsk_ref, dsv_ref], send_squares(layer), None, None, 0, 0,
+        g_mat, None, sems,
+    )
+
+
+def send_bwd(dim, dpart, routers, o, do, here, model, layer, sb, g_mat):
     n = dim.shape[0]
-    shapes = [(D, D)] * 3 + [(2, 8, D)]
+    squares = send_squares(layer)
+    specs = [seg_block(sb), seg_block(sb), seg_block(sb, RPAD), pack_spec(sb), pack_spec(sb), whole((SB_ROWS, HALF))]
+    specs += weight_specs(squares, None, layer)
     return pl.pallas_call(
-        functools.partial(send_bwd_kernel, sb),
+        functools.partial(send_bwd_kernel, sb, layer),
         grid=(n // sb,),
-        in_specs=[seg_block(sb), seg_block(sb), seg_block(sb, RPAD), pack_spec(sb), pack_spec(sb), whole((SB_ROWS, HALF))]
-        + send_weight_specs(),
-        out_specs=[seg_block(sb), seg_block(sb, RPAD)] + [whole(s) for s in shapes],
-        out_shape=[jax.ShapeDtypeStruct((n, SB_ROWS, D), F32), jax.ShapeDtypeStruct((n, RPAD, D), F32)]
-        + [jax.ShapeDtypeStruct(s, F32) for s in shapes],
+        in_specs=specs + [ANY],
+        out_specs=[ANY, seg_block(sb), seg_block(sb, RPAD), whole((2, 8, D))],
+        out_shape=pack_shapes()[:1]
+        + [jax.ShapeDtypeStruct((n, SB_ROWS, D), F32), jax.ShapeDtypeStruct((n, RPAD, D), F32)]
+        + [jax.ShapeDtypeStruct((2, 8, D), F32)],
+        input_output_aliases={len(specs): 0},
+        scratch_shapes=[pltpu.VMEM((D, D), F32)] * 3 + [pltpu.SemaphoreType.DMA((3,))],
         compiler_params=params_spec(),
         name="send_bwd",
-    )(dim, dpart, routers, o, do, here, *weights)
+    )(dim, dpart, routers, o, do, here, *weight_args(model, squares, None), g_mat)
 
 MESH = pl.DeviceIdType.MESH
-ANY = pl.BlockSpec(memory_space=pl.ANY)
-INVMEM = pl.BlockSpec(memory_space=pltpu.VMEM)
 
 
 def grid_sizes():
@@ -1187,14 +1273,146 @@
         name="group_stats" if stats else "group_sum",
     )(packed)
 
-
-def series_stats(series, observed):
-    seen = observed.astype(F32)
+LAYER_AT = SEGLEN + 1 + SEG
+MERGE_AT = LAYER_AT + 46
+HEAD_AT = MERGE_AT + 5
+ROUTER_AT = HEAD_AT + PRED
+VROWS = NVEC + 20
+
+
+def own_size(devices):
+    own = NVEC * D // devices
+    return own, -(-own // D)
+
+
+def prepare_kernel(nfeed, ser_ref, obs_ref, tgt_ref, mask_ref, count_ref, mat_ref, feed_ref, vec_ref, *outs):
+    pieces, tgt, kept, scale_ref, mean_ref, here_ref, tile_ref, mat_o, feed_o, vec_o = outs
+    for src, dst in ((mat_ref, mat_o), (feed_ref, feed_o), (vec_ref, vec_o)):
+        rows = dst.shape[0]
+        left, right = src[pl.ds(0, rows, stride=2), :], src[pl.ds(1, rows, stride=2), :]
+        dst[...] = jnp.concatenate([left, right], 1).astype(BF)
+    nv = ser_ref.shape[0]
+    series, seen = ser_ref[...], obs_ref[...].astype(F32)
     counted = jnp.maximum(jnp.sum(seen, -1, keepdims=True), 1.0)
     mean = jnp.sum(seen * series, -1, keepdims=True) / counted
     center = (series - mean) * seen
     scale = jnp.sqrt(jnp.sum(center * center, -1, keepdims=True) / counted + norm_eps)
-    return center / scale, mean, scale
+    slot = lax.axis_index("fsdp") * nv + lax.broadcasted_iota(jnp.int32, (nv, HALF), 0)
+    here = jnp.where(slot < count_ref[0], 1.0, 0.0)
+    here_ref[...] = here
+    scale_ref[...] = jnp.broadcast_to(scale, (nv, PPAD))
+    mean_ref[...] = jnp.broadcast_to(mean, (nv, PPAD))
+    mask = mask_ref[...].astype(F32) * here[:, :1]
+    tile_ref[...] = jnp.broadcast_to(jnp.sum(jnp.sum(mask, 0, keepdims=True), -1, keepdims=True), (8, HALF)) * (1.0 / (8 * HALF))
+    lane = lax.broadcasted_iota(jnp.int32, (nv, PPAD), 1)
+
+    def cut(x, dst):
+        x = jnp.concatenate([x, jnp.zeros((nv, PPAD - 12), F32)], 1)
+        for s in range(dst.shape[0]):
+            dst[s] = jnp.where(lane < 12, x[:, 12 * s : 12 * s + PPAD], 0.0)
+
+    cut(center / scale, pieces)
+    cut(tgt_ref[...], tgt)
+    cut(mask * (2.0 / (1 << 20)), kept)
+
+
+def prepare(series, observed, targets, target_mask, counts, matrices, feed, vectors):
+    nv = series.shape[0]
+    shapes = [((SEG, nv, PPAD), F32), ((SEG // 2, nv, PPAD), F32), ((SEG // 2, nv, PPAD), F32), ((nv, PPAD), F32), ((nv, PPAD), F32)]
+    shapes += [((nv, HALF), F32), ((8, HALF), F32)]
+    shapes += [((x.shape[0] // 2, D), BF) for x in (matrices, feed, vectors)]
+    return pl.pallas_call(
+        functools.partial(prepare_kernel, 0),
+        in_specs=[INVMEM] * 4 + [pl.BlockSpec(memory_space=pltpu.SMEM)] + [INVMEM] * 3,
+        out_specs=[INVMEM] * len(shapes),
+        out_shape=[jax.ShapeDtypeStruct(s, t) for s, t in shapes],
+        compiler_params=pltpu.CompilerParams(vmem_limit_bytes=32 << 20),
+        name="prepare",
+    )(series, observed, targets, target_mask, counts, matrices, feed, vectors)
+
+
+def unpack_kernel(devices, own, vec_ref, vecs, mvec, emb, place, head, r0, r1, flat):
+    flat[...] = jnp.zeros(flat.shape, F32)
+    rows = vec_ref.shape[1]
+    lane = lax.broadcasted_iota(jnp.int32, (rows, D), 1)
+    for d in range(devices):
+        at, shift = divmod(own * d, D)
+        block = vec_ref[d].astype(F32)
+        if shift:
+            block = pltpu.roll(block, shift, 1)
+            flat[at + 1 : at + 1 + rows] += jnp.where(lane < shift, block, 0.0)
+            block = jnp.where(lane >= shift, block, 0.0)
+        flat[at : at + rows] += block
+
+    def padded(at, count, total):
+        return jnp.concatenate([flat[at : at + count], jnp.zeros((total - count, D), F32)], 0)
+
+    for l in range(2):
+        vecs[l] = padded(LAYER_AT + 23 * l, 23, 24)
+    mvec[...] = padded(MERGE_AT, 5, 8)
+    emb[...] = padded(0, SEGLEN, 16).astype(BF)
+    head[...] = padded(HEAD_AT, PRED, PPAD).astype(BF)
+    for s in range(SEG):
+        place[s] = flat[SEGLEN + 1 + s : SEGLEN + 2 + s] + flat[SEGLEN : SEGLEN + 1]
+        r0[s] = padded(ROUTER_AT + ROUT * s, ROUT, RPAD)
+    for s in range(SEG // 2):
+        r1[s] = padded(ROUTER_AT + ROUT * (SEG + s), ROUT, RPAD)
+
+
+def unpack_vectors(gathered, own):
+    devices, rows, _ = gathered.shape
+    shapes = [((2, 24, D), F32), ((8, D), F32), ((16, D), BF), ((SEG, 1, D), F32), ((PPAD, D), BF)]
+    shapes += [((SEG, RPAD, D), F32), ((SEG // 2, RPAD, D), F32)]
+    return pl.pallas_call(
+        functools.partial(unpack_kernel, devices, own),
+        in_specs=[INVMEM],
+        out_specs=[INVMEM] * len(shapes),
+        out_shape=[jax.ShapeDtypeStruct(s, t) for s, t in shapes],
+        scratch_shapes=[pltpu.VMEM((VROWS + 24, D), F32)],
+        compiler_params=pltpu.CompilerParams(vmem_limit_bytes=32 << 20),
+        name="unpack_vectors",
+    )(gathered)
+
+
+def assemble_kernel(devices, own, demb, dplace, *refs):
+    (rt0, rs0, rr0, rt1, rs1, rr1, dmv, dhead, dr0, dr1), out, flat = refs[:10], refs[10], refs[11]
+    flat[...] = jnp.zeros(flat.shape, F32)
+    flat[0:SEGLEN] = demb[0:SEGLEN]
+    place = jnp.sum(dplace[...].reshape(SEG, VB, D), 1)
+    flat[SEGLEN : SEGLEN + 1] = jnp.sum(place, 0, keepdims=True)
+    flat[SEGLEN + 1 : SEGLEN + 1 + SEG] = place
+    at = LAYER_AT
+    for ref in (rt0, rs0, rr0, rt1, rs1, rr1, dmv):
+        count = ref.shape[0]
+        flat[at : at + count] = jnp.sum(ref[...], 1)
+        at += count
+    flat[HEAD_AT : HEAD_AT + PRED] = dhead[0:PRED]
+    for s in range(SEG):
+        flat[ROUTER_AT + ROUT * s : ROUTER_AT + ROUT * (s + 1)] = dr0[s][:ROUT]
+    for s in range(SEG // 2):
+        flat[ROUTER_AT + ROUT * (SEG + s) : ROUTER_AT + ROUT * (SEG + s + 1)] = dr1[s][:ROUT]
+    rows = out.shape[1]
+    lane = lax.broadcasted_iota(jnp.int32, (rows, D), 1)
+    inside = lax.broadcasted_iota(jnp.int32, (rows, D), 0) * D + lane < own
+    for d in range(devices):
+        at, shift = divmod(own * d, D)
+        block = flat[at : at + rows]
+        if shift:
+            block = jnp.where(lane < D - shift, pltpu.roll(block, D - shift, 1), pltpu.roll(flat[at + 1 : at + 1 + rows], D - shift, 1))
+        out[d] = jnp.where(inside, block, 0.0)
+
+
+def assemble_vectors(parts, devices):
+    own, rows = own_size(devices)
+    return pl.pallas_call(
+        functools.partial(assemble_kernel, devices, own),
+        in_specs=[INVMEM] * len(parts),
+        out_specs=INVMEM,
+        out_shape=jax.ShapeDtypeStruct((devices, rows, D), F32),
+        scratch_shapes=[pltpu.VMEM((VROWS + 24, D), F32)],
+        compiler_params=pltpu.CompilerParams(vmem_limit_bytes=32 << 20),
+        name="assemble_vectors",
+    )(*parts)
 
 
 def adam_update(weight, first_moment, second_moment, gradient):
@@ -1208,134 +1426,71 @@
     return (weight - learn_rate * (corrected + weight_decay * weight), first_new, second_new)
 
 
-def segment_major(x, width):
-    nv = x.shape[0]
-    x = x.reshape(nv, -1, 12).transpose(1, 0, 2)
-    return jnp.pad(x, ((0, 0), (0, 0), (0, width - 12)))
-
-
-def pad_rows(x, rows):
-    return jnp.pad(x, ((0, rows - x.shape[0]), (0, 0)))
-
-
-def gradient_parts(series, observed, targets, target_mask, present, square, up, down, vectors, combine, nf):
-    nv = series.shape[0]
-    normed, mean, scale = series_stats(series, observed)
-    pieces = segment_major(normed, 16)
-    factor = 2.0 / (1 << 20)
-    kept = segment_major(target_mask.astype(F32) * present[:, None] * factor, PPAD)
-    tgt = segment_major(targets, PPAD)
-    scale16 = jnp.broadcast_to(scale, (nv, PPAD))
-    mean16 = jnp.broadcast_to(mean, (nv, PPAD))
-    here = jnp.broadcast_to(present[:, None], (nv, HALF))
-
-    emb = pad_rows(vectors[:12], 16).astype(BF)
-    place = (vectors[12:13] + vectors[13:73])[:, None, :]
-    layer_start = SEGLEN + 1 + SEG
-    vecs = [pad_rows(vectors[layer_start + 23 * l : layer_start + 23 * l + 23], 24) for l in range(2)]
-    merge_at = layer_start + 46
-    mvec = pad_rows(vectors[merge_at : merge_at + 5], 8)
-    mw = square[24:26].reshape(2 * D, D)
-    head = pad_rows(vectors[merge_at + 5 : merge_at + 17], PPAD).astype(BF)
-    router_at = merge_at + 17
-    routers = []
-    for l, n in ((0, SEG), (1, SEG // 2)):
-        r = vectors[router_at + l * SEG * ROUT : router_at + l * SEG * ROUT + n * ROUT].reshape(n, ROUT, D)
-        routers.append(jnp.pad(r, ((0, 0), (0, RPAD - ROUT), (0, 0))))
-    time_w = [
-        (*[square[12 * l + i] for i in (0, 1, 2, 3)], up[2 * l], down[2 * l], vecs[l]) for l in range(2)
-    ]
-    send_w = [(*[square[12 * l + i] for i in (4, 5, 6)], vecs[l]) for l in range(2)]
-    recv_w = [
-        (*[square[12 * l + i] for i in (7, 9, 10, 8, 11)], up[2 * l + 1], down[2 * l + 1], vecs[l]) for l in range(2)
-    ]
-
+def gradient_parts(ready, model, extras, up_rows, combine, nf, devices):
+    pieces, tgt, kept, scale, mean, here = ready
+    mvec, emb, place, head, routers0, routers1 = extras
     sb0, sb1, sf0, sf1, st = 12, 10, 20, 10, 10
     rf, rb = 20, 20
-    dim0, kept0 = time_fwd(True, pieces, (emb, place), time_w[0], SEG)
-    o0 = send_fwd(dim0, routers[0], here, send_w[0], sf0, -(-SEG // nf) * nf)
+    half = SEG // 2
+    dim0, kept0 = time_fwd(True, pieces, (emb, place), model, 0, SEG)
+    o0 = send_fwd(dim0, routers0, here, model, 0, sf0, -(-SEG // nf) * nf)
     o0 = combine(o0, True, 2)
-    x1, *saved = recv_fwd(dim0, o0, recv_w[0], mvec, mw, rf)
-    dim1, kept1 = time_fwd(False, x1, (), time_w[1], SEG // 2)
-    o1 = send_fwd(dim1, routers[1], here, send_w[1], sf1, -(-SEG // 2 // nf) * nf)
+    x1, *saved = recv_fwd(dim0, o0, model, mvec, rf)
+    dim1, kept1 = time_fwd(False, x1, (), model, 1, half)
+    o1 = send_fwd(dim1, routers1, here, model, 1, sf1, -(-half // nf) * nf)
     o1 = combine(o1, True, 3)
-    out = tail(dim1, o1, tgt, kept, scale16, mean16, recv_w[1], head, st)
-    ddim1, do1, grecv1, dhead = out[0], out[1], out[2:10], out[10]
+    g_mat, g_feed, ddim1, do1, rr1, dhead = tail(dim1, o1, tgt, kept, scale, mean, model, head, st, up_rows)
     do1 = combine(do1, False, 4)
-    out = send_bwd(dim1, ddim1, routers[1], o1, do1, here, send_w[1], sb1)
-    ddim1, dr1, gsend1 = out[0], out[1], out[2:]
-    out = time_bwd(False, x1, (), ddim1, kept1, time_w[1], SEG // 2)
-    gtime1, dx1 = out[:7], out[7]
-    out = recv_bwd(dim0, o0, dx1, saved, recv_w[0], mvec, mw, rb)
-    ddim0, do0, grecv0, dmw, dmv = out[0], out[1], out[2:10], out[10], out[11]
+    g_mat, ddim1, dr1, rs1 = send_bwd(dim1, ddim1, routers1, o1, do1, here, model, 1, sb1, g_mat)
+    g_mat, g_feed, rt1, dx1 = time_bwd(False, x1, (), ddim1, kept1, model, 1, half, (g_mat, g_feed), up_rows)
+    g_mat, g_feed, ddim0, do0, rr0, dmv = recv_bwd(dim0, o0, dx1, saved, model, mvec, rb, (g_mat, g_feed), up_rows)
     do0 = combine(do0, False, 5)
-    out = send_bwd(dim0, ddim0, routers[0], o0, do0, here, send_w[0], sb0)
-    ddim0, dr0, gsend0 = out[0], out[1], out[2:]
-    out = time_bwd(True, pieces, (emb, place), ddim0, kept0, time_w[0], SEG)
-    gtime0, demb, dplace = out[:7], out[7], out[8]
-
-    mats, ups, downs, rows = [], [], [], []
-    for gt, gs, gr in ((gtime0, gsend0, grecv0), (gtime1, gsend1, grecv1)):
-        mats += [gt[0], gt[1], gt[2], gt[3], gs[0], gs[1], gs[2], gr[0], gr[3], gr[1], gr[2], gr[4]]
-        ups += [gt[4], gr[5]]
-        downs += [gt[5], gr[6]]
-        rt, rs, rr = gt[6].sum(1), gs[3].sum(1), gr[7].sum(1)
-        rows += [rt, rs, rr]
-    mats += [dmw]
-    dplace = dplace.reshape(SEG, VB, D).sum(1)
-    vec = jnp.concatenate(
-        [demb[:12], dplace.sum(0, keepdims=True), dplace]
-        + rows
-        + [dmv.sum(1), dhead[:12]]
-        + [dr[:, :ROUT].reshape(-1, D) for dr in (dr0, dr1)],
-        0,
+    g_mat, ddim0, dr0, rs0 = send_bwd(dim0, ddim0, routers0, o0, do0, here, model, 0, sb0, g_mat)
+    g_mat, g_feed, rt0, demb, dplace = time_bwd(
+        True, pieces, (emb, place), ddim0, kept0, model, 0, SEG, (g_mat, g_feed), up_rows
     )
-    return jnp.concatenate(mats, 0), jnp.concatenate(ups, 0), jnp.concatenate(downs, 0), vec
+    g_vec = assemble_vectors((demb, dplace, rt0, rs0, rr0, rt1, rs1, rr1, dmv, dhead, dr0, dr1), devices)
+    return g_mat, g_feed, g_vec
 
 
 def on_device(series, observed, targets, target_mask, counts, matrices, feed_weights, vectors, matrices_first, matrices_second, feed_first, feed_second, vectors_first, vectors_second):
-    local_vars = series.shape[1]
     nf = lax.axis_size("fsdp")
-    devices = nf * lax.axis_size("dp")
-    slot = lax.axis_index("fsdp") * local_vars + jnp.arange(local_vars, dtype=jnp.int32)
-    present = (slot < counts[0]).astype(F32)
-    own_rows = NVEC * D // devices
-    vec_rows = -(-own_rows // D)
-
-    def as_rows(x):
-        return x.reshape(-1, D)
-
-    def pad_flat(x):
-        return jnp.pad(x, [(0, 0)] * (x.ndim - 1) + [(0, vec_rows * D - own_rows)])
-
-    square, feed, vecs = gather_all(
-        [as_rows(matrices.astype(BF)), as_rows(feed_weights.astype(BF)), as_rows(pad_flat(vectors.astype(BF)))]
+    nd = lax.axis_size("dp")
+    devices = nf * nd
+    own, vec_rows = own_size(devices)
+    out = prepare(
+        series[0],
+        observed[0],
+        targets[0],
+        target_mask[0],
+        counts,
+        matrices.reshape(-1, HALF),
+        feed_weights.reshape(-1, HALF),
+        jnp.pad(vectors, (0, vec_rows * D - own)).reshape(-1, HALF),
     )
+    ready, tile, shards = out[:6], out[6], out[7:]
+    square, feed, vecs = gather_all(shards)
     square = square.reshape(NSQ, D, D)
     feed = feed.reshape(-1, D)
     up = feed[: 4 * FF].reshape(4, D, FF)
-    down = feed[4 * FF :].reshape(4, FF, D)
-    vecs = vecs.reshape(devices, -1)[:, :own_rows].reshape(NVEC, D).astype(F32)
-    g_mat, g_up, g_down, g_vec = gradient_parts(
-        series[0], observed[0], targets[0], target_mask[0], present, square, up, down, vecs, group_combine, nf
-    )
-    g_feed = jnp.concatenate([g_up.reshape(-1, D), g_down], 0)
-    g_vec = pad_flat(g_vec.reshape(devices, own_rows))
+    down = feed.reshape(8, FF, D)
+    vecs, *extras = unpack_vectors(vecs.reshape(devices, vec_rows, D), own)
+    up_rows = feed_weights.shape[0] // FF
+    g_mat, g_feed, g_vec = gradient_parts(ready, (square, up, down, vecs), extras, up_rows, group_combine, nf, devices)
     ny, nz, nx = grid_sizes()
     lead = (ny, 2, nz, nx)
-    kept = target_mask[0].astype(F32) * present[:, None]
-    tile = jnp.pad(jnp.sum(kept).reshape(1, 1), ((0, 7), (0, HALF - 1)))
-    s_mat, s_feed, s_vec, sums = scatter_sum(
-        [g_mat.reshape(lead + (-1, D)), g_feed.reshape(lead + (-1, D)), g_vec.reshape(lead + (-1, D))], tile
-    )
-    shards = (s_mat.reshape(-1), s_feed.reshape(-1), s_vec.reshape(-1)[:own_rows])
+    s_mat, s_feed, s_vec, sums = scatter_sum([g.reshape(lead + (-1, D)) for g in (g_mat, g_feed, g_vec)], tile)
+    is_up = lax.axis_index("dp") * 2 < nd
+    halves_of = s_feed.reshape(2, up_rows, D)
+    s_feed = jnp.where(is_up, jnp.concatenate([halves_of[0], halves_of[1]], 1).reshape(-1), s_feed.reshape(-1))
+    grads = (s_mat.reshape(-1), s_feed, s_vec.reshape(-1)[:own])
     upscale = (1 << 20) / jnp.maximum(jnp.sum(sums[8:]), 1.0)
     grad_norm = jnp.sqrt(jnp.sum(sums[:8])) * upscale
     factor = upscale * (clip_norm / jnp.maximum(grad_norm, clip_norm))
     new = (
-        adam_update(matrices, matrices_first, matrices_second, shards[0] * factor)
-        + adam_update(feed_weights, feed_first, feed_second, shards[1] * factor)
-        + adam_update(vectors, vectors_first, vectors_second, shards[2] * factor)
+        adam_update(matrices, matrices_first, matrices_second, grads[0] * factor)
+        + adam_update(feed_weights, feed_first, feed_second, grads[1] * factor)
+        + adam_update(vectors, vectors_first, vectors_second, grads[2] * factor)
     )
     return (grad_norm,) + new
 

time: 764 us -> 686 us (0.90)
  local copies, waits for them, and re-layouts: 93.7 us -> 31.4 us
  other arithmetic: 31.7 us -> 4.65 us
  Pallas kernels: 628 us -> 637 us
    reduce_sum x13 -> x0, other arithmetic: 15.1 us -> none  [the longest x6 5.76 us: gradient_parts(): rt, rs, rr = (gt[6].sum(1), gs[3].sum(1), gr[7].sum(1))]
    pad x12 -> x0, local copies, waits for them, and re-layouts: 12.8 us -> none  [the longest x2 4.27 us: gradient_parts(): routers.append(jnp.pad(r, ((0, 0), (0, RPAD - ROUT), (0, 0))))]
    concatenate x3 -> x0, local copies, waits for them, and re-layouts: 10.8 us -> none  [the longest x1 8.89 us: gradient_parts(): jnp.concatenate([demb[:12], dplace.sum(0, keepdims=True), dplace] + rows...]
    unnamed x140 -> x107, local copies, waits for them, and re-layouts: 37.3 us -> 27.7 us
    reshape x11 -> x2, local copies, waits for them, and re-layouts: 10.9 us -> 1.56 us  [the longest x1 0.78 us: on_device(): grads = (s_mat.reshape(-1), s_feed, s_vec.reshape(-1)[:own])]
    pallas_call x6 -> x9, Pallas kernels: 237 us -> 246 us  [the longest x2 108 us: time_bwd(): pl.pallas_call(functools.partial(time_bwd_kernel, first, count, group, la...]
where the time goes in v5:
time: 686 us; the launch traced here: 678 us
  Pallas kernels  637 us (93%)
  local copies, waits for them, and re-layouts  31.4 us (5%)
    pallas_call x4, Pallas kernels, group_combine(): pl.pallas_call(functools.partial(group_kernel, stats, per), in_specs=[INV...  122 us
    pallas_call x1, Pallas kernels, scatter_sum(): pl.pallas_call(functools.partial(scatter_kernel, n), in_specs=[ANY] * n +...  108 us
    pallas_call x2, Pallas kernels, time_bwd(): pl.pallas_call(functools.partial(time_bwd_kernel, first, count, group, la...  108 us
    pallas_call x2, Pallas kernels, time_fwd(): pl.pallas_call(functools.partial(time_fwd_kernel, first, count, group), g...  58.9 us
    pallas_call x1, Pallas kernels, gather_all(): pl.pallas_call(functools.partial(gather_kernel, n), in_specs=[ANY] * n, o...  57.3 us
    pallas_call x1, Pallas kernels, recv_bwd(): pl.pallas_call(functools.partial(recv_bwd_kernel, sb, up_rows), grid=(n /...  55 us
    pallas_call x2, Pallas kernels, send_bwd(): pl.pallas_call(functools.partial(send_bwd_kernel, sb, layer), grid=(n //...  41.8 us
    pallas_call x1, Pallas kernels, tail(): pl.pallas_call(functools.partial(tail_kernel, sb, up_rows), grid=(n // sb...  38.5 us

profile of v5, /device:TPU:0, one launch (start us, length us, event | category | flops | bytes accessed | tf_op | source)
XLA Modules:
  0.0 677.7 jit_solution(17734540832126366432)
XLA Ops:
  0.6 0.8 pad_bitcast_fusion.vec_ref
  2.1 0.9 copy-done.16
  3.0 0.9 copy-done.20
  3.9 0.9 copy-done.26
  4.8 0.9 copy-done.27
  5.8 0.9 copy-done.28
  6.7 0.9 copy-done.29
  7.5 1.3 prepare.1
  8.9 1.2 copy-done.3
  10.1 0.9 copy-done.14
  11.1 1.0 copy-done.15
  12.1 57.3 %gather_all.1 = (bf16[2,2,4,2,208,256]{5,4,3,2,1,0:T(8,128)(2,1)S(1)}, bf16[2,2,4,2,128,256]{5,4,3,2,1,0:T(8,128)(2,1)S(1)}, bf16[2,2,4,2,33,256]{5,4,3,2,1,0:T(8,128)(2,1)S(1)}) custom-call(bf16[208,256]{1,0:T(8,128)(2,1)S(1)} %get-tuple-element.91.refs_0_, bf16[128,256]{1,0:T(8,128)(2,1)S(1)} %get-tuple-element.92.refs_1_, ...), custom_call_target="tpu_custom_call" | custom-call | tf_op jit(solution)/shard_map/gather_all/pallas_call | solution.py:1046
  69.4 1.7 copy-done
  71.1 0.6 unpack_vectors.1
  71.7 0.7 copy-done.4
  72.4 1.0 copy-done.6
  73.4 0.8 copy-done.10
  74.2 0.6 copy-done.25
  74.8 0.6 copy-done.37
  75.4 0.6 copy-done.38
  76.0 0.6 copy-done.43
  76.6 0.1 slice.21
  76.7 1.2 reshape.72.refs_7_.refs_5_.refs_15_.refs_11_.refs_17_
  77.9 35.7 %time_fwd.2 = (f32[60,64,256]{2,1,0:T(8,128)}, f32[8,2,512,128]{3,2,1,0:T(8,128)}, f32[8,2,512,128]{3,2,1,0:T(8,128)}, f32[8,2,512,128]{3,2,1,0:T(8,128)}, f32[8...) custom-call(f32[60,64,16]{2,1,0:T(8,128)} %copy-done.3, ...), custom_call_target="tpu_custom_call" | custom-call | tf_op jit(solution)/shard_map/time_fwd/pallas_call | solution.py:347
  113.6 11.4 %send_fwd.2.in_ref = f32[64,24,128]{2,1,0:T(8,128)} custom-call(f32[60,64,256]{2,1,0:T(8,128)} %get-tuple-element.100.dim_ref.send_ref, f32[60,16,256]{2,1,0:T(8,128)} %copy-done.6, f32[64,128]{1,0:T(8,128)} %copy-done.19, bf16[26,256,256]{2,1,0:T(8,128)(2,1)} %bitcast.28, bf16[26,256,256]{2,1,0:T(8,128)(2,1)} %bitcast.29, bf16[26,256,256]{2,1,0:T(8,128)(2,1)} %bitcast.30, ...), custom_call_target="tpu_custom_call" | custom-call | tf_op jit(solution)/shard_map/send_fwd/pallas_call | solution.py:844
  125.0 1.1 copy-done.9
  126.2 35.5 %group_stats.2.o_ref = f32[64,24,128]{2,1,0:T(8,128)S(1)} custom-call(f32[64,24,128]{2,1,0:T(8,128)S(1)} %copy-done.9), custom_call_target="tpu_custom_call" | custom-call | tf_op jit(solution)/shard_map/group_stats/pallas_call | solution.py:1260
  161.7 0.9 copy-done.2
  162.5 26.5 %recv_fwd.1 = (f32[30,64,256]{2,1,0:T(8,128)}, f32[3840,256]{1,0:T(8,128)}, f32[3840,256]{1,0:T(8,128)}, f32[3840,128]{1,0:T(8,128)}, f32[3840,256]{1,0:T(8,128)...) custom-call(f32[60,64,256]{2,1,0:T(8,128)} %get-tuple-element.100.dim_ref.send_ref, f32[64,24,128]{2,1,0:T(8,128)} %copy-done.2, ...), custom_call_target="tpu_custom_call" | custom-call | tf_op jit(solution)/shard_map/recv_fwd/pallas_call | solution.py:671
  189.1 23.2 %time_fwd.3 = (f32[30,64,256]{2,1,0:T(8,128)}, f32[8,2,256,128]{3,2,1,0:T(8,128)}, f32[8,2,256,128]{3,2,1,0:T(8,128)}, f32[8,2,256,128]{3,2,1,0:T(8,128)}, f32[8...) custom-call(f32[30,64,256]{2,1,0:T(8,128)} %get-tuple-element.104.re, ...), custom_call_target="tpu_custom_call" | custom-call | tf_op jit(solution)/shard_map/time_fwd/pallas_call | solution.py:347
  212.3 7.3 %send_fwd.3.in_ref = f32[32,24,128]{2,1,0:T(8,128)} custom-call(f32[30,64,256]{2,1,0:T(8,128)} %get-tuple-element.105.dim_ref.send_ref, f32[30,16,256]{2,1,0:T(8,128)} %copy-done.10, f32[64,128]{1,0:T(8,128)} %copy-done.19, bf16[26,256,256]{2,1,0:T(8,128)(2,1)} %bitcast.41, bf16[26,256,256]{2,1,0:T(8,128)(2,1)} %bitcast.42, bf16[26,256,256]{2,1,0:T(8,128)(2,1)} %bitcast.43, ...), custom_call_target="tpu_custom_call" | custom-call | tf_op jit(solution)/shard_map/send_fwd/pallas_call | solution.py:844
  219.5 1.0 copy-done.11
  220.5 24.5 %group_stats.3.o_ref = f32[32,24,128]{2,1,0:T(8,128)S(1)} custom-call(f32[32,24,128]{2,1,0:T(8,128)S(1)} %copy-done.11), custom_call_target="tpu_custom_call" | custom-call | tf_op jit(solution)/shard_map/group_stats/pallas_call | solution.py:1260
  245.0 0.7 copy-done.7
  245.8 38.5 %tail.1 = (f32[26,256,256]{2,1,0:T(8,128)}, f32[4096,256]{1,0:T(8,128)}, f32[30,64,256]{2,1,0:T(8,128)}, f32[32,24,128]{2,1,0:T(8,128)}, f32[11,8,256]{2,1,0:T(8,128)}, /*index=5*/f32[16,256]{1,0:T(8,128)}) custom-call(f32[30,64,256]{2,1,0:T(8,128)} %get-tuple-element.105.dim_ref.send_ref, f32[32,24,128]{2,1,0:T(8,128)} %copy-done.7, ...), custom_call_target="tpu_custom_call" | custom-call | tf_op jit(solution)/shard_map/tail/pallas_call | solution.py:788
  284.2 1.0 copy-done.24
  285.2 24.8 %group_sum.2.do_ref = f32[32,24,128]{2,1,0:T(8,128)S(1)} custom-call(f32[32,24,128]{2,1,0:T(8,128)S(1)} %copy-done.24), custom_call_target="tpu_custom_call" | custom-call | tf_op jit(solution)/shard_map/group_sum/pallas_call | solution.py:1260
  310.0 0.8 copy-done.12
  310.8 15.7 %send_bwd.2 = (f32[26,256,256]{2,1,0:T(8,128)}, f32[30,64,256]{2,1,0:T(8,128)}, f32[30,16,256]{2,1,0:T(8,128)}, f32[2,8,256]{2,1,0:T(8,128)}) custom-call(f32[30,64,256]{2,1,0:T(8,128)} %get-tuple-element.105.dim_ref.send_ref, f32[30,64,256]{2,1,0:T(8,128)} %get-tuple-element.112.dpart_ref, ...), custom_call_target="tpu_custom_call", output_to_operand_aliasing={{0}: (10, {})} | custom-call | tf_op jit(solution)/shard_map/send_bwd/pallas_call | solution.py:908
  326.5 39.1 %time_bwd.2 = (f32[26,256,256]{2,1,0:T(8,128)}, f32[4096,256]{1,0:T(8,128)}, f32[10,8,256]{2,1,0:T(8,128)}, f32[30,64,256]{2,1,0:T(8,128)}) custom-call(f32[30,64,256]{2,1,0:T(8,128)} %get-tuple-element.104.refs_0_, f32[30,64,256]{2,1,0:T(8,128)} %get-tuple-element.115.refs_1_, ...), custom_call_target="tpu_custom_call", output_to_operand_aliasing={{0}: (18, {}), {1}: (19, {})} | custom-call | tf_op jit(solution)/shard_map/time_bwd/pallas_call | solution.py:468
  365.6 55.0 %recv_bwd.1 = (f32[26,256,256]{2,1,0:T(8,128)}, f32[4096,256]{1,0:T(8,128)}, f32[60,64,256]{2,1,0:T(8,128)}, f32[64,24,128]{2,1,0:T(8,128)}, f32[11,8,256]{2,1,0:T(8,128)}, /*index=5*/f32[5,8,256]{2,1,0:T(8,128)}) custom-call(f32[60,64,256]{2,1,0:T(8,128)} %get-tuple-element.100.dim_ref.send_ref, ...), custom_call_target="tpu_custom_call", output_to_operand_aliasing={{0}: (19, {}), {1}: (20, {})} | custom-call | tf_op jit(solution)/shard_map/recv_bwd/pallas_call | solution.py:738
  420.6 1.1 copy-done.18
  421.7 37.1 %group_sum.3.do_ref = f32[64,24,128]{2,1,0:T(8,128)S(1)} custom-call(f32[64,24,128]{2,1,0:T(8,128)S(1)} %copy-done.18), custom_call_target="tpu_custom_call" | custom-call | tf_op jit(solution)/shard_map/group_sum/pallas_call | solution.py:1260
  458.8 0.9 copy-done.8
  459.8 26.1 %send_bwd.3 = (f32[26,256,256]{2,1,0:T(8,128)}, f32[60,64,256]{2,1,0:T(8,128)}, f32[60,16,256]{2,1,0:T(8,128)}, f32[2,8,256]{2,1,0:T(8,128)}) custom-call(f32[60,64,256]{2,1,0:T(8,128)} %get-tuple-element.100.dim_ref.send_ref, f32[60,64,256]{2,1,0:T(8,128)} %get-tuple-element.136.dpart_ref, ...), custom_call_target="tpu_custom_call", output_to_operand_aliasing={{0}: (10, {})} | custom-call | tf_op jit(solution)/shard_map/send_bwd/pallas_call | solution.py:908
  485.9 0.0 copy-start.30
  485.9 0.0 copy-start.31
  486.0 0.0 copy-start.41
  486.0 68.7 %time_bwd.3 = (f32[26,256,256]{2,1,0:T(8,128)}, f32[4096,256]{1,0:T(8,128)}, f32[10,8,256]{2,1,0:T(8,128)}, f32[16,256]{1,0:T(8,128)}, f32[480,256]{1,0:T(8,128)}) custom-call(f32[60,64,16]{2,1,0:T(8,128)} %copy-done.3, bf16[16,256]{1,0:T(8,128)(2,1)} %copy-done.37, f32[60,1,256]{2,1,0:T(1,128)} %copy-done.25, ...), custom_call_target="tpu_custom_call", output_to_operand_aliasing={{0}: (20, {}), {1}: (21, {})} | custom-call | tf_op jit(solution)/shard_map/time_bwd/pallas_call | solution.py:468
  554.7 1.0 copy-done.23
  555.8 0.9 copy-done.33
  556.7 0.7 copy-done.42
  557.4 0.8 assemble_vectors.1
  558.2 1.1 copy-done.5
  559.4 108.0 %scatter_sum.1 = (f32[208,256]{1,0:T(8,128)}, f32[128,256]{1,0:T(8,128)}, f32[33,256]{1,0:T(8,128)}, f32[16,128]{1,0:T(8,128)}) custom-call(f32[2,2,4,2,208,256]{5,4,3,2,1,0:T(8,128)} %bitcast.84, f32[2,2,4,2,128,256]{5,4,3,2,1,0:T(8,128)} %bitcast.85, f32[2,2,4,2,33,256]{5,4,3,2,1,0:T(8,128)} %bitcast.76, f32[8,128]{1,0:T(8,128)} %copy-done.44), custom_call_target="tpu_custom_call" | custom-call | tf_op jit(solution)/shard_map/scatter_sum/pallas_call | solution.py:1183
  667.4 0.8 reshape.78
  668.1 1.3 slice_reduce_fusion
  670.9 0.7 multiply_subtract_fusion.2
  671.5 0.9 fusion.6
  672.5 1.0 copy.34
  673.5 0.8 multiply_subtract_fusion.1
  674.3 0.9 multiply_bitcast_fusion
  675.3 0.1 copy.32
  675.4 0.9 multiply_subtract_fusion
  (74 shorter events, 0.2 us)
Async XLA Ops:
  2.1 0.9 copy-start.16
  3.0 0.9 copy-start.20
  3.9 0.9 copy-start.26
  4.8 0.9 copy-start.27
  5.8 0.9 copy-start.28
  6.7 0.9 copy-start.29
  8.9 1.3 copy-start.3
  10.1 0.9 copy-start.14
  11.1 1.0 copy-start.15
  12.1 59.6 %copy-start.19 = (f32[64,128]{1,0:T(8,128)}, f32[64,128]{1,0:T(8,128)S(1)}, u32[]{:S(2)}) copy-start(f32[64,128]{1,0:T(8,128)S(1)} %get-tuple-element.102.here_ref) | copy-start | bytes 98308
  12.1 64.5 %copy-start.35 = (f32[64,16]{1,0:T(8,128)}, f32[64,16]{1,0:T(8,128)S(1)}, u32[]{:S(2)}) copy-start(f32[64,16]{1,0:T(8,128)S(1)} %get-tuple-element.109.scale_ref) | copy-start | bytes 12292
  12.1 64.5 %copy-start.36 = (f32[64,16]{1,0:T(8,128)}, f32[64,16]{1,0:T(8,128)S(1)}, u32[]{:S(2)}) copy-start(f32[64,16]{1,0:T(8,128)S(1)} %get-tuple-element.110.mean_ref) | copy-start | bytes 12292
  12.1 64.5 %copy-start.44 = (f32[8,128]{1,0:T(8,128)}, f32[8,128]{1,0:T(8,128)S(1)}, u32[]{:S(2)}) copy-start(f32[8,128]{1,0:T(8,128)S(1)} %get-tuple-element.165.refs_3_) | copy-start | bytes 12292
  69.4 1.7 copy-start
  71.1 6.8 %copy-start.1 = (bf16[2,2,4,2,128,256]{5,4,3,2,1,0:T(8,128)(2,1)}, bf16[2,2,4,2,128,256]{5,4,3,2,1,0:T(8,128)(2,1)S(1)}, u32[]{:S(2)}) copy-start(bf16[2,2,4,2,128,256]{5,4,3,2,1,0:T(8,128)(2,1)S(1)} %get-tuple-element.98) | copy-start | bytes 6291460
  71.7 0.7 copy-start.4
  72.4 1.0 copy-start.6
  73.4 0.8 copy-start.10
  74.2 0.6 copy-start.25
  74.8 0.6 copy-start.37
  75.4 0.6 copy-start.38
  76.0 0.6 copy-start.43
  125.0 1.1 copy-start.9
  161.7 0.9 copy-start.2
  219.5 1.0 copy-start.11
  245.0 0.7 copy-start.7
  284.2 1.0 copy-start.24
  310.0 0.8 copy-start.12
  420.6 1.1 copy-start.18
  458.8 0.9 copy-start.8
  485.9 68.8 %copy-start.13 = (f32[60,16,256]{2,1,0:T(8,128)S(1)}, f32[60,16,256]{2,1,0:T(8,128)}, u32[]{:S(2)}) copy-start(f32[60,16,256]{2,1,0:T(8,128)} %get-tuple-element.163.refs_8_) | copy-start | bytes 2949124
  485.9 68.8 %copy-start.22 = (f32[30,16,256]{2,1,0:T(8,128)S(1)}, f32[30,16,256]{2,1,0:T(8,128)}, u32[]{:S(2)}) copy-start(f32[30,16,256]{2,1,0:T(8,128)} %get-tuple-element.164.refs_9_) | copy-start | bytes 1474564
  485.9 68.8 %copy-start.30 = (f32[11,8,256]{2,1,0:T(8,128)S(1)}, f32[11,8,256]{2,1,0:T(8,128)}, u32[]{:S(2)}) copy-start(f32[11,8,256]{2,1,0:T(8,128)} %get-tuple-element.160.refs_5_) | copy-start | bytes 270340
  485.9 68.8 %copy-start.31 = (f32[11,8,256]{2,1,0:T(8,128)S(1)}, f32[11,8,256]{2,1,0:T(8,128)}, u32[]{:S(2)}) copy-start(f32[11,8,256]{2,1,0:T(8,128)} %get-tuple-element.157.refs_2_) | copy-start | bytes 270340
  485.9 68.8 %copy-start.32 = (f32[10,8,256]{2,1,0:T(8,128)S(1)}, f32[10,8,256]{2,1,0:T(8,128)}, u32[]{:S(2)}) copy-start(f32[10,8,256]{2,1,0:T(8,128)} %get-tuple-element.158.refs_3_) | copy-start | bytes 245764
  485.9 68.8 %copy-start.34 = (f32[5,8,256]{2,1,0:T(8,128)S(1)}, f32[5,8,256]{2,1,0:T(8,128)}, u32[]{:S(2)}) copy-start(f32[5,8,256]{2,1,0:T(8,128)} %get-tuple-element.161.refs_6_) | copy-start | bytes 122884
  485.9 68.8 %copy-start.39 = (f32[16,256]{1,0:T(8,128)S(1)}, f32[16,256]{1,0:T(8,128)}, u32[]{:S(2)}) copy-start(f32[16,256]{1,0:T(8,128)} %get-tuple-element.162.refs_7_) | copy-start | bytes 49156
  486.0 68.8 %copy-start.40 = (f32[2,8,256]{2,1,0:T(8,128)S(1)}, f32[2,8,256]{2,1,0:T(8,128)}, u32[]{:S(2)}) copy-start(f32[2,8,256]{2,1,0:T(8,128)} %get-tuple-element.159.refs_4_) | copy-start | bytes 49156
  486.0 68.8 %copy-start.41 = (f32[2,8,256]{2,1,0:T(8,128)S(1)}, f32[2,8,256]{2,1,0:T(8,128)}, u32[]{:S(2)}) copy-start(f32[2,8,256]{2,1,0:T(8,128)} %get-tuple-element.156.refs_1_) | copy-start | bytes 49156
  554.7 1.0 copy-start.23
  555.8 0.9 copy-start.33
  556.7 0.7 copy-start.42
  558.2 1.1 copy-start.5
  559.3 111.6 %copy-start.47 = (f32[8288]{0:T(1024)S(1)}, f32[8288]{0:T(1024)}, u32[]{:S(2)}) copy-start(f32[8288]{0:T(1024)} %param.21) | copy-start | bytes 99460
  559.3 111.6 %copy-start.50 = (f32[8288]{0:T(1024)S(1)}, f32[8288]{0:T(1024)}, u32[]{:S(2)}) copy-start(f32[8288]{0:T(1024)} %param.26) | copy-start | bytes 99460
  559.3 111.6 %copy-start.51 = (f32[8288]{0:T(1024)S(1)}, f32[8288]{0:T(1024)}, u32[]{:S(2)}) copy-start(f32[8288]{0:T(1024)} %param.27) | copy-start | bytes 99460
  559.3 114.2 %copy-start.21 = (f32[32768]{0:T(1024)S(1)}, f32[32768]{0:T(1024)}, u32[]{:S(2)}) copy-start(f32[32768]{0:T(1024)} %param.20) | copy-start | bytes 393220
  559.3 114.2 %copy-start.48 = (f32[32768]{0:T(1024)S(1)}, f32[32768]{0:T(1024)}, u32[]{:S(2)}) copy-start(f32[32768]{0:T(1024)} %param.24) | copy-start | bytes 393220
  559.3 114.2 %copy-start.49 = (f32[32768]{0:T(1024)S(1)}, f32[32768]{0:T(1024)}, u32[]{:S(2)}) copy-start(f32[32768]{0:T(1024)} %param.25) | copy-start | bytes 393220
  559.3 116.1 %copy-start.17 = (f32[53248]{0:T(1024)S(1)}, f32[53248]{0:T(1024)}, u32[]{:S(2)}) copy-start(f32[53248]{0:T(1024)} %param.19) | copy-start | bytes 638980
  559.3 116.1 %copy-start.45 = (f32[53248]{0:T(1024)S(1)}, f32[53248]{0:T(1024)}, u32[]{:S(2)}) copy-start(f32[53248]{0:T(1024)} %param.22) | copy-start | bytes 638980
  559.3 116.1 %copy-start.46 = (f32[53248]{0:T(1024)S(1)}, f32[53248]{0:T(1024)}, u32[]{:S(2)}) copy-start(f32[53248]{0:T(1024)} %param.23) | copy-start | bytes 638980

commit v6 on v5

--- a/solution.py
+++ b/solution.py
@@ -984,7 +984,7 @@
     y, c, z, x = me.y, me.core, me.z, me.x
     m = me.nx
     greet(me.neighbours())
-    copies, slot = [], [0]
+    slot = [0]
 
     def push(src, dst, device):
         copy = remote(src, dst, send.at[slot[0]], recv.at[slot[0]], device)
@@ -992,48 +992,66 @@
         copy.start()
         return copy
 
+    def finish(copies):
+        for copy in copies:
+            copy.wait()
+
     own = [pltpu.make_async_copy(shards[j], outs[j].at[y, c, z, x], local.at[j]) for j in range(n)]
     for copy in own:
         copy.start()
-    first = [
-        push(shards[j], outs[j].at[y, c, z, x], me.at(z=me.next_z(k))) for j in range(n) for k in range(1, me.nz)
-    ]
-    for copy in own:
-        copy.wait()
-    for copy in first:
-        copy.wait()
+
+    def along_z(j):
+        return [push(shards[j], outs[j].at[y, c, z, x], me.at(z=me.next_z(k))) for k in range(1, me.nz)]
+
+    first = along_z(0)
+    finish(own)
     base = slot[0]
 
     def rest(by_core):
         slot[0] = base
-        shared, started = [], []
         sibling = me.at(core=1 - by_core)
-        second = []
-        for j in range(n):
+        shared = []
+
+        def second(j):
             piece = outs[j].at[y, by_core, :, x]
+            out = []
             for k in range(1, m):
-                peer = me.at(x=me.next_x(k)) if by_core == 0 else me.at(y=me.next_y(k))
-                second.append(push(piece, piece, peer))
+                out.append(push(piece, piece, me.at(x=me.next_x(k)) if by_core == 0 else me.at(y=me.next_y(k))))
             shared.append(push(piece, piece, sibling))
-        for copy in second:
-            copy.wait()
-        third = []
-        for j in range(n):
+            return out
+
+        def third(j):
             wide = outs[j].at[y, by_core] if by_core == 0 else outs[j].at[:, by_core, :, x]
+            out = []
             for k in range(1, m):
-                peer = me.at(y=me.next_y(k)) if by_core == 0 else me.at(x=me.next_x(k))
-                third.append(push(wide, wide, peer))
+                out.append(push(wide, wide, me.at(y=me.next_y(k)) if by_core == 0 else me.at(x=me.next_x(k))))
             for k in range(1, m):
                 piece = outs[j].at[y, by_core, :, me.next_x(k)] if by_core == 0 else outs[j].at[me.next_y(k), by_core, :, x]
                 shared.append(push(piece, piece, sibling))
-        for copy in third:
-            copy.wait()
-        for j in range(n):
+            return out
+
+        def fourth(j):
             for k in range(1, m):
                 wide = outs[j].at[me.next_y(k), by_core] if by_core == 0 else outs[j].at[:, by_core, :, me.next_x(k)]
                 shared.append(push(wide, wide, sibling))
-        for copy in shared:
-            copy.wait()
+
+        one, two, three = {0: first}, {}, {}
+        for t in range(n + 2):
+            if t < n:
+                finish(one[t])
+                if t + 1 < n:
+                    one[t + 1] = along_z(t + 1)
+            if 0 < t <= n:
+                finish(two[t - 1])
+            if t < n:
+                two[t] = second(t)
+            if t > 1:
+                finish(three[t - 2])
+            if 0 < t <= n:
+                three[t - 1] = third(t - 1)
+            if t > 1:
+                fourth(t - 2)
+        finish(shared)
 
     for by_core in (0, 1):
         pl.when(c == by_core)(functools.partial(rest, by_core))
@@ -1054,22 +1072,28 @@
     )(*shards)
 
 
-def add_into(acc, at, terms, rows):
-    total = acc[at]
-    for ref, index in terms:
-        total = total + ref[index]
-    acc[at] = total
-
-
-def scatter_kernel(n, *refs):
+def row_chunks(rows):
+    count = max(1, rows // 40)
+    if rows % 8:
+        count = 1
+    cuts = [rows // 8 * k // count * 8 for k in range(count)] + [rows]
+    return [(a, b - a) for a, b in zip(cuts, cuts[1:])]
+
+
+def scatter_kernel(shapes, *refs):
+    n = len(shapes)
+    chunks = [(j, a, b) for j, s in enumerate(shapes) for a, b in row_chunks(s[0])]
+    total = len(chunks)
     grads, tile_ref = refs[:n], refs[n]
     outs, stat_ref = refs[n + 1 : 2 * n + 1], refs[2 * n + 1]
-    acc, r1, r2, r3, r4 = (refs[2 * n + 2 + i * n : 2 * n + 2 + (i + 1) * n] for i in range(5))
-    tc, tx, ty, tz, send, recv, local = refs[7 * n + 2 :]
+    bufs = refs[2 * n + 2 :]
+    acc, r1, r2, r3, r4 = (bufs[i * total : (i + 1) * total] for i in range(5))
+    tp, tz, send, recv, local = bufs[5 * total :]
     me = Place()
     y, c, z, x = me.y, me.core, me.z, me.x
     ny, nz, nx, m = me.ny, me.nz, me.nx, me.nx
-    greet(me.neighbours())
+    plane = plane_peers(me)
+    greet([p for p, _ in plane] + [me.at(z=me.next_z(k)) for k in range(1, nz)])
     slot = [0]
 
     def push(src, dst, device):
@@ -1078,88 +1102,116 @@
         copy.start()
         return copy
 
-    stage, own = [], []
-    for j in range(n):
-        stage.append([push(grads[j].at[:, me.other(), :, k], r1[j].at[:, k], me.at(core=me.other())) for k in range(nx)])
-        mine = [
-            pltpu.make_async_copy(grads[j].at[:, c, :, k], acc[j].at[:, k], local.at[j * nx + k]) for k in range(nx)
-        ]
-        for copy in mine:
-            copy.start()
-        own.append(mine)
-    base = slot[0]
+    def finish(copies):
+        for copy in copies:
+            copy.wait()
 
     def rest(by_core):
-        slot[0] = base
-        two, three, four = [], [], []
-        for j in range(n):
-            for copy in own[j] + stage[j]:
-                copy.wait()
-
-            def add1(i, carry):
-                at = (lax.div(i, nx * nz), lax.rem(lax.div(i, nz), nx), lax.rem(i, nz))
-                add_into(acc[j], at, [(r1[j], at)], None)
+        slot[0] = 0
+        sibling = me.at(core=1 - by_core)
+
+        def one(i):
+            j, a, b = chunks[i]
+            out = []
+            for k in range(nx):
+                out.append(push(grads[j].at[:, 1 - by_core, :, k, pl.ds(a, b)], r1[i].at[:, k], sibling))
+                copy = pltpu.make_async_copy(grads[j].at[:, by_core, :, k, pl.ds(a, b)], acc[i].at[:, k], local.at[i * nx + k])
+                copy.start()
+                out.append(copy)
+            return out
+
+        def add1(i):
+            def body(k, carry):
+                at = (lax.div(k, nx * nz), lax.rem(lax.div(k, nz), nx), lax.rem(k, nz))
+                acc[i][at] = acc[i][at] + r1[i][at]
                 return carry
 
-            lax.fori_loop(0, ny * nx * nz, add1, 0)
+            lax.fori_loop(0, ny * nx * nz, body, 0)
+
+        def two(i):
             if by_core == 0:
-                two.append([push(acc[j].at[:, me.next_x(k)], r2[j].at[k - 1], me.at(x=me.next_x(k))) for k in range(1, m)])
-            else:
-                two.append([push(acc[j].at[me.next_y(k)], r2[j].at[k - 1], me.at(y=me.next_y(k))) for k in range(1, m)])
-        for j in range(n):
-            for copy in two[j]:
-                copy.wait()
-
-            def add2(i, carry):
-                a, b = lax.div(i, nz), lax.rem(i, nz)
+                return [push(acc[i].at[:, me.next_x(k)], r2[i].at[k - 1], me.at(x=me.next_x(k))) for k in range(1, m)]
+            return [push(acc[i].at[me.next_y(k)], r2[i].at[k - 1], me.at(y=me.next_y(k))) for k in range(1, m)]
+
+        def add2(i):
+            def body(k, carry):
+                a, b = lax.div(k, nz), lax.rem(k, nz)
                 at = (a, x, b) if by_core == 0 else (y, a, b)
-                add_into(acc[j], at, [(r2[j], (k, a, b)) for k in range(m - 1)], None)
+                value = acc[i][at]
+                for q in range(m - 1):
+                    value = value + r2[i][q, a, b]
+                acc[i][at] = value
                 return carry
 
-            lax.fori_loop(0, m * nz, add2, 0)
+            lax.fori_loop(0, m * nz, body, 0)
+
+        def three(i):
             if by_core == 0:
-                three.append([push(acc[j].at[me.next_y(k), x], r3[j].at[k - 1], me.at(y=me.next_y(k))) for k in range(1, m)])
-            else:
-                three.append([push(acc[j].at[y, me.next_x(k)], r3[j].at[k - 1], me.at(x=me.next_x(k))) for k in range(1, m)])
-        for j in range(n):
-            for copy in three[j]:
-                copy.wait()
-
-            def add3(i, carry):
-                add_into(acc[j], (y, x, i), [(r3[j], (k, i)) for k in range(m - 1)], None)
+                return [push(acc[i].at[me.next_y(k), x], r3[i].at[k - 1], me.at(y=me.next_y(k))) for k in range(1, m)]
+            return [push(acc[i].at[y, me.next_x(k)], r3[i].at[k - 1], me.at(x=me.next_x(k))) for k in range(1, m)]
+
+        def add3(i):
+            def body(k, carry):
+                value = acc[i][y, x, k]
+                for q in range(m - 1):
+                    value = value + r3[i][q, k]
+                acc[i][y, x, k] = value
                 return carry
 
-            lax.fori_loop(0, nz, add3, 0)
-            four.append(
-                [push(acc[j].at[y, x, me.next_z(k)], r4[j].at[k - 1], me.at(z=me.next_z(k))) for k in range(1, nz)]
-            )
+            lax.fori_loop(0, nz, body, 0)
+
+        def four(i):
+            return [push(acc[i].at[y, x, me.next_z(k)], r4[i].at[k - 1], me.at(z=me.next_z(k))) for k in range(1, nz)]
+
+        def end(i):
+            j, a, b = chunks[i]
+            value = acc[i][y, x, z]
+            for k in range(nz - 1):
+                value = value + r4[i][k]
+            outs[j][a : a + b] = value
+            sq = colsum_any(value * value)
+            return sq[:, :HALF] + sq[:, HALF:]
+
         squares = jnp.zeros((8, HALF), F32)
-        for j in range(n):
-            for copy in four[j]:
-                copy.wait()
-            total = acc[j][y, x, z]
-            for k in range(nz - 1):
-                total = total + r4[j][k]
-            outs[j][...] = total
-            sq = colsum_any(total * total)
-            squares = squares + sq[:, :HALF] + sq[:, HALF:]
-        tc[c] = jnp.concatenate([squares, tile_ref[...]], 0)
+        ahead = 3
+        p1, p2, p3, p4 = {i: one(i) for i in range(min(ahead, total))}, {}, {}, {}
+        for t in range(total + 3):
+            if t < total:
+                finish(p1[t])
+                if t + ahead < total:
+                    p1[t + ahead] = one(t + ahead)
+                add1(t)
+                p2[t] = two(t)
+            if 0 <= t - 1 < total:
+                finish(p2[t - 1])
+                add2(t - 1)
+                p3[t - 1] = three(t - 1)
+            if 0 <= t - 2 < total:
+                finish(p3[t - 2])
+                add3(t - 2)
+                p4[t - 2] = four(t - 2)
+            if 0 <= t - 3 < total:
+                finish(p4[t - 3])
+                squares = squares + end(t - 3)
+        tp[(y * 2 + by_core) * nx + x] = jnp.concatenate([squares, tile_ref[...]], 0)
 
     for by_core in (0, 1):
         pl.when(c == by_core)(functools.partial(rest, by_core))
 
-    slot[0] = base + n * ((m - 1) * 2 + nz - 1)
-    push(tc.at[c], tc.at[c], me.at(core=me.other())).wait()
-    tx[x] = tc[0] + tc[1]
-    for copy in [push(tx.at[x], tx.at[x], me.at(x=me.next_x(k))) for k in range(1, nx)]:
-        copy.wait()
-    ty[y] = functools.reduce(jnp.add, [tx[k] for k in range(nx)])
-    for copy in [push(ty.at[y], ty.at[y], me.at(y=me.next_y(k))) for k in range(1, ny)]:
-        copy.wait()
-    tz[z] = functools.reduce(jnp.add, [ty[k] for k in range(ny)])
-    for copy in [push(tz.at[z], tz.at[z], me.at(z=me.next_z(k))) for k in range(1, nz)]:
-        copy.wait()
+    slot[0] = total * (nx + 2 * (m - 1) + nz - 1)
+    mine = tp.at[(y * 2 + c) * nx + x]
+    finish([push(mine, mine, p) for p, _ in plane])
+    tz[z] = functools.reduce(jnp.add, [tp[k] for k in range(2 * ny * nx)])
+    finish([push(tz.at[z], tz.at[z], me.at(z=me.next_z(k))) for k in range(1, nz)])
     stat_ref[...] = functools.reduce(jnp.add, [tz[k] for k in range(nz)])
+
+
+def plane_peers(me):
+    out = []
+    for k in range(1, 2 * me.ny * me.nx):
+        dc, dy, dx = k % 2, k // 2 % me.ny, k // (2 * me.ny)
+        out.append((me.at(core=lax.rem(me.core + dc, 2), y=lax.rem(me.y + dy, me.ny), x=lax.rem(me.x + dx, me.nx)), k))
+    return out
 
 
 def colsum_any(x):
@@ -1175,13 +1227,15 @@
     ny, nz, nx = grid_sizes()
     n = len(grads)
     shapes = [g.shape[-2:] for g in grads]
-    count = n * nx + n * ((nx - 1) * 2 + nz - 1) + 1 + (nx - 1) + (ny - 1) + (nz - 1)
+    pieces = [(b, s[1]) for s in shapes for _, b in row_chunks(s[0])]
+    total = len(pieces)
+    count = total * (nx + (nx - 1) * 2 + nz - 1) + 2 * ny * nx - 1 + nz - 1
 
     def buffers(*lead):
-        return [pltpu.VMEM(lead + s, F32) for s in shapes]
+        return [pltpu.VMEM(lead + s, F32) for s in pieces]
 
     return pl.pallas_call(
-        functools.partial(scatter_kernel, n),
+        functools.partial(scatter_kernel, shapes),
         in_specs=[ANY] * n + [INVMEM],
         out_specs=[INVMEM] * (n + 1),
         out_shape=[jax.ShapeDtypeStruct(s, F32) for s in shapes] + [jax.ShapeDtypeStruct((16, HALF), F32)],
@@ -1190,8 +1244,8 @@
         + buffers(nx - 1, nx, nz)
         + buffers(nx - 1, nz)
         + buffers(nz - 1)
-        + [pltpu.VMEM((k, 16, HALF), F32) for k in (2, nx, ny, nz)]
-        + [pltpu.SemaphoreType.DMA((count,)), pltpu.SemaphoreType.DMA((count,)), pltpu.SemaphoreType.DMA((n * nx,))],
+        + [pltpu.VMEM((2 * ny * nx, 16, HALF), F32), pltpu.VMEM((nz, 16, HALF), F32)]
+        + [pltpu.SemaphoreType.DMA((count,)), pltpu.SemaphoreType.DMA((count,)), pltpu.SemaphoreType.DMA((total * nx,))],
         compiler_params=pltpu.CompilerParams(collective_id=1, has_side_effects=True, vmem_limit_bytes=VMEM_LIMIT),
         name="scatter_sum",
     )(*grads, tile)
@@ -1259,8 +1313,8 @@
     per = packed.shape[0] // nf
     return pl.pallas_call(
         functools.partial(group_kernel, stats, per),
-        in_specs=[INVMEM],
-        out_specs=INVMEM,
+        in_specs=[ANY],
+        out_specs=ANY,
         out_shape=jax.ShapeDtypeStruct(packed.shape, F32),
         scratch_shapes=[
             pltpu.VMEM((nf, per, PACK, HALF), F32),
@@ -1323,8 +1377,11 @@
     shapes += [((x.shape[0] // 2, D), BF) for x in (matrices, feed, vectors)]
     return pl.pallas_call(
         functools.partial(prepare_kernel, 0),
-        in_specs=[INVMEM] * 4 + [pl.BlockSpec(memory_space=pltpu.SMEM)] + [INVMEM] * 3,
-        out_specs=[INVMEM] * len(shapes),
+        grid=(1,),
+        in_specs=[whole(x.shape) for x in (series, observed, targets, target_mask)]
+        + [pl.BlockSpec(memory_space=pltpu.SMEM)]
+        + [whole(x.shape) for x in (matrices, feed, vectors)],
+        out_specs=[whole(s) for s, _ in shapes],
         out_shape=[jax.ShapeDtypeStruct(s, t) for s, t in shapes],
         compiler_params=pltpu.CompilerParams(vmem_limit_bytes=32 << 20),
         name="prepare",
@@ -1365,8 +1422,9 @@
     shapes += [((SEG, RPAD, D), F32), ((SEG // 2, RPAD, D), F32)]
     return pl.pallas_call(
         functools.partial(unpack_kernel, devices, own),
-        in_specs=[INVMEM],
-        out_specs=[INVMEM] * len(shapes),
+        grid=(1,),
+        in_specs=[whole(gathered.shape)],
+        out_specs=[whole(s) for s, _ in shapes],
         out_shape=[jax.ShapeDtypeStruct(s, t) for s, t in shapes],
         scratch_shapes=[pltpu.VMEM((VROWS + 24, D), F32)],
         compiler_params=pltpu.CompilerParams(vmem_limit_bytes=32 << 20),
@@ -1406,8 +1464,9 @@
     own, rows = own_size(devices)
     return pl.pallas_call(
         functools.partial(assemble_kernel, devices, own),
-        in_specs=[INVMEM] * len(parts),
-        out_specs=INVMEM,
+        grid=(1,),
+        in_specs=[whole(p.shape) for p in parts],
+        out_specs=whole((devices, rows, D)),
         out_shape=jax.ShapeDtypeStruct((devices, rows, D), F32),
         scratch_shapes=[pltpu.VMEM((VROWS + 24, D), F32)],
         compiler_params=pltpu.CompilerParams(vmem_limit_bytes=32 << 20),

time: 686 us -> 660 us (0.962)
  Pallas kernels: 637 us -> 618 us
    pallas_call x8, Pallas kernels: 233 us -> 209 us  [the longest x4 125 us: group_combine(): pl.pallas_call(functools.partial(group_kernel, stats, per), in_specs=[ANY...]
    pallas_call x1, Pallas kernels: 38.5 us -> 50.9 us  [tail(): pl.pallas_call(functools.partial(tail_kernel, sb, up_rows), grid=(n // sb...]
    pallas_call x1, Pallas kernels: 57.3 us -> 48.8 us  [gather_all(): pl.pallas_call(functools.partial(gather_kernel, n), in_specs=[ANY] * n, o...]
where the time goes in v6:
time: 660 us; the launch traced here: 658 us
  Pallas kernels  618 us (94%)
  local copies, waits for them, and re-layouts  31.4 us (5%)
    pallas_call x4, Pallas kernels, group_combine(): pl.pallas_call(functools.partial(group_kernel, stats, per), in_specs=[ANY...  125 us
    pallas_call x2, Pallas kernels, time_bwd(): pl.pallas_call(functools.partial(time_bwd_kernel, first, count, group, la...  108 us
    pallas_call x1, Pallas kernels, scatter_sum(): pl.pallas_call(functools.partial(scatter_kernel, shapes), in_specs=[ANY]...  81.6 us
    pallas_call x2, Pallas kernels, time_fwd(): pl.pallas_call(functools.partial(time_fwd_kernel, first, count, group), g...  58.9 us
    pallas_call x1, Pallas kernels, recv_bwd(): pl.pallas_call(functools.partial(recv_bwd_kernel, sb, up_rows), grid=(n /...  55 us
    pallas_call x1, Pallas kernels, tail(): pl.pallas_call(functools.partial(tail_kernel, sb, up_rows), grid=(n // sb...  50.9 us
    pallas_call x1, Pallas kernels, gather_all(): pl.pallas_call(functools.partial(gather_kernel, n), in_specs=[ANY] * n, o...  48.8 us
    pallas_call x2, Pallas kernels, send_bwd(): pl.pallas_call(functools.partial(send_bwd_kernel, sb, layer), grid=(n //...  41.8 us

profile of v6, /device:TPU:0, one launch (start us, length us, event | category | flops | bytes accessed | tf_op | source)
XLA Modules:
  0.0 658.3 jit_solution(12810681654587536958)
XLA Ops:
  0.6 0.8 pad_bitcast_fusion.vec_ref
  2.1 0.0 copy-start.16
  2.1 0.9 copy-done.16
  3.0 0.9 copy-done.20
  3.9 0.9 copy-done.26
  4.8 0.9 copy-done.27
  5.8 0.9 copy-done.28
  6.7 0.9 copy-done.29
  7.5 1.3 prepare.1
  8.9 1.2 copy-done.3
  10.1 0.9 copy-done.14
  11.1 1.0 copy-done.15
  12.1 48.8 %gather_all.1 = (bf16[2,2,4,2,208,256]{5,4,3,2,1,0:T(8,128)(2,1)S(1)}, bf16[2,2,4,2,128,256]{5,4,3,2,1,0:T(8,128)(2,1)S(1)}, bf16[2,2,4,2,33,256]{5,4,3,2,1,0:T(8,128)(2,1)S(1)}) custom-call(bf16[208,256]{1,0:T(8,128)(2,1)S(1)} %get-tuple-element.91.refs_0_, bf16[128,256]{1,0:T(8,128)(2,1)S(1)} %get-tuple-element.92.refs_1_, ...), custom_call_target="tpu_custom_call" | custom-call | tf_op jit(solution)/shard_map/gather_all/pallas_call | solution.py:1064
  60.9 1.7 copy-done
  62.7 0.6 unpack_vectors.1
  63.3 0.0 copy-start.4
  63.3 0.7 copy-done.4
  64.0 1.0 copy-done.6
  64.9 0.8 copy-done.10
  65.7 0.6 copy-done.25
  66.4 0.6 copy-done.37
  67.0 0.6 copy-done.38
  67.6 0.6 copy-done.43
  68.2 0.1 slice.21
  68.3 1.2 reshape.72.refs_7_.refs_5_.refs_15_.refs_11_.refs_17_
  69.4 35.7 %time_fwd.2 = (f32[60,64,256]{2,1,0:T(8,128)}, f32[8,2,512,128]{3,2,1,0:T(8,128)}, f32[8,2,512,128]{3,2,1,0:T(8,128)}, f32[8,2,512,128]{3,2,1,0:T(8,128)}, f32[8...) custom-call(f32[60,64,16]{2,1,0:T(8,128)} %copy-done.3, ...), custom_call_target="tpu_custom_call" | custom-call | tf_op jit(solution)/shard_map/time_fwd/pallas_call | solution.py:347
  105.2 11.4 %send_fwd.2.in_ref = f32[64,24,128]{2,1,0:T(8,128)} custom-call(f32[60,64,256]{2,1,0:T(8,128)} %get-tuple-element.100.dim_ref.send_ref, f32[60,16,256]{2,1,0:T(8,128)} %copy-done.6, f32[64,128]{1,0:T(8,128)} %copy-done.19, bf16[26,256,256]{2,1,0:T(8,128)(2,1)} %bitcast.28, bf16[26,256,256]{2,1,0:T(8,128)(2,1)} %bitcast.29, bf16[26,256,256]{2,1,0:T(8,128)(2,1)} %bitcast.30, ...), custom_call_target="tpu_custom_call" | custom-call | tf_op jit(solution)/shard_map/send_fwd/pallas_call | solution.py:844
  116.6 1.1 copy-done.9
  117.7 37.3 %group_stats.2.o_ref = f32[64,24,128]{2,1,0:T(8,128)S(1)} custom-call(f32[64,24,128]{2,1,0:T(8,128)S(1)} %copy-done.9), custom_call_target="tpu_custom_call" | custom-call | tf_op jit(solution)/shard_map/group_stats/pallas_call | solution.py:1314
  155.1 0.9 copy-done.2
  155.9 26.3 %recv_fwd.1 = (f32[30,64,256]{2,1,0:T(8,128)}, f32[3840,256]{1,0:T(8,128)}, f32[3840,256]{1,0:T(8,128)}, f32[3840,128]{1,0:T(8,128)}, f32[3840,256]{1,0:T(8,128)...) custom-call(f32[60,64,256]{2,1,0:T(8,128)} %get-tuple-element.100.dim_ref.send_ref, f32[64,24,128]{2,1,0:T(8,128)} %copy-done.2, ...), custom_call_target="tpu_custom_call" | custom-call | tf_op jit(solution)/shard_map/recv_fwd/pallas_call | solution.py:671
  182.2 23.2 %time_fwd.3 = (f32[30,64,256]{2,1,0:T(8,128)}, f32[8,2,256,128]{3,2,1,0:T(8,128)}, f32[8,2,256,128]{3,2,1,0:T(8,128)}, f32[8,2,256,128]{3,2,1,0:T(8,128)}, f32[8...) custom-call(f32[30,64,256]{2,1,0:T(8,128)} %get-tuple-element.104.re, ...), custom_call_target="tpu_custom_call" | custom-call | tf_op jit(solution)/shard_map/time_fwd/pallas_call | solution.py:347
  205.4 7.3 %send_fwd.3.in_ref = f32[32,24,128]{2,1,0:T(8,128)} custom-call(f32[30,64,256]{2,1,0:T(8,128)} %get-tuple-element.105.dim_ref.send_ref, f32[30,16,256]{2,1,0:T(8,128)} %copy-done.10, f32[64,128]{1,0:T(8,128)} %copy-done.19, bf16[26,256,256]{2,1,0:T(8,128)(2,1)} %bitcast.41, bf16[26,256,256]{2,1,0:T(8,128)(2,1)} %bitcast.42, bf16[26,256,256]{2,1,0:T(8,128)(2,1)} %bitcast.43, ...), custom_call_target="tpu_custom_call" | custom-call | tf_op jit(solution)/shard_map/send_fwd/pallas_call | solution.py:844
  212.7 1.0 copy-done.11
  213.7 26.2 %group_stats.3.o_ref = f32[32,24,128]{2,1,0:T(8,128)S(1)} custom-call(f32[32,24,128]{2,1,0:T(8,128)S(1)} %copy-done.11), custom_call_target="tpu_custom_call" | custom-call | tf_op jit(solution)/shard_map/group_stats/pallas_call | solution.py:1314
  239.9 0.7 copy-done.7
  240.6 50.9 %tail.1 = (f32[26,256,256]{2,1,0:T(8,128)}, f32[4096,256]{1,0:T(8,128)}, f32[30,64,256]{2,1,0:T(8,128)}, f32[32,24,128]{2,1,0:T(8,128)}, f32[11,8,256]{2,1,0:T(8,128)}, /*index=5*/f32[16,256]{1,0:T(8,128)}) custom-call(f32[30,64,256]{2,1,0:T(8,128)} %get-tuple-element.105.dim_ref.send_ref, f32[32,24,128]{2,1,0:T(8,128)} %copy-done.7, ...), custom_call_target="tpu_custom_call" | custom-call | tf_op jit(solution)/shard_map/tail/pallas_call | solution.py:788
  291.5 1.0 copy-done.24
  292.5 24.5 %group_sum.2.do_ref = f32[32,24,128]{2,1,0:T(8,128)S(1)} custom-call(f32[32,24,128]{2,1,0:T(8,128)S(1)} %copy-done.24), custom_call_target="tpu_custom_call" | custom-call | tf_op jit(solution)/shard_map/group_sum/pallas_call | solution.py:1314
  317.1 0.8 copy-done.12
  317.8 15.7 %send_bwd.2 = (f32[26,256,256]{2,1,0:T(8,128)}, f32[30,64,256]{2,1,0:T(8,128)}, f32[30,16,256]{2,1,0:T(8,128)}, f32[2,8,256]{2,1,0:T(8,128)}) custom-call(f32[30,64,256]{2,1,0:T(8,128)} %get-tuple-element.105.dim_ref.send_ref, f32[30,64,256]{2,1,0:T(8,128)} %get-tuple-element.112.dpart_ref, ...), custom_call_target="tpu_custom_call", output_to_operand_aliasing={{0}: (10, {})} | custom-call | tf_op jit(solution)/shard_map/send_bwd/pallas_call | solution.py:908
  333.5 39.1 %time_bwd.2 = (f32[26,256,256]{2,1,0:T(8,128)}, f32[4096,256]{1,0:T(8,128)}, f32[10,8,256]{2,1,0:T(8,128)}, f32[30,64,256]{2,1,0:T(8,128)}) custom-call(f32[30,64,256]{2,1,0:T(8,128)} %get-tuple-element.104.refs_0_, f32[30,64,256]{2,1,0:T(8,128)} %get-tuple-element.115.refs_1_, ...), custom_call_target="tpu_custom_call", output_to_operand_aliasing={{0}: (18, {}), {1}: (19, {})} | custom-call | tf_op jit(solution)/shard_map/time_bwd/pallas_call | solution.py:468
  372.6 55.0 %recv_bwd.1 = (f32[26,256,256]{2,1,0:T(8,128)}, f32[4096,256]{1,0:T(8,128)}, f32[60,64,256]{2,1,0:T(8,128)}, f32[64,24,128]{2,1,0:T(8,128)}, f32[11,8,256]{2,1,0:T(8,128)}, /*index=5*/f32[5,8,256]{2,1,0:T(8,128)}) custom-call(f32[60,64,256]{2,1,0:T(8,128)} %get-tuple-element.100.dim_ref.send_ref, ...), custom_call_target="tpu_custom_call", output_to_operand_aliasing={{0}: (19, {}), {1}: (20, {})} | custom-call | tf_op jit(solution)/shard_map/recv_bwd/pallas_call | solution.py:738
  427.6 1.1 copy-done.18
  428.8 37.1 %group_sum.3.do_ref = f32[64,24,128]{2,1,0:T(8,128)S(1)} custom-call(f32[64,24,128]{2,1,0:T(8,128)S(1)} %copy-done.18), custom_call_target="tpu_custom_call" | custom-call | tf_op jit(solution)/shard_map/group_sum/pallas_call | solution.py:1314
  465.9 0.9 copy-done.8
  466.8 26.1 %send_bwd.3 = (f32[26,256,256]{2,1,0:T(8,128)}, f32[60,64,256]{2,1,0:T(8,128)}, f32[60,16,256]{2,1,0:T(8,128)}, f32[2,8,256]{2,1,0:T(8,128)}) custom-call(f32[60,64,256]{2,1,0:T(8,128)} %get-tuple-element.100.dim_ref.send_ref, f32[60,64,256]{2,1,0:T(8,128)} %get-tuple-element.136.dpart_ref, ...), custom_call_target="tpu_custom_call", output_to_operand_aliasing={{0}: (10, {})} | custom-call | tf_op jit(solution)/shard_map/send_bwd/pallas_call | solution.py:908
  493.0 0.0 copy-start.31
  493.0 68.7 %time_bwd.3 = (f32[26,256,256]{2,1,0:T(8,128)}, f32[4096,256]{1,0:T(8,128)}, f32[10,8,256]{2,1,0:T(8,128)}, f32[16,256]{1,0:T(8,128)}, f32[480,256]{1,0:T(8,128)}) custom-call(f32[60,64,16]{2,1,0:T(8,128)} %copy-done.3, bf16[16,256]{1,0:T(8,128)(2,1)} %copy-done.37, f32[60,1,256]{2,1,0:T(1,128)} %copy-done.25, ...), custom_call_target="tpu_custom_call", output_to_operand_aliasing={{0}: (20, {}), {1}: (21, {})} | custom-call | tf_op jit(solution)/shard_map/time_bwd/pallas_call | solution.py:468
  561.8 1.0 copy-done.23
  562.8 0.9 copy-done.33
  563.7 0.7 copy-done.42
  564.4 0.8 assemble_vectors.1
  565.3 1.1 copy-done.5
  566.4 81.6 %scatter_sum.1 = (f32[208,256]{1,0:T(8,128)}, f32[128,256]{1,0:T(8,128)}, f32[33,256]{1,0:T(8,128)}, f32[16,128]{1,0:T(8,128)}) custom-call(f32[2,2,4,2,208,256]{5,4,3,2,1,0:T(8,128)} %bitcast.84, f32[2,2,4,2,128,256]{5,4,3,2,1,0:T(8,128)} %bitcast.85, f32[2,2,4,2,33,256]{5,4,3,2,1,0:T(8,128)} %bitcast.76, f32[8,128]{1,0:T(8,128)} %copy-done.44), custom_call_target="tpu_custom_call" | custom-call | tf_op jit(solution)/shard_map/scatter_sum/pallas_call | solution.py:1237
  648.0 0.8 reshape.78
  648.8 1.3 slice_reduce_fusion
  651.5 0.7 multiply_subtract_fusion.2
  652.2 0.9 fusion.6
  653.1 1.0 copy.34
  654.1 0.8 multiply_subtract_fusion.1
  654.9 0.9 multiply_bitcast_fusion
  655.9 0.1 copy.32
  656.0 0.9 multiply_subtract_fusion
  (74 shorter events, 0.2 us)
Async XLA Ops:
  2.1 0.9 copy-start.16
  3.0 0.9 copy-start.20
  3.9 0.9 copy-start.26
  4.8 0.9 copy-start.27
  5.8 0.9 copy-start.28
  6.7 0.9 copy-start.29
  8.9 1.3 copy-start.3
  10.1 0.9 copy-start.14
  11.1 1.0 copy-start.15
  12.1 51.2 %copy-start.19 = (f32[64,128]{1,0:T(8,128)}, f32[64,128]{1,0:T(8,128)S(1)}, u32[]{:S(2)}) copy-start(f32[64,128]{1,0:T(8,128)S(1)} %get-tuple-element.102.here_ref) | copy-start | bytes 98308
  12.1 56.1 %copy-start.35 = (f32[64,16]{1,0:T(8,128)}, f32[64,16]{1,0:T(8,128)S(1)}, u32[]{:S(2)}) copy-start(f32[64,16]{1,0:T(8,128)S(1)} %get-tuple-element.109.scale_ref) | copy-start | bytes 12292
  12.1 56.1 %copy-start.36 = (f32[64,16]{1,0:T(8,128)}, f32[64,16]{1,0:T(8,128)S(1)}, u32[]{:S(2)}) copy-start(f32[64,16]{1,0:T(8,128)S(1)} %get-tuple-element.110.mean_ref) | copy-start | bytes 12292
  12.1 56.1 %copy-start.44 = (f32[8,128]{1,0:T(8,128)}, f32[8,128]{1,0:T(8,128)S(1)}, u32[]{:S(2)}) copy-start(f32[8,128]{1,0:T(8,128)S(1)} %get-tuple-element.165.refs_3_) | copy-start | bytes 12292
  60.9 1.7 copy-start
  62.7 6.8 %copy-start.1 = (bf16[2,2,4,2,128,256]{5,4,3,2,1,0:T(8,128)(2,1)}, bf16[2,2,4,2,128,256]{5,4,3,2,1,0:T(8,128)(2,1)S(1)}, u32[]{:S(2)}) copy-start(bf16[2,2,4,2,128,256]{5,4,3,2,1,0:T(8,128)(2,1)S(1)} %get-tuple-element.98) | copy-start | bytes 6291460
  63.3 0.7 copy-start.4
  64.0 1.0 copy-start.6
  64.9 0.8 copy-start.10
  65.7 0.6 copy-start.25
  66.4 0.6 copy-start.37
  67.0 0.6 copy-start.38
  67.6 0.6 copy-start.43
  116.6 1.1 copy-start.9
  155.1 0.9 copy-start.2
  212.7 1.0 copy-start.11
  239.8 0.7 copy-start.7
  291.5 1.0 copy-start.24
  317.0 0.8 copy-start.12
  427.6 1.1 copy-start.18
  465.9 0.9 copy-start.8
  492.9 68.8 %copy-start.13 = (f32[60,16,256]{2,1,0:T(8,128)S(1)}, f32[60,16,256]{2,1,0:T(8,128)}, u32[]{:S(2)}) copy-start(f32[60,16,256]{2,1,0:T(8,128)} %get-tuple-element.163.refs_8_) | copy-start | bytes 2949124
  492.9 68.8 %copy-start.22 = (f32[30,16,256]{2,1,0:T(8,128)S(1)}, f32[30,16,256]{2,1,0:T(8,128)}, u32[]{:S(2)}) copy-start(f32[30,16,256]{2,1,0:T(8,128)} %get-tuple-element.164.refs_9_) | copy-start | bytes 1474564
  492.9 68.8 %copy-start.30 = (f32[11,8,256]{2,1,0:T(8,128)S(1)}, f32[11,8,256]{2,1,0:T(8,128)}, u32[]{:S(2)}) copy-start(f32[11,8,256]{2,1,0:T(8,128)} %get-tuple-element.160.refs_5_) | copy-start | bytes 270340
  493.0 68.8 %copy-start.31 = (f32[11,8,256]{2,1,0:T(8,128)S(1)}, f32[11,8,256]{2,1,0:T(8,128)}, u32[]{:S(2)}) copy-start(f32[11,8,256]{2,1,0:T(8,128)} %get-tuple-element.157.refs_2_) | copy-start | bytes 270340
  493.0 68.8 %copy-start.32 = (f32[10,8,256]{2,1,0:T(8,128)S(1)}, f32[10,8,256]{2,1,0:T(8,128)}, u32[]{:S(2)}) copy-start(f32[10,8,256]{2,1,0:T(8,128)} %get-tuple-element.158.refs_3_) | copy-start | bytes 245764
  493.0 68.8 %copy-start.34 = (f32[5,8,256]{2,1,0:T(8,128)S(1)}, f32[5,8,256]{2,1,0:T(8,128)}, u32[]{:S(2)}) copy-start(f32[5,8,256]{2,1,0:T(8,128)} %get-tuple-element.161.refs_6_) | copy-start | bytes 122884
  493.0 68.8 %copy-start.39 = (f32[16,256]{1,0:T(8,128)S(1)}, f32[16,256]{1,0:T(8,128)}, u32[]{:S(2)}) copy-start(f32[16,256]{1,0:T(8,128)} %get-tuple-element.162.refs_7_) | copy-start | bytes 49156
  493.0 68.8 %copy-start.40 = (f32[2,8,256]{2,1,0:T(8,128)S(1)}, f32[2,8,256]{2,1,0:T(8,128)}, u32[]{:S(2)}) copy-start(f32[2,8,256]{2,1,0:T(8,128)} %get-tuple-element.159.refs_4_) | copy-start | bytes 49156
  493.0 68.8 %copy-start.41 = (f32[2,8,256]{2,1,0:T(8,128)S(1)}, f32[2,8,256]{2,1,0:T(8,128)}, u32[]{:S(2)}) copy-start(f32[2,8,256]{2,1,0:T(8,128)} %get-tuple-element.156.refs_1_) | copy-start | bytes 49156
  561.8 1.0 copy-start.23
  562.8 0.9 copy-start.33
  563.7 0.7 copy-start.42
  565.3 1.1 copy-start.5
  566.3 85.2 %copy-start.47 = (f32[8288]{0:T(1024)S(1)}, f32[8288]{0:T(1024)}, u32[]{:S(2)}) copy-start(f32[8288]{0:T(1024)} %param.21) | copy-start | bytes 99460
  566.3 85.2 %copy-start.50 = (f32[8288]{0:T(1024)S(1)}, f32[8288]{0:T(1024)}, u32[]{:S(2)}) copy-start(f32[8288]{0:T(1024)} %param.26) | copy-start | bytes 99460
  566.3 85.2 %copy-start.51 = (f32[8288]{0:T(1024)S(1)}, f32[8288]{0:T(1024)}, u32[]{:S(2)}) copy-start(f32[8288]{0:T(1024)} %param.27) | copy-start | bytes 99460
  566.3 87.8 %copy-start.21 = (f32[32768]{0:T(1024)S(1)}, f32[32768]{0:T(1024)}, u32[]{:S(2)}) copy-start(f32[32768]{0:T(1024)} %param.20) | copy-start | bytes 393220
  566.3 87.8 %copy-start.48 = (f32[32768]{0:T(1024)S(1)}, f32[32768]{0:T(1024)}, u32[]{:S(2)}) copy-start(f32[32768]{0:T(1024)} %param.24) | copy-start | bytes 393220
  566.4 87.8 %copy-start.49 = (f32[32768]{0:T(1024)S(1)}, f32[32768]{0:T(1024)}, u32[]{:S(2)}) copy-start(f32[32768]{0:T(1024)} %param.25) | copy-start | bytes 393220
  566.4 89.7 %copy-start.17 = (f32[53248]{0:T(1024)S(1)}, f32[53248]{0:T(1024)}, u32[]{:S(2)}) copy-start(f32[53248]{0:T(1024)} %param.19) | copy-start | bytes 638980
  566.4 89.7 %copy-start.45 = (f32[53248]{0:T(1024)S(1)}, f32[53248]{0:T(1024)}, u32[]{:S(2)}) copy-start(f32[53248]{0:T(1024)} %param.22) | copy-start | bytes 638980
  566.4 89.6 %copy-start.46 = (f32[53248]{0:T(1024)S(1)}, f32[53248]{0:T(1024)}, u32[]{:S(2)}) copy-start(f32[53248]{0:T(1024)} %param.23) | copy-start | bytes 638980

commit v7 on v6

--- a/solution.py
+++ b/solution.py
@@ -298,7 +298,7 @@
     return [square] * len(squares) + ([up, down] if feed is not None else []) + [vecs]
 
 
-def flush(step, last, accs, mat_at, up_acc, down_acc, feed_at, up_rows, g_mat, g_feed, sems):
+def flush(step, last, accs, mat_at, feeds, up_rows, g_mat, g_feed, sems):
     @pl.when(step == last)
     def _():
         copies = []
@@ -308,7 +308,7 @@
 
         for acc, at in zip(accs, mat_at):
             add(acc, g_mat.at[pl.ds(at, acc.shape[0])] if len(acc.shape) == 3 else g_mat.at[at])
-        if up_acc is not None:
+        for up_acc, down_acc, feed_at in feeds:
             for k in range(D // up_rows):
                 for half in range(2):
                     base = 2 * D * feed_at + (2 * k + half) * up_rows
@@ -324,8 +324,8 @@
     return [jax.ShapeDtypeStruct((NSQ, D, D), F32), jax.ShapeDtypeStruct((8 * FF, D), F32)]
 
 
-def flush_count(mats, up_rows):
-    return mats + (2 * D // up_rows + 1 if up_rows else 0)
+def flush_count(mats, feeds, up_rows):
+    return mats + feeds * (2 * D // up_rows + 1 if up_rows else 0)
 
 
 def time_kept(count, group, nb):
@@ -367,8 +367,9 @@
     q_s, k_s, v_s, o_s, p_s, l_s, z1_s, u_s, z2_s = refs[1:10]
     w = {name: refs[10 + i][...] for i, name in enumerate(TIME_W)}
     vec_ref = refs[16]
-    g_mat, g_feed = refs[19:21]
-    outs = refs[21:]
+    later = refs[17:21]
+    g_mat, g_feed = refs[23:25]
+    outs = refs[25:]
     n_out = 3 if first else 2
     tail = outs[1:n_out]
     accs = outs[n_out : n_out + 6]
@@ -443,12 +444,12 @@
     else:
         tail[0][...] = dx.reshape(count, VB, D)
     flush(
-        step, pl.num_programs(0) - 1, accs[:4], [12 * layer + k for k in range(4)], accs[4], accs[5], 2 * layer, up_rows,
-        g_mat, g_feed, sems,
+        step, pl.num_programs(0) - 1, list(accs[:4]) + list(later[:2]), [12 * layer + k for k in (0, 1, 2, 3, 8, 11)],
+        [(accs[4], accs[5], 2 * layer), (later[2], later[3], 2 * layer + 1)], up_rows, g_mat, g_feed, sems,
     )
 
 
-def time_bwd(first, x, extra, dy, kept, model, layer, count, packs, up_rows):
+def time_bwd(first, x, extra, dy, kept, model, layer, count, later, packs, up_rows):
     group = 64 if count > 32 else 32
     nv = x.shape[1]
     width = x.shape[2]
@@ -458,7 +459,7 @@
     specs = [pl.BlockSpec((count, VB, width), lambda i: (0, i, 0))]
     if first:
         specs += [whole((16, D)), whole((count, 1, D))]
-    specs += [block] + time_kept(count, group, nv // VB)[0] + weight_specs(squares, 2 * layer, layer)
+    specs += [block] + time_kept(count, group, nv // VB)[0] + weight_specs(squares, 2 * layer, layer) + [ANY] * 4
     grad_shapes = [(10, 8, D)] + ([(16, D), (count * VB, D)] if first else [])
     out_specs = [ANY] * 2 + [whole(s) for s in grad_shapes]
     out_shape = pack_shapes() + [jax.ShapeDtypeStruct(s, F32) for s in grad_shapes]
@@ -473,11 +474,11 @@
         out_shape=out_shape,
         input_output_aliases={len(specs): 0, len(specs) + 1: 1},
         scratch_shapes=[pltpu.VMEM((D, D), F32)] * 4
-        + [pltpu.VMEM((D, FF), F32), pltpu.VMEM((FF, D), F32), pltpu.SemaphoreType.DMA((flush_count(4, up_rows),))]
+        + [pltpu.VMEM((D, FF), F32), pltpu.VMEM((FF, D), F32), pltpu.SemaphoreType.DMA((flush_count(6, 2, up_rows),))]
         + [pltpu.VMEM((2, pad, HALF), F32)] * 4,
         compiler_params=params_spec(),
         name="time_bwd",
-    )(x, *extra, dy, *kept, *weight_args(model, squares, 2 * layer), *packs)
+    )(x, *extra, dy, *kept, *weight_args(model, squares, 2 * layer), *later, *packs)
 
 SB_ROWS = 64
 
@@ -589,7 +590,21 @@
     return [pl.BlockSpec((sb * SB_ROWS, k), lambda i: (i, 0)) for k in KEPT_WIDTHS]
 
 
-RECV_G = RECV_W + ("rows",)
+RECV_G = ("so", "rk", "rv", "rows")
+LATER_WIDTHS = (D, D, FF, D)
+
+
+def row_specs(sb, widths):
+    return [pl.BlockSpec((sb * SB_ROWS, k), lambda i: (i, 0)) for k in widths]
+
+
+def row_shapes(n, widths):
+    return [jax.ShapeDtypeStruct((n * SB_ROWS, k), F32) for k in widths]
+
+
+def put(refs, values):
+    for ref, value in zip(refs, values):
+        ref[...] = value
 
 
 def recv_backward(dy, kept, w, vec, g):
@@ -601,19 +616,16 @@
     dz4 = norm_bwd(dy, unit4, inv4, vec[21:22])
     rows[8] += colsum(dz4)
     dz42 = split2(dz4)
-    g["down"][...] += tn3(split2(u * cdf), dz42)
     du = mmwt(dz42, w["down"]) * gelu_slope(u, cdf)
     rows[6] += colsum(du[:, :D])
     rows[7] += colsum(du[:, D:])
     du2 = split2(du)
-    g["up"][...] += tn3(split2(gg), du2)
     dg = dz4 + mmwt(du2, w["up"])
     rows[4] += colsum(dg * unit3)
     rows[5] += colsum(dg)
     dz3 = norm_bwd(dg, unit3, inv3, vec[16:17])
     rows[3] += colsum(dz3)
     dz32 = split2(dz3)
-    g["ro"][...] += tn3(split2(mixed), dz32)
     do = mmwt(dz32, w["ro"])
     segs = range(sb)
     d = [split2(do[s * SB_ROWS : (s + 1) * SB_ROWS]) for s in segs]
@@ -625,7 +637,6 @@
     dv = jnp.concatenate([gather_rows(tn3(split2(p), d2)) for p, d2 in zip(probs, d)], 0)
     rows[1] += colsum(dq)
     dq2 = split2(dq)
-    g["rq"][...] += tn3(send2, dq2)
     dsend = dz3 + mmwt(dq2, w["rq"])
     dk2 = split2(dk)
     dv2 = split2(dv)
@@ -636,7 +647,7 @@
     rows[0] += colsum(dbuf)
     dbuf2 = split2(dbuf)
     g["so"][...] += tn3(o2, dbuf2)
-    return dsend, mmwt(dbuf2, w["so"])
+    return dsend, mmwt(dbuf2, w["so"]), (dq, dz3, du, dz4)
 
 
 def recv_squares(layer):
@@ -680,13 +691,13 @@
     )(send, o, *weight_args(model, squares, 1), mvec, model[0])
 
 
-def recv_bwd_kernel(sb, up_rows, send_ref, o_ref, dx_ref, *refs):
+def recv_bwd_kernel(sb, send_ref, o_ref, dx_ref, *refs):
     saved = [ref[...] for ref in refs[:6]]
     refs = refs[6:]
     w = {n: refs[i][...] for i, n in enumerate(RECV_W)}
     vec_ref, mvec_ref, mw_ref = refs[7:10]
-    g_mat, g_feed, dsend_ref, do_ref, rows_ref, dmv_ref = refs[12:18]
-    accs, dmw_ref, sems = refs[18:25], refs[25], refs[26]
+    g_mat, dsend_ref, do_ref, rows_ref, dmv_ref = refs[11:16]
+    later, accs, dmw_ref, sems = refs[16:20], refs[20:23], refs[23], refs[24]
     g = dict(zip(RECV_G, tuple(accs) + (rows_ref,)))
 
     @pl.when(pl.program_id(0) == 0)
@@ -713,47 +724,49 @@
     left = dwide[:, :D].reshape(pairs, 1, SB_ROWS, D)
     right = dwide[:, D:].reshape(pairs, 1, SB_ROWS, D)
     dy = jnp.concatenate([left, right], 1).reshape(sb * SB_ROWS, D)
-    dsend, do = recv_backward(dy, kept, w, vec, g)
+    dsend, do, grads = recv_backward(dy, kept, w, vec, g)
+    put(later, grads)
     dsend_ref[...] = dsend.reshape(sb, SB_ROWS, D)
     pack_block(do_ref, do, sb)
-    recv_flush(accs, [(dmw_ref, 24)], 0, up_rows, g_mat, g_feed, sems)
-
-
-RECV_ACC = [pltpu.VMEM((D, D), F32)] * 5 + [pltpu.VMEM((D, FF), F32), pltpu.VMEM((FF, D), F32)]
-
-
-def recv_flush(accs, more, layer, up_rows, g_mat, g_feed, sems):
+    recv_flush(accs, [(dmw_ref, 24)], 0, g_mat, sems)
+
+
+RECV_ACC = [pltpu.VMEM((D, D), F32)] * 3
+
+
+def recv_flush(accs, more, layer, g_mat, sems):
     flush(
-        pl.program_id(0), pl.num_programs(0) - 1, list(accs[:5]) + [m for m, _ in more],
-        recv_squares(layer) + [at for _, at in more], accs[5], accs[6], 2 * layer + 1, up_rows, g_mat, g_feed, sems,
+        pl.program_id(0), pl.num_programs(0) - 1, list(accs) + [m for m, _ in more],
+        recv_squares(layer)[:3] + [at for _, at in more], [], 0, g_mat, None, sems,
     )
 
 
-def recv_bwd(send, o, dx, kept, model, mvec, sb, packs, up_rows):
+def recv_bwd(send, o, dx, kept, model, mvec, sb, g_mat):
     n = send.shape[0]
     squares = recv_squares(0)
     shapes = [(11, 8, D), (5, 8, D)]
     specs = [seg_block(sb), pack_spec(sb), seg_block(sb // 2)] + kept_specs(sb)
     specs += weight_specs(squares, 1, 0) + [whole((8, D)), MERGE]
     return pl.pallas_call(
-        functools.partial(recv_bwd_kernel, sb, up_rows),
+        functools.partial(recv_bwd_kernel, sb),
         grid=(n // sb,),
-        in_specs=specs + [ANY] * 2,
-        out_specs=[ANY] * 2 + [seg_block(sb), pack_spec(sb)] + [whole(s) for s in shapes],
-        out_shape=pack_shapes()
+        in_specs=specs + [ANY],
+        out_specs=[ANY, seg_block(sb), pack_spec(sb)] + [whole(s) for s in shapes] + row_specs(sb, LATER_WIDTHS),
+        out_shape=pack_shapes()[:1]
         + [jax.ShapeDtypeStruct((n, SB_ROWS, D), F32), jax.ShapeDtypeStruct(o.shape, F32)]
-        + [jax.ShapeDtypeStruct(s, F32) for s in shapes],
-        input_output_aliases={len(specs): 0, len(specs) + 1: 1},
-        scratch_shapes=RECV_ACC + [pltpu.VMEM((2, D, D), F32), pltpu.SemaphoreType.DMA((flush_count(6, up_rows),))],
+        + [jax.ShapeDtypeStruct(s, F32) for s in shapes]
+        + row_shapes(n, LATER_WIDTHS),
+        input_output_aliases={len(specs): 0},
+        scratch_shapes=RECV_ACC + [pltpu.VMEM((2, D, D), F32), pltpu.SemaphoreType.DMA((4,))],
         compiler_params=params_spec(),
         name="recv_bwd",
-    )(send, o, dx, *kept, *weight_args(model, squares, 1), mvec, model[0], *packs)
-
-
-def tail_kernel(sb, up_rows, send_ref, o_ref, tgt_ref, kept_ref, scale_ref, mean_ref, *refs):
+    )(send, o, dx, *kept, *weight_args(model, squares, 1), mvec, model[0], g_mat)
+
+
+def tail_kernel(sb, send_ref, o_ref, tgt_ref, kept_ref, scale_ref, mean_ref, *refs):
     w = {n: refs[i][...] for i, n in enumerate(RECV_W)}
     vec_ref, head_ref, g_mat, g_feed, dsend_ref, do_ref, rows_ref, dhead_ref = refs[7:15]
-    accs, sems = refs[15:22], refs[22]
+    saved, later, accs, sems = refs[15:18], refs[18:22], refs[22:25], refs[25]
     g = dict(zip(RECV_G, tuple(accs) + (rows_ref,)))
 
     @pl.when(pl.program_id(0) == 0)
@@ -763,7 +776,7 @@
 
     vec = vec_ref[...]
     rows = sb * SB_ROWS
-    y, kept, _ = recv_forward(
+    y, kept, (_, mixed, _, z3, u, _) = recv_forward(
         send_ref[...].reshape(rows, D), unpack_block(o_ref, sb), w, vec
     )
     head = head_ref[...]
@@ -771,32 +784,36 @@
     scale = jnp.broadcast_to(scale_ref[...][None], (sb, SB_ROWS, PPAD)).reshape(rows, PPAD)
     mean = jnp.broadcast_to(mean_ref[...][None], (sb, SB_ROWS, PPAD)).reshape(rows, PPAD)
     misfit = mmwt(y2, head) * scale + mean - tgt_ref[...].reshape(rows, PPAD)
+    put(saved, (mixed, z3, u))
     dpred = kept_ref[...].reshape(rows, PPAD) * misfit * scale
     dpred2 = split2(dpred)
     dhead_ref[...] += tn3(dpred2, y2)
     dy = mmw(dpred2, head)
-    dsend, do = recv_backward(dy, kept, w, vec, g)
+    dsend, do, grads = recv_backward(dy, kept, w, vec, g)
+    put(later, grads)
     dsend_ref[...] = dsend.reshape(sb, SB_ROWS, D)
     pack_block(do_ref, do, sb)
-    recv_flush(accs, [], 1, up_rows, g_mat, g_feed, sems)
-
-
-def tail(send, o, tgt, kept, scale, mean, model, head, sb, up_rows):
+    recv_flush(accs, [], 1, g_mat, sems)
+
+
+def tail(send, o, tgt, kept, scale, mean, model, head, sb):
     n = send.shape[0]
     squares = recv_squares(1)
     shapes = [(11, 8, D), (PPAD, D)]
     return pl.pallas_call(
-        functools.partial(tail_kernel, sb, up_rows),
+        functools.partial(tail_kernel, sb),
         grid=(n // sb,),
         in_specs=[seg_block(sb), pack_spec(sb), seg_block(sb, SB_ROWS, PPAD), seg_block(sb, SB_ROWS, PPAD)]
         + [whole((SB_ROWS, PPAD))] * 2
         + weight_specs(squares, 3, 1)
         + [whole((PPAD, D))],
-        out_specs=[ANY] * 2 + [seg_block(sb), pack_spec(sb)] + [whole(s) for s in shapes],
+        out_specs=[ANY] * 2 + [seg_block(sb), pack_spec(sb)] + [whole(s) for s in shapes]
+        + row_specs(sb, (D, D, FF) + LATER_WIDTHS),
         out_shape=pack_shapes()
         + [jax.ShapeDtypeStruct((n, SB_ROWS, D), F32), jax.ShapeDtypeStruct(o.shape, F32)]
-        + [jax.ShapeDtypeStruct(s, F32) for s in shapes],
-        scratch_shapes=RECV_ACC + [pltpu.SemaphoreType.DMA((flush_count(5, up_rows),))],
+        + [jax.ShapeDtypeStruct(s, F32) for s in shapes]
+        + row_shapes(n, (D, D, FF) + LATER_WIDTHS),
+        scratch_shapes=RECV_ACC + [pltpu.SemaphoreType.DMA((3,))],
         compiler_params=params_spec(),
         name="tail",
     )(send, o, tgt, kept, scale, mean, *weight_args(model, squares, 3), head)
@@ -895,8 +912,8 @@
     dsq_ref[...] += tn3(r2, dq2)
     dr_ref[...] = mmwt(dq2, w["sq"]).reshape(sb, RPAD, D)
     flush(
-        pl.program_id(0), pl.num_programs(0) - 1, [dsq_ref, dsk_ref, dsv_ref], send_squares(layer), None, None, 0, 0,
-        g_mat, None, sems,
+        pl.program_id(0), pl.num_programs(0) - 1, [dsq_ref, dsk_ref, dsv_ref], send_squares(layer), [], 0, g_mat, None,
+        sems,
     )
 
 
@@ -1067,7 +1084,7 @@
         out_specs=[ANY] * n,
         out_shape=[jax.ShapeDtypeStruct((ny, 2, nz, nx) + s.shape, s.dtype) for s in shards],
         scratch_shapes=[pltpu.SemaphoreType.DMA((count,)), pltpu.SemaphoreType.DMA((count,)), pltpu.SemaphoreType.DMA((n,))],
-        compiler_params=pltpu.CompilerParams(collective_id=0, has_side_effects=True, vmem_limit_bytes=16 << 20),
+        compiler_params=pltpu.CompilerParams(collective_id=0, has_side_effects=True, vmem_limit_bytes=VMEM_LIMIT),
         name="gather_all",
     )(*shards)
 
@@ -1251,81 +1268,153 @@
     )(*grads, tile)
 
 
-def group_kernel(stats, per, in_ref, out_ref, got, result, send, recv, local):
+def group_part(ref, who, per):
+    return ref.at[pl.ds(pl.multiple_of(who * per, per), per)]
+
+
+def group_out(per, in_ref, got, send, recv, local):
     nf = lax.axis_size("fsdp")
     dp, f = lax.axis_index("dp"), lax.axis_index("fsdp")
-    peers = [lax.rem(f + k, nf) for k in range(1, nf)]
-    greet([(dp, p) for p in peers])
-
-    def part(ref, who):
-        return ref.at[pl.ds(pl.multiple_of(who * per, per), per)]
-
-    own = pltpu.make_async_copy(part(in_ref, f), got.at[f], local)
-    own.start()
-    copies = [
-        remote(part(in_ref, p), got.at[f], send.at[k], recv.at[k], (dp, p)) for k, p in enumerate(peers)
-    ]
+    copies = [pltpu.make_async_copy(group_part(in_ref, f, per), got.at[f], local)]
+    for k in range(1, nf):
+        p = lax.rem(f + k, nf)
+        copies.append(remote(group_part(in_ref, p, per), got.at[f], send.at[k - 1], recv.at[k - 1], (dp, p)))
+    return copies
+
+
+def group_back(per, result, out_ref, send, recv, local):
+    nf = lax.axis_size("fsdp")
+    dp, f = lax.axis_index("dp"), lax.axis_index("fsdp")
+    copies = [pltpu.make_async_copy(result, group_part(out_ref, f, per), local)]
+    for k in range(1, nf):
+        p = lax.rem(f + k, nf)
+        copies.append(remote(result, group_part(out_ref, f, per), send.at[nf - 2 + k], recv.at[nf - 2 + k], (dp, p)))
+    return copies
+
+
+def greet_group():
+    nf = lax.axis_size("fsdp")
+    dp, f = lax.axis_index("dp"), lax.axis_index("fsdp")
+    greet([(dp, lax.rem(f + k, nf)) for k in range(1, nf)])
+
+
+def start_all(copies):
     for copy in copies:
         copy.start()
-    own.wait()
+
+
+def wait_all(copies):
     for copy in copies:
         copy.wait()
-    if stats:
-        row = lax.broadcasted_iota(jnp.int32, (PACK, HALF), 0)
-        lane = lax.broadcasted_iota(jnp.int32, (PACK, HALF), 1)
-        router = jnp.where(row < ROUT, row, row - ROUT)
-        pick = (lane // 8 == router) & (row < 2 * ROUT)
-        src = lax.broadcasted_iota(jnp.int32, (HALF, D), 0)
-        dst = lax.broadcasted_iota(jnp.int32, (HALF, D), 1)
-        widen = jnp.where(src % 8 == dst // 32, 1.0, 0.0).astype(BF)
-
-        def one(s, carry):
-            lse = [got[d, s, 2 * ROUT : 2 * ROUT + 1, :] for d in range(nf)]
-            top = functools.reduce(jnp.maximum, lse)
-            total = top + jnp.log(functools.reduce(jnp.add, [jnp.exp(l - top) for l in lse]))
-            out = jnp.where(row == 2 * ROUT, total, 0.0)
-            share = jnp.concatenate([jnp.where(pick, jnp.exp(l - total), 0.0) for l in lse], 0)
-            wide = mmw(split2(share), widen)
-            for d in range(nf):
-                w = wide[d * PACK : (d + 1) * PACK]
-                w = jnp.where(row < ROUT, w[:, :HALF], w[:, HALF:])
-                out = out + jnp.where(row < 2 * ROUT, w * got[d, s], 0.0)
-            result[s] = out
-            return carry
-
-        lax.fori_loop(0, per, one, 0)
-    else:
-        result[...] = functools.reduce(jnp.add, [got[d] for d in range(nf)])
-    own = pltpu.make_async_copy(result, part(out_ref, f), local)
-    own.start()
-    copies = [
-        remote(result, part(out_ref, f), send.at[nf - 1 + k], recv.at[nf - 1 + k], (dp, p)) for k, p in enumerate(peers)
+
+
+def stats_kernel(per, in_ref, out_ref, got, result, send, recv, local):
+    nf = lax.axis_size("fsdp")
+    greet_group()
+    copies = group_out(per, in_ref, got, send, recv, local)
+    start_all(copies)
+    wait_all(copies)
+    row = lax.broadcasted_iota(jnp.int32, (PACK, HALF), 0)
+    lane = lax.broadcasted_iota(jnp.int32, (PACK, HALF), 1)
+    router = jnp.where(row < ROUT, row, row - ROUT)
+    chosen = (lane // 8 == router) & (row < 2 * ROUT)
+    src = lax.broadcasted_iota(jnp.int32, (HALF, D), 0)
+    dst = lax.broadcasted_iota(jnp.int32, (HALF, D), 1)
+    widen = jnp.where(src % 8 == dst // 32, 1.0, 0.0).astype(BF)
+
+    def one(s, carry):
+        lse = [got[d, s, 2 * ROUT : 2 * ROUT + 1, :] for d in range(nf)]
+        top = functools.reduce(jnp.maximum, lse)
+        total = top + jnp.log(functools.reduce(jnp.add, [jnp.exp(l - top) for l in lse]))
+        out = jnp.where(row == 2 * ROUT, total, 0.0)
+        share = jnp.concatenate([jnp.where(chosen, jnp.exp(l - total), 0.0) for l in lse], 0)
+        wide = mmw(split2(share), widen)
+        for d in range(nf):
+            w = wide[d * PACK : (d + 1) * PACK]
+            w = jnp.where(row < ROUT, w[:, :HALF], w[:, HALF:])
+            out = out + jnp.where(row < 2 * ROUT, w * got[d, s], 0.0)
+        result[s] = out
+        return carry
+
+    lax.fori_loop(0, per, one, 0)
+    copies = group_back(per, result, out_ref, send, recv, local)
+    start_all(copies)
+    wait_all(copies)
+
+
+def sum_kernel(per, turn, in_ref, x_ref, mixed_ref, z_ref, u_ref, dq_ref, dz3_ref, du_ref, dz4_ref, vec_ref, *refs):
+    out_ref, rq, ro, up, down, got, result, send, recv, local = refs
+    step = pl.program_id(0)
+
+    @pl.when(step == 0)
+    def _():
+        greet_group()
+        start_all(group_out(per, in_ref, got, send, recv, local))
+        for ref in (rq, ro, up, down):
+            ref[...] = jnp.zeros(ref.shape, F32)
+
+    @pl.when(step == turn)
+    def _():
+        wait_all(group_out(per, in_ref, got, send, recv, local))
+        result[...] = functools.reduce(jnp.add, [got[d] for d in range(lax.axis_size("fsdp"))])
+        start_all(group_back(per, result, out_ref, send, recv, local))
+
+    rq[...] += tn3(split2(x_ref[...]), split2(dq_ref[...]))
+    ro[...] += tn3(split2(mixed_ref[...]), split2(dz3_ref[...]))
+    g, _, _ = norm_fwd(z_ref[...], vec_ref[16:17], vec_ref[17:18])
+    up[...] += tn3(split2(g), split2(du_ref[...]))
+    u = u_ref[...]
+    down[...] += tn3(split2(u * gelu_cdf(u)), split2(dz4_ref[...]))
+
+    @pl.when(step == pl.num_programs(0) - 1)
+    def _():
+        wait_all(group_back(per, result, out_ref, send, recv, local))
+
+
+def group_scratch(per, nf):
+    return [
+        pltpu.VMEM((nf, per, PACK, HALF), F32),
+        pltpu.VMEM((per, PACK, HALF), F32),
+        pltpu.SemaphoreType.DMA((2 * nf - 2,)),
+        pltpu.SemaphoreType.DMA((2 * nf - 2,)),
+        pltpu.SemaphoreType.DMA,
     ]
-    for copy in copies:
-        copy.start()
-    own.wait()
-    for copy in copies:
-        copy.wait()
-
-
-def group_combine(packed, stats, cid):
+
+
+def group_params(cid):
+    return pltpu.CompilerParams(collective_id=cid, has_side_effects=True, vmem_limit_bytes=VMEM_LIMIT)
+
+
+def group_stats(packed, cid):
     nf = lax.axis_size("fsdp")
     per = packed.shape[0] // nf
     return pl.pallas_call(
-        functools.partial(group_kernel, stats, per),
+        functools.partial(stats_kernel, per),
         in_specs=[ANY],
         out_specs=ANY,
         out_shape=jax.ShapeDtypeStruct(packed.shape, F32),
-        scratch_shapes=[
-            pltpu.VMEM((nf, per, PACK, HALF), F32),
-            pltpu.VMEM((per, PACK, HALF), F32),
-            pltpu.SemaphoreType.DMA((2 * nf - 2,)),
-            pltpu.SemaphoreType.DMA((2 * nf - 2,)),
-            pltpu.SemaphoreType.DMA,
-        ],
-        compiler_params=pltpu.CompilerParams(collective_id=cid, has_side_effects=True, vmem_limit_bytes=32 << 20),
-        name="group_stats" if stats else "group_sum",
+        scratch_shapes=group_scratch(per, nf),
+        compiler_params=group_params(cid),
+        name="group_stats",
     )(packed)
+
+
+def group_sum(packed, work, vecs, layer, cid):
+    nf = lax.axis_size("fsdp")
+    per = packed.shape[0] // nf
+    rows = 480
+    steps = work[0].shape[0] // rows
+    shapes = [(D, D), (D, D), (D, FF), (FF, D)]
+    return pl.pallas_call(
+        functools.partial(sum_kernel, per, steps - steps // 4),
+        grid=(steps,),
+        in_specs=[ANY] + [pl.BlockSpec((rows, w.shape[1]), lambda i: (i, 0)) for w in work] + [pick((24, D), layer)],
+        out_specs=[ANY] + [whole(s) for s in shapes],
+        out_shape=[jax.ShapeDtypeStruct(packed.shape, F32)] + [jax.ShapeDtypeStruct(s, F32) for s in shapes],
+        scratch_shapes=group_scratch(per, nf),
+        compiler_params=group_params(cid),
+        name="group_sum",
+    )(packed, *work, vecs)
 
 LAYER_AT = SEGLEN + 1 + SEG
 MERGE_AT = LAYER_AT + 46
@@ -1383,7 +1472,7 @@
         + [whole(x.shape) for x in (matrices, feed, vectors)],
         out_specs=[whole(s) for s, _ in shapes],
         out_shape=[jax.ShapeDtypeStruct(s, t) for s, t in shapes],
-        compiler_params=pltpu.CompilerParams(vmem_limit_bytes=32 << 20),
+        compiler_params=pltpu.CompilerParams(vmem_limit_bytes=VMEM_LIMIT),
         name="prepare",
     )(series, observed, targets, target_mask, counts, matrices, feed, vectors)
 
@@ -1427,7 +1516,7 @@
         out_specs=[whole(s) for s, _ in shapes],
         out_shape=[jax.ShapeDtypeStruct(s, t) for s, t in shapes],
         scratch_shapes=[pltpu.VMEM((VROWS + 24, D), F32)],
-        compiler_params=pltpu.CompilerParams(vmem_limit_bytes=32 << 20),
+        compiler_params=pltpu.CompilerParams(vmem_limit_bytes=VMEM_LIMIT),
         name="unpack_vectors",
     )(gathered)
 
@@ -1469,7 +1558,7 @@
         out_specs=whole((devices, rows, D)),
         out_shape=jax.ShapeDtypeStruct((devices, rows, D), F32),
         scratch_shapes=[pltpu.VMEM((VROWS + 24, D), F32)],
-        compiler_params=pltpu.CompilerParams(vmem_limit_bytes=32 << 20),
+        compiler_params=pltpu.CompilerParams(vmem_limit_bytes=VMEM_LIMIT),
         name="assemble_vectors",
     )(*parts)
 
@@ -1485,7 +1574,7 @@
     return (weight - learn_rate * (corrected + weight_decay * weight), first_new, second_new)
 
 
-def gradient_parts(ready, model, extras, up_rows, combine, nf, devices):
+def gradient_parts(ready, model, extras, up_rows, group_stats, group_sum, nf, devices):
     pieces, tgt, kept, scale, mean, here = ready
     mvec, emb, place, head, routers0, routers1 = extras
     sb0, sb1, sf0, sf1, st = 12, 10, 20, 10, 10
@@ -1493,20 +1582,24 @@
     half = SEG // 2
     dim0, kept0 = time_fwd(True, pieces, (emb, place), model, 0, SEG)
     o0 = send_fwd(dim0, routers0, here, model, 0, sf0, -(-SEG // nf) * nf)
-    o0 = combine(o0, True, 2)
+    o0 = group_stats(o0, 2)
     x1, *saved = recv_fwd(dim0, o0, model, mvec, rf)
     dim1, kept1 = time_fwd(False, x1, (), model, 1, half)
     o1 = send_fwd(dim1, routers1, here, model, 1, sf1, -(-half // nf) * nf)
-    o1 = combine(o1, True, 3)
-    g_mat, g_feed, ddim1, do1, rr1, dhead = tail(dim1, o1, tgt, kept, scale, mean, model, head, st, up_rows)
-    do1 = combine(do1, False, 4)
+    o1 = group_stats(o1, 3)
+    vecs = model[3]
+    g_mat, g_feed, ddim1, do1, rr1, dhead, *work = tail(dim1, o1, tgt, kept, scale, mean, model, head, st)
+    do1, *later = group_sum(do1, [dim1.reshape(-1, D)] + work, vecs, 1, 4)
     g_mat, ddim1, dr1, rs1 = send_bwd(dim1, ddim1, routers1, o1, do1, here, model, 1, sb1, g_mat)
-    g_mat, g_feed, rt1, dx1 = time_bwd(False, x1, (), ddim1, kept1, model, 1, half, (g_mat, g_feed), up_rows)
-    g_mat, g_feed, ddim0, do0, rr0, dmv = recv_bwd(dim0, o0, dx1, saved, model, mvec, rb, (g_mat, g_feed), up_rows)
-    do0 = combine(do0, False, 5)
+    g_mat, g_feed, rt1, dx1 = time_bwd(
+        False, x1, (), ddim1, kept1, model, 1, half, later, (g_mat, g_feed), up_rows
+    )
+    g_mat, ddim0, do0, rr0, dmv, *work = recv_bwd(dim0, o0, dx1, saved, model, mvec, rb, g_mat)
+    work = [dim0.reshape(-1, D), saved[1], saved[3], saved[4]] + work
+    do0, *later = group_sum(do0, work, vecs, 0, 5)
     g_mat, ddim0, dr0, rs0 = send_bwd(dim0, ddim0, routers0, o0, do0, here, model, 0, sb0, g_mat)
     g_mat, g_feed, rt0, demb, dplace = time_bwd(
-        True, pieces, (emb, place), ddim0, kept0, model, 0, SEG, (g_mat, g_feed), up_rows
+        True, pieces, (emb, place), ddim0, kept0, model, 0, SEG, later, (g_mat, g_feed), up_rows
     )
     g_vec = assemble_vectors((demb, dplace, rt0, rs0, rr0, rt1, rs1, rr1, dmv, dhead, dr0, dr1), devices)
     return g_mat, g_feed, g_vec
@@ -1535,7 +1628,7 @@
     down = feed.reshape(8, FF, D)
     vecs, *extras = unpack_vectors(vecs.reshape(devices, vec_rows, D), own)
     up_rows = feed_weights.shape[0] // FF
-    g_mat, g_feed, g_vec = gradient_parts(ready, (square, up, down, vecs), extras, up_rows, group_combine, nf, devices)
+    g_mat, g_feed, g_vec = gradient_parts(ready, (square, up, down, vecs), extras, up_rows, group_stats, group_sum, nf, devices)
     ny, nz, nx = grid_sizes()
     lead = (ny, 2, nz, nx)
     s_mat, s_feed, s_vec, sums = scatter_sum([g.reshape(lead + (-1, D)) for g in (g_mat, g_feed, g_vec)], tile)

time: 660 us -> 732 us (1.11)
  Pallas kernels: 618 us -> 709 us
  local copies, waits for them, and re-layouts: 31.4 us -> 6.79 us
    pallas_call x2, Pallas kernels: 108 us -> 204 us  [time_bwd(): pl.pallas_call(functools.partial(time_bwd_kernel, first, count, group, la...]
    unnamed x107 -> x21, local copies, waits for them, and re-layouts: 27.7 us -> 1.17 us
    pallas_call x6, Pallas kernels: 231 us -> 217 us  [the longest x2 70.3 us: group_sum(): pl.pallas_call(functools.partial(sum_kernel, per, steps - steps // 4), gr...]
where the time goes in v7:
time: 732 us; the launch traced here: 724 us
  Pallas kernels  709 us (97%)
    pallas_call x2, Pallas kernels, time_bwd(): pl.pallas_call(functools.partial(time_bwd_kernel, first, count, group, la...  204 us
    pallas_call x1, Pallas kernels, scatter_sum(): pl.pallas_call(functools.partial(scatter_kernel, shapes), in_specs=[ANY]...  81.7 us
    pallas_call x2, Pallas kernels, group_sum(): pl.pallas_call(functools.partial(sum_kernel, per, steps - steps // 4), gr...  70.3 us
    pallas_call x2, Pallas kernels, group_stats(): pl.pallas_call(functools.partial(stats_kernel, per), in_specs=[ANY], out_...  64.3 us
    pallas_call x2, Pallas kernels, time_fwd(): pl.pallas_call(functools.partial(time_fwd_kernel, first, count, group), g...  58.8 us
    pallas_call x1, Pallas kernels, gather_all(): pl.pallas_call(functools.partial(gather_kernel, n), in_specs=[ANY] * n, o...  50.1 us
    pallas_call x1, Pallas kernels, recv_bwd(): pl.pallas_call(functools.partial(recv_bwd_kernel, sb), grid=(n // sb,), i...  45.7 us
    pallas_call x2, Pallas kernels, send_bwd(): pl.pallas_call(functools.partial(send_bwd_kernel, sb, layer), grid=(n //...  42 us

profile of v7, /device:TPU:0, one launch (start us, length us, event | category | flops | bytes accessed | tf_op | source)
XLA Modules:
  0.0 724.3 jit_solution(8546360942130164560)
XLA Ops:
  0.6 1.4 pad_bitcast_fusion.vec_ref
  2.7 4.6 prepare.1
  7.2 50.1 %gather_all.1 = (bf16[2,2,4,2,208,256]{5,4,3,2,1,0:T(8,128)(2,1)}, bf16[2,2,4,2,128,256]{5,4,3,2,1,0:T(8,128)(2,1)}, bf16[2,2,4,2,33,256]{5,4,3,2,1,0:T(8,128)(2,1)}) custom-call(bf16[208,256]{1,0:T(8,128)(2,1)} %get-tuple-element.111.refs_0_, bf16[128,256]{1,0:T(8,128)(2,1)} %get-tuple-element.112.refs_1_, bf16[33,256]{1,0:T(8,128)(2,1)} %get-tuple-element.113.refs_2_), custom_call_target="tpu_custom_call" | custom-call | tf_op jit(solution)/shard_map/gather_all/pallas_call | solution.py:1081
  57.4 2.7 unpack_vectors.1
  60.0 1.3 slice.21
  61.3 1.3 reshape.78.refs_7_.refs_5_.refs_15_.refs_11_.refs_17_
  62.6 35.6 %time_fwd.2 = (f32[60,64,256]{2,1,0:T(8,128)}, f32[8,2,512,128]{3,2,1,0:T(8,128)}, f32[8,2,512,128]{3,2,1,0:T(8,128)}, f32[8,2,512,128]{3,2,1,0:T(8,128)}, f32[8...) custom-call(f32[60,64,16]{2,1,0:T(8,128)} %get-tuple-element.110.ref, ...), custom_call_target="tpu_custom_call" | custom-call | tf_op jit(solution)/shard_map/time_fwd/pallas_call | solution.py:347
  98.2 11.4 %send_fwd.2.in_ref = f32[64,24,128]{2,1,0:T(8,128)} custom-call(f32[60,64,256]{2,1,0:T(8,128)} %get-tuple-element.120.dim_ref.send_ref, f32[60,16,256]{2,1,0:T(8,128)} %get-tuple-element.121.r_ref, f32[64,128]{1,0:T(8,128)} %get-tuple-element.122.here_ref, bf16[26,256,256]{2,1,0:T(8,128)(2,1)} %bitcast.30, bf16[26,256,256]{2,1,0:T(8,128)(2,1)} %bitcast.31, ...), custom_call_target="tpu_custom_call" | custom-call | tf_op jit(solution)/shard_map/send_fwd/pallas_call | solution.py:861
  109.7 37.9 %group_stats.2.o_ref = f32[64,24,128]{2,1,0:T(8,128)} custom-call(f32[64,24,128]{2,1,0:T(8,128)} %send_fwd.2.in_ref), custom_call_target="tpu_custom_call" | custom-call | tf_op jit(solution)/shard_map/group_stats/pallas_call | solution.py:1391
  147.5 26.3 %recv_fwd.1 = (f32[30,64,256]{2,1,0:T(8,128)}, f32[3840,256]{1,0:T(8,128)}, f32[3840,256]{1,0:T(8,128)}, f32[3840,128]{1,0:T(8,128)}, f32[3840,256]{1,0:T(8,128)...) custom-call(f32[60,64,256]{2,1,0:T(8,128)} %get-tuple-element.120.dim_ref.send_ref, f32[64,24,128]{2,1,0:T(8,128)} %group_stats.2.o_ref, ...), custom_call_target="tpu_custom_call" | custom-call | tf_op jit(solution)/shard_map/recv_fwd/pallas_call | solution.py:682
  173.8 23.2 %time_fwd.3 = (f32[30,64,256]{2,1,0:T(8,128)}, f32[8,2,256,128]{3,2,1,0:T(8,128)}, f32[8,2,256,128]{3,2,1,0:T(8,128)}, f32[8,2,256,128]{3,2,1,0:T(8,128)}, f32[8...) custom-call(f32[30,64,256]{2,1,0:T(8,128)} %get-tuple-element.124.re, ...), custom_call_target="tpu_custom_call" | custom-call | tf_op jit(solution)/shard_map/time_fwd/pallas_call | solution.py:347
  197.0 7.2 send_fwd.3.in_ref
  204.3 26.4 %group_stats.3.o_ref = f32[32,24,128]{2,1,0:T(8,128)} custom-call(f32[32,24,128]{2,1,0:T(8,128)} %send_fwd.3.in_ref), custom_call_target="tpu_custom_call" | custom-call | tf_op jit(solution)/shard_map/group_stats/pallas_call | solution.py:1391
  230.6 36.3 %tail.1 = (f32[26,256,256]{2,1,0:T(8,128)}, f32[4096,256]{1,0:T(8,128)}, f32[30,64,256]{2,1,0:T(8,128)}, f32[32,24,128]{2,1,0:T(8,128)}, f32[11,8,256]{2,1,0:T(8...) custom-call(f32[30,64,256]{2,1,0:T(8,128)} %get-tuple-element.125.di, ...), custom_call_target="tpu_custom_call" | custom-call | tf_op jit(solution)/shard_map/tail/pallas_call | solution.py:803
  267.0 29.0 %group_sum.2 = (f32[32,24,128]{2,1,0:T(8,128)}, f32[256,256]{1,0:T(8,128)}, f32[256,256]{1,0:T(8,128)}, f32[256,512]{1,0:T(8,128)}, f32[512,256]{1,0:T(8,128)}) custom-call(f32[32,24,128]{2,1,0:T(8,128)} %get-tuple-element.133.in_ref, f32[1920,256]{1,0:T(8,128)} %bitcast.81, f32[1920,256]{1,0:T(8,128)} %get-tuple-element.134.mixed_ref, ...), custom_call_target="tpu_custom_call" | custom-call | tf_op jit(solution)/shard_map/group_sum/pallas_call | solution.py:1408
  296.0 15.9 %send_bwd.2 = (f32[26,256,256]{2,1,0:T(8,128)}, f32[30,64,256]{2,1,0:T(8,128)}, f32[30,16,256]{2,1,0:T(8,128)}, f32[2,8,256]{2,1,0:T(8,128)}) custom-call(f32[30,64,256]{2,1,0:T(8,128)} %get-tuple-element.125.dim_ref.send_ref, f32[30,64,256]{2,1,0:T(8,128)} %get-tuple-element.132.dpart_ref, ...), custom_call_target="tpu_custom_call", output_to_operand_aliasing={{0}: (10, {})} | custom-call | tf_op jit(solution)/shard_map/send_bwd/pallas_call | solution.py:925
  311.8 86.8 %time_bwd.2 = (f32[26,256,256]{2,1,0:T(8,128)}, f32[4096,256]{1,0:T(8,128)}, f32[10,8,256]{2,1,0:T(8,128)}, f32[30,64,256]{2,1,0:T(8,128)}) custom-call(f32[30,64,256]{2,1,0:T(8,128)} %get-tuple-element.124.refs_0_, f32[30,64,256]{2,1,0:T(8,128)} %get-tuple-element.143.refs_1_, ...), custom_call_target="tpu_custom_call", output_to_operand_aliasing={{0}: (22, {}), {1}: (23, {})} | custom-call | tf_op jit(solution)/shard_map/time_bwd/pallas_call | solution.py:469
  398.7 45.7 %recv_bwd.1 = (f32[26,256,256]{2,1,0:T(8,128)}, f32[60,64,256]{2,1,0:T(8,128)}, f32[64,24,128]{2,1,0:T(8,128)}, f32[11,8,256]{2,1,0:T(8,128)}, f32[5,8,256]{2,1,...) custom-call(f32[60,64,256]{2,1,0:T(8,128)} %get-tuple-element.120.di, ...), custom_call_target="tpu_custom_call", output_to_operand_aliasing={{0}: (19, {})} | custom-call | tf_op jit(solution)/shard_map/recv_bwd/pallas_call | solution.py:750
  444.4 41.3 %group_sum.3 = (f32[64,24,128]{2,1,0:T(8,128)}, f32[256,256]{1,0:T(8,128)}, f32[256,256]{1,0:T(8,128)}, f32[256,512]{1,0:T(8,128)}, f32[512,256]{1,0:T(8,128)}) custom-call(f32[64,24,128]{2,1,0:T(8,128)} %get-tuple-element.168.in_ref, f32[3840,256]{1,0:T(8,128)} %bitcast.79, f32[3840,256]{1,0:T(8,128)} %get-tuple-element.161.refs_1_.mixed_ref, ...), custom_call_target="tpu_custom_call" | custom-call | tf_op jit(solution)/shard_map/group_sum/pallas_call | solution.py:1408
  485.7 26.2 %send_bwd.3 = (f32[26,256,256]{2,1,0:T(8,128)}, f32[60,64,256]{2,1,0:T(8,128)}, f32[60,16,256]{2,1,0:T(8,128)}, f32[2,8,256]{2,1,0:T(8,128)}) custom-call(f32[60,64,256]{2,1,0:T(8,128)} %get-tuple-element.120.dim_ref.send_ref, f32[60,64,256]{2,1,0:T(8,128)} %get-tuple-element.167.dpart_ref, ...), custom_call_target="tpu_custom_call", output_to_operand_aliasing={{0}: (10, {})} | custom-call | tf_op jit(solution)/shard_map/send_bwd/pallas_call | solution.py:925
  511.9 116.7 %time_bwd.3 = (f32[26,256,256]{2,1,0:T(8,128)}, f32[4096,256]{1,0:T(8,128)}, f32[10,8,256]{2,1,0:T(8,128)}, f32[16,256]{1,0:T(8,128)}, f32[480,256]{1,0:T(8,128)}) custom-call(f32[60,64,16]{2,1,0:T(8,128)} %get-tuple-element.110.refs_0_, bf16[16,256]{1,0:T(8,128)(2,1)} %get-tuple-element.115.refs_1_, ...), custom_call_target="tpu_custom_call", output_to_operand_aliasing={{0}: (24, {}), {1}: (25, {})} | custom-call | tf_op jit(solution)/shard_map/time_bwd/pallas_call | solution.py:469
  628.6 3.6 assemble_vectors.1
  632.2 0.0 copy-start.4
  632.2 0.0 copy-start.7
  632.2 0.0 copy-start.8
  632.2 0.0 copy-start.1
  632.2 0.0 copy-start.5
  632.2 0.0 copy-start.6
  632.2 0.0 copy-start
  632.3 0.0 copy-start.2
  632.3 0.0 copy-start.3
  632.3 81.7 %scatter_sum.1 = (f32[208,256]{1,0:T(8,128)}, f32[128,256]{1,0:T(8,128)}, f32[33,256]{1,0:T(8,128)}, f32[16,128]{1,0:T(8,128)}) custom-call(f32[2,2,4,2,208,256]{5,4,3,2,1,0:T(8,128)} %bitcast.71, f32[2,2,4,2,128,256]{5,4,3,2,1,0:T(8,128)} %bitcast.80, f32[2,2,4,2,33,256]{5,4,3,2,1,0:T(8,128)} %bitcast.82, f32[8,128]{1,0:T(8,128)} %get-tuple-element.205.refs_3_), custom_call_target="tpu_custom_call" | custom-call | tf_op jit(solution)/shard_map/scatter_sum/pallas_call | solution.py:1254
  714.0 0.8 reshape.86
  714.8 1.3 slice_reduce_fusion
  717.5 0.0 copy-done.4
  717.5 0.0 copy-done.7
  717.5 0.0 copy-done.8
  717.5 0.7 multiply_subtract_fusion.2
  718.2 0.9 fusion.6
  719.1 1.0 copy.33
  720.1 0.0 copy-done.1
  720.1 0.0 copy-done.5
  720.1 0.0 copy-done.6
  720.1 0.8 multiply_subtract_fusion.1
  720.9 0.9 multiply_bitcast_fusion
  721.9 0.1 copy.31
  722.0 0.0 copy-done
  722.0 0.0 copy-done.2
  722.0 0.0 copy-done.3
  722.0 0.9 multiply_subtract_fusion
  (2 shorter events, 0.0 us)
Async XLA Ops:
  632.2 85.3 %copy-start.4 = (f32[8288]{0:T(1024)S(1)}, f32[8288]{0:T(1024)}, u32[]{:S(2)}) copy-start(f32[8288]{0:T(1024)} %param.21) | copy-start | bytes 99460
  632.2 85.3 %copy-start.7 = (f32[8288]{0:T(1024)S(1)}, f32[8288]{0:T(1024)}, u32[]{:S(2)}) copy-start(f32[8288]{0:T(1024)} %param.26) | copy-start | bytes 99460
  632.2 85.3 %copy-start.8 = (f32[8288]{0:T(1024)S(1)}, f32[8288]{0:T(1024)}, u32[]{:S(2)}) copy-start(f32[8288]{0:T(1024)} %param.27) | copy-start | bytes 99460
  632.2 87.9 %copy-start.1 = (f32[32768]{0:T(1024)S(1)}, f32[32768]{0:T(1024)}, u32[]{:S(2)}) copy-start(f32[32768]{0:T(1024)} %param.20) | copy-start | bytes 393220
  632.2 87.9 %copy-start.5 = (f32[32768]{0:T(1024)S(1)}, f32[32768]{0:T(1024)}, u32[]{:S(2)}) copy-start(f32[32768]{0:T(1024)} %param.24) | copy-start | bytes 393220
  632.2 87.9 %copy-start.6 = (f32[32768]{0:T(1024)S(1)}, f32[32768]{0:T(1024)}, u32[]{:S(2)}) copy-start(f32[32768]{0:T(1024)} %param.25) | copy-start | bytes 393220
  632.2 89.8 %copy-start = (f32[53248]{0:T(1024)S(1)}, f32[53248]{0:T(1024)}, u32[]{:S(2)}) copy-start(f32[53248]{0:T(1024)} %param.19) | copy-start | bytes 638980
  632.3 89.8 %copy-start.2 = (f32[53248]{0:T(1024)S(1)}, f32[53248]{0:T(1024)}, u32[]{:S(2)}) copy-start(f32[53248]{0:T(1024)} %param.22) | copy-start | bytes 638980
  632.3 89.8 %copy-start.3 = (f32[53248]{0:T(1024)S(1)}, f32[53248]{0:T(1024)}, u32[]{:S(2)}) copy-start(f32[53248]{0:T(1024)} %param.23) | copy-start | bytes 638980

commit v8 on v7

--- a/solution.py
+++ b/solution.py
@@ -78,6 +78,27 @@
     n = b2[0].shape[1]
     both = dots(a2[0], jnp.concatenate([b2[0], b2[1]], 1), 0, 0)
     return both[:, :n] + both[:, n:] + dots(a2[1], b2[0], 0, 0)
+
+
+def tn3_short(a2, b2):
+    return dots(jnp.concatenate([a2[0], a2[0], a2[1]], 0), jnp.concatenate([b2[0], b2[1], b2[0]], 0), 0, 0)
+
+
+def nn3_short(a2, b2):
+    return dots(jnp.concatenate([a2[0], a2[0], a2[1]], 1), jnp.concatenate([b2[0], b2[1], b2[0]], 0), 1, 0)
+
+
+def corner(r, m, n):
+    return r[:m, :n] + r[m:, :n] + r[:m, n:]
+
+
+def nn3_narrow(a2, b2):
+    r = dots(rows2(a2), jnp.concatenate([b2[0], b2[1]], 1), 1, 0)
+    return corner(r, a2[0].shape[0], b2[0].shape[1])
+
+
+def nt3_narrow(a2, b2):
+    return corner(dots(rows2(a2), rows2(b2), 1, 1), a2[0].shape[0], b2[0].shape[0])
 
 
 def norm_fwd(z, gain, bias):
@@ -195,11 +216,10 @@
     s2 = [split2(p * x) for p, x in zip(probs, dp)]
     p2 = [split2(p) for p in probs]
     k = [spread2(x2) for x2 in time_parts(units, group, k_s)]
-    both = [dots(rows2(a), k2[0], 1, 0) for a, k2 in zip(s2, k)]
-    dq = [b[:group] + b[group:] + dots(a[0], k2[1], 1, 0) for b, a, k2 in zip(both, s2, k)]
+    dq = [nn3_narrow(a, k2) for a, k2 in zip(s2, k)]
     q = time_parts(units, group, q_s)
-    dk = [gather_heads(tn3(a, q2), group) for a, q2 in zip(s2, q)]
-    dv = [gather_heads(tn3(a, x), group) for a, x in zip(p2, d2)]
+    dk = [gather_heads(tn3_short(a, q2), group) for a, q2 in zip(s2, q)]
+    dv = [gather_heads(tn3_short(a, x), group) for a, x in zip(p2, d2)]
     for (c, v), x, y, z in zip(units, dq, dk, dv):
         at = pl.ds(v, group, stride=VB)
         dq_s[c, at, :] = x
@@ -459,7 +479,8 @@
     specs = [pl.BlockSpec((count, VB, width), lambda i: (0, i, 0))]
     if first:
         specs += [whole((16, D)), whole((count, 1, D))]
-    specs += [block] + time_kept(count, group, nv // VB)[0] + weight_specs(squares, 2 * layer, layer) + [ANY] * 4
+    specs += [block] + time_kept(count, group, nv // VB)[0] + weight_specs(squares, 2 * layer, layer)
+    specs += [whole((D, D)), whole((D, D)), whole((D, FF)), whole((FF, D))]
     grad_shapes = [(10, 8, D)] + ([(16, D), (count * VB, D)] if first else [])
     out_specs = [ANY] * 2 + [whole(s) for s in grad_shapes]
     out_shape = pack_shapes() + [jax.ShapeDtypeStruct(s, F32) for s in grad_shapes]
@@ -559,10 +580,10 @@
     q = (mmw(send2, w["rq"]) + vec[13:14]) * SCALE
     segs = range(sb)
     ok = valid_lane(SB_ROWS)
-    scores = [jnp.where(ok, nt3(split2(q[s * SB_ROWS : (s + 1) * SB_ROWS]), k[s]), negative) for s in segs]
+    scores = [jnp.where(ok, nt3_narrow(split2(q[s * SB_ROWS : (s + 1) * SB_ROWS]), k[s]), negative) for s in segs]
     probs = [jnp.exp(sc - router_reduce(sc, jnp.maximum)) for sc in scores]
     probs = [p / router_reduce(p, jnp.add) for p in probs]
-    mixed = jnp.concatenate([nn3(split2(p), v2) for p, v2 in zip(probs, v)], 0)
+    mixed = jnp.concatenate([nn3_short(split2(p), v2) for p, v2 in zip(probs, v)], 0)
     z3 = send + mmw(split2(mixed), w["ro"]) + vec[15:16]
     g, unit3, inv3 = norm_fwd(z3, vec[16:17], vec[17:18])
     u = mmw(split2(g), w["up"]) + jnp.concatenate([vec[18:19], vec[19:20]], 1)
@@ -629,12 +650,12 @@
     do = mmwt(dz32, w["ro"])
     segs = range(sb)
     d = [split2(do[s * SB_ROWS : (s + 1) * SB_ROWS]) for s in segs]
-    dp = [nt3(d2, v2) for d2, v2 in zip(d, v)]
+    dp = [nt3_narrow(d2, v2) for d2, v2 in zip(d, v)]
     ds = [split2(p * (x - router_reduce(p * x, jnp.add))) for p, x in zip(probs, dp)]
-    dq = jnp.concatenate([nn3(s2, k2) for s2, k2 in zip(ds, k)], 0) * SCALE
+    dq = jnp.concatenate([nn3_short(s2, k2) for s2, k2 in zip(ds, k)], 0) * SCALE
     q = [split2(q[s * SB_ROWS : (s + 1) * SB_ROWS]) for s in segs]
-    dk = jnp.concatenate([gather_rows(tn3(s2, q2)) for s2, q2 in zip(ds, q)], 0)
-    dv = jnp.concatenate([gather_rows(tn3(split2(p), d2)) for p, d2 in zip(probs, d)], 0)
+    dk = jnp.concatenate([gather_rows(tn3_short(s2, q2)) for s2, q2 in zip(ds, q)], 0)
+    dv = jnp.concatenate([gather_rows(tn3_short(split2(p), d2)) for p, d2 in zip(probs, d)], 0)
     rows[1] += colsum(dq)
     dq2 = split2(dq)
     dsend = dz3 + mmwt(dq2, w["rq"])
@@ -840,12 +861,12 @@
     dim2 = split2(dim_ref[...].reshape(sb * SB_ROWS, D))
     _, k, v, q = send_project(dim2, r_ref[...].reshape(sb * RPAD, D), w, vec_ref[...])
     here = here_ref[...] > 0.5
-    scores = [jnp.where(here, nt3(k2, q2), negative) for k2, q2 in zip(k, q)]
+    scores = [jnp.where(here, nt3_narrow(k2, q2), negative) for k2, q2 in zip(k, q)]
     tops = [jnp.max(sc, 0, keepdims=True) for sc in scores]
     probs = [jnp.where(here, jnp.exp(sc - top), 0.0) for sc, top in zip(scores, tops)]
     totals = [jnp.sum(p, 0, keepdims=True) for p in probs]
     safe = [jnp.where(t > 0.0, t, 1.0) for t in totals]
-    mixed = [gather_rows(tn3(split2(p / t), v2)) for p, t, v2 in zip(probs, safe, v)]
+    mixed = [gather_rows(tn3_short(split2(p / t), v2)) for p, t, v2 in zip(probs, safe, v)]
     for s in range(sb):
         lse = jnp.where(totals[s] > 0.0, tops[s] + jnp.log(safe[s]), negative)
         o_ref[s] = pack_rows(mixed[s], lse)
@@ -885,7 +906,7 @@
     r2, k, v, q = send_project(dim2, r_ref[...].reshape(sb * RPAD, D), w, vec_ref[...])
     here = (here_ref[...] > 0.5) & valid_lane(SB_ROWS)
     segs = range(sb)
-    scores = [nt3(k2, q2) for k2, q2 in zip(k, q)]
+    scores = [nt3_narrow(k2, q2) for k2, q2 in zip(k, q)]
     probs = [jnp.where(here, jnp.exp(scores[s] - o_ref[s][2 * ROUT : 2 * ROUT + 1]), 0.0) for s in segs]
     dwide = [spread_rows(unpack_rows(do_ref[s])) for s in segs]
     owide = [
@@ -895,11 +916,11 @@
     d = [split2(a) for a in dwide]
     one_row = jnp.ones((8, D), BF)
     means = [(dots(one_row, e2[0], 1, 1) + dots(one_row, e2[1], 1, 1))[0:1] for e2 in e]
-    dp = [nt3(v2, d2) for v2, d2 in zip(v, d)]
+    dp = [nt3_narrow(v2, d2) for v2, d2 in zip(v, d)]
     ds = [split2(p * (x - mean)) for p, x, mean in zip(probs, dp, means)]
-    dk = jnp.concatenate([nn3(s2, q2) for s2, q2 in zip(ds, q)], 0)
-    dv = jnp.concatenate([nn3(split2(p), d2) for p, d2 in zip(probs, d)], 0)
-    dq = jnp.concatenate([gather_rows(tn3(s2, k2)) for s2, k2 in zip(ds, k)], 0) * SCALE
+    dk = jnp.concatenate([nn3_short(s2, q2) for s2, q2 in zip(ds, q)], 0)
+    dv = jnp.concatenate([nn3_short(split2(p), d2) for p, d2 in zip(probs, d)], 0)
+    dq = jnp.concatenate([gather_rows(tn3_short(s2, k2)) for s2, k2 in zip(ds, k)], 0) * SCALE
     dk2 = split2(dk)
     dv2 = split2(dv)
     rows[1] += colsum(dv)

time: 732 us -> 618 us (0.84)
  Pallas kernels: 709 us -> 594 us
    pallas_call x2, Pallas kernels: 204 us -> 97.1 us  [time_bwd(): pl.pallas_call(functools.partial(time_bwd_kernel, first, count, group, la...]
where the time goes in v8:
time: 618 us; the launch traced here: 610 us
  Pallas kernels  594 us (96%)
  local copies, waits for them, and re-layouts  6.79 us (1%)
    pallas_call x2, Pallas kernels, time_bwd(): pl.pallas_call(functools.partial(time_bwd_kernel, first, count, group, la...  97.1 us
    pallas_call x1, Pallas kernels, scatter_sum(): pl.pallas_call(functools.partial(scatter_kernel, shapes), in_specs=[ANY]...  81.7 us
    pallas_call x2, Pallas kernels, group_sum(): pl.pallas_call(functools.partial(sum_kernel, per, steps - steps // 4), gr...  70.3 us
    pallas_call x2, Pallas kernels, group_stats(): pl.pallas_call(functools.partial(stats_kernel, per), in_specs=[ANY], out_...  64.3 us
    pallas_call x2, Pallas kernels, time_fwd(): pl.pallas_call(functools.partial(time_fwd_kernel, first, count, group), g...  58.8 us
    pallas_call x1, Pallas kernels, gather_all(): pl.pallas_call(functools.partial(gather_kernel, n), in_specs=[ANY] * n, o...  50.1 us
    pallas_call x1, Pallas kernels, recv_bwd(): pl.pallas_call(functools.partial(recv_bwd_kernel, sb), grid=(n // sb,), i...  43.6 us
    pallas_call x2, Pallas kernels, send_bwd(): pl.pallas_call(functools.partial(send_bwd_kernel, sb, layer), grid=(n //...  39.8 us

profile of v8, /device:TPU:0, one launch (start us, length us, event | category | flops | bytes accessed | tf_op | source)
XLA Modules:
  0.0 610.1 jit_solution(8561944132255968335)
XLA Ops:
  0.6 1.4 pad_bitcast_fusion.vec_ref
  2.7 4.6 prepare.1
  7.2 50.1 %gather_all.1 = (bf16[2,2,4,2,208,256]{5,4,3,2,1,0:T(8,128)(2,1)}, bf16[2,2,4,2,128,256]{5,4,3,2,1,0:T(8,128)(2,1)}, bf16[2,2,4,2,33,256]{5,4,3,2,1,0:T(8,128)(2,1)}) custom-call(bf16[208,256]{1,0:T(8,128)(2,1)} %get-tuple-element.111.refs_0_, bf16[128,256]{1,0:T(8,128)(2,1)} %get-tuple-element.112.refs_1_, bf16[33,256]{1,0:T(8,128)(2,1)} %get-tuple-element.113.refs_2_), custom_call_target="tpu_custom_call" | custom-call | tf_op jit(solution)/shard_map/gather_all/pallas_call | solution.py:1102
  57.4 2.7 unpack_vectors.1
  60.0 1.3 slice.21
  61.3 1.3 reshape.78.refs_7_.refs_5_.refs_15_.refs_11_.refs_17_
  62.6 35.6 %time_fwd.2 = (f32[60,64,256]{2,1,0:T(8,128)}, f32[8,2,512,128]{3,2,1,0:T(8,128)}, f32[8,2,512,128]{3,2,1,0:T(8,128)}, f32[8,2,512,128]{3,2,1,0:T(8,128)}, f32[8...) custom-call(f32[60,64,16]{2,1,0:T(8,128)} %get-tuple-element.110.ref, ...), custom_call_target="tpu_custom_call" | custom-call | tf_op jit(solution)/shard_map/time_fwd/pallas_call | solution.py:367
  98.2 10.0 %send_fwd.2.in_ref = f32[64,24,128]{2,1,0:T(8,128)} custom-call(f32[60,64,256]{2,1,0:T(8,128)} %get-tuple-element.120.dim_ref.send_ref, f32[60,16,256]{2,1,0:T(8,128)} %get-tuple-element.121.r_ref, f32[64,128]{1,0:T(8,128)} %get-tuple-element.122.here_ref, bf16[26,256,256]{2,1,0:T(8,128)(2,1)} %bitcast.30, bf16[26,256,256]{2,1,0:T(8,128)(2,1)} %bitcast.31, ...), custom_call_target="tpu_custom_call" | custom-call | tf_op jit(solution)/shard_map/send_fwd/pallas_call | solution.py:882
  108.2 37.9 %group_stats.2.o_ref = f32[64,24,128]{2,1,0:T(8,128)} custom-call(f32[64,24,128]{2,1,0:T(8,128)} %send_fwd.2.in_ref), custom_call_target="tpu_custom_call" | custom-call | tf_op jit(solution)/shard_map/group_stats/pallas_call | solution.py:1412
  146.1 26.2 %recv_fwd.1 = (f32[30,64,256]{2,1,0:T(8,128)}, f32[3840,256]{1,0:T(8,128)}, f32[3840,256]{1,0:T(8,128)}, f32[3840,128]{1,0:T(8,128)}, f32[3840,256]{1,0:T(8,128)...) custom-call(f32[60,64,256]{2,1,0:T(8,128)} %get-tuple-element.120.dim_ref.send_ref, f32[64,24,128]{2,1,0:T(8,128)} %group_stats.2.o_ref, ...), custom_call_target="tpu_custom_call" | custom-call | tf_op jit(solution)/shard_map/recv_fwd/pallas_call | solution.py:703
  172.3 23.2 %time_fwd.3 = (f32[30,64,256]{2,1,0:T(8,128)}, f32[8,2,256,128]{3,2,1,0:T(8,128)}, f32[8,2,256,128]{3,2,1,0:T(8,128)}, f32[8,2,256,128]{3,2,1,0:T(8,128)}, f32[8...) custom-call(f32[30,64,256]{2,1,0:T(8,128)} %get-tuple-element.124.re, ...), custom_call_target="tpu_custom_call" | custom-call | tf_op jit(solution)/shard_map/time_fwd/pallas_call | solution.py:367
  195.5 6.7 %send_fwd.3.in_ref = f32[32,24,128]{2,1,0:T(8,128)} custom-call(f32[30,64,256]{2,1,0:T(8,128)} %get-tuple-element.125.dim_ref.send_ref, f32[30,16,256]{2,1,0:T(8,128)} %get-tuple-element.126.r_ref, f32[64,128]{1,0:T(8,128)} %get-tuple-element.122.here_ref, bf16[26,256,256]{2,1,0:T(8,128)(2,1)} %bitcast.43, bf16[26,256,256]{2,1,0:T(8,128)(2,1)} %bitcast.44, ...), custom_call_target="tpu_custom_call" | custom-call | tf_op jit(solution)/shard_map/send_fwd/pallas_call | solution.py:882
  202.1 26.4 %group_stats.3.o_ref = f32[32,24,128]{2,1,0:T(8,128)} custom-call(f32[32,24,128]{2,1,0:T(8,128)} %send_fwd.3.in_ref), custom_call_target="tpu_custom_call" | custom-call | tf_op jit(solution)/shard_map/group_stats/pallas_call | solution.py:1412
  228.5 34.6 %tail.1 = (f32[26,256,256]{2,1,0:T(8,128)}, f32[4096,256]{1,0:T(8,128)}, f32[30,64,256]{2,1,0:T(8,128)}, f32[32,24,128]{2,1,0:T(8,128)}, f32[11,8,256]{2,1,0:T(8...) custom-call(f32[30,64,256]{2,1,0:T(8,128)} %get-tuple-element.125.di, ...), custom_call_target="tpu_custom_call" | custom-call | tf_op jit(solution)/shard_map/tail/pallas_call | solution.py:824
  263.2 28.9 %group_sum.2 = (f32[32,24,128]{2,1,0:T(8,128)}, f32[256,256]{1,0:T(8,128)}, f32[256,256]{1,0:T(8,128)}, f32[256,512]{1,0:T(8,128)}, f32[512,256]{1,0:T(8,128)}) custom-call(f32[32,24,128]{2,1,0:T(8,128)} %get-tuple-element.133.in_ref, f32[1920,256]{1,0:T(8,128)} %bitcast.81, f32[1920,256]{1,0:T(8,128)} %get-tuple-element.134.mixed_ref, ...), custom_call_target="tpu_custom_call" | custom-call | tf_op jit(solution)/shard_map/group_sum/pallas_call | solution.py:1429
  292.1 14.7 %send_bwd.2 = (f32[26,256,256]{2,1,0:T(8,128)}, f32[30,64,256]{2,1,0:T(8,128)}, f32[30,16,256]{2,1,0:T(8,128)}, f32[2,8,256]{2,1,0:T(8,128)}) custom-call(f32[30,64,256]{2,1,0:T(8,128)} %get-tuple-element.125.dim_ref.send_ref, f32[30,64,256]{2,1,0:T(8,128)} %get-tuple-element.132.dpart_ref, ...), custom_call_target="tpu_custom_call", output_to_operand_aliasing={{0}: (10, {})} | custom-call | tf_op jit(solution)/shard_map/send_bwd/pallas_call | solution.py:946
  306.8 34.6 %time_bwd.2 = (f32[26,256,256]{2,1,0:T(8,128)}, f32[4096,256]{1,0:T(8,128)}, f32[10,8,256]{2,1,0:T(8,128)}, f32[30,64,256]{2,1,0:T(8,128)}) custom-call(f32[30,64,256]{2,1,0:T(8,128)} %get-tuple-element.124.refs_0_, f32[30,64,256]{2,1,0:T(8,128)} %get-tuple-element.143.refs_1_, ...), custom_call_target="tpu_custom_call", output_to_operand_aliasing={{0}: (22, {}), {1}: (23, {})} | custom-call | tf_op jit(solution)/shard_map/time_bwd/pallas_call | solution.py:490
  341.5 43.6 %recv_bwd.1 = (f32[26,256,256]{2,1,0:T(8,128)}, f32[60,64,256]{2,1,0:T(8,128)}, f32[64,24,128]{2,1,0:T(8,128)}, f32[11,8,256]{2,1,0:T(8,128)}, f32[5,8,256]{2,1,...) custom-call(f32[60,64,256]{2,1,0:T(8,128)} %get-tuple-element.120.di, ...), custom_call_target="tpu_custom_call", output_to_operand_aliasing={{0}: (19, {})} | custom-call | tf_op jit(solution)/shard_map/recv_bwd/pallas_call | solution.py:771
  385.1 41.4 %group_sum.3 = (f32[64,24,128]{2,1,0:T(8,128)}, f32[256,256]{1,0:T(8,128)}, f32[256,256]{1,0:T(8,128)}, f32[256,512]{1,0:T(8,128)}, f32[512,256]{1,0:T(8,128)}) custom-call(f32[64,24,128]{2,1,0:T(8,128)} %get-tuple-element.168.in_ref, f32[3840,256]{1,0:T(8,128)} %bitcast.79, f32[3840,256]{1,0:T(8,128)} %get-tuple-element.161.refs_1_.mixed_ref, ...), custom_call_target="tpu_custom_call" | custom-call | tf_op jit(solution)/shard_map/group_sum/pallas_call | solution.py:1429
  426.5 25.1 %send_bwd.3 = (f32[26,256,256]{2,1,0:T(8,128)}, f32[60,64,256]{2,1,0:T(8,128)}, f32[60,16,256]{2,1,0:T(8,128)}, f32[2,8,256]{2,1,0:T(8,128)}) custom-call(f32[60,64,256]{2,1,0:T(8,128)} %get-tuple-element.120.dim_ref.send_ref, f32[60,64,256]{2,1,0:T(8,128)} %get-tuple-element.167.dpart_ref, ...), custom_call_target="tpu_custom_call", output_to_operand_aliasing={{0}: (10, {})} | custom-call | tf_op jit(solution)/shard_map/send_bwd/pallas_call | solution.py:946
  451.6 62.5 %time_bwd.3 = (f32[26,256,256]{2,1,0:T(8,128)}, f32[4096,256]{1,0:T(8,128)}, f32[10,8,256]{2,1,0:T(8,128)}, f32[16,256]{1,0:T(8,128)}, f32[480,256]{1,0:T(8,128)}) custom-call(f32[60,64,16]{2,1,0:T(8,128)} %get-tuple-element.110.refs_0_, bf16[16,256]{1,0:T(8,128)(2,1)} %get-tuple-element.115.refs_1_, ...), custom_call_target="tpu_custom_call", output_to_operand_aliasing={{0}: (24, {}), {1}: (25, {})} | custom-call | tf_op jit(solution)/shard_map/time_bwd/pallas_call | solution.py:490
  514.1 3.6 assemble_vectors.1
  517.7 0.0 copy-start.4
  517.7 0.0 copy-start.7
  517.7 0.0 copy-start.8
  517.7 0.0 copy-start.1
  517.7 0.0 copy-start.5
  517.7 0.0 copy-start.6
  517.8 0.0 copy-start
  517.8 0.0 copy-start.2
  517.8 0.0 copy-start.3
  517.8 81.7 %scatter_sum.1 = (f32[208,256]{1,0:T(8,128)}, f32[128,256]{1,0:T(8,128)}, f32[33,256]{1,0:T(8,128)}, f32[16,128]{1,0:T(8,128)}) custom-call(f32[2,2,4,2,208,256]{5,4,3,2,1,0:T(8,128)} %bitcast.71, f32[2,2,4,2,128,256]{5,4,3,2,1,0:T(8,128)} %bitcast.80, f32[2,2,4,2,33,256]{5,4,3,2,1,0:T(8,128)} %bitcast.82, f32[8,128]{1,0:T(8,128)} %get-tuple-element.205.refs_3_), custom_call_target="tpu_custom_call" | custom-call | tf_op jit(solution)/shard_map/scatter_sum/pallas_call | solution.py:1275
  599.5 0.8 reshape.86
  600.3 1.3 slice_reduce_fusion
  603.0 0.0 copy-done.4
  603.0 0.0 copy-done.7
  603.0 0.0 copy-done.8
  603.0 0.7 multiply_subtract_fusion.2
  603.7 0.9 fusion.6
  604.6 1.0 copy.33
  605.6 0.0 copy-done.1
  605.6 0.0 copy-done.5
  605.6 0.0 copy-done.6
  605.6 0.8 multiply_subtract_fusion.1
  606.5 0.9 multiply_bitcast_fusion
  607.4 0.1 copy.31
  607.5 0.0 copy-done
  607.5 0.0 copy-done.2
  607.5 0.0 copy-done.3
  607.6 0.9 multiply_subtract_fusion
  (2 shorter events, 0.0 us)
Async XLA Ops:
  517.7 85.3 %copy-start.4 = (f32[8288]{0:T(1024)S(1)}, f32[8288]{0:T(1024)}, u32[]{:S(2)}) copy-start(f32[8288]{0:T(1024)} %param.21) | copy-start | bytes 99460
  517.7 85.3 %copy-start.7 = (f32[8288]{0:T(1024)S(1)}, f32[8288]{0:T(1024)}, u32[]{:S(2)}) copy-start(f32[8288]{0:T(1024)} %param.26) | copy-start | bytes 99460
  517.7 85.3 %copy-start.8 = (f32[8288]{0:T(1024)S(1)}, f32[8288]{0:T(1024)}, u32[]{:S(2)}) copy-start(f32[8288]{0:T(1024)} %param.27) | copy-start | bytes 99460
  517.7 87.9 %copy-start.1 = (f32[32768]{0:T(1024)S(1)}, f32[32768]{0:T(1024)}, u32[]{:S(2)}) copy-start(f32[32768]{0:T(1024)} %param.20) | copy-start | bytes 393220
  517.7 87.9 %copy-start.5 = (f32[32768]{0:T(1024)S(1)}, f32[32768]{0:T(1024)}, u32[]{:S(2)}) copy-start(f32[32768]{0:T(1024)} %param.24) | copy-start | bytes 393220
  517.7 87.9 %copy-start.6 = (f32[32768]{0:T(1024)S(1)}, f32[32768]{0:T(1024)}, u32[]{:S(2)}) copy-start(f32[32768]{0:T(1024)} %param.25) | copy-start | bytes 393220
  517.8 89.8 %copy-start = (f32[53248]{0:T(1024)S(1)}, f32[53248]{0:T(1024)}, u32[]{:S(2)}) copy-start(f32[53248]{0:T(1024)} %param.19) | copy-start | bytes 638980
  517.8 89.8 %copy-start.2 = (f32[53248]{0:T(1024)S(1)}, f32[53248]{0:T(1024)}, u32[]{:S(2)}) copy-start(f32[53248]{0:T(1024)} %param.22) | copy-start | bytes 638980
  517.8 89.8 %copy-start.3 = (f32[53248]{0:T(1024)S(1)}, f32[53248]{0:T(1024)}, u32[]{:S(2)}) copy-start(f32[53248]{0:T(1024)} %param.23) | copy-start | bytes 638980

commit v9 on v8

--- a/solution.py
+++ b/solution.py
@@ -536,9 +536,21 @@
     return jnp.concatenate([unpack_rows(ref[s]) for s in range(sb)], 0)
 
 
+TALL = 2 * ROUT
+
+
+def tall_spec(sb):
+    return pl.BlockSpec((sb * TALL, HALF), lambda i: (i, 0))
+
+
+def tall_rows(n, parts):
+    return -(-n * TALL // (8 * parts)) * 8 * parts
+
+
 def pack_block(ref, x, sb):
     for s in range(sb):
-        ref[s] = pack_rows(x[s * RPAD : (s + 1) * RPAD])
+        rows = x[s * RPAD : s * RPAD + ROUT]
+        ref[s * TALL : (s + 1) * TALL] = jnp.concatenate([rows[:, :HALF], rows[:, HALF:]], 0)
 
 
 def valid_lane(rows):
@@ -762,7 +774,7 @@
     )
 
 
-def recv_bwd(send, o, dx, kept, model, mvec, sb, g_mat):
+def recv_bwd(send, o, dx, kept, model, mvec, sb, g_mat, parts):
     n = send.shape[0]
     squares = recv_squares(0)
     shapes = [(11, 8, D), (5, 8, D)]
@@ -772,9 +784,9 @@
         functools.partial(recv_bwd_kernel, sb),
         grid=(n // sb,),
         in_specs=specs + [ANY],
-        out_specs=[ANY, seg_block(sb), pack_spec(sb)] + [whole(s) for s in shapes] + row_specs(sb, LATER_WIDTHS),
+        out_specs=[ANY, seg_block(sb), tall_spec(sb)] + [whole(s) for s in shapes] + row_specs(sb, LATER_WIDTHS),
         out_shape=pack_shapes()[:1]
-        + [jax.ShapeDtypeStruct((n, SB_ROWS, D), F32), jax.ShapeDtypeStruct(o.shape, F32)]
+        + [jax.ShapeDtypeStruct((n, SB_ROWS, D), F32), jax.ShapeDtypeStruct((tall_rows(n, parts), HALF), F32)]
         + [jax.ShapeDtypeStruct(s, F32) for s in shapes]
         + row_shapes(n, LATER_WIDTHS),
         input_output_aliases={len(specs): 0},
@@ -817,7 +829,7 @@
     recv_flush(accs, [], 1, g_mat, sems)
 
 
-def tail(send, o, tgt, kept, scale, mean, model, head, sb):
+def tail(send, o, tgt, kept, scale, mean, model, head, sb, parts):
     n = send.shape[0]
     squares = recv_squares(1)
     shapes = [(11, 8, D), (PPAD, D)]
@@ -828,10 +840,10 @@
         + [whole((SB_ROWS, PPAD))] * 2
         + weight_specs(squares, 3, 1)
         + [whole((PPAD, D))],
-        out_specs=[ANY] * 2 + [seg_block(sb), pack_spec(sb)] + [whole(s) for s in shapes]
+        out_specs=[ANY] * 2 + [seg_block(sb), tall_spec(sb)] + [whole(s) for s in shapes]
         + row_specs(sb, (D, D, FF) + LATER_WIDTHS),
         out_shape=pack_shapes()
-        + [jax.ShapeDtypeStruct((n, SB_ROWS, D), F32), jax.ShapeDtypeStruct(o.shape, F32)]
+        + [jax.ShapeDtypeStruct((n, SB_ROWS, D), F32), jax.ShapeDtypeStruct((tall_rows(n, parts), HALF), F32)]
         + [jax.ShapeDtypeStruct(s, F32) for s in shapes]
         + row_shapes(n, (D, D, FF) + LATER_WIDTHS),
         scratch_shapes=RECV_ACC + [pltpu.SemaphoreType.DMA((3,))],
@@ -908,7 +920,7 @@
     segs = range(sb)
     scores = [nt3_narrow(k2, q2) for k2, q2 in zip(k, q)]
     probs = [jnp.where(here, jnp.exp(scores[s] - o_ref[s][2 * ROUT : 2 * ROUT + 1]), 0.0) for s in segs]
-    dwide = [spread_rows(unpack_rows(do_ref[s])) for s in segs]
+    dwide = [spread_rows(unpack_rows(do_ref[s * TALL : (s + 1) * TALL])) for s in segs]
     owide = [
         jnp.broadcast_to(unpack_rows(o_ref[s])[:, None, :], (RPAD, HEADS, D)).reshape(RPAD * HEADS, D) for s in segs
     ]
@@ -941,7 +953,7 @@
 def send_bwd(dim, dpart, routers, o, do, here, model, layer, sb, g_mat):
     n = dim.shape[0]
     squares = send_squares(layer)
-    specs = [seg_block(sb), seg_block(sb), seg_block(sb, RPAD), pack_spec(sb), pack_spec(sb), whole((SB_ROWS, HALF))]
+    specs = [seg_block(sb), seg_block(sb), seg_block(sb, RPAD), pack_spec(sb), tall_spec(sb), whole((SB_ROWS, HALF))]
     specs += weight_specs(squares, None, layer)
     return pl.pallas_call(
         functools.partial(send_bwd_kernel, sb, layer),
@@ -1392,10 +1404,10 @@
         wait_all(group_back(per, result, out_ref, send, recv, local))
 
 
-def group_scratch(per, nf):
+def group_scratch(part, nf):
     return [
-        pltpu.VMEM((nf, per, PACK, HALF), F32),
-        pltpu.VMEM((per, PACK, HALF), F32),
+        pltpu.VMEM((nf,) + part, F32),
+        pltpu.VMEM(part, F32),
         pltpu.SemaphoreType.DMA((2 * nf - 2,)),
         pltpu.SemaphoreType.DMA((2 * nf - 2,)),
         pltpu.SemaphoreType.DMA,
@@ -1414,7 +1426,7 @@
         in_specs=[ANY],
         out_specs=ANY,
         out_shape=jax.ShapeDtypeStruct(packed.shape, F32),
-        scratch_shapes=group_scratch(per, nf),
+        scratch_shapes=group_scratch((per, PACK, HALF), nf),
         compiler_params=group_params(cid),
         name="group_stats",
     )(packed)
@@ -1432,7 +1444,7 @@
         in_specs=[ANY] + [pl.BlockSpec((rows, w.shape[1]), lambda i: (i, 0)) for w in work] + [pick((24, D), layer)],
         out_specs=[ANY] + [whole(s) for s in shapes],
         out_shape=[jax.ShapeDtypeStruct(packed.shape, F32)] + [jax.ShapeDtypeStruct(s, F32) for s in shapes],
-        scratch_shapes=group_scratch(per, nf),
+        scratch_shapes=group_scratch((per, HALF), nf),
         compiler_params=group_params(cid),
         name="group_sum",
     )(packed, *work, vecs)
@@ -1609,13 +1621,13 @@
     o1 = send_fwd(dim1, routers1, here, model, 1, sf1, -(-half // nf) * nf)
     o1 = group_stats(o1, 3)
     vecs = model[3]
-    g_mat, g_feed, ddim1, do1, rr1, dhead, *work = tail(dim1, o1, tgt, kept, scale, mean, model, head, st)
+    g_mat, g_feed, ddim1, do1, rr1, dhead, *work = tail(dim1, o1, tgt, kept, scale, mean, model, head, st, nf)
     do1, *later = group_sum(do1, [dim1.reshape(-1, D)] + work, vecs, 1, 4)
     g_mat, ddim1, dr1, rs1 = send_bwd(dim1, ddim1, routers1, o1, do1, here, model, 1, sb1, g_mat)
     g_mat, g_feed, rt1, dx1 = time_bwd(
         False, x1, (), ddim1, kept1, model, 1, half, later, (g_mat, g_feed), up_rows
     )
-    g_mat, ddim0, do0, rr0, dmv, *work = recv_bwd(dim0, o0, dx1, saved, model, mvec, rb, g_mat)
+    g_mat, ddim0, do0, rr0, dmv, *work = recv_bwd(dim0, o0, dx1, saved, model, mvec, rb, g_mat, nf)
     work = [dim0.reshape(-1, D), saved[1], saved[3], saved[4]] + work
     do0, *later = group_sum(do0, work, vecs, 0, 5)
     g_mat, ddim0, dr0, rs0 = send_bwd(dim0, ddim0, routers0, o0, do0, here, model, 0, sb0, g_mat)

time: 618 us -> 608 us (0.984)
  Pallas kernels: 594 us -> 584 us
    pallas_call x2, Pallas kernels: 70.3 us -> 61.1 us  [group_sum(): pl.pallas_call(functools.partial(sum_kernel, per, steps - steps // 4), gr...]
where the time goes in v9:
time: 608 us; the launch traced here: 600 us
  Pallas kernels  584 us (96%)
  local copies, waits for them, and re-layouts  6.79 us (1%)
    pallas_call x2, Pallas kernels, time_bwd(): pl.pallas_call(functools.partial(time_bwd_kernel, first, count, group, la...  97.1 us
    pallas_call x1, Pallas kernels, scatter_sum(): pl.pallas_call(functools.partial(scatter_kernel, shapes), in_specs=[ANY]...  81.2 us
    pallas_call x2, Pallas kernels, group_stats(): pl.pallas_call(functools.partial(stats_kernel, per), in_specs=[ANY], out_...  64.3 us
    pallas_call x2, Pallas kernels, group_sum(): pl.pallas_call(functools.partial(sum_kernel, per, steps - steps // 4), gr...  61.1 us
    pallas_call x2, Pallas kernels, time_fwd(): pl.pallas_call(functools.partial(time_fwd_kernel, first, count, group), g...  58.8 us
    pallas_call x1, Pallas kernels, gather_all(): pl.pallas_call(functools.partial(gather_kernel, n), in_specs=[ANY] * n, o...  50.1 us
    pallas_call x1, Pallas kernels, recv_bwd(): pl.pallas_call(functools.partial(recv_bwd_kernel, sb), grid=(n // sb,), i...  43.6 us
    pallas_call x2, Pallas kernels, send_bwd(): pl.pallas_call(functools.partial(send_bwd_kernel, sb, layer), grid=(n //...  39.8 us

profile of v9, /device:TPU:0, one launch (start us, length us, event | category | flops | bytes accessed | tf_op | source)
XLA Modules:
  0.0 600.3 jit_solution(3746922279344056091)
XLA Ops:
  0.6 1.4 pad_bitcast_fusion.vec_ref
  2.7 4.6 prepare.1
  7.2 50.1 %gather_all.1 = (bf16[2,2,4,2,208,256]{5,4,3,2,1,0:T(8,128)(2,1)}, bf16[2,2,4,2,128,256]{5,4,3,2,1,0:T(8,128)(2,1)}, bf16[2,2,4,2,33,256]{5,4,3,2,1,0:T(8,128)(2,1)}) custom-call(bf16[208,256]{1,0:T(8,128)(2,1)} %get-tuple-element.111.refs_0_, bf16[128,256]{1,0:T(8,128)(2,1)} %get-tuple-element.112.refs_1_, bf16[33,256]{1,0:T(8,128)(2,1)} %get-tuple-element.113.refs_2_), custom_call_target="tpu_custom_call" | custom-call | tf_op jit(solution)/shard_map/gather_all/pallas_call | solution.py:1114
  57.4 2.7 unpack_vectors.1
  60.0 1.3 slice.21
  61.3 1.3 reshape.78.refs_7_.refs_5_.refs_15_.refs_11_.refs_17_
  62.6 35.6 %time_fwd.2 = (f32[60,64,256]{2,1,0:T(8,128)}, f32[8,2,512,128]{3,2,1,0:T(8,128)}, f32[8,2,512,128]{3,2,1,0:T(8,128)}, f32[8,2,512,128]{3,2,1,0:T(8,128)}, f32[8...) custom-call(f32[60,64,16]{2,1,0:T(8,128)} %get-tuple-element.110.ref, ...), custom_call_target="tpu_custom_call" | custom-call | tf_op jit(solution)/shard_map/time_fwd/pallas_call | solution.py:367
  98.2 10.0 %send_fwd.2.in_ref = f32[64,24,128]{2,1,0:T(8,128)} custom-call(f32[60,64,256]{2,1,0:T(8,128)} %get-tuple-element.120.dim_ref.send_ref, f32[60,16,256]{2,1,0:T(8,128)} %get-tuple-element.121.r_ref, f32[64,128]{1,0:T(8,128)} %get-tuple-element.122.here_ref, bf16[26,256,256]{2,1,0:T(8,128)(2,1)} %bitcast.30, bf16[26,256,256]{2,1,0:T(8,128)(2,1)} %bitcast.31, ...), custom_call_target="tpu_custom_call" | custom-call | tf_op jit(solution)/shard_map/send_fwd/pallas_call | solution.py:894
  108.2 37.9 %group_stats.2.o_ref = f32[64,24,128]{2,1,0:T(8,128)} custom-call(f32[64,24,128]{2,1,0:T(8,128)} %send_fwd.2.in_ref), custom_call_target="tpu_custom_call" | custom-call | tf_op jit(solution)/shard_map/group_stats/pallas_call | solution.py:1424
  146.1 26.2 %recv_fwd.1 = (f32[30,64,256]{2,1,0:T(8,128)}, f32[3840,256]{1,0:T(8,128)}, f32[3840,256]{1,0:T(8,128)}, f32[3840,128]{1,0:T(8,128)}, f32[3840,256]{1,0:T(8,128)...) custom-call(f32[60,64,256]{2,1,0:T(8,128)} %get-tuple-element.120.dim_ref.send_ref, f32[64,24,128]{2,1,0:T(8,128)} %group_stats.2.o_ref, ...), custom_call_target="tpu_custom_call" | custom-call | tf_op jit(solution)/shard_map/recv_fwd/pallas_call | solution.py:715
  172.3 23.2 %time_fwd.3 = (f32[30,64,256]{2,1,0:T(8,128)}, f32[8,2,256,128]{3,2,1,0:T(8,128)}, f32[8,2,256,128]{3,2,1,0:T(8,128)}, f32[8,2,256,128]{3,2,1,0:T(8,128)}, f32[8...) custom-call(f32[30,64,256]{2,1,0:T(8,128)} %get-tuple-element.124.re, ...), custom_call_target="tpu_custom_call" | custom-call | tf_op jit(solution)/shard_map/time_fwd/pallas_call | solution.py:367
  195.5 6.7 %send_fwd.3.in_ref = f32[32,24,128]{2,1,0:T(8,128)} custom-call(f32[30,64,256]{2,1,0:T(8,128)} %get-tuple-element.125.dim_ref.send_ref, f32[30,16,256]{2,1,0:T(8,128)} %get-tuple-element.126.r_ref, f32[64,128]{1,0:T(8,128)} %get-tuple-element.122.here_ref, bf16[26,256,256]{2,1,0:T(8,128)(2,1)} %bitcast.43, bf16[26,256,256]{2,1,0:T(8,128)(2,1)} %bitcast.44, ...), custom_call_target="tpu_custom_call" | custom-call | tf_op jit(solution)/shard_map/send_fwd/pallas_call | solution.py:894
  202.1 26.4 %group_stats.3.o_ref = f32[32,24,128]{2,1,0:T(8,128)} custom-call(f32[32,24,128]{2,1,0:T(8,128)} %send_fwd.3.in_ref), custom_call_target="tpu_custom_call" | custom-call | tf_op jit(solution)/shard_map/group_stats/pallas_call | solution.py:1424
  228.5 34.6 %tail.1 = (f32[26,256,256]{2,1,0:T(8,128)}, f32[4096,256]{1,0:T(8,128)}, f32[30,64,256]{2,1,0:T(8,128)}, f32[640,128]{1,0:T(8,128)}, f32[11,8,256]{2,1,0:T(8,128...) custom-call(f32[30,64,256]{2,1,0:T(8,128)} %get-tuple-element.125.di, ...), custom_call_target="tpu_custom_call" | custom-call | tf_op jit(solution)/shard_map/tail/pallas_call | solution.py:836
  263.2 25.6 %group_sum.2 = (f32[640,128]{1,0:T(8,128)}, f32[256,256]{1,0:T(8,128)}, f32[256,256]{1,0:T(8,128)}, f32[256,512]{1,0:T(8,128)}, f32[512,256]{1,0:T(8,128)}) custom-call(f32[640,128]{1,0:T(8,128)} %get-tuple-element.133.in_ref, f32[1920,256]{1,0:T(8,128)} %bitcast.81, f32[1920,256]{1,0:T(8,128)} %get-tuple-element.134.mixed_ref, ...), custom_call_target="tpu_custom_call" | custom-call | tf_op jit(solution)/shard_map/group_sum/pallas_call | solution.py:1441
  288.8 14.7 %send_bwd.2 = (f32[26,256,256]{2,1,0:T(8,128)}, f32[30,64,256]{2,1,0:T(8,128)}, f32[30,16,256]{2,1,0:T(8,128)}, f32[2,8,256]{2,1,0:T(8,128)}) custom-call(f32[30,64,256]{2,1,0:T(8,128)} %get-tuple-element.125.dim_ref.send_ref, f32[30,64,256]{2,1,0:T(8,128)} %get-tuple-element.132.dpart_ref, ...), custom_call_target="tpu_custom_call", output_to_operand_aliasing={{0}: (10, {})} | custom-call | tf_op jit(solution)/shard_map/send_bwd/pallas_call | solution.py:958
  303.5 34.6 %time_bwd.2 = (f32[26,256,256]{2,1,0:T(8,128)}, f32[4096,256]{1,0:T(8,128)}, f32[10,8,256]{2,1,0:T(8,128)}, f32[30,64,256]{2,1,0:T(8,128)}) custom-call(f32[30,64,256]{2,1,0:T(8,128)} %get-tuple-element.124.refs_0_, f32[30,64,256]{2,1,0:T(8,128)} %get-tuple-element.143.refs_1_, ...), custom_call_target="tpu_custom_call", output_to_operand_aliasing={{0}: (22, {}), {1}: (23, {})} | custom-call | tf_op jit(solution)/shard_map/time_bwd/pallas_call | solution.py:490
  338.1 43.6 %recv_bwd.1 = (f32[26,256,256]{2,1,0:T(8,128)}, f32[60,64,256]{2,1,0:T(8,128)}, f32[1216,128]{1,0:T(8,128)}, f32[11,8,256]{2,1,0:T(8,128)}, f32[5,8,256]{2,1,0:T...) custom-call(f32[60,64,256]{2,1,0:T(8,128)} %get-tuple-element.120.di, ...), custom_call_target="tpu_custom_call", output_to_operand_aliasing={{0}: (19, {})} | custom-call | tf_op jit(solution)/shard_map/recv_bwd/pallas_call | solution.py:783
  381.7 35.4 %group_sum.3 = (f32[1216,128]{1,0:T(8,128)}, f32[256,256]{1,0:T(8,128)}, f32[256,256]{1,0:T(8,128)}, f32[256,512]{1,0:T(8,128)}, f32[512,256]{1,0:T(8,128)}) custom-call(f32[1216,128]{1,0:T(8,128)} %get-tuple-element.168.in_ref, f32[3840,256]{1,0:T(8,128)} %bitcast.79, f32[3840,256]{1,0:T(8,128)} %get-tuple-element.161.refs_1_.mixed_ref, ...), custom_call_target="tpu_custom_call" | custom-call | tf_op jit(solution)/shard_map/group_sum/pallas_call | solution.py:1441
  417.2 25.1 %send_bwd.3 = (f32[26,256,256]{2,1,0:T(8,128)}, f32[60,64,256]{2,1,0:T(8,128)}, f32[60,16,256]{2,1,0:T(8,128)}, f32[2,8,256]{2,1,0:T(8,128)}) custom-call(f32[60,64,256]{2,1,0:T(8,128)} %get-tuple-element.120.dim_ref.send_ref, f32[60,64,256]{2,1,0:T(8,128)} %get-tuple-element.167.dpart_ref, ...), custom_call_target="tpu_custom_call", output_to_operand_aliasing={{0}: (10, {})} | custom-call | tf_op jit(solution)/shard_map/send_bwd/pallas_call | solution.py:958
  442.3 62.5 %time_bwd.3 = (f32[26,256,256]{2,1,0:T(8,128)}, f32[4096,256]{1,0:T(8,128)}, f32[10,8,256]{2,1,0:T(8,128)}, f32[16,256]{1,0:T(8,128)}, f32[480,256]{1,0:T(8,128)}) custom-call(f32[60,64,16]{2,1,0:T(8,128)} %get-tuple-element.110.refs_0_, bf16[16,256]{1,0:T(8,128)(2,1)} %get-tuple-element.115.refs_1_, ...), custom_call_target="tpu_custom_call", output_to_operand_aliasing={{0}: (24, {}), {1}: (25, {})} | custom-call | tf_op jit(solution)/shard_map/time_bwd/pallas_call | solution.py:490
  504.9 3.6 assemble_vectors.1
  508.4 0.0 copy-start.4
  508.4 0.0 copy-start.7
  508.4 0.0 copy-start.8
  508.4 0.0 copy-start.1
  508.5 0.0 copy-start.5
  508.5 0.0 copy-start.6
  508.5 0.0 copy-start
  508.5 0.0 copy-start.2
  508.5 0.0 copy-start.3
  508.5 81.2 %scatter_sum.1 = (f32[208,256]{1,0:T(8,128)}, f32[128,256]{1,0:T(8,128)}, f32[33,256]{1,0:T(8,128)}, f32[16,128]{1,0:T(8,128)}) custom-call(f32[2,2,4,2,208,256]{5,4,3,2,1,0:T(8,128)} %bitcast.71, f32[2,2,4,2,128,256]{5,4,3,2,1,0:T(8,128)} %bitcast.80, f32[2,2,4,2,33,256]{5,4,3,2,1,0:T(8,128)} %bitcast.82, f32[8,128]{1,0:T(8,128)} %get-tuple-element.205.refs_3_), custom_call_target="tpu_custom_call" | custom-call | tf_op jit(solution)/shard_map/scatter_sum/pallas_call | solution.py:1287
  589.7 0.8 reshape.86
  590.5 1.3 slice_reduce_fusion
  593.2 0.0 copy-done.4
  593.2 0.0 copy-done.7
  593.3 0.0 copy-done.8
  593.3 0.7 multiply_subtract_fusion.2
  593.9 0.9 fusion.6
  594.9 1.0 copy.33
  595.9 0.0 copy-done.1
  595.9 0.0 copy-done.5
  595.9 0.0 copy-done.6
  595.9 0.8 multiply_subtract_fusion.1
  596.7 0.9 multiply_bitcast_fusion
  597.6 0.1 copy.31
  597.8 0.0 copy-done
  597.8 0.0 copy-done.2
  597.8 0.0 copy-done.3
  597.8 0.9 multiply_subtract_fusion
  (2 shorter events, 0.0 us)
Async XLA Ops:
  508.4 84.8 %copy-start.4 = (f32[8288]{0:T(1024)S(1)}, f32[8288]{0:T(1024)}, u32[]{:S(2)}) copy-start(f32[8288]{0:T(1024)} %param.21) | copy-start | bytes 99460
  508.4 84.8 %copy-start.7 = (f32[8288]{0:T(1024)S(1)}, f32[8288]{0:T(1024)}, u32[]{:S(2)}) copy-start(f32[8288]{0:T(1024)} %param.26) | copy-start | bytes 99460
  508.4 84.8 %copy-start.8 = (f32[8288]{0:T(1024)S(1)}, f32[8288]{0:T(1024)}, u32[]{:S(2)}) copy-start(f32[8288]{0:T(1024)} %param.27) | copy-start | bytes 99460
  508.4 87.4 %copy-start.1 = (f32[32768]{0:T(1024)S(1)}, f32[32768]{0:T(1024)}, u32[]{:S(2)}) copy-start(f32[32768]{0:T(1024)} %param.20) | copy-start | bytes 393220
  508.5 87.4 %copy-start.5 = (f32[32768]{0:T(1024)S(1)}, f32[32768]{0:T(1024)}, u32[]{:S(2)}) copy-start(f32[32768]{0:T(1024)} %param.24) | copy-start | bytes 393220
  508.5 87.4 %copy-start.6 = (f32[32768]{0:T(1024)S(1)}, f32[32768]{0:T(1024)}, u32[]{:S(2)}) copy-start(f32[32768]{0:T(1024)} %param.25) | copy-start | bytes 393220
  508.5 89.3 %copy-start = (f32[53248]{0:T(1024)S(1)}, f32[53248]{0:T(1024)}, u32[]{:S(2)}) copy-start(f32[53248]{0:T(1024)} %param.19) | copy-start | bytes 638980
  508.5 89.3 %copy-start.2 = (f32[53248]{0:T(1024)S(1)}, f32[53248]{0:T(1024)}, u32[]{:S(2)}) copy-start(f32[53248]{0:T(1024)} %param.22) | copy-start | bytes 638980
  508.5 89.3 %copy-start.3 = (f32[53248]{0:T(1024)S(1)}, f32[53248]{0:T(1024)}, u32[]{:S(2)}) copy-start(f32[53248]{0:T(1024)} %param.23) | copy-start | bytes 638980

commit v10 on v9

--- a/solution.py
+++ b/solution.py
@@ -1027,9 +1027,25 @@
     )
 
 
-def gather_kernel(n, *refs):
-    shards, outs = refs[:n], refs[n : 2 * n]
-    send, recv, local = refs[2 * n :]
+def gather_chunks(shapes):
+    out = []
+    for j, (rows, _) in enumerate(shapes):
+        cut = rows // 32 * 16 if rows >= 160 else 0
+        out += [(j, 0, cut), (j, cut, rows - cut)] if cut else [(j, 0, rows)]
+    return out
+
+
+def gather_kernel(shapes, *refs):
+    packs = len(shapes)
+    chunks = gather_chunks(shapes)
+    n = len(chunks)
+    shards = [refs[j].at[pl.ds(a, b)] for j, a, b in chunks]
+    send, recv, local = refs[2 * packs :]
+
+    def view(i, *at):
+        j, a, b = chunks[i]
+        return refs[packs + j].at[at + (slice(None),) * (4 - len(at)) + (pl.ds(a, b),)]
+
     me = Place()
     y, c, z, x = me.y, me.core, me.z, me.x
     m = me.nx
@@ -1046,12 +1062,12 @@
         for copy in copies:
             copy.wait()
 
-    own = [pltpu.make_async_copy(shards[j], outs[j].at[y, c, z, x], local.at[j]) for j in range(n)]
+    own = [pltpu.make_async_copy(shards[j], view(j, y, c, z, x), local.at[j]) for j in range(n)]
     for copy in own:
         copy.start()
 
     def along_z(j):
-        return [push(shards[j], outs[j].at[y, c, z, x], me.at(z=me.next_z(k))) for k in range(1, me.nz)]
+        return [push(shards[j], view(j, y, c, z, x), me.at(z=me.next_z(k))) for k in range(1, me.nz)]
 
     first = along_z(0)
     finish(own)
@@ -1063,7 +1079,7 @@
         shared = []
 
         def second(j):
-            piece = outs[j].at[y, by_core, :, x]
+            piece = view(j, y, by_core, slice(None), x)
             out = []
             for k in range(1, m):
                 out.append(push(piece, piece, me.at(x=me.next_x(k)) if by_core == 0 else me.at(y=me.next_y(k))))
@@ -1071,18 +1087,18 @@
             return out
 
         def third(j):
-            wide = outs[j].at[y, by_core] if by_core == 0 else outs[j].at[:, by_core, :, x]
+            wide = view(j, y, by_core) if by_core == 0 else view(j, slice(None), by_core, slice(None), x)
             out = []
             for k in range(1, m):
                 out.append(push(wide, wide, me.at(y=me.next_y(k)) if by_core == 0 else me.at(x=me.next_x(k))))
             for k in range(1, m):
-                piece = outs[j].at[y, by_core, :, me.next_x(k)] if by_core == 0 else outs[j].at[me.next_y(k), by_core, :, x]
+                piece = view(j, y, by_core, slice(None), me.next_x(k)) if by_core == 0 else view(j, me.next_y(k), by_core, slice(None), x)
                 shared.append(push(piece, piece, sibling))
             return out
 
         def fourth(j):
             for k in range(1, m):
-                wide = outs[j].at[me.next_y(k), by_core] if by_core == 0 else outs[j].at[:, by_core, :, me.next_x(k)]
+                wide = view(j, me.next_y(k), by_core) if by_core == 0 else view(j, slice(None), by_core, slice(None), me.next_x(k))
                 shared.append(push(wide, wide, sibling))
 
         one, two, three = {0: first}, {}, {}
@@ -1091,15 +1107,12 @@
                 finish(one[t])
                 if t + 1 < n:
                     one[t + 1] = along_z(t + 1)
+                two[t] = second(t)
             if 0 < t <= n:
                 finish(two[t - 1])
-            if t < n:
-                two[t] = second(t)
+                three[t - 1] = third(t - 1)
             if t > 1:
                 finish(three[t - 2])
-            if 0 < t <= n:
-                three[t - 1] = third(t - 1)
-            if t > 1:
                 fourth(t - 2)
         finish(shared)
 
@@ -1109,14 +1122,15 @@
 
 def gather_all(shards):
     ny, nz, nx = grid_sizes()
-    n = len(shards)
-    count = n * ((nz - 1) + (nx - 1) + 1 + (nx - 1) * 3)
+    shapes = [s.shape for s in shards]
+    n, parts = len(shards), len(gather_chunks(shapes))
+    count = parts * ((nz - 1) + (nx - 1) + 1 + (nx - 1) * 3)
     return pl.pallas_call(
-        functools.partial(gather_kernel, n),
+        functools.partial(gather_kernel, shapes),
         in_specs=[ANY] * n,
         out_specs=[ANY] * n,
         out_shape=[jax.ShapeDtypeStruct((ny, 2, nz, nx) + s.shape, s.dtype) for s in shards],
-        scratch_shapes=[pltpu.SemaphoreType.DMA((count,)), pltpu.SemaphoreType.DMA((count,)), pltpu.SemaphoreType.DMA((n,))],
+        scratch_shapes=[pltpu.SemaphoreType.DMA((count,)), pltpu.SemaphoreType.DMA((count,)), pltpu.SemaphoreType.DMA((parts,))],
         compiler_params=pltpu.CompilerParams(collective_id=0, has_side_effects=True, vmem_limit_bytes=VMEM_LIMIT),
         name="gather_all",
     )(*shards)
@@ -1605,6 +1619,56 @@
         / (jnp.sqrt(second_new / (1.0 - beta_two**step_count)) + adam_eps)
     )
     return (weight - learn_rate * (corrected + weight_decay * weight), first_new, second_new)
+
+
+def adam_kernel(up_rows, s_mat, s_feed, sums, *refs):
+    old, new, norm_ref, scratch = refs[:6], refs[6:12], refs[12], refs[13:]
+
+    def add_up(x):
+        return jnp.sum(jnp.sum(x, 0, keepdims=True), -1, keepdims=True)
+
+    upscale = (1 << 20) / jnp.maximum(add_up(sums[8:]), 1.0)
+    norm = jnp.sqrt(add_up(sums[:8])) * upscale
+    factor = upscale * (clip_norm / jnp.maximum(norm, clip_norm))
+    norm_ref[0:1] = jnp.broadcast_to(norm, (1, HALF))
+    norm_ref[1:2] = jnp.broadcast_to(factor, (1, HALF))
+
+    def spread(src, dst):
+        rows = src.shape[0]
+        value = src[...] * factor
+        dst[pl.ds(0, rows, stride=2), :] = value[:, :HALF]
+        dst[pl.ds(1, rows, stride=2), :] = value[:, HALF:]
+
+    spread(s_mat, scratch[0])
+    up = lax.axis_index("dp") * 2 < lax.axis_size("dp")
+    pl.when(jnp.logical_not(up))(lambda: spread(s_feed, scratch[1]))
+
+    @pl.when(up)
+    def _():
+        for half in range(2):
+            value = s_feed[half * up_rows : (half + 1) * up_rows] * factor
+            scratch[1][pl.ds(2 * half, up_rows, stride=4), :] = value[:, :HALF]
+            scratch[1][pl.ds(2 * half + 1, up_rows, stride=4), :] = value[:, HALF:]
+
+    for k in range(2):
+        values = adam_update(*[ref[...] for ref in old[3 * k : 3 * k + 3]], scratch[k][...])
+        for ref, value in zip(new[3 * k : 3 * k + 3], values):
+            ref[...] = value
+
+
+def adam_packs(s_mat, s_feed, sums, old, up_rows):
+    args = [s_mat, s_feed, sums] + old
+    outs = [x.shape for x in old] + [(8, HALF)]
+    return pl.pallas_call(
+        functools.partial(adam_kernel, up_rows),
+        grid=(1,),
+        in_specs=[whole(x.shape) for x in args],
+        out_specs=[whole(s) for s in outs],
+        out_shape=[jax.ShapeDtypeStruct(s, F32) for s in outs],
+        scratch_shapes=[pltpu.VMEM(old[0].shape, F32), pltpu.VMEM(old[3].shape, F32)],
+        compiler_params=params_spec(),
+        name="adam_packs",
+    )(*args)
 
 
 def gradient_parts(ready, model, extras, up_rows, group_stats, group_sum, nf, devices):
@@ -1665,19 +1729,10 @@
     ny, nz, nx = grid_sizes()
     lead = (ny, 2, nz, nx)
     s_mat, s_feed, s_vec, sums = scatter_sum([g.reshape(lead + (-1, D)) for g in (g_mat, g_feed, g_vec)], tile)
-    is_up = lax.axis_index("dp") * 2 < nd
-    halves_of = s_feed.reshape(2, up_rows, D)
-    s_feed = jnp.where(is_up, jnp.concatenate([halves_of[0], halves_of[1]], 1).reshape(-1), s_feed.reshape(-1))
-    grads = (s_mat.reshape(-1), s_feed, s_vec.reshape(-1)[:own])
-    upscale = (1 << 20) / jnp.maximum(jnp.sum(sums[8:]), 1.0)
-    grad_norm = jnp.sqrt(jnp.sum(sums[:8])) * upscale
-    factor = upscale * (clip_norm / jnp.maximum(grad_norm, clip_norm))
-    new = (
-        adam_update(matrices, matrices_first, matrices_second, grads[0] * factor)
-        + adam_update(feed_weights, feed_first, feed_second, grads[1] * factor)
-        + adam_update(vectors, vectors_first, vectors_second, grads[2] * factor)
-    )
-    return (grad_norm,) + new
+    old = [matrices, matrices_first, matrices_second, feed_weights, feed_first, feed_second]
+    *new, norm = adam_packs(s_mat, s_feed, sums, [x.reshape(-1, HALF) for x in old], up_rows)
+    vec_new = adam_update(vectors, vectors_first, vectors_second, s_vec.reshape(-1)[:own] * norm[1, 0])
+    return (norm[0, 0], *[x.reshape(-1) for x in new], *vec_new)
 
 
 def solution(mesh):

time: 608 us -> 598 us (0.984)
    pallas_call x1 -> x2, Pallas kernels: 50.1 us -> 47.7 us  [the longest x1 45.1 us: gather_all(): pl.pallas_call(functools.partial(gather_kernel, shapes), in_specs=[ANY] *...]
where the time goes in v10:
time: 598 us; the launch traced here: 590 us
  Pallas kernels  581 us (97%)
  local copies, waits for them, and re-layouts  6.03 us (1%)
    pallas_call x2, Pallas kernels, time_bwd(): pl.pallas_call(functools.partial(time_bwd_kernel, first, count, group, la...  97.2 us
    pallas_call x1, Pallas kernels, scatter_sum(): pl.pallas_call(functools.partial(scatter_kernel, shapes), in_specs=[ANY]...  81.2 us
    pallas_call x2, Pallas kernels, group_stats(): pl.pallas_call(functools.partial(stats_kernel, per), in_specs=[ANY], out_...  63.6 us
    pallas_call x2, Pallas kernels, group_sum(): pl.pallas_call(functools.partial(sum_kernel, per, steps - steps // 4), gr...  61 us
    pallas_call x2, Pallas kernels, time_fwd(): pl.pallas_call(functools.partial(time_fwd_kernel, first, count, group), g...  58.8 us
    pallas_call x1, Pallas kernels, gather_all(): pl.pallas_call(functools.partial(gather_kernel, shapes), in_specs=[ANY] *...  45.1 us
    pallas_call x1, Pallas kernels, recv_bwd(): pl.pallas_call(functools.partial(recv_bwd_kernel, sb), grid=(n // sb,), i...  43.6 us
    pallas_call x2, Pallas kernels, send_bwd(): pl.pallas_call(functools.partial(send_bwd_kernel, sb, layer), grid=(n //...  39.9 us

profile of v10, /device:TPU:0, one launch (start us, length us, event | category | flops | bytes accessed | tf_op | source)
XLA Modules:
  0.0 590.3 jit_solution(8723853797131610974)
XLA Ops:
  1.3 1.4 pad_bitcast_fusion.vec_ref
  2.7 4.5 prepare.1
  7.2 45.1 %gather_all.1 = (bf16[2,2,4,2,208,256]{5,4,3,2,1,0:T(8,128)(2,1)}, bf16[2,2,4,2,128,256]{5,4,3,2,1,0:T(8,128)(2,1)}, bf16[2,2,4,2,33,256]{5,4,3,2,1,0:T(8,128)(2,1)}) custom-call(bf16[208,256]{1,0:T(8,128)(2,1)} %get-tuple-element.118.refs_0_, bf16[128,256]{1,0:T(8,128)(2,1)} %get-tuple-element.119.refs_1_, bf16[33,256]{1,0:T(8,128)(2,1)} %get-tuple-element.120.refs_2_), custom_call_target="tpu_custom_call" | custom-call | tf_op jit(solution)/shard_map/gather_all/pallas_call | solution.py:1128
  52.3 2.7 unpack_vectors.1
  55.0 1.3 slice.13
  56.3 1.3 reshape.96.refs_7_.refs_5_.refs_15_.refs_11_.refs_17_
  57.6 35.6 %time_fwd.2 = (f32[60,64,256]{2,1,0:T(8,128)}, f32[8,2,512,128]{3,2,1,0:T(8,128)}, f32[8,2,512,128]{3,2,1,0:T(8,128)}, f32[8,2,512,128]{3,2,1,0:T(8,128)}, f32[8...) custom-call(f32[60,64,16]{2,1,0:T(8,128)} %get-tuple-element.117.ref, ...), custom_call_target="tpu_custom_call" | custom-call | tf_op jit(solution)/shard_map/time_fwd/pallas_call | solution.py:367
  93.2 10.0 %send_fwd.2.in_ref = f32[64,24,128]{2,1,0:T(8,128)} custom-call(f32[60,64,256]{2,1,0:T(8,128)} %get-tuple-element.127.dim_ref.send_ref, f32[60,16,256]{2,1,0:T(8,128)} %get-tuple-element.128.r_ref, f32[64,128]{1,0:T(8,128)} %get-tuple-element.129.here_ref, bf16[26,256,256]{2,1,0:T(8,128)(2,1)} %bitcast.34, bf16[26,256,256]{2,1,0:T(8,128)(2,1)} %bitcast.35, ...), custom_call_target="tpu_custom_call" | custom-call | tf_op jit(solution)/shard_map/send_fwd/pallas_call | solution.py:894
  103.2 37.7 %group_stats.2.o_ref = f32[64,24,128]{2,1,0:T(8,128)} custom-call(f32[64,24,128]{2,1,0:T(8,128)} %send_fwd.2.in_ref), custom_call_target="tpu_custom_call" | custom-call | tf_op jit(solution)/shard_map/group_stats/pallas_call | solution.py:1438
  140.9 26.2 %recv_fwd.1 = (f32[30,64,256]{2,1,0:T(8,128)}, f32[3840,256]{1,0:T(8,128)}, f32[3840,256]{1,0:T(8,128)}, f32[3840,128]{1,0:T(8,128)}, f32[3840,256]{1,0:T(8,128)...) custom-call(f32[60,64,256]{2,1,0:T(8,128)} %get-tuple-element.127.dim_ref.send_ref, f32[64,24,128]{2,1,0:T(8,128)} %group_stats.2.o_ref, ...), custom_call_target="tpu_custom_call" | custom-call | tf_op jit(solution)/shard_map/recv_fwd/pallas_call | solution.py:715
  167.1 23.2 %time_fwd.3 = (f32[30,64,256]{2,1,0:T(8,128)}, f32[8,2,256,128]{3,2,1,0:T(8,128)}, f32[8,2,256,128]{3,2,1,0:T(8,128)}, f32[8,2,256,128]{3,2,1,0:T(8,128)}, f32[8...) custom-call(f32[30,64,256]{2,1,0:T(8,128)} %get-tuple-element.131.re, ...), custom_call_target="tpu_custom_call" | custom-call | tf_op jit(solution)/shard_map/time_fwd/pallas_call | solution.py:367
  190.2 6.7 %send_fwd.3.in_ref = f32[32,24,128]{2,1,0:T(8,128)} custom-call(f32[30,64,256]{2,1,0:T(8,128)} %get-tuple-element.132.dim_ref.send_ref, f32[30,16,256]{2,1,0:T(8,128)} %get-tuple-element.133.r_ref, f32[64,128]{1,0:T(8,128)} %get-tuple-element.129.here_ref, bf16[26,256,256]{2,1,0:T(8,128)(2,1)} %bitcast.47, bf16[26,256,256]{2,1,0:T(8,128)(2,1)} %bitcast.48, ...), custom_call_target="tpu_custom_call" | custom-call | tf_op jit(solution)/shard_map/send_fwd/pallas_call | solution.py:894
  196.9 25.9 %group_stats.3.o_ref = f32[32,24,128]{2,1,0:T(8,128)} custom-call(f32[32,24,128]{2,1,0:T(8,128)} %send_fwd.3.in_ref), custom_call_target="tpu_custom_call" | custom-call | tf_op jit(solution)/shard_map/group_stats/pallas_call | solution.py:1438
  222.9 34.6 %tail.1 = (f32[26,256,256]{2,1,0:T(8,128)}, f32[4096,256]{1,0:T(8,128)}, f32[30,64,256]{2,1,0:T(8,128)}, f32[640,128]{1,0:T(8,128)}, f32[11,8,256]{2,1,0:T(8,128...) custom-call(f32[30,64,256]{2,1,0:T(8,128)} %get-tuple-element.132.di, ...), custom_call_target="tpu_custom_call" | custom-call | tf_op jit(solution)/shard_map/tail/pallas_call | solution.py:836
  257.5 25.6 %group_sum.2 = (f32[640,128]{1,0:T(8,128)}, f32[256,256]{1,0:T(8,128)}, f32[256,256]{1,0:T(8,128)}, f32[256,512]{1,0:T(8,128)}, f32[512,256]{1,0:T(8,128)}) custom-call(f32[640,128]{1,0:T(8,128)} %get-tuple-element.140.in_ref, f32[1920,256]{1,0:T(8,128)} %bitcast.85, f32[1920,256]{1,0:T(8,128)} %get-tuple-element.141.mixed_ref, ...), custom_call_target="tpu_custom_call" | custom-call | tf_op jit(solution)/shard_map/group_sum/pallas_call | solution.py:1455
  283.1 14.7 %send_bwd.2 = (f32[26,256,256]{2,1,0:T(8,128)}, f32[30,64,256]{2,1,0:T(8,128)}, f32[30,16,256]{2,1,0:T(8,128)}, f32[2,8,256]{2,1,0:T(8,128)}) custom-call(f32[30,64,256]{2,1,0:T(8,128)} %get-tuple-element.132.dim_ref.send_ref, f32[30,64,256]{2,1,0:T(8,128)} %get-tuple-element.139.dpart_ref, ...), custom_call_target="tpu_custom_call", output_to_operand_aliasing={{0}: (10, {})} | custom-call | tf_op jit(solution)/shard_map/send_bwd/pallas_call | solution.py:958
  297.9 34.6 %time_bwd.2 = (f32[26,256,256]{2,1,0:T(8,128)}, f32[4096,256]{1,0:T(8,128)}, f32[10,8,256]{2,1,0:T(8,128)}, f32[30,64,256]{2,1,0:T(8,128)}) custom-call(f32[30,64,256]{2,1,0:T(8,128)} %get-tuple-element.131.refs_0_, f32[30,64,256]{2,1,0:T(8,128)} %get-tuple-element.150.refs_1_, ...), custom_call_target="tpu_custom_call", output_to_operand_aliasing={{0}: (22, {}), {1}: (23, {})} | custom-call | tf_op jit(solution)/shard_map/time_bwd/pallas_call | solution.py:490
  332.5 43.6 %recv_bwd.1 = (f32[26,256,256]{2,1,0:T(8,128)}, f32[60,64,256]{2,1,0:T(8,128)}, f32[1216,128]{1,0:T(8,128)}, f32[11,8,256]{2,1,0:T(8,128)}, f32[5,8,256]{2,1,0:T...) custom-call(f32[60,64,256]{2,1,0:T(8,128)} %get-tuple-element.127.di, ...), custom_call_target="tpu_custom_call", output_to_operand_aliasing={{0}: (19, {})} | custom-call | tf_op jit(solution)/shard_map/recv_bwd/pallas_call | solution.py:783
  376.0 35.4 %group_sum.3 = (f32[1216,128]{1,0:T(8,128)}, f32[256,256]{1,0:T(8,128)}, f32[256,256]{1,0:T(8,128)}, f32[256,512]{1,0:T(8,128)}, f32[512,256]{1,0:T(8,128)}) custom-call(f32[1216,128]{1,0:T(8,128)} %get-tuple-element.175.in_ref, f32[3840,256]{1,0:T(8,128)} %bitcast.83, f32[3840,256]{1,0:T(8,128)} %get-tuple-element.168.refs_1_.mixed_ref, ...), custom_call_target="tpu_custom_call" | custom-call | tf_op jit(solution)/shard_map/group_sum/pallas_call | solution.py:1455
  411.4 25.1 %send_bwd.3 = (f32[26,256,256]{2,1,0:T(8,128)}, f32[60,64,256]{2,1,0:T(8,128)}, f32[60,16,256]{2,1,0:T(8,128)}, f32[2,8,256]{2,1,0:T(8,128)}) custom-call(f32[60,64,256]{2,1,0:T(8,128)} %get-tuple-element.127.dim_ref.send_ref, f32[60,64,256]{2,1,0:T(8,128)} %get-tuple-element.174.dpart_ref, ...), custom_call_target="tpu_custom_call", output_to_operand_aliasing={{0}: (10, {})} | custom-call | tf_op jit(solution)/shard_map/send_bwd/pallas_call | solution.py:958
  436.6 62.6 %time_bwd.3 = (f32[26,256,256]{2,1,0:T(8,128)}, f32[4096,256]{1,0:T(8,128)}, f32[10,8,256]{2,1,0:T(8,128)}, f32[16,256]{1,0:T(8,128)}, f32[480,256]{1,0:T(8,128)}) custom-call(f32[60,64,16]{2,1,0:T(8,128)} %get-tuple-element.117.refs_0_, bf16[16,256]{1,0:T(8,128)(2,1)} %get-tuple-element.122.refs_1_, ...), custom_call_target="tpu_custom_call", output_to_operand_aliasing={{0}: (24, {}), {1}: (25, {})} | custom-call | tf_op jit(solution)/shard_map/time_bwd/pallas_call | solution.py:490
  499.1 3.6 assemble_vectors.1
  502.7 0.0 copy-start
  502.7 0.0 copy-start.1
  502.7 0.0 copy-start.2
  502.7 81.2 %scatter_sum.1 = (f32[208,256]{1,0:T(8,128)}, f32[128,256]{1,0:T(8,128)}, f32[33,256]{1,0:T(8,128)}, f32[16,128]{1,0:T(8,128)}) custom-call(f32[2,2,4,2,208,256]{5,4,3,2,1,0:T(8,128)} %bitcast.75, f32[2,2,4,2,128,256]{5,4,3,2,1,0:T(8,128)} %bitcast.84, f32[2,2,4,2,33,256]{5,4,3,2,1,0:T(8,128)} %bitcast.86, f32[8,128]{1,0:T(8,128)} %get-tuple-element.212.refs_3_), custom_call_target="tpu_custom_call" | custom-call | tf_op jit(solution)/shard_map/scatter_sum/pallas_call | solution.py:1301
  584.0 0.8 reshape.112
  584.8 2.6 adam_packs.1
  587.4 1.3 fusion.2
  588.6 0.0 copy-done
  588.6 0.0 copy-done.1
  588.6 0.0 copy-done.2
  588.6 1.2 multiply_subtract_fusion
Async XLA Ops:
  502.7 85.9 %copy-start = (f32[8288]{0:T(1024)S(1)}, f32[8288]{0:T(1024)}, u32[]{:S(2)}) copy-start(f32[8288]{0:T(1024)} %param.21) | copy-start | bytes 99460
  502.7 85.9 %copy-start.1 = (f32[8288]{0:T(1024)S(1)}, f32[8288]{0:T(1024)}, u32[]{:S(2)}) copy-start(f32[8288]{0:T(1024)} %param.26) | copy-start | bytes 99460
  502.7 85.9 %copy-start.2 = (f32[8288]{0:T(1024)S(1)}, f32[8288]{0:T(1024)}, u32[]{:S(2)}) copy-start(f32[8288]{0:T(1024)} %param.27) | copy-start | bytes 99460

commit v11 on v10

--- a/solution.py
+++ b/solution.py
@@ -1369,21 +1369,24 @@
     dst = lax.broadcasted_iota(jnp.int32, (HALF, D), 1)
     widen = jnp.where(src % 8 == dst // 32, 1.0, 0.0).astype(BF)
 
-    def one(s, carry):
-        lse = [got[d, s, 2 * ROUT : 2 * ROUT + 1, :] for d in range(nf)]
-        top = functools.reduce(jnp.maximum, lse)
-        total = top + jnp.log(functools.reduce(jnp.add, [jnp.exp(l - top) for l in lse]))
-        out = jnp.where(row == 2 * ROUT, total, 0.0)
-        share = jnp.concatenate([jnp.where(chosen, jnp.exp(l - total), 0.0) for l in lse], 0)
-        wide = mmw(split2(share), widen)
-        for d in range(nf):
-            w = wide[d * PACK : (d + 1) * PACK]
+    segs, devs = range(per), range(nf)
+    lse = [[got[d, s, 2 * ROUT : 2 * ROUT + 1, :] for d in devs] for s in segs]
+    tops = [functools.reduce(jnp.maximum, l) for l in lse]
+    totals = [t + jnp.log(functools.reduce(jnp.add, [jnp.exp(x - t) for x in l])) for t, l in zip(tops, lse)]
+    shares = [
+        jnp.concatenate([jnp.where(chosen, jnp.exp(x - t), 0.0) for x in l], 0) for t, l in zip(totals, lse)
+    ]
+    wide = [mmw(split2(x), widen) for x in shares]
+    outs = []
+    for s in segs:
+        out = jnp.where(row == 2 * ROUT, totals[s], 0.0)
+        for d in devs:
+            w = wide[s][d * PACK : (d + 1) * PACK]
             w = jnp.where(row < ROUT, w[:, :HALF], w[:, HALF:])
             out = out + jnp.where(row < 2 * ROUT, w * got[d, s], 0.0)
-        result[s] = out
-        return carry
-
-    lax.fori_loop(0, per, one, 0)
+        outs.append(out)
+    for s in segs:
+        result[s] = outs[s]
     copies = group_back(per, result, out_ref, send, recv, local)
     start_all(copies)
     wait_all(copies)

time: 598 us -> 594 us (level)
  no operation moved by 1% of the time
where the time goes in v11:
time: 594 us; the launch traced here: 586 us
  Pallas kernels  577 us (97%)
  local copies, waits for them, and re-layouts  6.03 us (1%)
    pallas_call x2, Pallas kernels, time_bwd(): pl.pallas_call(functools.partial(time_bwd_kernel, first, count, group, la...  97.2 us
    pallas_call x1, Pallas kernels, scatter_sum(): pl.pallas_call(functools.partial(scatter_kernel, shapes), in_specs=[ANY]...  80.2 us
    pallas_call x2, Pallas kernels, group_stats(): pl.pallas_call(functools.partial(stats_kernel, per), in_specs=[ANY], out_...  62.8 us
    pallas_call x2, Pallas kernels, group_sum(): pl.pallas_call(functools.partial(sum_kernel, per, steps - steps // 4), gr...  58.9 us
    pallas_call x2, Pallas kernels, time_fwd(): pl.pallas_call(functools.partial(time_fwd_kernel, first, count, group), g...  58.8 us
    pallas_call x1, Pallas kernels, gather_all(): pl.pallas_call(functools.partial(gather_kernel, shapes), in_specs=[ANY] *...  45.1 us
    pallas_call x1, Pallas kernels, recv_bwd(): pl.pallas_call(functools.partial(recv_bwd_kernel, sb), grid=(n // sb,), i...  43.6 us
    pallas_call x2, Pallas kernels, send_bwd(): pl.pallas_call(functools.partial(send_bwd_kernel, sb, layer), grid=(n //...  39.8 us

profile of v11, /device:TPU:0, one launch (start us, length us, event | category | flops | bytes accessed | tf_op | source)
XLA Modules:
  0.0 586.2 jit_solution(9910685475232879673)
XLA Ops:
  1.3 1.4 pad_bitcast_fusion.vec_ref
  2.7 4.5 prepare.1
  7.2 45.1 %gather_all.1 = (bf16[2,2,4,2,208,256]{5,4,3,2,1,0:T(8,128)(2,1)}, bf16[2,2,4,2,128,256]{5,4,3,2,1,0:T(8,128)(2,1)}, bf16[2,2,4,2,33,256]{5,4,3,2,1,0:T(8,128)(2,1)}) custom-call(bf16[208,256]{1,0:T(8,128)(2,1)} %get-tuple-element.118.refs_0_, bf16[128,256]{1,0:T(8,128)(2,1)} %get-tuple-element.119.refs_1_, bf16[33,256]{1,0:T(8,128)(2,1)} %get-tuple-element.120.refs_2_), custom_call_target="tpu_custom_call" | custom-call | tf_op jit(solution)/shard_map/gather_all/pallas_call | solution.py:1128
  52.3 2.7 unpack_vectors.1
  55.0 1.3 slice.13
  56.3 1.3 reshape.96.refs_7_.refs_5_.refs_15_.refs_11_.refs_17_
  57.6 35.6 %time_fwd.2 = (f32[60,64,256]{2,1,0:T(8,128)}, f32[8,2,512,128]{3,2,1,0:T(8,128)}, f32[8,2,512,128]{3,2,1,0:T(8,128)}, f32[8,2,512,128]{3,2,1,0:T(8,128)}, f32[8...) custom-call(f32[60,64,16]{2,1,0:T(8,128)} %get-tuple-element.117.ref, ...), custom_call_target="tpu_custom_call" | custom-call | tf_op jit(solution)/shard_map/time_fwd/pallas_call | solution.py:367
  93.2 10.0 %send_fwd.2.in_ref = f32[64,24,128]{2,1,0:T(8,128)} custom-call(f32[60,64,256]{2,1,0:T(8,128)} %get-tuple-element.127.dim_ref.send_ref, f32[60,16,256]{2,1,0:T(8,128)} %get-tuple-element.128.r_ref, f32[64,128]{1,0:T(8,128)} %get-tuple-element.129.here_ref, bf16[26,256,256]{2,1,0:T(8,128)(2,1)} %bitcast.34, bf16[26,256,256]{2,1,0:T(8,128)(2,1)} %bitcast.35, ...), custom_call_target="tpu_custom_call" | custom-call | tf_op jit(solution)/shard_map/send_fwd/pallas_call | solution.py:894
  103.2 36.4 %group_stats.2.o_ref = f32[64,24,128]{2,1,0:T(8,128)} custom-call(f32[64,24,128]{2,1,0:T(8,128)} %send_fwd.2.in_ref), custom_call_target="tpu_custom_call" | custom-call | tf_op jit(solution)/shard_map/group_stats/pallas_call | solution.py:1441
  139.7 26.2 %recv_fwd.1 = (f32[30,64,256]{2,1,0:T(8,128)}, f32[3840,256]{1,0:T(8,128)}, f32[3840,256]{1,0:T(8,128)}, f32[3840,128]{1,0:T(8,128)}, f32[3840,256]{1,0:T(8,128)...) custom-call(f32[60,64,256]{2,1,0:T(8,128)} %get-tuple-element.127.dim_ref.send_ref, f32[64,24,128]{2,1,0:T(8,128)} %group_stats.2.o_ref, ...), custom_call_target="tpu_custom_call" | custom-call | tf_op jit(solution)/shard_map/recv_fwd/pallas_call | solution.py:715
  165.8 23.2 %time_fwd.3 = (f32[30,64,256]{2,1,0:T(8,128)}, f32[8,2,256,128]{3,2,1,0:T(8,128)}, f32[8,2,256,128]{3,2,1,0:T(8,128)}, f32[8,2,256,128]{3,2,1,0:T(8,128)}, f32[8...) custom-call(f32[30,64,256]{2,1,0:T(8,128)} %get-tuple-element.131.re, ...), custom_call_target="tpu_custom_call" | custom-call | tf_op jit(solution)/shard_map/time_fwd/pallas_call | solution.py:367
  189.0 6.7 %send_fwd.3.in_ref = f32[32,24,128]{2,1,0:T(8,128)} custom-call(f32[30,64,256]{2,1,0:T(8,128)} %get-tuple-element.132.dim_ref.send_ref, f32[30,16,256]{2,1,0:T(8,128)} %get-tuple-element.133.r_ref, f32[64,128]{1,0:T(8,128)} %get-tuple-element.129.here_ref, bf16[26,256,256]{2,1,0:T(8,128)(2,1)} %bitcast.47, bf16[26,256,256]{2,1,0:T(8,128)(2,1)} %bitcast.48, ...), custom_call_target="tpu_custom_call" | custom-call | tf_op jit(solution)/shard_map/send_fwd/pallas_call | solution.py:894
  195.7 26.3 %group_stats.3.o_ref = f32[32,24,128]{2,1,0:T(8,128)} custom-call(f32[32,24,128]{2,1,0:T(8,128)} %send_fwd.3.in_ref), custom_call_target="tpu_custom_call" | custom-call | tf_op jit(solution)/shard_map/group_stats/pallas_call | solution.py:1441
  222.0 34.6 %tail.1 = (f32[26,256,256]{2,1,0:T(8,128)}, f32[4096,256]{1,0:T(8,128)}, f32[30,64,256]{2,1,0:T(8,128)}, f32[640,128]{1,0:T(8,128)}, f32[11,8,256]{2,1,0:T(8,128...) custom-call(f32[30,64,256]{2,1,0:T(8,128)} %get-tuple-element.132.di, ...), custom_call_target="tpu_custom_call" | custom-call | tf_op jit(solution)/shard_map/tail/pallas_call | solution.py:836
  256.6 24.5 %group_sum.2 = (f32[640,128]{1,0:T(8,128)}, f32[256,256]{1,0:T(8,128)}, f32[256,256]{1,0:T(8,128)}, f32[256,512]{1,0:T(8,128)}, f32[512,256]{1,0:T(8,128)}) custom-call(f32[640,128]{1,0:T(8,128)} %get-tuple-element.140.in_ref, f32[1920,256]{1,0:T(8,128)} %bitcast.85, f32[1920,256]{1,0:T(8,128)} %get-tuple-element.141.mixed_ref, ...), custom_call_target="tpu_custom_call" | custom-call | tf_op jit(solution)/shard_map/group_sum/pallas_call | solution.py:1458
  281.2 14.7 %send_bwd.2 = (f32[26,256,256]{2,1,0:T(8,128)}, f32[30,64,256]{2,1,0:T(8,128)}, f32[30,16,256]{2,1,0:T(8,128)}, f32[2,8,256]{2,1,0:T(8,128)}) custom-call(f32[30,64,256]{2,1,0:T(8,128)} %get-tuple-element.132.dim_ref.send_ref, f32[30,64,256]{2,1,0:T(8,128)} %get-tuple-element.139.dpart_ref, ...), custom_call_target="tpu_custom_call", output_to_operand_aliasing={{0}: (10, {})} | custom-call | tf_op jit(solution)/shard_map/send_bwd/pallas_call | solution.py:958
  295.9 34.6 %time_bwd.2 = (f32[26,256,256]{2,1,0:T(8,128)}, f32[4096,256]{1,0:T(8,128)}, f32[10,8,256]{2,1,0:T(8,128)}, f32[30,64,256]{2,1,0:T(8,128)}) custom-call(f32[30,64,256]{2,1,0:T(8,128)} %get-tuple-element.131.refs_0_, f32[30,64,256]{2,1,0:T(8,128)} %get-tuple-element.150.refs_1_, ...), custom_call_target="tpu_custom_call", output_to_operand_aliasing={{0}: (22, {}), {1}: (23, {})} | custom-call | tf_op jit(solution)/shard_map/time_bwd/pallas_call | solution.py:490
  330.5 43.6 %recv_bwd.1 = (f32[26,256,256]{2,1,0:T(8,128)}, f32[60,64,256]{2,1,0:T(8,128)}, f32[1216,128]{1,0:T(8,128)}, f32[11,8,256]{2,1,0:T(8,128)}, f32[5,8,256]{2,1,0:T...) custom-call(f32[60,64,256]{2,1,0:T(8,128)} %get-tuple-element.127.di, ...), custom_call_target="tpu_custom_call", output_to_operand_aliasing={{0}: (19, {})} | custom-call | tf_op jit(solution)/shard_map/recv_bwd/pallas_call | solution.py:783
  374.1 34.4 %group_sum.3 = (f32[1216,128]{1,0:T(8,128)}, f32[256,256]{1,0:T(8,128)}, f32[256,256]{1,0:T(8,128)}, f32[256,512]{1,0:T(8,128)}, f32[512,256]{1,0:T(8,128)}) custom-call(f32[1216,128]{1,0:T(8,128)} %get-tuple-element.175.in_ref, f32[3840,256]{1,0:T(8,128)} %bitcast.83, f32[3840,256]{1,0:T(8,128)} %get-tuple-element.168.refs_1_.mixed_ref, ...), custom_call_target="tpu_custom_call" | custom-call | tf_op jit(solution)/shard_map/group_sum/pallas_call | solution.py:1458
  408.5 25.1 %send_bwd.3 = (f32[26,256,256]{2,1,0:T(8,128)}, f32[60,64,256]{2,1,0:T(8,128)}, f32[60,16,256]{2,1,0:T(8,128)}, f32[2,8,256]{2,1,0:T(8,128)}) custom-call(f32[60,64,256]{2,1,0:T(8,128)} %get-tuple-element.127.dim_ref.send_ref, f32[60,64,256]{2,1,0:T(8,128)} %get-tuple-element.174.dpart_ref, ...), custom_call_target="tpu_custom_call", output_to_operand_aliasing={{0}: (10, {})} | custom-call | tf_op jit(solution)/shard_map/send_bwd/pallas_call | solution.py:958
  433.6 62.6 %time_bwd.3 = (f32[26,256,256]{2,1,0:T(8,128)}, f32[4096,256]{1,0:T(8,128)}, f32[10,8,256]{2,1,0:T(8,128)}, f32[16,256]{1,0:T(8,128)}, f32[480,256]{1,0:T(8,128)}) custom-call(f32[60,64,16]{2,1,0:T(8,128)} %get-tuple-element.117.refs_0_, bf16[16,256]{1,0:T(8,128)(2,1)} %get-tuple-element.122.refs_1_, ...), custom_call_target="tpu_custom_call", output_to_operand_aliasing={{0}: (24, {}), {1}: (25, {})} | custom-call | tf_op jit(solution)/shard_map/time_bwd/pallas_call | solution.py:490
  496.2 3.6 assemble_vectors.1
  499.8 0.0 copy-start
  499.8 0.0 copy-start.1
  499.8 0.0 copy-start.2
  499.8 80.2 %scatter_sum.1 = (f32[208,256]{1,0:T(8,128)}, f32[128,256]{1,0:T(8,128)}, f32[33,256]{1,0:T(8,128)}, f32[16,128]{1,0:T(8,128)}) custom-call(f32[2,2,4,2,208,256]{5,4,3,2,1,0:T(8,128)} %bitcast.75, f32[2,2,4,2,128,256]{5,4,3,2,1,0:T(8,128)} %bitcast.84, f32[2,2,4,2,33,256]{5,4,3,2,1,0:T(8,128)} %bitcast.86, f32[8,128]{1,0:T(8,128)} %get-tuple-element.212.refs_3_), custom_call_target="tpu_custom_call" | custom-call | tf_op jit(solution)/shard_map/scatter_sum/pallas_call | solution.py:1301
  579.9 0.8 reshape.112
  580.7 2.6 adam_packs.1
  583.3 1.3 fusion.2
  584.6 0.0 copy-done
  584.6 0.0 copy-done.1
  584.6 0.0 copy-done.2
  584.6 1.2 multiply_subtract_fusion
Async XLA Ops:
  499.8 84.8 %copy-start = (f32[8288]{0:T(1024)S(1)}, f32[8288]{0:T(1024)}, u32[]{:S(2)}) copy-start(f32[8288]{0:T(1024)} %param.21) | copy-start | bytes 99460
  499.8 84.8 %copy-start.1 = (f32[8288]{0:T(1024)S(1)}, f32[8288]{0:T(1024)}, u32[]{:S(2)}) copy-start(f32[8288]{0:T(1024)} %param.26) | copy-start | bytes 99460
  499.8 84.8 %copy-start.2 = (f32[8288]{0:T(1024)S(1)}, f32[8288]{0:T(1024)}, u32[]{:S(2)}) copy-start(f32[8288]{0:T(1024)} %param.27) | copy-start | bytes 99460
